TPU v7x, 32 devices: a whole 2x2x4 slice. The times are simulated.
32 devices in a mesh: date: 8 (over y, x, core), bucket: 4 (over z).
Axes of the slice: x: 2, y: 2, z: 4, core: 2. Of those that a mesh axis runs over, the one named last changes fastest.
Arguments:
- transition: bfloat16 [32, 8, 512, 512], P('date', 'bucket'), may hold values from -1 to 1, as said below
- shocks: bfloat16 [32, 8, 512, 16, 128], P('date', 'bucket'), may hold values from -1.5 to 1.5
- step_days: int32 [32], P('date'), may hold values from 7 to 31
- readout: bfloat16 [8, 64, 512], P('bucket'), may hold values from -0.25 to 0.25
- risk_weight: float32 [8, 64], P('bucket'), may hold values from 0.05 to 0.5
- correlation: float32 [8, 64, 64], P('bucket'), may hold values from -1 to 1, as said below
- cross_gamma: float32 [8, 8], replicated, may hold values from 0.1 to 0.3
- discount: float32 [32, 16, 128], P('date', 'bucket'), may hold values from 0.1 to 1
- path_counts: int32 [16], replicated, may hold values from 64 to 128
Outputs:
- margin: float32 [32, 16, 128], P('date', 'bucket')
- adjustment: float32 [], replicated
Inputs may be any that keep to these rules, and one draw needn't show every extreme that they name: Each matrix transition[t, b] has entries of magnitude at most one. Each correlation[b] is symmetric positive definite with unit diagonal.
All inputs are finite; a program needn't handle non-finite values.
Results may differ from a plain program's by a relative error of at most 0.013.
Values may be sent and summed in bfloat16 or wider, within the bound.
No kernel may reach another device: no remote copies, remote signals or barrier semaphores. Data moves between devices by JAX's collectives and lax.ppermute only.
A program may use at most 64 MiB of HBM per device.

v0:
```python
import jax
import jax.numpy as jnp
from jax import lax
from jax.sharding import PartitionSpec as P

epsilon = 1e-06


def shifted(x, axis, by):
    count = lax.axis_size(axis)
    pairs = [(i, i + by) for i in range(count) if 0 <= i + by < count]
    return lax.ppermute(x, axis, pairs)


def advance_section(carried, shock_slice, scales, transition, readout, risk_weight, correlation):
    within_list = []
    net_list = []
    for date_local in range(transition.shape[0]):
        propagated = jnp.einsum(
            "bij,bjp->bip", transition[date_local], carried, preferred_element_type=jnp.float32
        )
        carried = (
            propagated + scales[date_local] * shock_slice[date_local].astype(jnp.float32)
        ).astype(jnp.bfloat16)
        sensitivity = jnp.einsum(
            "bsf,bfp->bsp", readout, carried, preferred_element_type=jnp.float32
        )
        weighted = risk_weight[:, :, None] * sensitivity
        correlated = jnp.einsum(
            "bst,btp->bsp", correlation, weighted, precision=lax.Precision.HIGHEST
        )
        within_sq = jnp.sum(weighted * correlated, axis=1) + epsilon
        within_root = jnp.sqrt(within_sq)
        net_sum = jnp.clip(jnp.sum(weighted, axis=1), -within_root, within_root)
        within_list.append(within_sq)
        net_list.append(net_sum)
    return (carried, jnp.stack(within_list), jnp.stack(net_list))


def shards(
    transition,
    shocks,
    step_days,
    readout,
    risk_weight,
    correlation,
    cross_gamma,
    discount,
    path_counts,
):
    position = lax.axis_index("date")
    segments = lax.axis_size("date")
    dates_local = shocks.shape[0]
    buckets_local = shocks.shape[1]
    features = shocks.shape[2]
    batches = shocks.shape[3]
    batch_lanes_width = shocks.shape[4]
    scales = jnp.sqrt(step_days.astype(jnp.float32) / 30.0)
    grouped = 1

    def forward(outgoing):
        return shifted(outgoing, "date", 1)

    columns = grouped * batch_lanes_width
    rounds = batches // grouped
    within_buf = jnp.zeros((dates_local, buckets_local, batches, batch_lanes_width), jnp.float32)
    net_buf = jnp.zeros((dates_local, buckets_local, batches, batch_lanes_width), jnp.float32)
    outgoing = jnp.zeros((buckets_local, features, columns), jnp.bfloat16)

    def one_tick(tick_index, iteration_state):
        outgoing, within_buf, net_buf = iteration_state
        incoming = forward(outgoing)
        batch_slot = tick_index - position
        active = jnp.logical_and(batch_slot >= 0, batch_slot < rounds)
        first_slot = jnp.clip(batch_slot, 0, rounds - 1) * grouped

        def process(unused):
            shock_slice = lax.dynamic_slice_in_dim(shocks, first_slot, grouped, 3)
            shock_slice = shock_slice.reshape(dates_local, buckets_local, features, columns)
            leaving, within_new, net_new = advance_section(
                incoming, shock_slice, scales, transition, readout, risk_weight, correlation
            )
            within_new = within_new.reshape(dates_local, buckets_local, grouped, batch_lanes_width)
            net_new = net_new.reshape(dates_local, buckets_local, grouped, batch_lanes_width)
            within_next = lax.dynamic_update_slice_in_dim(within_buf, within_new, first_slot, 2)
            net_next = lax.dynamic_update_slice_in_dim(net_buf, net_new, first_slot, 2)
            return (leaving, within_next, net_next)

        def unchanged(unused):
            return (outgoing, within_buf, net_buf)

        return lax.cond(active, process, unchanged, 0)

    outgoing, within_all, net_all = lax.fori_loop(
        0, segments + rounds - 1, one_tick, (outgoing, within_buf, net_buf)
    )
    gamma_off = (
        0.5
        * (cross_gamma + cross_gamma.T)
        * (1.0 - jnp.eye(cross_gamma.shape[0], dtype=jnp.float32))
    )
    bucket_base = lax.axis_index("bucket") * buckets_local
    gathered = lax.all_gather(net_all.astype(jnp.bfloat16), "bucket", axis=1, tiled=True).astype(
        net_all.dtype
    )
    gamma_rows = lax.dynamic_slice_in_dim(gamma_off, bucket_base, buckets_local, 0)
    coupled = jnp.einsum("bc,dcmp->dbmp", gamma_rows, gathered, precision=lax.Precision.HIGHEST)
    partial_value = jnp.sum(within_all + net_all * coupled, axis=1)
    squares = lax.psum_scatter(
        partial_value.astype(jnp.bfloat16), "bucket", scatter_dimension=1, tiled=True
    ).astype(jnp.float32)
    local_micro = squares.shape[1]
    counts = lax.dynamic_slice_in_dim(
        path_counts, lax.axis_index("bucket") * local_micro, local_micro
    )
    alive_mask = jnp.arange(batch_lanes_width, dtype=jnp.int32)[None, :] < counts[:, None]
    margin = jnp.where(alive_mask[None], jnp.sqrt(squares), jnp.float32(0.0))
    weights = step_days.astype(jnp.float32) / 365.0
    local_total = jnp.sum(
        weights[:, None, None] * discount * margin / counts.astype(jnp.float32)[None, :, None]
    )
    adjustment = lax.psum(local_total, ("date", "bucket"))
    return (margin, adjustment)


def solution(mesh):
    in_specs = (
        P("date", "bucket", None, None),
        P("date", "bucket", None, None, None),
        P("date"),
        P("bucket", None, None),
        P("bucket", None),
        P("bucket", None, None),
        P(),
        P("date", "bucket", None),
        P(),
    )
    out_specs = (P("date", "bucket", None), P())
    return jax.shard_map(shards, mesh=mesh, in_specs=in_specs, out_specs=out_specs, check_vma=False)
```

profile of v0, /device:TPU:0, one launch (start us, length us, event | category | flops | bytes accessed | tf_op | source)
XLA Modules:
  0.0 561.4 jit_solution(11735822941953934686)
XLA Ops:
  1.3 15.1 %copy.46 = bf16[4,2,512,16,128]{4,2,1,3,0:T(8,128)(2,1)} copy(bf16[4,2,512,16,128]{4,3,2,1,0:T(8,128)(2,1)} %param.14) | data formatting | bytes 33554432 | tf_op jit(solution)/shard_map/while | solution.py:94
  17.3 423.1 %while.17 = (s32[]{:T(128)}, bf16[2,512,128]{2,1,0:T(8,128)(2,1)}, f32[4,2,16,128]{3,2,1,0:T(8,128)S(1)}, f32[4,2,16,128]{3,1,0,2:T(2,128)S(1)}, s32[]{:T(128)},...) while((s32[]{:T(128)}, bf16[2,512,128]{2,1,0:T(8,128)(2,1)}, ...), condition=%wide.region_11.12_spmd, body=%wide.region_0.11_spmd.sunk | while | flops 656679936 | bytes 10674651 | solution.py:94
  21.1 13.4 %conditional.2 = ((bf16[2,512,128]{2,1,0:T(8,128)(2,1)}, f32[4,2,16,128]{3,2,1,0:T(8,128)S(1)}, f32[4,2,16,128]{3,1,0,2:T(2,128)S(1)})) conditional(s32[]{:T(128)} %convert_element_type.85, (bf16[2,512,128]{2,1,0:T(8,128)(2,1)}, f32[4,2,16,128]{3,2,1,0:T(8,128)S(1)}, f32[4,2,16,128]{3,1,0,2:T(2,128)S(1)}) %tuple.62, ...), branch_computations={%region_1.1_spmd, %region_2.10_spmd} | conditional | flops 656679936 | bytes 9625760 | solution.py:92
  37.2 13.4 %conditional.2 = ((bf16[2,512,128]{2,1,0:T(8,128)(2,1)}, f32[4,2,16,128]{3,2,1,0:T(8,128)S(1)}, f32[4,2,16,128]{3,1,0,2:T(2,128)S(1)})) conditional(s32[]{:T(128)} %convert_element_type.85, (bf16[2,512,128]{2,1,0:T(8,128)(2,1)}, f32[4,2,16,128]{3,2,1,0:T(8,128)S(1)}, f32[4,2,16,128]{3,1,0,2:T(2,128)S(1)}) %tuple.62, ...), branch_computations={%region_1.1_spmd, %region_2.10_spmd} | conditional | flops 656679936 | bytes 9625760 | solution.py:92
  54.2 13.4 %conditional.2 = ((bf16[2,512,128]{2,1,0:T(8,128)(2,1)}, f32[4,2,16,128]{3,2,1,0:T(8,128)S(1)}, f32[4,2,16,128]{3,1,0,2:T(2,128)S(1)})) conditional(s32[]{:T(128)} %convert_element_type.85, (bf16[2,512,128]{2,1,0:T(8,128)(2,1)}, f32[4,2,16,128]{3,2,1,0:T(8,128)S(1)}, f32[4,2,16,128]{3,1,0,2:T(2,128)S(1)}) %tuple.62, ...), branch_computations={%region_1.1_spmd, %region_2.10_spmd} | conditional | flops 656679936 | bytes 9625760 | solution.py:92
  73.2 13.4 %conditional.2 = ((bf16[2,512,128]{2,1,0:T(8,128)(2,1)}, f32[4,2,16,128]{3,2,1,0:T(8,128)S(1)}, f32[4,2,16,128]{3,1,0,2:T(2,128)S(1)})) conditional(s32[]{:T(128)} %convert_element_type.85, (bf16[2,512,128]{2,1,0:T(8,128)(2,1)}, f32[4,2,16,128]{3,2,1,0:T(8,128)S(1)}, f32[4,2,16,128]{3,1,0,2:T(2,128)S(1)}) %tuple.62, ...), branch_computations={%region_1.1_spmd, %region_2.10_spmd} | conditional | flops 656679936 | bytes 9625760 | solution.py:92
  94.5 13.4 %conditional.2 = ((bf16[2,512,128]{2,1,0:T(8,128)(2,1)}, f32[4,2,16,128]{3,2,1,0:T(8,128)S(1)}, f32[4,2,16,128]{3,1,0,2:T(2,128)S(1)})) conditional(s32[]{:T(128)} %convert_element_type.85, (bf16[2,512,128]{2,1,0:T(8,128)(2,1)}, f32[4,2,16,128]{3,2,1,0:T(8,128)S(1)}, f32[4,2,16,128]{3,1,0,2:T(2,128)S(1)}) %tuple.62, ...), branch_computations={%region_1.1_spmd, %region_2.10_spmd} | conditional | flops 656679936 | bytes 9625760 | solution.py:92
  115.9 13.4 %conditional.2 = ((bf16[2,512,128]{2,1,0:T(8,128)(2,1)}, f32[4,2,16,128]{3,2,1,0:T(8,128)S(1)}, f32[4,2,16,128]{3,1,0,2:T(2,128)S(1)})) conditional(s32[]{:T(128)} %convert_element_type.85, (bf16[2,512,128]{2,1,0:T(8,128)(2,1)}, f32[4,2,16,128]{3,2,1,0:T(8,128)S(1)}, f32[4,2,16,128]{3,1,0,2:T(2,128)S(1)}) %tuple.62, ...), branch_computations={%region_1.1_spmd, %region_2.10_spmd} | conditional | flops 656679936 | bytes 9625760 | solution.py:92
  137.2 13.4 %conditional.2 = ((bf16[2,512,128]{2,1,0:T(8,128)(2,1)}, f32[4,2,16,128]{3,2,1,0:T(8,128)S(1)}, f32[4,2,16,128]{3,1,0,2:T(2,128)S(1)})) conditional(s32[]{:T(128)} %convert_element_type.85, (bf16[2,512,128]{2,1,0:T(8,128)(2,1)}, f32[4,2,16,128]{3,2,1,0:T(8,128)S(1)}, f32[4,2,16,128]{3,1,0,2:T(2,128)S(1)}) %tuple.62, ...), branch_computations={%region_1.1_spmd, %region_2.10_spmd} | conditional | flops 656679936 | bytes 9625760 | solution.py:92
  158.5 13.4 %conditional.2 = ((bf16[2,512,128]{2,1,0:T(8,128)(2,1)}, f32[4,2,16,128]{3,2,1,0:T(8,128)S(1)}, f32[4,2,16,128]{3,1,0,2:T(2,128)S(1)})) conditional(s32[]{:T(128)} %convert_element_type.85, (bf16[2,512,128]{2,1,0:T(8,128)(2,1)}, f32[4,2,16,128]{3,2,1,0:T(8,128)S(1)}, f32[4,2,16,128]{3,1,0,2:T(2,128)S(1)}) %tuple.62, ...), branch_computations={%region_1.1_spmd, %region_2.10_spmd} | conditional | flops 656679936 | bytes 9625760 | solution.py:92
  179.9 13.4 %conditional.2 = ((bf16[2,512,128]{2,1,0:T(8,128)(2,1)}, f32[4,2,16,128]{3,2,1,0:T(8,128)S(1)}, f32[4,2,16,128]{3,1,0,2:T(2,128)S(1)})) conditional(s32[]{:T(128)} %convert_element_type.85, (bf16[2,512,128]{2,1,0:T(8,128)(2,1)}, f32[4,2,16,128]{3,2,1,0:T(8,128)S(1)}, f32[4,2,16,128]{3,1,0,2:T(2,128)S(1)}) %tuple.62, ...), branch_computations={%region_1.1_spmd, %region_2.10_spmd} | conditional | flops 656679936 | bytes 9625760 | solution.py:92
  201.2 13.4 %conditional.2 = ((bf16[2,512,128]{2,1,0:T(8,128)(2,1)}, f32[4,2,16,128]{3,2,1,0:T(8,128)S(1)}, f32[4,2,16,128]{3,1,0,2:T(2,128)S(1)})) conditional(s32[]{:T(128)} %convert_element_type.85, (bf16[2,512,128]{2,1,0:T(8,128)(2,1)}, f32[4,2,16,128]{3,2,1,0:T(8,128)S(1)}, f32[4,2,16,128]{3,1,0,2:T(2,128)S(1)}) %tuple.62, ...), branch_computations={%region_1.1_spmd, %region_2.10_spmd} | conditional | flops 656679936 | bytes 9625760 | solution.py:92
  222.6 13.4 %conditional.2 = ((bf16[2,512,128]{2,1,0:T(8,128)(2,1)}, f32[4,2,16,128]{3,2,1,0:T(8,128)S(1)}, f32[4,2,16,128]{3,1,0,2:T(2,128)S(1)})) conditional(s32[]{:T(128)} %convert_element_type.85, (bf16[2,512,128]{2,1,0:T(8,128)(2,1)}, f32[4,2,16,128]{3,2,1,0:T(8,128)S(1)}, f32[4,2,16,128]{3,1,0,2:T(2,128)S(1)}) %tuple.62, ...), branch_computations={%region_1.1_spmd, %region_2.10_spmd} | conditional | flops 656679936 | bytes 9625760 | solution.py:92
  243.9 13.4 %conditional.2 = ((bf16[2,512,128]{2,1,0:T(8,128)(2,1)}, f32[4,2,16,128]{3,2,1,0:T(8,128)S(1)}, f32[4,2,16,128]{3,1,0,2:T(2,128)S(1)})) conditional(s32[]{:T(128)} %convert_element_type.85, (bf16[2,512,128]{2,1,0:T(8,128)(2,1)}, f32[4,2,16,128]{3,2,1,0:T(8,128)S(1)}, f32[4,2,16,128]{3,1,0,2:T(2,128)S(1)}) %tuple.62, ...), branch_computations={%region_1.1_spmd, %region_2.10_spmd} | conditional | flops 656679936 | bytes 9625760 | solution.py:92
  265.2 13.4 %conditional.2 = ((bf16[2,512,128]{2,1,0:T(8,128)(2,1)}, f32[4,2,16,128]{3,2,1,0:T(8,128)S(1)}, f32[4,2,16,128]{3,1,0,2:T(2,128)S(1)})) conditional(s32[]{:T(128)} %convert_element_type.85, (bf16[2,512,128]{2,1,0:T(8,128)(2,1)}, f32[4,2,16,128]{3,2,1,0:T(8,128)S(1)}, f32[4,2,16,128]{3,1,0,2:T(2,128)S(1)}) %tuple.62, ...), branch_computations={%region_1.1_spmd, %region_2.10_spmd} | conditional | flops 656679936 | bytes 9625760 | solution.py:92
  286.6 13.4 %conditional.2 = ((bf16[2,512,128]{2,1,0:T(8,128)(2,1)}, f32[4,2,16,128]{3,2,1,0:T(8,128)S(1)}, f32[4,2,16,128]{3,1,0,2:T(2,128)S(1)})) conditional(s32[]{:T(128)} %convert_element_type.85, (bf16[2,512,128]{2,1,0:T(8,128)(2,1)}, f32[4,2,16,128]{3,2,1,0:T(8,128)S(1)}, f32[4,2,16,128]{3,1,0,2:T(2,128)S(1)}) %tuple.62, ...), branch_computations={%region_1.1_spmd, %region_2.10_spmd} | conditional | flops 656679936 | bytes 9625760 | solution.py:92
  307.9 13.4 %conditional.2 = ((bf16[2,512,128]{2,1,0:T(8,128)(2,1)}, f32[4,2,16,128]{3,2,1,0:T(8,128)S(1)}, f32[4,2,16,128]{3,1,0,2:T(2,128)S(1)})) conditional(s32[]{:T(128)} %convert_element_type.85, (bf16[2,512,128]{2,1,0:T(8,128)(2,1)}, f32[4,2,16,128]{3,2,1,0:T(8,128)S(1)}, f32[4,2,16,128]{3,1,0,2:T(2,128)S(1)}) %tuple.62, ...), branch_computations={%region_1.1_spmd, %region_2.10_spmd} | conditional | flops 656679936 | bytes 9625760 | solution.py:92
  329.3 13.4 %conditional.2 = ((bf16[2,512,128]{2,1,0:T(8,128)(2,1)}, f32[4,2,16,128]{3,2,1,0:T(8,128)S(1)}, f32[4,2,16,128]{3,1,0,2:T(2,128)S(1)})) conditional(s32[]{:T(128)} %convert_element_type.85, (bf16[2,512,128]{2,1,0:T(8,128)(2,1)}, f32[4,2,16,128]{3,2,1,0:T(8,128)S(1)}, f32[4,2,16,128]{3,1,0,2:T(2,128)S(1)}) %tuple.62, ...), branch_computations={%region_1.1_spmd, %region_2.10_spmd} | conditional | flops 656679936 | bytes 9625760 | solution.py:92
  350.6 20.0 %collective-permute-start = (bf16[2,512,128]{2,1,0:T(8,128)(2,1)}, bf16[2,512,128]{2,1,0:T(8,128)(2,1)S(1)}, u32[]{:S(2)}, u32[]{:S(2)}) collective-permute-start(bf16[2,512,128]{2,1,0:T(8,128)(2,1)} %get-tuple-element.435), channel_id=1, source_target_pairs={{0,4},{4,8},{8,12},{12,16},{16,20},{20,24},{24,28},{1,5},{5,9},{9,... | collective-permute-start | bytes 786440 | tf_op jit(solution)/shard_map/while/body/eval_jaxpr/ppermute | solution.py:12
  379.8 20.0 %collective-permute-start = (bf16[2,512,128]{2,1,0:T(8,128)(2,1)}, bf16[2,512,128]{2,1,0:T(8,128)(2,1)S(1)}, u32[]{:S(2)}, u32[]{:S(2)}) collective-permute-start(bf16[2,512,128]{2,1,0:T(8,128)(2,1)} %get-tuple-element.435), channel_id=1, source_target_pairs={{0,4},{4,8},{8,12},{12,16},{16,20},{20,24},{24,28},{1,5},{5,9},{9,... | collective-permute-start | bytes 786440 | tf_op jit(solution)/shard_map/while/body/eval_jaxpr/ppermute | solution.py:12
  409.4 20.9 %collective-permute-start = (bf16[2,512,128]{2,1,0:T(8,128)(2,1)}, bf16[2,512,128]{2,1,0:T(8,128)(2,1)S(1)}, u32[]{:S(2)}, u32[]{:S(2)}) collective-permute-start(bf16[2,512,128]{2,1,0:T(8,128)(2,1)} %get-tuple-element.435), channel_id=1, source_target_pairs={{0,4},{4,8},{8,12},{12,16},{16,20},{20,24},{24,28},{1,5},{5,9},{9,... | collective-permute-start | bytes 786440 | tf_op jit(solution)/shard_map/while/body/eval_jaxpr/ppermute | solution.py:12
  440.4 14.4 %all_gather.3 = bf16[4,8,16,128]{3,2,0,1:T(8,128)(2,1)S(1)} all-gather(bf16[4,2,16,128]{3,2,0,1:T(8,128)(2,1)S(1)} %copy.68), channel_id=1, replica_groups=mesh['date'=8,'bucket'=4] {'bucket'}, dimensions={1}, use_global_device_ids=true | all-gather | bytes 163840 | tf_op jit(solution)/shard_map/all_gather | solution.py:103
  455.3 18.8 %all-reduce = bf16[4,16,128]{2,1,0:T(8,128)(2,1)S(1)} all-reduce(bf16[4,16,128]{2,1,0:T(8,128)(2,1)S(1)} %fusion.31), channel_id=2, replica_groups=mesh['date'=8,'bucket'=4] {'bucket'}, use_global_device_ids=true, to_apply=%region_13.14.clone | all-reduce | flops 8192 | bytes 32768
  476.7 84.7 %psum.7 = f32[]{:T(128)} all-reduce(f32[]{:T(128)} %get-tuple-element.315), channel_id=1, replica_groups=mesh['date'=8,'bucket'=4] {'date','bucket'}, use_global_device_ids=true, to_apply=%region_15.16 | all-reduce | flops 1 | bytes 8 | tf_op jit(solution)/shard_map/psum | solution.py:122
  (397 shorter events, 364.3 us)
Async XLA Ops:
  17.3 458.2 %copy-start.4 = (f32[4,4,128]{2,1,0:T(4,128)S(1)}, f32[4,4,128]{2,1,0:T(4,128)}, u32[]{:S(2)}) copy-start(f32[4,4,128]{2,1,0:T(4,128)} %param.20) | copy-start | bytes 24580
  17.3 3.8 collective-permute-start
  34.5 2.7 collective-permute-start
  50.6 3.6 collective-permute-start
  67.7 5.5 collective-permute-start
  86.6 7.9 %collective-permute-start = (bf16[2,512,128]{2,1,0:T(8,128)(2,1)}, bf16[2,512,128]{2,1,0:T(8,128)(2,1)S(1)}, u32[]{:S(2)}, u32[]{:S(2)}) collective-permute-start(bf16[2,512,128]{2,1,0:T(8,128)(2,1)} %get-tuple-element.435), channel_id=1, source_target_pairs={{0,4},{4,8},{8,12},{12,16},{16,20},{20,24},{24,28},{1,5},{5,9},{9,... | collective-permute-start | bytes 786440 | tf_op jit(solution)/shard_map/while/body/eval_jaxpr/ppermute | solution.py:12
  108.0 7.9 %collective-permute-start = (bf16[2,512,128]{2,1,0:T(8,128)(2,1)}, bf16[2,512,128]{2,1,0:T(8,128)(2,1)S(1)}, u32[]{:S(2)}, u32[]{:S(2)}) collective-permute-start(bf16[2,512,128]{2,1,0:T(8,128)(2,1)} %get-tuple-element.435), channel_id=1, source_target_pairs={{0,4},{4,8},{8,12},{12,16},{16,20},{20,24},{24,28},{1,5},{5,9},{9,... | collective-permute-start | bytes 786440 | tf_op jit(solution)/shard_map/while/body/eval_jaxpr/ppermute | solution.py:12
  129.3 7.9 %collective-permute-start = (bf16[2,512,128]{2,1,0:T(8,128)(2,1)}, bf16[2,512,128]{2,1,0:T(8,128)(2,1)S(1)}, u32[]{:S(2)}, u32[]{:S(2)}) collective-permute-start(bf16[2,512,128]{2,1,0:T(8,128)(2,1)} %get-tuple-element.435), channel_id=1, source_target_pairs={{0,4},{4,8},{8,12},{12,16},{16,20},{20,24},{24,28},{1,5},{5,9},{9,... | collective-permute-start | bytes 786440 | tf_op jit(solution)/shard_map/while/body/eval_jaxpr/ppermute | solution.py:12
  150.6 7.9 %collective-permute-start = (bf16[2,512,128]{2,1,0:T(8,128)(2,1)}, bf16[2,512,128]{2,1,0:T(8,128)(2,1)S(1)}, u32[]{:S(2)}, u32[]{:S(2)}) collective-permute-start(bf16[2,512,128]{2,1,0:T(8,128)(2,1)} %get-tuple-element.435), channel_id=1, source_target_pairs={{0,4},{4,8},{8,12},{12,16},{16,20},{20,24},{24,28},{1,5},{5,9},{9,... | collective-permute-start | bytes 786440 | tf_op jit(solution)/shard_map/while/body/eval_jaxpr/ppermute | solution.py:12
  172.0 7.9 %collective-permute-start = (bf16[2,512,128]{2,1,0:T(8,128)(2,1)}, bf16[2,512,128]{2,1,0:T(8,128)(2,1)S(1)}, u32[]{:S(2)}, u32[]{:S(2)}) collective-permute-start(bf16[2,512,128]{2,1,0:T(8,128)(2,1)} %get-tuple-element.435), channel_id=1, source_target_pairs={{0,4},{4,8},{8,12},{12,16},{16,20},{20,24},{24,28},{1,5},{5,9},{9,... | collective-permute-start | bytes 786440 | tf_op jit(solution)/shard_map/while/body/eval_jaxpr/ppermute | solution.py:12
  193.3 7.9 %collective-permute-start = (bf16[2,512,128]{2,1,0:T(8,128)(2,1)}, bf16[2,512,128]{2,1,0:T(8,128)(2,1)S(1)}, u32[]{:S(2)}, u32[]{:S(2)}) collective-permute-start(bf16[2,512,128]{2,1,0:T(8,128)(2,1)} %get-tuple-element.435), channel_id=1, source_target_pairs={{0,4},{4,8},{8,12},{12,16},{16,20},{20,24},{24,28},{1,5},{5,9},{9,... | collective-permute-start | bytes 786440 | tf_op jit(solution)/shard_map/while/body/eval_jaxpr/ppermute | solution.py:12
  214.7 7.9 %collective-permute-start = (bf16[2,512,128]{2,1,0:T(8,128)(2,1)}, bf16[2,512,128]{2,1,0:T(8,128)(2,1)S(1)}, u32[]{:S(2)}, u32[]{:S(2)}) collective-permute-start(bf16[2,512,128]{2,1,0:T(8,128)(2,1)} %get-tuple-element.435), channel_id=1, source_target_pairs={{0,4},{4,8},{8,12},{12,16},{16,20},{20,24},{24,28},{1,5},{5,9},{9,... | collective-permute-start | bytes 786440 | tf_op jit(solution)/shard_map/while/body/eval_jaxpr/ppermute | solution.py:12
  236.0 7.9 %collective-permute-start = (bf16[2,512,128]{2,1,0:T(8,128)(2,1)}, bf16[2,512,128]{2,1,0:T(8,128)(2,1)S(1)}, u32[]{:S(2)}, u32[]{:S(2)}) collective-permute-start(bf16[2,512,128]{2,1,0:T(8,128)(2,1)} %get-tuple-element.435), channel_id=1, source_target_pairs={{0,4},{4,8},{8,12},{12,16},{16,20},{20,24},{24,28},{1,5},{5,9},{9,... | collective-permute-start | bytes 786440 | tf_op jit(solution)/shard_map/while/body/eval_jaxpr/ppermute | solution.py:12
  257.3 7.9 %collective-permute-start = (bf16[2,512,128]{2,1,0:T(8,128)(2,1)}, bf16[2,512,128]{2,1,0:T(8,128)(2,1)S(1)}, u32[]{:S(2)}, u32[]{:S(2)}) collective-permute-start(bf16[2,512,128]{2,1,0:T(8,128)(2,1)} %get-tuple-element.435), channel_id=1, source_target_pairs={{0,4},{4,8},{8,12},{12,16},{16,20},{20,24},{24,28},{1,5},{5,9},{9,... | collective-permute-start | bytes 786440 | tf_op jit(solution)/shard_map/while/body/eval_jaxpr/ppermute | solution.py:12
  278.7 7.9 %collective-permute-start = (bf16[2,512,128]{2,1,0:T(8,128)(2,1)}, bf16[2,512,128]{2,1,0:T(8,128)(2,1)S(1)}, u32[]{:S(2)}, u32[]{:S(2)}) collective-permute-start(bf16[2,512,128]{2,1,0:T(8,128)(2,1)} %get-tuple-element.435), channel_id=1, source_target_pairs={{0,4},{4,8},{8,12},{12,16},{16,20},{20,24},{24,28},{1,5},{5,9},{9,... | collective-permute-start | bytes 786440 | tf_op jit(solution)/shard_map/while/body/eval_jaxpr/ppermute | solution.py:12
  300.0 7.9 %collective-permute-start = (bf16[2,512,128]{2,1,0:T(8,128)(2,1)}, bf16[2,512,128]{2,1,0:T(8,128)(2,1)S(1)}, u32[]{:S(2)}, u32[]{:S(2)}) collective-permute-start(bf16[2,512,128]{2,1,0:T(8,128)(2,1)} %get-tuple-element.435), channel_id=1, source_target_pairs={{0,4},{4,8},{8,12},{12,16},{16,20},{20,24},{24,28},{1,5},{5,9},{9,... | collective-permute-start | bytes 786440 | tf_op jit(solution)/shard_map/while/body/eval_jaxpr/ppermute | solution.py:12
  321.4 7.9 %collective-permute-start = (bf16[2,512,128]{2,1,0:T(8,128)(2,1)}, bf16[2,512,128]{2,1,0:T(8,128)(2,1)S(1)}, u32[]{:S(2)}, u32[]{:S(2)}) collective-permute-start(bf16[2,512,128]{2,1,0:T(8,128)(2,1)} %get-tuple-element.435), channel_id=1, source_target_pairs={{0,4},{4,8},{8,12},{12,16},{16,20},{20,24},{24,28},{1,5},{5,9},{9,... | collective-permute-start | bytes 786440 | tf_op jit(solution)/shard_map/while/body/eval_jaxpr/ppermute | solution.py:12
  342.7 7.9 %collective-permute-start = (bf16[2,512,128]{2,1,0:T(8,128)(2,1)}, bf16[2,512,128]{2,1,0:T(8,128)(2,1)S(1)}, u32[]{:S(2)}, u32[]{:S(2)}) collective-permute-start(bf16[2,512,128]{2,1,0:T(8,128)(2,1)} %get-tuple-element.435), channel_id=1, source_target_pairs={{0,4},{4,8},{8,12},{12,16},{16,20},{20,24},{24,28},{1,5},{5,9},{9,... | collective-permute-start | bytes 786440 | tf_op jit(solution)/shard_map/while/body/eval_jaxpr/ppermute | solution.py:12
  350.6 21.3 %collective-permute-start = (bf16[2,512,128]{2,1,0:T(8,128)(2,1)}, bf16[2,512,128]{2,1,0:T(8,128)(2,1)S(1)}, u32[]{:S(2)}, u32[]{:S(2)}) collective-permute-start(bf16[2,512,128]{2,1,0:T(8,128)(2,1)} %get-tuple-element.435), channel_id=1, source_target_pairs={{0,4},{4,8},{8,12},{12,16},{16,20},{20,24},{24,28},{1,5},{5,9},{9,... | collective-permute-start | bytes 786440 | tf_op jit(solution)/shard_map/while/body/eval_jaxpr/ppermute | solution.py:12
  371.9 7.9 %collective-permute-start = (bf16[2,512,128]{2,1,0:T(8,128)(2,1)}, bf16[2,512,128]{2,1,0:T(8,128)(2,1)S(1)}, u32[]{:S(2)}, u32[]{:S(2)}) collective-permute-start(bf16[2,512,128]{2,1,0:T(8,128)(2,1)} %get-tuple-element.435), channel_id=1, source_target_pairs={{0,4},{4,8},{8,12},{12,16},{16,20},{20,24},{24,28},{1,5},{5,9},{9,... | collective-permute-start | bytes 786440 | tf_op jit(solution)/shard_map/while/body/eval_jaxpr/ppermute | solution.py:12
  379.8 21.3 %collective-permute-start = (bf16[2,512,128]{2,1,0:T(8,128)(2,1)}, bf16[2,512,128]{2,1,0:T(8,128)(2,1)S(1)}, u32[]{:S(2)}, u32[]{:S(2)}) collective-permute-start(bf16[2,512,128]{2,1,0:T(8,128)(2,1)} %get-tuple-element.435), channel_id=1, source_target_pairs={{0,4},{4,8},{8,12},{12,16},{16,20},{20,24},{24,28},{1,5},{5,9},{9,... | collective-permute-start | bytes 786440 | tf_op jit(solution)/shard_map/while/body/eval_jaxpr/ppermute | solution.py:12
  401.2 8.2 %collective-permute-start = (bf16[2,512,128]{2,1,0:T(8,128)(2,1)}, bf16[2,512,128]{2,1,0:T(8,128)(2,1)S(1)}, u32[]{:S(2)}, u32[]{:S(2)}) collective-permute-start(bf16[2,512,128]{2,1,0:T(8,128)(2,1)} %get-tuple-element.435), channel_id=1, source_target_pairs={{0,4},{4,8},{8,12},{12,16},{16,20},{20,24},{24,28},{1,5},{5,9},{9,... | collective-permute-start | bytes 786440 | tf_op jit(solution)/shard_map/while/body/eval_jaxpr/ppermute | solution.py:12
  409.4 22.2 %collective-permute-start = (bf16[2,512,128]{2,1,0:T(8,128)(2,1)}, bf16[2,512,128]{2,1,0:T(8,128)(2,1)S(1)}, u32[]{:S(2)}, u32[]{:S(2)}) collective-permute-start(bf16[2,512,128]{2,1,0:T(8,128)(2,1)} %get-tuple-element.435), channel_id=1, source_target_pairs={{0,4},{4,8},{8,12},{12,16},{16,20},{20,24},{24,28},{1,5},{5,9},{9,... | collective-permute-start | bytes 786440 | tf_op jit(solution)/shard_map/while/body/eval_jaxpr/ppermute | solution.py:12
  431.6 8.8 %collective-permute-start = (bf16[2,512,128]{2,1,0:T(8,128)(2,1)}, bf16[2,512,128]{2,1,0:T(8,128)(2,1)S(1)}, u32[]{:S(2)}, u32[]{:S(2)}) collective-permute-start(bf16[2,512,128]{2,1,0:T(8,128)(2,1)} %get-tuple-element.435), channel_id=1, source_target_pairs={{0,4},{4,8},{8,12},{12,16},{16,20},{20,24},{24,28},{1,5},{5,9},{9,... | collective-permute-start | bytes 786440 | tf_op jit(solution)/shard_map/while/body/eval_jaxpr/ppermute | solution.py:12
  (6 other events, 1399.2 us)
where the time goes:
time: 566 us; the launch traced here: 561 us
  matrix products  202 us (36%)
  starting transfers between devices  177 us (31%)
  blocking collectives  118 us (21%)
  waiting for transfers between devices  30.6 us (5%)
  local copies, waits for them, and re-layouts  27.8 us (5%)
    ppermute x23, starting transfers between devices, shifted(): return lax.ppermute(x, axis, pairs)  177 us
    dot_general x64, matrix products, advance_section(): jnp.einsum('bij,bjp->bip', transition[date_local], carried, preferred_ele...  160 us
    psum x1, blocking collectives, shards(): adjustment = lax.psum(local_total, ('date', 'bucket'))  84.7 us
    ppermute x23, waiting for transfers between devices, shifted(): return lax.ppermute(x, axis, pairs)  30.6 us
    dot_general x64, matrix products, advance_section(): jnp.einsum('bsf,bfp->bsp', readout, carried, preferred_element_type=jnp.f...  27.5 us
    unnamed x1, blocking collectives  18.8 us
    while x2, local copies, waits for them, and re-layouts, shards(): lax.fori_loop(0, segments + rounds - 1, one_tick, (outgoing, within_buf,...  15.2 us
    all_gather x1, blocking collectives, shards(): lax.all_gather(net_all.astype(jnp.bfloat16), 'bucket', axis=1, tiled=True)  14.4 us
  transfers between devices with their start and end apart: 23, of which 23 were waited for; matrix products, arithmetic and copies ran while one was open for 0% of the time, Pallas kernels for 0%

commit v1 on v0

v1 whole, which is shorter than its diff:
```python
import functools

import jax
import jax.numpy as jnp
from jax import lax
from jax.experimental import pallas as pl
from jax.experimental.pallas import tpu as pltpu
from jax.sharding import PartitionSpec as P

epsilon = 1e-06
f32 = jnp.float32
bf16 = jnp.bfloat16


def dot(a, b):
    return jnp.dot(a, b, preferred_element_type=f32)


def split(x):
    high = x.astype(bf16)
    return high, (x - high.astype(f32)).astype(bf16)


def operator_kernel(dates, a_ref, r_ref, w_ref):
    features = a_ref.shape[-1]
    sens = r_ref.shape[1]
    product = a_ref[0, 0]
    for t in range(dates):
        if t:
            product = dot(a_ref[t, 0], product).astype(bf16)
        row = features + t * sens
        w_ref[0, row : row + sens, :] = dot(r_ref[0], product).astype(bf16)
    w_ref[0, :features, :] = product


def local_kernel(dates, scale_ref, x_ref, a_ref, r_ref, e_ref, s_ref, rows_ref, state_ref):
    features, micro, lanes = x_ref.shape[2:]
    sens = r_ref.shape[1]
    pair = 2
    for t in range(dates):
        rows_ref[...] = x_ref[t, 0].astype(f32).reshape(features * micro, lanes)
        scale = scale_ref[t]
        for m in range(0, micro, pair):
            cols = slice(m * lanes, (m + pair) * lanes)
            shock = jnp.concatenate(
                [rows_ref[pl.ds(m + i, features, stride=micro), :] for i in range(pair)], axis=1
            )
            total = scale * shock
            if t:
                total = total + dot(a_ref[t, 0], state_ref[(t - 1) % 2, :, cols])
            state = total.astype(bf16)
            state_ref[t % 2, :, cols] = state
            seen = dot(r_ref[0], state)
            for i in range(pair):
                part = slice(i * lanes, (i + 1) * lanes)
                s_ref[m + i, 0, t * sens : (t + 1) * sens, :] = seen[:, part]
                if t == dates - 1:
                    e_ref[m + i, 0] = state[:, part]


def tick_kernel(dates, at_ref, in_ref, w_ref, e_ref, s_ref, rw_ref, c_ref, out_ref, stat_ref):
    features = in_ref.shape[1]
    lanes = in_ref.shape[2]
    sens = rw_ref.shape[1]
    bucket = pl.program_id(0)
    buckets = pl.num_programs(0)
    moved = dot(w_ref[0], in_ref[0])
    out_ref[0] = (moved[:features] + e_ref[0, 0].astype(f32)).astype(bf16)
    seen = moved[features:] + s_ref[0, 0]
    ws = jnp.concatenate(
        [rw_ref[0] * seen[t * sens : (t + 1) * sens] for t in range(dates)], axis=1
    )
    c_high, c_low = split(c_ref[0])
    w_high, w_low = split(ws)
    mixed = dot(
        jnp.concatenate([c_high, c_low, c_high], axis=1),
        jnp.concatenate([w_high, w_high, w_low], axis=0),
    )
    within = jnp.sum(ws * mixed, axis=0, keepdims=True) + epsilon
    root = jnp.sqrt(within)
    net = jnp.clip(jnp.sum(ws, axis=0, keepdims=True), -root, root)

    @pl.when(bucket == 0)
    def _():
        stat_ref[0:1, :] = within

    @pl.when(bucket > 0)
    def _():
        stat_ref[0:1, :] += within

    stat_ref[pl.ds(bucket + 1, 1), :] = net


def shards(
    transition,
    shocks,
    step_days,
    readout,
    risk_weight,
    correlation,
    cross_gamma,
    discount,
    path_counts,
):
    position = lax.axis_index("date")
    segments = lax.axis_size("date")
    zs = lax.axis_size("bucket")
    z = lax.axis_index("bucket")
    dates, buckets, features, batches, lanes = shocks.shape
    sens = readout.shape[1]
    scales = jnp.sqrt(step_days.astype(f32) / 30.0)
    group = batches // 2
    rows = features + dates * sens

    ends, seen = pl.pallas_call(
        functools.partial(local_kernel, dates),
        out_shape=(
            jax.ShapeDtypeStruct((batches, buckets, features, lanes), bf16),
            jax.ShapeDtypeStruct((batches, buckets, dates * sens, lanes), f32),
        ),
        grid=(buckets, 2),
        in_specs=[
            pl.BlockSpec(memory_space=pltpu.SMEM),
            pl.BlockSpec((dates, 1, features, group, lanes), lambda b, g: (0, b, 0, g, 0)),
            pl.BlockSpec((dates, 1, features, features), lambda b, g: (0, b, 0, 0)),
            pl.BlockSpec((1, sens, features), lambda b, g: (b, 0, 0)),
        ],
        out_specs=(
            pl.BlockSpec((group, 1, features, lanes), lambda b, g: (g, b, 0, 0)),
            pl.BlockSpec((group, 1, dates * sens, lanes), lambda b, g: (g, b, 0, 0)),
        ),
        scratch_shapes=[
            pltpu.VMEM((features * group, lanes), f32),
            pltpu.VMEM((2, features, group * lanes), bf16),
        ],
        name="local",
    )(scales, shocks, transition, readout)

    operators = pl.pallas_call(
        functools.partial(operator_kernel, dates),
        out_shape=jax.ShapeDtypeStruct((buckets, rows, features), bf16),
        grid=(buckets,),
        in_specs=[
            pl.BlockSpec((dates, 1, features, features), lambda b: (0, b, 0, 0)),
            pl.BlockSpec((1, sens, features), lambda b: (b, 0, 0)),
        ],
        out_specs=pl.BlockSpec((1, rows, features), lambda b: (b, 0, 0)),
        name="operators",
    )(transition, readout)

    weight_column = risk_weight[:, :, None]
    tick = pl.pallas_call(
        functools.partial(tick_kernel, dates),
        out_shape=(
            jax.ShapeDtypeStruct((buckets, features, lanes), bf16),
            jax.ShapeDtypeStruct((buckets + 1, dates * lanes), f32),
        ),
        grid_spec=pltpu.PrefetchScalarGridSpec(
            num_scalar_prefetch=1,
            grid=(buckets,),
            in_specs=[
                pl.BlockSpec((1, features, lanes), lambda b, c: (b, 0, 0)),
                pl.BlockSpec((1, rows, features), lambda b, c: (b, 0, 0)),
                pl.BlockSpec((1, 1, features, lanes), lambda b, c: (c[0], b, 0, 0)),
                pl.BlockSpec((1, 1, dates * sens, lanes), lambda b, c: (c[0], b, 0, 0)),
                pl.BlockSpec((1, sens, 1), lambda b, c: (b, 0, 0)),
                pl.BlockSpec((1, sens, sens), lambda b, c: (b, 0, 0)),
            ],
            out_specs=(
                pl.BlockSpec((1, features, lanes), lambda b, c: (b, 0, 0)),
                pl.BlockSpec((buckets + 1, dates * lanes), lambda b, c: (0, 0)),
            ),
        ),
        cost_estimate=pl.CostEstimate(
            flops=2 * buckets * rows * features * lanes, bytes_accessed=2**22, transcendentals=0
        ),
        name="tick",
    )

    skew = 2
    ticks = batches + skew * (segments - 1)
    forward = [(i, i + 1) for i in range(segments - 1)]
    received = [jnp.zeros((buckets, features, lanes), bf16)] * skew
    stats = []
    for step in range(ticks):
        at = jnp.clip(step - skew * position, 0, batches - 1).astype(jnp.int32).reshape(1)
        leaving, stat = tick(
            at, received[step], operators, ends, seen, weight_column, correlation
        )
        stats.append(stat)
        if step < ticks - skew:
            received.append(lax.ppermute(leaving, "date", forward))
    stats = jnp.stack(stats)
    mine = lax.dynamic_slice_in_dim(stats, skew * position, batches, 0)

    message = jnp.concatenate(
        [mine.reshape(-1, lanes), discount.reshape(-1, lanes)], axis=0
    )
    gathered = [message]
    for k in range(1, zs):
        gathered.append(
            lax.ppermute(message, "bucket", [(i, (i + k) % zs) for i in range(zs)])
        )
    gathered = jnp.roll(jnp.stack(gathered[::-1]), z + 1, axis=0)
    count_rows = mine.size // lanes
    parts = gathered[:, :count_rows].reshape(zs, batches, buckets + 1, dates, lanes)
    local_micro = discount.shape[1]
    discounts = gathered[:, count_rows:].reshape(zs, dates, local_micro, lanes)
    discounts = jnp.swapaxes(discounts, 0, 1).reshape(dates, batches, lanes)
    within = jnp.sum(parts[:, :, 0], axis=0)
    nets = jnp.swapaxes(parts[:, :, 1:], 1, 2).reshape(zs * buckets, batches, dates, lanes)
    gamma = (
        0.5
        * (cross_gamma + cross_gamma.T)
        * (1.0 - jnp.eye(cross_gamma.shape[0], dtype=f32))
    )
    coupled = jnp.sum(gamma[:, :, None, None, None] * nets[None], axis=1)
    squares = within + jnp.sum(nets * coupled, axis=0)
    squares = jnp.swapaxes(squares, 0, 1)
    alive = jnp.arange(lanes, dtype=jnp.int32)[None, :] < path_counts[:, None]
    margins = jnp.where(alive[None], jnp.sqrt(squares), f32(0.0))
    weights = step_days.astype(f32) / 365.0
    total = jnp.sum(
        weights[:, None, None] * discounts * margins / path_counts.astype(f32)[None, :, None]
    )
    total = jnp.full((8, lanes), total)
    step = 1
    while step < segments:
        total = total + lax.ppermute(
            total, "date", [(i, i ^ step) for i in range(segments)]
        )
        step *= 2
    margin = lax.dynamic_slice_in_dim(margins, z * local_micro, local_micro, 1)
    return (margin, total[0, 0])


def solution(mesh):
    in_specs = (
        P("date", "bucket", None, None),
        P("date", "bucket", None, None, None),
        P("date"),
        P("bucket", None, None),
        P("bucket", None),
        P("bucket", None, None),
        P(),
        P("date", "bucket", None),
        P(),
    )
    out_specs = (P("date", "bucket", None), P())
    return jax.shard_map(shards, mesh=mesh, in_specs=in_specs, out_specs=out_specs, check_vma=False)
```

time: 566 us -> 224 us (0.40)
  matrix products: 202 us -> 0 us
  blocking collectives: 118 us -> 0 us
  starting transfers between devices: 177 us -> 96.5 us
  local copies, waits for them, and re-layouts: 27.8 us -> 68.4 us
  Pallas kernels: 0 us -> 37.5 us
  waiting for transfers between devices: 30.6 us -> 14.5 us
    dot_general x193 -> x0, matrix products: 202 us -> none  [the longest x64 160 us: advance_section(): jnp.einsum('bij,bjp->bip', transition[date_local], carried, preferred_ele...]
    psum x1 -> x0, blocking collectives: 84.7 us -> none  [shards(): adjustment = lax.psum(local_total, ('date', 'bucket'))]
    ppermute x23 -> x34, starting transfers between devices: 177 us -> 96.5 us  [the longest x28 88.5 us: shards(): received.append(lax.ppermute(leaving, 'date', forward))]
    pallas_call x0 -> x29, local copies, waits for them, and re-layouts: none -> 63.4 us  [shards(): tick(at, received[step], operators, ends, seen, weight_column, correlation)]
    pallas_call x0 -> x3, Pallas kernels: none -> 37.5 us  [the longest x1 28.6 us: shards(): pl.pallas_call(functools.partial(local_kernel, dates), out_shape=(jax.Sha...]
    unnamed x1 -> x0, blocking collectives: 18.8 us -> none
    ppermute x23 -> x34, waiting for transfers between devices: 30.6 us -> 14.5 us  [the longest x3 9.64 us: shards(): lax.ppermute(message, 'bucket', [(i, (i + k) % zs) for i in range(zs)])]
    while x2 -> x0, local copies, waits for them, and re-layouts: 15.2 us -> none  [shards(): lax.fori_loop(0, segments + rounds - 1, one_tick, (outgoing, within_buf,...]
  transfers between devices with their start and end apart: 23 -> 34, of which waited for: 23 -> 5; matrix products, arithmetic and copies ran while one was open for 0% -> 28% of each run, Pallas kernels for 0% -> 0%
where the time goes in v1:
time: 224 us; the launch traced here: 222 us
  starting transfers between devices  96.5 us (43%)
  local copies, waits for them, and re-layouts  68.4 us (31%)
  Pallas kernels  37.5 us (17%)
  waiting for transfers between devices  14.5 us (6%)
  other arithmetic  3.6 us (2%)
    ppermute x28, starting transfers between devices, shards(): received.append(lax.ppermute(leaving, 'date', forward))  88.5 us
    pallas_call x29, local copies, waits for them, and re-layouts, shards(): tick(at, received[step], operators, ends, seen, weight_column, correlation)  63.4 us
    pallas_call x1, Pallas kernels, shards(): pl.pallas_call(functools.partial(local_kernel, dates), out_shape=(jax.Sha...  28.6 us
    ppermute x3, waiting for transfers between devices, shards(): lax.ppermute(message, 'bucket', [(i, (i + k) % zs) for i in range(zs)])  9.64 us
    pallas_call x1, Pallas kernels, shards(): pl.pallas_call(functools.partial(operator_kernel, dates), out_shape=jax.S...  5.67 us
    ppermute x3, waiting for transfers between devices, shards(): lax.ppermute(total, 'date', [(i, i ^ step) for i in range(segments)])  4.77 us
    ppermute x3, starting transfers between devices, shards(): lax.ppermute(message, 'bucket', [(i, (i + k) % zs) for i in range(zs)])  4.69 us
  transfers between devices with their start and end apart: 34, of which 5 were waited for; matrix products, arithmetic and copies ran while one was open for 28% of the time, Pallas kernels for 0%

profile of v1, /device:TPU:0, one launch (start us, length us, event | category | flops | bytes accessed | tf_op | source)
XLA Modules:
  0.0 222.1 jit_solution(12582061160165024467)
XLA Ops:
  3.2 5.7 %operators.1.w_ref = bf16[2,768,512]{2,1,0:T(8,128)(2,1)} custom-call(bf16[4,2,512,512]{3,2,1,0:T(8,128)(2,1)} %a_ref.3, bf16[2,64,512]{2,1,0:T(8,128)(2,1)} %r_ref.3), custom_call_target="tpu_custom_call" | custom-call | tf_op jit(solution)/shard_map/operators/pallas_call | solution.py:139
  8.9 28.6 %local.1 = (bf16[16,2,512,128]{3,2,1,0:T(8,128)(2,1)}, f32[16,2,256,128]{3,2,1,0:T(8,128)}) custom-call(f32[4]{0:T(128)} %get-tuple-element.249.scale_ref, bf16[4,2,512,16,128]{4,3,2,1,0:T(8,128)(2,1)} %x_ref.1, bf16[4,2,512,512]{3,2,1,0:T(8,128)(2,1)} %a_ref.3, bf16[2,64,512]{2,1,0:T(8,128)(2,1)} %r_ref.3), custom_call_target="tpu_custom_call" | custom-call | tf_op jit(solution)/shard_map/local/pallas_call | solution.py:115
  38.3 3.2 %tick.30 = (bf16[2,512,128]{2,1,0:T(8,128)(2,1)}, f32[3,512]{1,0:T(4,128)}) custom-call(s32[1]{0:T(128)} %bitcast.at_ref, bf16[2,512,128]{2,1,0:T(8,128)(2,1)} %broadcast_in_dim.28.in_ref, bf16[2,768,512]{2,1,0:T(8,128)(2,1)} %operators.1.w_ref, bf16[16,2,512,128]{3,2,1,0:T(8,128)(2,1)} %get-tuple-element.62.e_ref, ...), custom_call_target="tpu_custom_call" | custom-call | flops 201326592 | bytes 4194304 | tf_op jit(solution)/shard_map/tick/pallas_call | solution.py:187
  46.8 4.5 %collective-permute-start.1 = (bf16[2,512,128]{2,1,0:T(8,128)(2,1)S(1)}, bf16[2,512,128]{2,1,0:T(8,128)(2,1)S(1)}, u32[]{:S(2)}, u32[]{:S(2)}) collective-permute-start(bf16[2,512,128]{2,1,0:T(8,128)(2,1)S(1)} %get-tuple-element.200), channel_id=1, source_target_pairs={{0,4},{4,8},{8,12},{12,16},{16,20},{20,24},{24,28},{1,5},{5,9},{9,... | collective-permute-start | bytes 786440 | tf_op jit(solution)/shard_map/ppermute | solution.py:192
  57.5 3.5 %collective-permute-start.3 = (bf16[2,512,128]{2,1,0:T(8,128)(2,1)S(1)}, bf16[2,512,128]{2,1,0:T(8,128)(2,1)S(1)}, u32[]{:S(2)}, u32[]{:S(2)}) collective-permute-start(bf16[2,512,128]{2,1,0:T(8,128)(2,1)S(1)} %get-tuple-element.196), channel_id=1, source_target_pairs={{0,4},{4,8},{8,12},{12,16},{16,20},{20,24},{24,28},{1,5},{5,9},{9,... | collective-permute-start | bytes 786440 | tf_op jit(solution)/shard_map/ppermute | solution.py:192
  67.4 3.9 %collective-permute-start.5 = (bf16[2,512,128]{2,1,0:T(8,128)(2,1)S(1)}, bf16[2,512,128]{2,1,0:T(8,128)(2,1)S(1)}, u32[]{:S(2)}, u32[]{:S(2)}) collective-permute-start(bf16[2,512,128]{2,1,0:T(8,128)(2,1)S(1)} %get-tuple-element.208), channel_id=1, source_target_pairs={{0,4},{4,8},{8,12},{12,16},{16,20},{20,24},{24,28},{1,5},{5,9},{9,... | collective-permute-start | bytes 786440 | tf_op jit(solution)/shard_map/ppermute | solution.py:192
  73.4 2.4 %collective-permute-start.6 = (bf16[2,512,128]{2,1,0:T(8,128)(2,1)S(1)}, bf16[2,512,128]{2,1,0:T(8,128)(2,1)S(1)}, u32[]{:S(2)}, u32[]{:S(2)}) collective-permute-start(bf16[2,512,128]{2,1,0:T(8,128)(2,1)S(1)} %get-tuple-element.212), channel_id=1, source_target_pairs={{0,4},{4,8},{8,12},{12,16},{16,20},{20,24},{24,28},{1,5},{5,9},{9,... | collective-permute-start | bytes 786440 | tf_op jit(solution)/shard_map/ppermute | solution.py:192
  78.0 4.0 %collective-permute-start.7 = (bf16[2,512,128]{2,1,0:T(8,128)(2,1)S(1)}, bf16[2,512,128]{2,1,0:T(8,128)(2,1)S(1)}, u32[]{:S(2)}, u32[]{:S(2)}) collective-permute-start(bf16[2,512,128]{2,1,0:T(8,128)(2,1)S(1)} %get-tuple-element.216), channel_id=1, source_target_pairs={{0,4},{4,8},{8,12},{12,16},{16,20},{20,24},{24,28},{1,5},{5,9},{9,... | collective-permute-start | bytes 786440 | tf_op jit(solution)/shard_map/ppermute | solution.py:192
  88.7 4.0 %collective-permute-start.9 = (bf16[2,512,128]{2,1,0:T(8,128)(2,1)S(1)}, bf16[2,512,128]{2,1,0:T(8,128)(2,1)S(1)}, u32[]{:S(2)}, u32[]{:S(2)}) collective-permute-start(bf16[2,512,128]{2,1,0:T(8,128)(2,1)S(1)} %get-tuple-element.220), channel_id=1, source_target_pairs={{0,4},{4,8},{8,12},{12,16},{16,20},{20,24},{24,28},{1,5},{5,9},{9,... | collective-permute-start | bytes 786440 | tf_op jit(solution)/shard_map/ppermute | solution.py:192
  99.4 4.0 %collective-permute-start.11 = (bf16[2,512,128]{2,1,0:T(8,128)(2,1)S(1)}, bf16[2,512,128]{2,1,0:T(8,128)(2,1)S(1)}, u32[]{:S(2)}, u32[]{:S(2)}) collective-permute-start(bf16[2,512,128]{2,1,0:T(8,128)(2,1)S(1)} %get-tuple-element.228), channel_id=1, source_target_pairs={{0,4},{4,8},{8,12},{12,16},{16,20},{20,24},{24,28},{1,5},{5,9},{9,... | collective-permute-start | bytes 786440 | tf_op jit(solution)/shard_map/ppermute | solution.py:192
  105.6 2.6 %collective-permute-start.12 = (bf16[2,512,128]{2,1,0:T(8,128)(2,1)S(1)}, bf16[2,512,128]{2,1,0:T(8,128)(2,1)S(1)}, u32[]{:S(2)}, u32[]{:S(2)}) collective-permute-start(bf16[2,512,128]{2,1,0:T(8,128)(2,1)S(1)} %get-tuple-element.171), channel_id=1, source_target_pairs={{0,4},{4,8},{8,12},{12,16},{16,20},{20,24},{24,28},{1,5},{5,9},{9,... | collective-permute-start | bytes 786440 | tf_op jit(solution)/shard_map/ppermute | solution.py:192
  110.3 4.0 %collective-permute-start.13 = (bf16[2,512,128]{2,1,0:T(8,128)(2,1)S(1)}, bf16[2,512,128]{2,1,0:T(8,128)(2,1)S(1)}, u32[]{:S(2)}, u32[]{:S(2)}) collective-permute-start(bf16[2,512,128]{2,1,0:T(8,128)(2,1)S(1)} %get-tuple-element.175), channel_id=1, source_target_pairs={{0,4},{4,8},{8,12},{12,16},{16,20},{20,24},{24,28},{1,5},{5,9},{9,... | collective-permute-start | bytes 786440 | tf_op jit(solution)/shard_map/ppermute | solution.py:192
  116.5 2.4 %collective-permute-start.14 = (bf16[2,512,128]{2,1,0:T(8,128)(2,1)S(1)}, bf16[2,512,128]{2,1,0:T(8,128)(2,1)S(1)}, u32[]{:S(2)}, u32[]{:S(2)}) collective-permute-start(bf16[2,512,128]{2,1,0:T(8,128)(2,1)S(1)} %get-tuple-element.179), channel_id=1, source_target_pairs={{0,4},{4,8},{8,12},{12,16},{16,20},{20,24},{24,28},{1,5},{5,9},{9,... | collective-permute-start | bytes 786440 | tf_op jit(solution)/shard_map/ppermute | solution.py:192
  121.1 4.0 %collective-permute-start.15 = (bf16[2,512,128]{2,1,0:T(8,128)(2,1)S(1)}, bf16[2,512,128]{2,1,0:T(8,128)(2,1)S(1)}, u32[]{:S(2)}, u32[]{:S(2)}) collective-permute-start(bf16[2,512,128]{2,1,0:T(8,128)(2,1)S(1)} %get-tuple-element.135), channel_id=1, source_target_pairs={{0,4},{4,8},{8,12},{12,16},{16,20},{20,24},{24,28},{1,5},{5,9},{9,... | collective-permute-start | bytes 786440 | tf_op jit(solution)/shard_map/ppermute | solution.py:192
  131.6 4.1 %collective-permute-start.17 = (bf16[2,512,128]{2,1,0:T(8,128)(2,1)S(1)}, bf16[2,512,128]{2,1,0:T(8,128)(2,1)S(1)}, u32[]{:S(2)}, u32[]{:S(2)}) collective-permute-start(bf16[2,512,128]{2,1,0:T(8,128)(2,1)S(1)} %get-tuple-element.139), channel_id=1, source_target_pairs={{0,4},{4,8},{8,12},{12,16},{16,20},{20,24},{24,28},{1,5},{5,9},{9,... | collective-permute-start | bytes 786440 | tf_op jit(solution)/shard_map/ppermute | solution.py:192
  142.3 4.1 %collective-permute-start.19 = (bf16[2,512,128]{2,1,0:T(8,128)(2,1)S(1)}, bf16[2,512,128]{2,1,0:T(8,128)(2,1)S(1)}, u32[]{:S(2)}, u32[]{:S(2)}) collective-permute-start(bf16[2,512,128]{2,1,0:T(8,128)(2,1)S(1)} %get-tuple-element.163), channel_id=1, source_target_pairs={{0,4},{4,8},{8,12},{12,16},{16,20},{20,24},{24,28},{1,5},{5,9},{9,... | collective-permute-start | bytes 786440 | tf_op jit(solution)/shard_map/ppermute | solution.py:192
  153.0 4.1 %collective-permute-start.21 = (bf16[2,512,128]{2,1,0:T(8,128)(2,1)S(1)}, bf16[2,512,128]{2,1,0:T(8,128)(2,1)S(1)}, u32[]{:S(2)}, u32[]{:S(2)}) collective-permute-start(bf16[2,512,128]{2,1,0:T(8,128)(2,1)S(1)} %get-tuple-element.232), channel_id=1, source_target_pairs={{0,4},{4,8},{8,12},{12,16},{16,20},{20,24},{24,28},{1,5},{5,9},{9,... | collective-permute-start | bytes 786440 | tf_op jit(solution)/shard_map/ppermute | solution.py:192
  163.8 4.1 %collective-permute-start.23 = (bf16[2,512,128]{2,1,0:T(8,128)(2,1)S(1)}, bf16[2,512,128]{2,1,0:T(8,128)(2,1)S(1)}, u32[]{:S(2)}, u32[]{:S(2)}) collective-permute-start(bf16[2,512,128]{2,1,0:T(8,128)(2,1)S(1)} %get-tuple-element.245), channel_id=1, source_target_pairs={{0,4},{4,8},{8,12},{12,16},{16,20},{20,24},{24,28},{1,5},{5,9},{9,... | collective-permute-start | bytes 786440 | tf_op jit(solution)/shard_map/ppermute | solution.py:192
  174.5 4.1 %collective-permute-start.25 = (bf16[2,512,128]{2,1,0:T(8,128)(2,1)S(1)}, bf16[2,512,128]{2,1,0:T(8,128)(2,1)S(1)}, u32[]{:S(2)}, u32[]{:S(2)}) collective-permute-start(bf16[2,512,128]{2,1,0:T(8,128)(2,1)S(1)} %get-tuple-element.236), channel_id=1, source_target_pairs={{0,4},{4,8},{8,12},{12,16},{16,20},{20,24},{24,28},{1,5},{5,9},{9,... | collective-permute-start | bytes 786440 | tf_op jit(solution)/shard_map/ppermute | solution.py:192
  185.2 4.1 %collective-permute-start.27 = (bf16[2,512,128]{2,1,0:T(8,128)(2,1)S(1)}, bf16[2,512,128]{2,1,0:T(8,128)(2,1)S(1)}, u32[]{:S(2)}, u32[]{:S(2)}) collective-permute-start(bf16[2,512,128]{2,1,0:T(8,128)(2,1)S(1)} %get-tuple-element.167), channel_id=1, source_target_pairs={{0,4},{4,8},{8,12},{12,16},{16,20},{20,24},{24,28},{1,5},{5,9},{9,... | collective-permute-start | bytes 786440 | tf_op jit(solution)/shard_map/ppermute | solution.py:192
  189.5 2.8 %tick.32 = (f32[30,3,512]{2,1,0:T(4,128)S(1)}, bf16[2,512,128]{2,1,0:T(8,128)(2,1)}) fusion(f32[30,3,512]{2,1,0:T(4,128)S(1)} %get-tuple-element.166, s32[1]{0:T(128)} %bitcast.57, bf16[2,512,128]{2,1,0:T(8,128)(2,1)S(1)} %collective-permute-done.26, bf16[2,768,512]{2,1,0:T(8,128)(2,1)S(1)} %copy-done, ...), kind=kCustom, calls=%fused_computation.14 | custom fusion | bytes 10625028 | tf_op jit(solution)/shard_map/tick/pallas_call | solution.py:187
  192.3 2.8 %tick.31 = (f32[30,3,512]{2,1,0:T(4,128)S(1)}, bf16[2,512,128]{2,1,0:T(8,128)(2,1)}) fusion(f32[30,3,512]{2,1,0:T(4,128)S(1)} %get-tuple-element.183, s32[1]{0:T(128)} %bitcast.59, bf16[2,512,128]{2,1,0:T(8,128)(2,1)S(1)} %collective-permute-done.27, bf16[2,768,512]{2,1,0:T(8,128)(2,1)S(1)} %copy-done, ...), kind=kCustom, calls=%fused_computation.13 | custom fusion | bytes 10625028 | tf_op jit(solution)/shard_map/tick/pallas_call | solution.py:187
  195.2 3.6 %collective-permute-start.28 = (f32[208,128]{1,0:T(8,128)S(1)}, f32[208,128]{1,0:T(8,128)S(1)}, u32[]{:S(2)}, u32[]{:S(2)}) collective-permute-start(f32[208,128]{1,0:T(8,128)S(1)} %pad_maximum_fusion), channel_id=1, source_target_pairs={{0,3},{1,0},{2,1},{3,2},{4,7},{5,4},{6,5},{7,6},{8,11},{9,8},{10,9... | collective-permute-start | bytes 319496 | tf_op jit(solution)/shard_map/ppermute | solution.py:202
  202.2 7.4 %collective-permute-done.29 = f32[208,128]{1,0:T(8,128)S(1)} collective-permute-done((f32[208,128]{1,0:T(8,128)S(1)}, f32[208,128]{1,0:T(8,128)S(1)}, u32[]{:S(2)}, u32[]{:S(2)}) %collective-permute-start.29) | collective-permute-done | bytes 106528 | tf_op jit(solution)/shard_map/ppermute | solution.py:202
  (125 shorter events, 102.4 us)
Async XLA Ops:
  41.5 9.8 %collective-permute-start = (bf16[2,512,128]{2,1,0:T(8,128)(2,1)}, bf16[2,512,128]{2,1,0:T(8,128)(2,1)S(1)}, u32[]{:S(2)}, u32[]{:S(2)}) collective-permute-start(bf16[2,512,128]{2,1,0:T(8,128)(2,1)} %get-tuple-element.66), channel_id=1, source_target_pairs={{0,4},{4,8},{8,12},{12,16},{16,20},{20,24},{24,28},{1,5},{5,9},{9,... | collective-permute-start | bytes 786440 | tf_op jit(solution)/shard_map/ppermute | solution.py:192
  46.8 8.6 %collective-permute-start.1 = (bf16[2,512,128]{2,1,0:T(8,128)(2,1)S(1)}, bf16[2,512,128]{2,1,0:T(8,128)(2,1)S(1)}, u32[]{:S(2)}, u32[]{:S(2)}) collective-permute-start(bf16[2,512,128]{2,1,0:T(8,128)(2,1)S(1)} %get-tuple-element.200), channel_id=1, source_target_pairs={{0,4},{4,8},{8,12},{12,16},{16,20},{20,24},{24,28},{1,5},{5,9},{9,... | collective-permute-start | bytes 786440 | tf_op jit(solution)/shard_map/ppermute | solution.py:192
  73.4 8.6 %collective-permute-start.6 = (bf16[2,512,128]{2,1,0:T(8,128)(2,1)S(1)}, bf16[2,512,128]{2,1,0:T(8,128)(2,1)S(1)}, u32[]{:S(2)}, u32[]{:S(2)}) collective-permute-start(bf16[2,512,128]{2,1,0:T(8,128)(2,1)S(1)} %get-tuple-element.212), channel_id=1, source_target_pairs={{0,4},{4,8},{8,12},{12,16},{16,20},{20,24},{24,28},{1,5},{5,9},{9,... | collective-permute-start | bytes 786440 | tf_op jit(solution)/shard_map/ppermute | solution.py:192
  78.0 8.6 %collective-permute-start.7 = (bf16[2,512,128]{2,1,0:T(8,128)(2,1)S(1)}, bf16[2,512,128]{2,1,0:T(8,128)(2,1)S(1)}, u32[]{:S(2)}, u32[]{:S(2)}) collective-permute-start(bf16[2,512,128]{2,1,0:T(8,128)(2,1)S(1)} %get-tuple-element.216), channel_id=1, source_target_pairs={{0,4},{4,8},{8,12},{12,16},{16,20},{20,24},{24,28},{1,5},{5,9},{9,... | collective-permute-start | bytes 786440 | tf_op jit(solution)/shard_map/ppermute | solution.py:192
  84.1 8.6 %collective-permute-start.8 = (bf16[2,512,128]{2,1,0:T(8,128)(2,1)S(1)}, bf16[2,512,128]{2,1,0:T(8,128)(2,1)S(1)}, u32[]{:S(2)}, u32[]{:S(2)}) collective-permute-start(bf16[2,512,128]{2,1,0:T(8,128)(2,1)S(1)} %get-tuple-element.131), channel_id=1, source_target_pairs={{0,4},{4,8},{8,12},{12,16},{16,20},{20,24},{24,28},{1,5},{5,9},{9,... | collective-permute-start | bytes 786440 | tf_op jit(solution)/shard_map/ppermute | solution.py:192
  88.7 8.6 %collective-permute-start.9 = (bf16[2,512,128]{2,1,0:T(8,128)(2,1)S(1)}, bf16[2,512,128]{2,1,0:T(8,128)(2,1)S(1)}, u32[]{:S(2)}, u32[]{:S(2)}) collective-permute-start(bf16[2,512,128]{2,1,0:T(8,128)(2,1)S(1)} %get-tuple-element.220), channel_id=1, source_target_pairs={{0,4},{4,8},{8,12},{12,16},{16,20},{20,24},{24,28},{1,5},{5,9},{9,... | collective-permute-start | bytes 786440 | tf_op jit(solution)/shard_map/ppermute | solution.py:192
  94.9 8.6 %collective-permute-start.10 = (bf16[2,512,128]{2,1,0:T(8,128)(2,1)S(1)}, bf16[2,512,128]{2,1,0:T(8,128)(2,1)S(1)}, u32[]{:S(2)}, u32[]{:S(2)}) collective-permute-start(bf16[2,512,128]{2,1,0:T(8,128)(2,1)S(1)} %get-tuple-element.224), channel_id=1, source_target_pairs={{0,4},{4,8},{8,12},{12,16},{16,20},{20,24},{24,28},{1,5},{5,9},{9,... | collective-permute-start | bytes 786440 | tf_op jit(solution)/shard_map/ppermute | solution.py:192
  99.4 8.7 %collective-permute-start.11 = (bf16[2,512,128]{2,1,0:T(8,128)(2,1)S(1)}, bf16[2,512,128]{2,1,0:T(8,128)(2,1)S(1)}, u32[]{:S(2)}, u32[]{:S(2)}) collective-permute-start(bf16[2,512,128]{2,1,0:T(8,128)(2,1)S(1)} %get-tuple-element.228), channel_id=1, source_target_pairs={{0,4},{4,8},{8,12},{12,16},{16,20},{20,24},{24,28},{1,5},{5,9},{9,... | collective-permute-start | bytes 786440 | tf_op jit(solution)/shard_map/ppermute | solution.py:192
  105.6 8.7 %collective-permute-start.12 = (bf16[2,512,128]{2,1,0:T(8,128)(2,1)S(1)}, bf16[2,512,128]{2,1,0:T(8,128)(2,1)S(1)}, u32[]{:S(2)}, u32[]{:S(2)}) collective-permute-start(bf16[2,512,128]{2,1,0:T(8,128)(2,1)S(1)} %get-tuple-element.171), channel_id=1, source_target_pairs={{0,4},{4,8},{8,12},{12,16},{16,20},{20,24},{24,28},{1,5},{5,9},{9,... | collective-permute-start | bytes 786440 | tf_op jit(solution)/shard_map/ppermute | solution.py:192
  110.3 8.6 %collective-permute-start.13 = (bf16[2,512,128]{2,1,0:T(8,128)(2,1)S(1)}, bf16[2,512,128]{2,1,0:T(8,128)(2,1)S(1)}, u32[]{:S(2)}, u32[]{:S(2)}) collective-permute-start(bf16[2,512,128]{2,1,0:T(8,128)(2,1)S(1)} %get-tuple-element.175), channel_id=1, source_target_pairs={{0,4},{4,8},{8,12},{12,16},{16,20},{20,24},{24,28},{1,5},{5,9},{9,... | collective-permute-start | bytes 786440 | tf_op jit(solution)/shard_map/ppermute | solution.py:192
  116.5 8.6 %collective-permute-start.14 = (bf16[2,512,128]{2,1,0:T(8,128)(2,1)S(1)}, bf16[2,512,128]{2,1,0:T(8,128)(2,1)S(1)}, u32[]{:S(2)}, u32[]{:S(2)}) collective-permute-start(bf16[2,512,128]{2,1,0:T(8,128)(2,1)S(1)} %get-tuple-element.179), channel_id=1, source_target_pairs={{0,4},{4,8},{8,12},{12,16},{16,20},{20,24},{24,28},{1,5},{5,9},{9,... | collective-permute-start | bytes 786440 | tf_op jit(solution)/shard_map/ppermute | solution.py:192
  127.2 8.6 %collective-permute-start.16 = (bf16[2,512,128]{2,1,0:T(8,128)(2,1)S(1)}, bf16[2,512,128]{2,1,0:T(8,128)(2,1)S(1)}, u32[]{:S(2)}, u32[]{:S(2)}) collective-permute-start(bf16[2,512,128]{2,1,0:T(8,128)(2,1)S(1)} %get-tuple-element.204), channel_id=1, source_target_pairs={{0,4},{4,8},{8,12},{12,16},{16,20},{20,24},{24,28},{1,5},{5,9},{9,... | collective-permute-start | bytes 786440 | tf_op jit(solution)/shard_map/ppermute | solution.py:192
  131.6 8.6 %collective-permute-start.17 = (bf16[2,512,128]{2,1,0:T(8,128)(2,1)S(1)}, bf16[2,512,128]{2,1,0:T(8,128)(2,1)S(1)}, u32[]{:S(2)}, u32[]{:S(2)}) collective-permute-start(bf16[2,512,128]{2,1,0:T(8,128)(2,1)S(1)} %get-tuple-element.139), channel_id=1, source_target_pairs={{0,4},{4,8},{8,12},{12,16},{16,20},{20,24},{24,28},{1,5},{5,9},{9,... | collective-permute-start | bytes 786440 | tf_op jit(solution)/shard_map/ppermute | solution.py:192
  137.9 8.6 %collective-permute-start.18 = (bf16[2,512,128]{2,1,0:T(8,128)(2,1)S(1)}, bf16[2,512,128]{2,1,0:T(8,128)(2,1)S(1)}, u32[]{:S(2)}, u32[]{:S(2)}) collective-permute-start(bf16[2,512,128]{2,1,0:T(8,128)(2,1)S(1)} %get-tuple-element.155), channel_id=1, source_target_pairs={{0,4},{4,8},{8,12},{12,16},{16,20},{20,24},{24,28},{1,5},{5,9},{9,... | collective-permute-start | bytes 786440 | tf_op jit(solution)/shard_map/ppermute | solution.py:192
  142.3 8.6 %collective-permute-start.19 = (bf16[2,512,128]{2,1,0:T(8,128)(2,1)S(1)}, bf16[2,512,128]{2,1,0:T(8,128)(2,1)S(1)}, u32[]{:S(2)}, u32[]{:S(2)}) collective-permute-start(bf16[2,512,128]{2,1,0:T(8,128)(2,1)S(1)} %get-tuple-element.163), channel_id=1, source_target_pairs={{0,4},{4,8},{8,12},{12,16},{16,20},{20,24},{24,28},{1,5},{5,9},{9,... | collective-permute-start | bytes 786440 | tf_op jit(solution)/shard_map/ppermute | solution.py:192
  148.6 8.6 %collective-permute-start.20 = (bf16[2,512,128]{2,1,0:T(8,128)(2,1)S(1)}, bf16[2,512,128]{2,1,0:T(8,128)(2,1)S(1)}, u32[]{:S(2)}, u32[]{:S(2)}) collective-permute-start(bf16[2,512,128]{2,1,0:T(8,128)(2,1)S(1)} %get-tuple-element.151), channel_id=1, source_target_pairs={{0,4},{4,8},{8,12},{12,16},{16,20},{20,24},{24,28},{1,5},{5,9},{9,... | collective-permute-start | bytes 786440 | tf_op jit(solution)/shard_map/ppermute | solution.py:192
  153.0 8.6 %collective-permute-start.21 = (bf16[2,512,128]{2,1,0:T(8,128)(2,1)S(1)}, bf16[2,512,128]{2,1,0:T(8,128)(2,1)S(1)}, u32[]{:S(2)}, u32[]{:S(2)}) collective-permute-start(bf16[2,512,128]{2,1,0:T(8,128)(2,1)S(1)} %get-tuple-element.232), channel_id=1, source_target_pairs={{0,4},{4,8},{8,12},{12,16},{16,20},{20,24},{24,28},{1,5},{5,9},{9,... | collective-permute-start | bytes 786440 | tf_op jit(solution)/shard_map/ppermute | solution.py:192
  159.4 8.6 %collective-permute-start.22 = (bf16[2,512,128]{2,1,0:T(8,128)(2,1)S(1)}, bf16[2,512,128]{2,1,0:T(8,128)(2,1)S(1)}, u32[]{:S(2)}, u32[]{:S(2)}) collective-permute-start(bf16[2,512,128]{2,1,0:T(8,128)(2,1)S(1)} %get-tuple-element.188), channel_id=1, source_target_pairs={{0,4},{4,8},{8,12},{12,16},{16,20},{20,24},{24,28},{1,5},{5,9},{9,... | collective-permute-start | bytes 786440 | tf_op jit(solution)/shard_map/ppermute | solution.py:192
  163.8 8.6 %collective-permute-start.23 = (bf16[2,512,128]{2,1,0:T(8,128)(2,1)S(1)}, bf16[2,512,128]{2,1,0:T(8,128)(2,1)S(1)}, u32[]{:S(2)}, u32[]{:S(2)}) collective-permute-start(bf16[2,512,128]{2,1,0:T(8,128)(2,1)S(1)} %get-tuple-element.245), channel_id=1, source_target_pairs={{0,4},{4,8},{8,12},{12,16},{16,20},{20,24},{24,28},{1,5},{5,9},{9,... | collective-permute-start | bytes 786440 | tf_op jit(solution)/shard_map/ppermute | solution.py:192
  170.1 8.6 %collective-permute-start.24 = (bf16[2,512,128]{2,1,0:T(8,128)(2,1)S(1)}, bf16[2,512,128]{2,1,0:T(8,128)(2,1)S(1)}, u32[]{:S(2)}, u32[]{:S(2)}) collective-permute-start(bf16[2,512,128]{2,1,0:T(8,128)(2,1)S(1)} %get-tuple-element.159), channel_id=1, source_target_pairs={{0,4},{4,8},{8,12},{12,16},{16,20},{20,24},{24,28},{1,5},{5,9},{9,... | collective-permute-start | bytes 786440 | tf_op jit(solution)/shard_map/ppermute | solution.py:192
  174.5 8.6 %collective-permute-start.25 = (bf16[2,512,128]{2,1,0:T(8,128)(2,1)S(1)}, bf16[2,512,128]{2,1,0:T(8,128)(2,1)S(1)}, u32[]{:S(2)}, u32[]{:S(2)}) collective-permute-start(bf16[2,512,128]{2,1,0:T(8,128)(2,1)S(1)} %get-tuple-element.236), channel_id=1, source_target_pairs={{0,4},{4,8},{8,12},{12,16},{16,20},{20,24},{24,28},{1,5},{5,9},{9,... | collective-permute-start | bytes 786440 | tf_op jit(solution)/shard_map/ppermute | solution.py:192
  180.8 8.7 %collective-permute-start.26 = (bf16[2,512,128]{2,1,0:T(8,128)(2,1)S(1)}, bf16[2,512,128]{2,1,0:T(8,128)(2,1)S(1)}, u32[]{:S(2)}, u32[]{:S(2)}) collective-permute-start(bf16[2,512,128]{2,1,0:T(8,128)(2,1)S(1)} %get-tuple-element.143), channel_id=1, source_target_pairs={{0,4},{4,8},{8,12},{12,16},{16,20},{20,24},{24,28},{1,5},{5,9},{9,... | collective-permute-start | bytes 786440 | tf_op jit(solution)/shard_map/ppermute | solution.py:192
  198.9 10.7 %collective-permute-start.29 = (f32[208,128]{1,0:T(8,128)S(1)}, f32[208,128]{1,0:T(8,128)S(1)}, u32[]{:S(2)}, u32[]{:S(2)}) collective-permute-start(f32[208,128]{1,0:T(8,128)S(1)} %pad_maximum_fusion), channel_id=1, source_target_pairs={{0,2},{1,3},{2,0},{3,1},{4,6},{5,7},{6,4},{7,5},{8,10},{9,11},{10,... | collective-permute-start | bytes 319496 | tf_op jit(solution)/shard_map/ppermute | solution.py:202
  198.9 10.7 %collective-permute-start.30 = (f32[208,128]{1,0:T(8,128)S(1)}, f32[208,128]{1,0:T(8,128)S(1)}, u32[]{:S(2)}, u32[]{:S(2)}) collective-permute-start(f32[208,128]{1,0:T(8,128)S(1)} %pad_maximum_fusion), channel_id=1, source_target_pairs={{0,1},{1,2},{2,3},{3,0},{4,5},{5,6},{6,7},{7,4},{8,9},{9,10},{10,1... | collective-permute-start | bytes 319496 | tf_op jit(solution)/shard_map/ppermute | solution.py:202
  (17 other events, 104.0 us)

commit v2 on v1

v2 whole, which is shorter than its diff:
```python
import functools

import jax
import jax.numpy as jnp
from jax import lax
from jax.experimental import pallas as pl
from jax.experimental.pallas import tpu as pltpu
from jax.sharding import PartitionSpec as P

epsilon = 1e-06
f32 = jnp.float32
bf16 = jnp.bfloat16
pair = 2
flight = 3


def dot(a, b):
    return jnp.dot(a, b, preferred_element_type=f32)


def split(x):
    high = x.astype(bf16)
    return high, (x - high.astype(f32)).astype(bf16)


def cost(flops, read):
    return pl.CostEstimate(flops=flops, bytes_accessed=read, transcendentals=0)


def operator_kernel(dates, a_ref, r_ref, w_ref):
    features = a_ref.shape[-1]
    sens = r_ref.shape[1]
    product = a_ref[0, 0]
    for t in range(dates):
        if t:
            product = dot(a_ref[t, 0], product).astype(bf16)
        row = features + t * sens
        w_ref[0, row : row + sens, :] = dot(r_ref[0], product).astype(bf16)
    w_ref[0, :features, :] = product


def local_kernel(scale_ref, octet_ref, x_ref, a_ref, r_ref, out_ref, rows_ref, state_ref):
    features, micro, lanes = x_ref.shape[2:]
    sens = r_ref.shape[1]
    t = pl.program_id(1)
    rows_ref[...] = x_ref[0, 0].astype(f32).reshape(features * micro, lanes)
    scale = scale_ref[t]
    width = pair * lanes

    def shock(q):
        return scale * jnp.concatenate(
            [rows_ref[pl.ds(q * pair + i, features, stride=micro), :] for i in range(pair)],
            axis=1,
        )

    @pl.when(t == 0)
    def _():
        for q in range(micro // pair):
            state_ref[:, q * width : (q + 1) * width] = shock(q).astype(bf16)

    @pl.when(t > 0)
    def _():
        for q in range(micro // pair):
            cols = slice(q * width, (q + 1) * width)
            state_ref[:, cols] = (shock(q) + dot(a_ref[0, 0], state_ref[:, cols])).astype(bf16)

    row = pl.multiple_of(features + t * sens, sens)
    for q in range(micro // pair):
        state = state_ref[:, q * width : (q + 1) * width]
        out_ref[0, q, pl.ds(row, sens), :] = dot(r_ref[0], state).astype(bf16)

    @pl.when(t == pl.num_programs(1) - 1)
    def _():
        for q in range(micro // pair):
            out_ref[0, q, :features, :] = state_ref[:, q * width : (q + 1) * width]


def join_operator_kernel(core_ref, mine_ref, other_ref, p_ref, q_ref, late_ref):
    features = mine_ref.shape[2]
    first = core_ref[0] == 0
    mine, other = mine_ref[0], other_ref[0]
    early = jnp.where(first, mine, other)
    late = jnp.where(first, other, mine)
    joined = dot(late, early[:features]).astype(bf16)
    p_ref[0] = joined[:features]
    seen = late.shape[0] - features
    q_ref[0, :seen, :] = early[features:]
    q_ref[0, seen:, :] = joined[features:]
    late_ref[0] = late


def join_state_kernel(core_ref, mine_ref, other_ref, late_ref, seen_ref, *end_refs):
    features = late_ref.shape[2]
    first = core_ref[0] == 0
    mine, other = mine_ref[0, 0], other_ref[0, 0]
    early = jnp.where(first, mine, other)
    late = jnp.where(first, other, mine)
    joined = dot(late_ref[0], early[:features]) + late.astype(f32)
    seen = late.shape[0] - features
    seen_ref[0, :seen, :] = early[features:].astype(f32)
    seen_ref[0, seen:, :] = joined[features:]
    end = joined[:features].astype(bf16)
    for q, end_ref in enumerate(end_refs):

        @pl.when(pl.program_id(0) == q)
        def _():
            end_ref[...] = end


def stage_kernel(up_ref, mine_ref, other_ref, a_ref, out_ref):
    up = up_ref[0] == 1
    mine, other = mine_ref[...], other_ref[...]
    early = jnp.where(up, other, mine)
    late = jnp.where(up, mine, other)
    out_ref[...] = (dot(a_ref[0], early) + late.astype(f32)).astype(bf16)


def final_kernel(dates, up_ref, first_ref, last_ref, phi_ref, q_ref, seen_ref, rw_ref, c_ref, out_ref):
    sens = rw_ref.shape[1]
    width = first_ref.shape[1]
    first = first_ref[...].astype(f32)
    first = jnp.where(up_ref[0] == 1, first, jnp.zeros_like(first))
    entering = (first + dot(phi_ref[0], last_ref[...])).astype(bf16)
    seen = seen_ref[0] + dot(q_ref[0], entering)
    weight = rw_ref[0]
    ws = jnp.concatenate(
        [weight * seen[t * sens : (t + 1) * sens] for t in range(dates)], axis=1
    )
    c_high, c_low = split(c_ref[0])
    w_high, w_low = split(ws)
    mixed = dot(
        jnp.concatenate([c_high, c_low, c_high], axis=1),
        jnp.concatenate([w_high, w_high, w_low], axis=0),
    )
    within = jnp.sum(ws * mixed, axis=0, keepdims=True) + epsilon
    root = jnp.sqrt(within)
    net = jnp.clip(jnp.sum(ws, axis=0, keepdims=True), -root, root)
    for t in range(dates):
        out_ref[0, t : t + 1, :] = within[:, t * width : (t + 1) * width]
        out_ref[1, t : t + 1, :] = net[:, t * width : (t + 1) * width]


def shards(
    transition,
    shocks,
    step_days,
    readout,
    risk_weight,
    correlation,
    cross_gamma,
    discount,
    path_counts,
):
    position = lax.axis_index("date")
    segments = lax.axis_size("date")
    zs = lax.axis_size("bucket")
    z = lax.axis_index("bucket")
    dates, buckets, features, batches, lanes = shocks.shape
    sens = readout.shape[1]
    scales = jnp.sqrt(step_days.astype(f32) / 30.0)
    half = batches // 2
    pieces = half // pair
    width = pair * lanes
    seen_rows = dates * sens
    rows = features + seen_rows
    core = lax.rem(position, 2)
    core_flag = core.astype(jnp.int32).reshape(1)
    stages = (segments // 2).bit_length() - 1
    ups = [lax.rem(position // (2 << s), 2).astype(jnp.int32).reshape(1) for s in range(stages)]
    swap = [(i, i ^ 1) for i in range(segments)]
    smem = pl.BlockSpec(memory_space=pltpu.SMEM)

    operators = pl.pallas_call(
        functools.partial(operator_kernel, dates),
        out_shape=jax.ShapeDtypeStruct((buckets, rows, features), bf16),
        grid=(buckets,),
        in_specs=[
            pl.BlockSpec((dates, 1, features, features), lambda b: (0, b, 0, 0)),
            pl.BlockSpec((1, sens, features), lambda b: (b, 0, 0)),
        ],
        out_specs=pl.BlockSpec((1, rows, features), lambda b: (b, 0, 0)),
        cost_estimate=cost(2 * buckets * dates * features**3, 2**23),
        name="operators",
    )(transition, readout)

    def local(octet):
        return pl.pallas_call(
            local_kernel,
            out_shape=jax.ShapeDtypeStruct((buckets, pieces, rows, width), bf16),
            grid_spec=pltpu.PrefetchScalarGridSpec(
                num_scalar_prefetch=2,
                grid=(buckets, dates),
                in_specs=[
                    pl.BlockSpec(
                        (1, 1, features, half, lanes), lambda b, t, s, o: (t, b, 0, o[0], 0)
                    ),
                    pl.BlockSpec((1, 1, features, features), lambda b, t, s, o: (t, b, 0, 0)),
                    pl.BlockSpec((1, sens, features), lambda b, t, s, o: (b, 0, 0)),
                ],
                out_specs=pl.BlockSpec(
                    (1, pieces, rows, width), lambda b, t, s, o: (b, 0, 0, 0)
                ),
                scratch_shapes=[
                    pltpu.VMEM((features * half, lanes), f32),
                    pltpu.VMEM((features, half * lanes), bf16),
                ],
            ),
            cost_estimate=cost(2 * buckets * dates * rows * features * half * lanes // 2, 2**24),
            name="local",
        )(scales, octet, shocks, transition, readout)

    operators_other = lax.ppermute(operators, "date", swap)
    discount = (step_days.astype(f32) / 365.0)[:, None, None] * discount
    discount_other = lax.ppermute(discount, "date", swap)
    sent = local(1 - core_flag)
    late_half = lax.ppermute(sent, "date", swap)

    block3 = lambda r: pl.BlockSpec((1, r, features), lambda b: (b, 0, 0))
    block, seer, late = pl.pallas_call(
        join_operator_kernel,
        out_shape=(
            jax.ShapeDtypeStruct((buckets, features, features), bf16),
            jax.ShapeDtypeStruct((buckets, 2 * seen_rows, features), bf16),
            jax.ShapeDtypeStruct((buckets, rows, features), bf16),
        ),
        grid=(buckets,),
        in_specs=[smem, block3(rows), block3(rows)],
        out_specs=(block3(features), block3(2 * seen_rows), block3(rows)),
        cost_estimate=cost(2 * buckets * rows * features**2, 2**22),
        name="join_operators",
    )(core_flag, operators, operators_other)

    combiners = []
    eye = jnp.broadcast_to(jnp.eye(features, dtype=bf16), (buckets, features, features))
    prefix = eye
    for s in range(stages - 1):
        far = [(i, i ^ (2 << s)) for i in range(segments)]
        rows_half = features // 2
        part = lax.dynamic_slice_in_dim(block, core * rows_half, rows_half, 1)
        part = lax.ppermute(part, "date", far)
        part_other = lax.ppermute(part, "date", swap)
        first = core == 0
        other = jnp.concatenate(
            [jnp.where(first, part, part_other), jnp.where(first, part_other, part)], axis=1
        )
        up = ups[s][0] == 1
        combiners.append(jnp.where(up, block, other))
        if s == 0:
            prefix = jnp.where(up, other, eye)
        else:
            moved = jnp.einsum("bij,bjk->bik", prefix, other, preferred_element_type=f32)
            prefix = jnp.where(up, moved.astype(bf16), prefix)
        if s < stages - 2:
            above = jnp.where(up, block, other)
            below = jnp.where(up, other, block)
            block = jnp.einsum(
                "bij,bjk->bik", above, below, preferred_element_type=f32
            ).astype(bf16)

    own = local(core_flag)

    ends = []
    seens = []
    for b in range(buckets):
        piece = pl.BlockSpec((1, 1, rows, width), lambda q, b=b: (b, q, 0, 0))
        result = pl.pallas_call(
            join_state_kernel,
            out_shape=(jax.ShapeDtypeStruct((pieces, 2 * seen_rows, width), f32),)
            + (jax.ShapeDtypeStruct((features, width), bf16),) * pieces,
            grid=(pieces,),
            in_specs=[
                smem,
                piece,
                piece,
                pl.BlockSpec((1, rows, features), lambda q, b=b: (b, 0, 0)),
            ],
            out_specs=(pl.BlockSpec((1, 2 * seen_rows, width), lambda q: (q, 0, 0)),)
            + (pl.BlockSpec((features, width), lambda q: (0, 0)),) * pieces,
            cost_estimate=cost(2 * rows * features * half * lanes, 2**22),
            name="join_states",
        )(core_flag, own, late_half, late)
        seens.append(result[0])
        ends.extend(result[1:])

    weight_column = risk_weight[:, :, None]
    flat = pl.BlockSpec((features, width), lambda i: (0, 0))
    count = buckets * pieces

    def stage(j, up, mine, other, combiner):
        b = j // pieces
        return pl.pallas_call(
            stage_kernel,
            out_shape=jax.ShapeDtypeStruct((features, width), bf16),
            grid=(1,),
            in_specs=[
                smem,
                flat,
                flat,
                pl.BlockSpec((1, features, features), lambda i: (b, 0, 0)),
            ],
            out_specs=flat,
            cost_estimate=cost(2 * features**2 * width, 2**20),
            name="stage",
        )(up, mine, other, combiner)

    def final(j, up, first, last, operator):
        b, q = divmod(j, pieces)
        return pl.pallas_call(
            functools.partial(final_kernel, 2 * dates),
            out_shape=jax.ShapeDtypeStruct((2, 2 * dates, width), f32),
            grid=(1,),
            in_specs=[
                smem,
                flat,
                flat,
                pl.BlockSpec((1, features, features), lambda i: (b, 0, 0)),
                pl.BlockSpec((1, 2 * seen_rows, features), lambda i: (b, 0, 0)),
                pl.BlockSpec((1, 2 * seen_rows, width), lambda i: (q, 0, 0)),
                pl.BlockSpec((1, sens, 1), lambda i: (b, 0, 0)),
                pl.BlockSpec((1, sens, sens), lambda i: (b, 0, 0)),
            ],
            out_specs=pl.BlockSpec((2, 2 * dates, width), lambda i: (0, 0, 0)),
            cost_estimate=cost(4 * features**2 * width, 2**21),
            name="final",
        )(up, first, last, operator, seer, seens[b], weight_column, correlation)

    always = jnp.ones((1,), jnp.int32)
    hold = [jnp.zeros((features, width), bf16)] * count
    hold_flag = always
    for s in range(stages):
        last = s == stages - 1
        bit = 2 << s
        link = [(i, i ^ bit) for i in range(segments) if not (last and i & bit)]
        arrived = []
        for j in range(count):
            leaving = ends[j]
            if j >= flight:
                leaving, arrived[j - flight] = lax.optimization_barrier(
                    (leaving, arrived[j - flight])
                )
            arrived.append(lax.ppermute(leaving, "date", link))
        if last:
            results = [final(j, hold_flag, hold[j], arrived[j], prefix) for j in range(count)]
        else:
            if s == 0:
                hold = arrived
                hold_flag = ups[0]
            else:
                raise_by = [
                    hold[j].astype(f32)
                    + dot(prefix[j // pieces], arrived[j])
                    for j in range(count)
                ]
                hold = [jnp.where(ups[s][0] == 1, r, h).astype(bf16) for r, h in zip(raise_by, hold)]
            ends = [stage(j, ups[s], ends[j], arrived[j], combiners[s]) for j in range(count)]

    stats = jnp.stack(results).reshape(buckets, pieces, 2, 2 * dates, pair, lanes)
    stats = jnp.moveaxis(stats, 2, 0)
    stats = jnp.moveaxis(stats, 3, 2).reshape(2, buckets, 2 * dates, half, lanes)
    local_micro = discount.shape[1]
    both = jnp.where(
        core == 0,
        jnp.stack([discount, discount_other]),
        jnp.stack([discount_other, discount]),
    )
    body = jnp.concatenate([jnp.sum(stats[0], axis=0, keepdims=True), stats[1]], axis=0)
    message = jnp.concatenate([body.reshape(-1, lanes), both.reshape(-1, lanes)], axis=0)
    gathered = [message]
    for k in range(1, zs):
        gathered.append(lax.ppermute(message, "bucket", [(i, (i + k) % zs) for i in range(zs)]))
    gathered = jnp.roll(jnp.stack(gathered[::-1]), z + 1, axis=0)
    body_rows = body.size // lanes
    parts = gathered[:, :body_rows].reshape(zs, buckets + 1, 2 * dates, half, lanes)
    discounts = gathered[:, body_rows:].reshape(zs, 2 * dates, local_micro, lanes)
    discounts = jnp.swapaxes(discounts, 0, 1).reshape(2 * dates, batches, lanes)
    discounts = lax.dynamic_slice_in_dim(discounts, core * half, half, 1)
    within = jnp.sum(parts[:, 0], axis=0)
    nets = parts[:, 1:].reshape(zs * buckets, 2 * dates, half, lanes)
    gamma = (
        0.5
        * (cross_gamma + cross_gamma.T)
        * (1.0 - jnp.eye(cross_gamma.shape[0], dtype=f32))
    )
    coupled = jnp.sum(gamma[:, :, None, None, None] * nets[None], axis=1)
    squares = within + jnp.sum(nets * coupled, axis=0)
    counts = lax.dynamic_slice_in_dim(path_counts, core * half, half)
    alive = jnp.arange(lanes, dtype=jnp.int32)[None, :] < counts[:, None]
    margins = jnp.where(alive[None], jnp.sqrt(squares), f32(0.0))
    total = jnp.sum(discounts * margins / counts.astype(f32)[None, :, None])
    start = z * local_micro
    holder = start // half
    inside = start - holder * half
    block_of = lambda section: lax.dynamic_slice(
        margins, (section * dates, inside, 0), (dates, local_micro, lanes)
    )
    out = jnp.concatenate(
        [block_of(1 - core).reshape(-1, lanes), jnp.full((8, lanes), total)], axis=0
    )
    came = lax.ppermute(out, "date", swap)
    split_row = dates * local_micro
    margin = jnp.where(
        holder == core, block_of(core), came[:split_row].reshape(dates, local_micro, lanes)
    )
    total = jnp.full((8, lanes), total) + came[split_row:]
    step = 2
    while step < segments:
        total = total + lax.ppermute(total, "date", [(i, i ^ step) for i in range(segments)])
        step *= 2
    return (margin, total[0, 0])


def solution(mesh):
    in_specs = (
        P("date", "bucket", None, None),
        P("date", "bucket", None, None, None),
        P("date"),
        P("bucket", None, None),
        P("bucket", None),
        P("bucket", None, None),
        P(),
        P("date", "bucket", None),
        P(),
    )
    out_specs = (P("date", "bucket", None), P())
    return jax.shard_map(shards, mesh=mesh, in_specs=in_specs, out_specs=out_specs, check_vma=False)
```

time: 224 us -> 182 us (0.81)
  starting transfers between devices: 96.5 us -> 35 us
  local copies, waits for them, and re-layouts: 68.4 us -> 14.4 us
  Pallas kernels: 37.5 us -> 90.1 us
  waiting for transfers between devices: 14.5 us -> 31 us
  other arithmetic: 3.6 us -> 8.34 us
    pallas_call x29 -> x0, local copies, waits for them, and re-layouts: 63.4 us -> none  [shards(): tick(at, received[step], operators, ends, seen, weight_column, correlation)]
    ppermute x28 -> x22, starting transfers between devices: 88.5 us -> 28.7 us  [the longest x16 25.4 us: shards(): arrived.append(lax.ppermute(leaving, 'date', link))]
    pallas_call x2 -> x21, Pallas kernels: 31.8 us -> 84.4 us  [the longest x2 27.8 us: local(): pl.pallas_call(local_kernel, out_shape=jax.ShapeDtypeStruct((buckets, pie...]
    ppermute x28 -> x22, waiting for transfers between devices: 0.07 us -> 17.4 us  [the longest x1 12.5 us: shards(): part = lax.ppermute(part, 'date', far)]
    unnamed x24 -> x64, local copies, waits for them, and re-layouts: 1.51 us -> 9.77 us
    select_n x0 -> x4, other arithmetic: none -> 3.73 us  [the longest x1 1.84 us: shards(): prefix = jnp.where(up, other, eye)]
    ppermute x3 -> x2, waiting for transfers between devices: 4.77 us -> 5.09 us  [shards(): lax.ppermute(total, 'date', [(i, i ^ step) for i in range(segments)])]
  transfers between devices with their start and end apart: 34 -> 27, of which waited for: 5 -> 7; matrix products, arithmetic and copies ran while one was open for 28% -> 7% of each run, Pallas kernels for 0% -> 41%
where the time goes in v2:
time: 182 us; the launch traced here: 180 us
  Pallas kernels  90.1 us (50%)
  starting transfers between devices  35 us (19%)
  waiting for transfers between devices  31 us (17%)
  local copies, waits for them, and re-layouts  14.4 us (8%)
  other arithmetic  8.34 us (5%)
    pallas_call x2, Pallas kernels, local(): pl.pallas_call(local_kernel, out_shape=jax.ShapeDtypeStruct((buckets, pie...  27.8 us
    ppermute x16, starting transfers between devices, shards(): arrived.append(lax.ppermute(leaving, 'date', link))  25.4 us
    pallas_call x8, Pallas kernels, final(): pl.pallas_call(functools.partial(final_kernel, 2 * dates), out_shape=jax....  24.4 us
    pallas_call x8, Pallas kernels, stage(): pl.pallas_call(stage_kernel, out_shape=jax.ShapeDtypeStruct((features, wi...  17.8 us
    ppermute x1, waiting for transfers between devices, shards(): part = lax.ppermute(part, 'date', far)  12.5 us
    pallas_call x2, Pallas kernels, shards(): pl.pallas_call(join_state_kernel, out_shape=(jax.ShapeDtypeStruct((pieces...  10.7 us
    unnamed x64, local copies, waits for them, and re-layouts  9.77 us
    ppermute x3, waiting for transfers between devices, shards(): lax.ppermute(message, 'bucket', [(i, (i + k) % zs) for i in range(zs)])  8.48 us
  transfers between devices with their start and end apart: 27, of which 7 were waited for; matrix products, arithmetic and copies ran while one was open for 7% of the time, Pallas kernels for 41%

profile of v2, /device:TPU:0, one launch (start us, length us, event | category | flops | bytes accessed | tf_op | source)
XLA Modules:
  0.0 179.9 jit_solution(6066496030475466490)
XLA Ops:
  1.8 13.9 %local.3 = bf16[2,4,768,256]{3,2,1,0:T(8,128)(2,1)} custom-call(f32[4]{0:T(128)} %get-tuple-element.82.scale_ref, s32[1]{0:T(128)S(6)} %sub.28.octet_ref, bf16[4,2,512,16,128]{4,3,2,1,0:T(8,128)(2,1)} %x_ref.3, bf16[4,2,512,512]{3,2,1,0:T(8,128)(2,1)} %a_ref.5, bf16[2,64,512]{2,1,0:T(8,128)(2,1)} %r_ref.5), custom_call_target="tpu_custom_call" | custom-call | flops 3221225472 | bytes 16777216 | tf_op jit(solution)/shard_map/local/pallas_call | solution.py:187
  16.2 5.7 %operators.1.mine_ref = bf16[2,768,512]{2,1,0:T(8,128)(2,1)} custom-call(bf16[4,2,512,512]{3,2,1,0:T(8,128)(2,1)} %a_ref.5, bf16[2,64,512]{2,1,0:T(8,128)(2,1)} %r_ref.5), custom_call_target="tpu_custom_call" | custom-call | flops 2147483648 | bytes 8388608 | tf_op jit(solution)/shard_map/operators/pallas_call | solution.py:173
  21.9 3.7 %collective-permute-done.1.other_ref = bf16[2,768,512]{2,1,0:T(8,128)(2,1)} collective-permute-done((bf16[2,768,512]{2,1,0:T(8,128)(2,1)}, bf16[2,768,512]{2,1,0:T(8,128)(2,1)}, u32[]{:S(2)}, u32[]{:S(2)}) %collective-permute-start.1) | collective-permute-done | bytes 1572896 | tf_op jit(solution)/shard_map/ppermute | solution.py:212
  25.6 3.8 %join_operators.1 = (bf16[2,512,512]{2,1,0:T(8,128)(2,1)}, bf16[2,512,512]{2,1,0:T(8,128)(2,1)}, bf16[2,768,512]{2,1,0:T(8,128)(2,1)}) custom-call(s32[1]{0:T(128)} %bitcast.1.octet_ref.core_ref, bf16[2,768,512]{2,1,0:T(8,128)(2,1)} %operators.1.mine_ref, bf16[2,768,512]{2,1,0:T(8,128)(2,1)} %collective-permute-done.1.other_ref), custom_call_target="tpu_custom_call" | custom-call | flops 805306368 | bytes 4194304 | tf_op jit(solution)/shard_map/join_operators/pallas_call | solution.py:219
  31.3 2.6 %collective-permute-start.4 = (bf16[2,256,512]{2,1,0:T(8,128)(2,1)}, bf16[2,256,512]{2,1,0:T(8,128)(2,1)}, u32[]{:S(2)}, u32[]{:S(2)}) collective-permute-start(bf16[2,256,512]{2,1,0:T(8,128)(2,1)} %constant_dynamic-slice_fusion.4), channel_id=1, source_target_pairs={{0,8},{4,12},{8,0},{12,4},{16,24},{20,28},{24,16},{28,20},{1,9},{5... | collective-permute-start | bytes 1572872 | tf_op jit(solution)/shard_map/ppermute | solution.py:240
  34.2 12.5 %collective-permute-done.4 = bf16[2,256,512]{2,1,0:T(8,128)(2,1)} collective-permute-done((bf16[2,256,512]{2,1,0:T(8,128)(2,1)}, bf16[2,256,512]{2,1,0:T(8,128)(2,1)}, u32[]{:S(2)}, u32[]{:S(2)}) %collective-permute-start.4) | collective-permute-done | bytes 524320 | tf_op jit(solution)/shard_map/ppermute | solution.py:240
  48.3 13.9 %local.2.mine_ref = bf16[2,4,768,256]{3,2,1,0:T(8,128)(2,1)} custom-call(f32[4]{0:T(128)} %get-tuple-element.82.scale_ref, s32[1]{0:T(128)} %bitcast.1.octet_ref.core_ref, bf16[4,2,512,16,128]{4,3,2,1,0:T(8,128)(2,1)} %x_ref.3, bf16[4,2,512,512]{3,2,1,0:T(8,128)(2,1)} %a_ref.5, bf16[2,64,512]{2,1,0:T(8,128)(2,1)} %r_ref.5), custom_call_target="tpu_custom_call" | custom-call | flops 3221225472 | bytes 16777216 | tf_op jit(solution)/shard_map/local/pallas_call | solution.py:187
  63.9 5.3 %join_states.2 = (f32[4,512,256]{2,1,0:T(8,128)}, bf16[512,256]{1,0:T(8,128)(2,1)}, bf16[512,256]{1,0:T(8,128)(2,1)}, bf16[512,256]{1,0:T(8,128)(2,1)}, bf16[512,256]{1,0:T(8,128)(2,1)}) custom-call(s32[1]{0:T(128)} %bitcast.1.octet_ref.core_ref, bf16[2,4,768,256]{3,2,1,0:T(8,128)(2,1)} %local.2.mine_ref, bf16[2,4,768,256]{3,2,1,0:T(8,128)(2,1)} %copy-done, ...), custom_call_target="tpu_custom_call" | custom-call | flops 805306368 | bytes 4194304 | tf_op jit(solution)/shard_map/join_states/pallas_call | solution.py:266
  74.4 5.3 %join_states.3 = (f32[4,512,256]{2,1,0:T(8,128)}, bf16[512,256]{1,0:T(8,128)(2,1)}, bf16[512,256]{1,0:T(8,128)(2,1)}, bf16[512,256]{1,0:T(8,128)(2,1)}, bf16[512,256]{1,0:T(8,128)(2,1)}) custom-call(s32[1]{0:T(128)} %bitcast.1.octet_ref.core_ref, bf16[2,4,768,256]{3,2,1,0:T(8,128)(2,1)} %local.2.mine_ref, bf16[2,4,768,256]{3,2,1,0:T(8,128)(2,1)} %copy-done, ...), custom_call_target="tpu_custom_call" | custom-call | flops 805306368 | bytes 4194304 | tf_op jit(solution)/shard_map/join_states/pallas_call | solution.py:266
  82.2 2.3 %stage.11 = bf16[512,256]{1,0:T(8,128)(2,1)} custom-call(s32[1]{0:T(128)} %bitcast.up_ref, bf16[512,256]{1,0:T(8,128)(2,1)} %get-tuple-element.47.mine_ref, bf16[512,256]{1,0:T(8,128)(2,1)} %copy-done.4, bf16[2,512,512]{2,1,0:T(8,128)(2,1)} %get-tuple-element.77.a_ref), custom_call_target="tpu_custom_call" | custom-call | flops 134217728 | bytes 1048576 | tf_op jit(solution)/shard_map/stage/pallas_call | solution.py:291
  84.5 3.6 %collective-permute-start.9 = (bf16[512,256]{1,0:T(8,128)(2,1)}, bf16[512,256]{1,0:T(8,128)(2,1)S(1)}, u32[]{:S(2)}, u32[]{:S(2)}) collective-permute-start(bf16[512,256]{1,0:T(8,128)(2,1)} %stage.11), channel_id=1, source_target_pairs={{0,16},{4,20},{8,24},{12,28},{1,17},{5,21},{9,25},{13,29},{2,18},{... | collective-permute-start | bytes 786440 | tf_op jit(solution)/shard_map/ppermute | solution.py:341
  99.3 2.2 %stage.10 = bf16[512,256]{1,0:T(8,128)(2,1)} custom-call(s32[1]{0:T(128)} %bitcast.up_ref, bf16[512,256]{1,0:T(8,128)(2,1)} %get-tuple-element.50.mine_ref, bf16[512,256]{1,0:T(8,128)(2,1)} %copy-done.3, bf16[2,512,512]{2,1,0:T(8,128)(2,1)} %get-tuple-element.77.a_ref), custom_call_target="tpu_custom_call" | custom-call | flops 134217728 | bytes 1048576 | tf_op jit(solution)/shard_map/stage/pallas_call | solution.py:291
  113.9 3.1 %final.9 = f32[2,8,256]{2,1,0:T(8,128)} custom-call(s32[1]{0:T(128)} %bitcast.up_ref, bf16[512,256]{1,0:T(8,128)(2,1)} %copy-done.4, bf16[512,256]{1,0:T(8,128)(2,1)} %copy-done.10, bf16[2,512,512]{2,1,0:T(8,128)(2,1)} %get-tuple-element.76.phi_ref, bf16[2,512,512]{2,1,0:T(8,128)(2,1)} %get-tuple-element.44.q_ref, ...), custom_call_target="tpu_custom_call" | custom-call | flops 268435456 | bytes 2097152 | tf_op jit(solution)/shard_map/final/pallas_call | solution.py:308
  117.0 3.1 %final.8 = f32[2,8,256]{2,1,0:T(8,128)} custom-call(s32[1]{0:T(128)} %bitcast.up_ref, bf16[512,256]{1,0:T(8,128)(2,1)} %collective-permute-done.2.other_ref.first_ref, bf16[512,256]{1,0:T(8,128)(2,1)} %copy-done.12, bf16[2,512,512]{2,1,0:T(8,128)(2,1)} %get-tuple-element.76.phi_ref, bf16[2,512,512]{2,1,0:T(8,128)(2,1)} %get-tuple-element.44.q_ref, ...), custom_call_target="tpu_custom_call" | custom-call | flops 268435456 | bytes 2097152 | tf_op jit(solution)/shard_map/final/pallas_call | solution.py:308
  120.8 3.0 %final.10 = f32[2,8,256]{2,1,0:T(8,128)} custom-call(s32[1]{0:T(128)} %bitcast.up_ref, bf16[512,256]{1,0:T(8,128)(2,1)} %copy-done.5, bf16[512,256]{1,0:T(8,128)(2,1)} %copy-done.13, bf16[2,512,512]{2,1,0:T(8,128)(2,1)} %get-tuple-element.76.phi_ref, bf16[2,512,512]{2,1,0:T(8,128)(2,1)} %get-tuple-element.44.q_ref, ...), custom_call_target="tpu_custom_call" | custom-call | flops 268435456 | bytes 2097152 | tf_op jit(solution)/shard_map/final/pallas_call | solution.py:308
  133.2 3.1 %final.11 = f32[2,8,256]{2,1,0:T(8,128)} custom-call(s32[1]{0:T(128)} %bitcast.up_ref, bf16[512,256]{1,0:T(8,128)(2,1)} %copy-done.6, bf16[512,256]{1,0:T(8,128)(2,1)} %copy-done.15, bf16[2,512,512]{2,1,0:T(8,128)(2,1)} %get-tuple-element.76.phi_ref, bf16[2,512,512]{2,1,0:T(8,128)(2,1)} %get-tuple-element.44.q_ref, ...), custom_call_target="tpu_custom_call" | custom-call | flops 268435456 | bytes 2097152 | tf_op jit(solution)/shard_map/final/pallas_call | solution.py:308
  137.0 3.1 %final.12 = f32[2,8,256]{2,1,0:T(8,128)} custom-call(s32[1]{0:T(128)} %bitcast.up_ref, bf16[512,256]{1,0:T(8,128)(2,1)} %copy-done.3, bf16[512,256]{1,0:T(8,128)(2,1)} %copy-done.11, bf16[2,512,512]{2,1,0:T(8,128)(2,1)} %get-tuple-element.76.phi_ref, bf16[2,512,512]{2,1,0:T(8,128)(2,1)} %get-tuple-element.44.q_ref, ...), custom_call_target="tpu_custom_call" | custom-call | flops 268435456 | bytes 2097152 | tf_op jit(solution)/shard_map/final/pallas_call | solution.py:308
  141.5 3.1 %final.13 = f32[2,8,256]{2,1,0:T(8,128)} custom-call(s32[1]{0:T(128)} %bitcast.up_ref, bf16[512,256]{1,0:T(8,128)(2,1)} %copy-done.7, bf16[512,256]{1,0:T(8,128)(2,1)} %copy-done.14, bf16[2,512,512]{2,1,0:T(8,128)(2,1)} %get-tuple-element.76.phi_ref, bf16[2,512,512]{2,1,0:T(8,128)(2,1)} %get-tuple-element.44.q_ref, ...), custom_call_target="tpu_custom_call" | custom-call | flops 268435456 | bytes 2097152 | tf_op jit(solution)/shard_map/final/pallas_call | solution.py:308
  146.0 3.1 %final.14 = f32[2,8,256]{2,1,0:T(8,128)} custom-call(s32[1]{0:T(128)} %bitcast.up_ref, bf16[512,256]{1,0:T(8,128)(2,1)} %copy-done.9, bf16[512,256]{1,0:T(8,128)(2,1)} %copy-done.17, bf16[2,512,512]{2,1,0:T(8,128)(2,1)} %get-tuple-element.76.phi_ref, bf16[2,512,512]{2,1,0:T(8,128)(2,1)} %get-tuple-element.44.q_ref, ...), custom_call_target="tpu_custom_call" | custom-call | flops 268435456 | bytes 2097152 | tf_op jit(solution)/shard_map/final/pallas_call | solution.py:308
  150.5 3.0 %final.15 = f32[2,8,256]{2,1,0:T(8,128)} custom-call(s32[1]{0:T(128)} %bitcast.up_ref, bf16[512,256]{1,0:T(8,128)(2,1)} %copy-done.8, bf16[512,256]{1,0:T(8,128)(2,1)} %copy-done.16, bf16[2,512,512]{2,1,0:T(8,128)(2,1)} %get-tuple-element.76.phi_ref, bf16[2,512,512]{2,1,0:T(8,128)(2,1)} %get-tuple-element.44.q_ref, ...), custom_call_target="tpu_custom_call" | custom-call | flops 268435456 | bytes 2097152 | tf_op jit(solution)/shard_map/final/pallas_call | solution.py:308
  154.4 3.6 %collective-permute-start.21 = (f32[224,128]{1,0:T(8,128)S(1)}, f32[224,128]{1,0:T(8,128)S(1)}, u32[]{:S(2)}, u32[]{:S(2)}) collective-permute-start(f32[224,128]{1,0:T(8,128)S(1)} %pad_maximum_fusion.1), channel_id=1, source_target_pairs={{0,3},{1,0},{2,1},{3,2},{4,7},{5,4},{6,5},{7,6},{8,11},{9,8},{10,9... | collective-permute-start | bytes 344072 | tf_op jit(solution)/shard_map/ppermute | solution.py:370
  159.1 2.4 %collective-permute-done.21 = f32[224,128]{1,0:T(8,128)S(1)} collective-permute-done((f32[224,128]{1,0:T(8,128)S(1)}, f32[224,128]{1,0:T(8,128)S(1)}, u32[]{:S(2)}, u32[]{:S(2)}) %collective-permute-start.21) | collective-permute-done | bytes 114720 | tf_op jit(solution)/shard_map/ppermute | solution.py:370
  161.6 6.0 %collective-permute-done.22 = f32[224,128]{1,0:T(8,128)S(1)} collective-permute-done((f32[224,128]{1,0:T(8,128)S(1)}, f32[224,128]{1,0:T(8,128)S(1)}, u32[]{:S(2)}, u32[]{:S(2)}) %collective-permute-start.22) | collective-permute-done | bytes 114720 | tf_op jit(solution)/shard_map/ppermute | solution.py:370
  176.4 3.0 %collective-permute-done.26 = f32[8,128]{1,0:T(8,128)S(1)} collective-permute-done((f32[8,128]{1,0:T(8,128)S(1)}, f32[8,128]{1,0:T(8,128)S(1)}, u32[]{:S(2)}, u32[]{:S(2)}) %collective-permute-start.26) | collective-permute-done | bytes 4128 | tf_op jit(solution)/shard_map/ppermute | solution.py:407
  (153 shorter events, 64.5 us)
Async XLA Ops:
  15.7 46.5 %collective-permute-start = (bf16[2,4,768,256]{3,2,1,0:T(8,128)(2,1)}, bf16[2,4,768,256]{3,2,1,0:T(8,128)(2,1)S(1)}, u32[]{:S(2)}, u32[]{:S(2)}) collective-permute-start(bf16[2,4,768,256]{3,2,1,0:T(8,128)(2,1)} %local.3), channel_id=1, source_target_pairs={{0,4},{4,0},{8,12},{12,8},{16,20},{20,16},{24,28},{28,24},{1,5},{5... | collective-permute-start | bytes 9437192 | tf_op jit(solution)/shard_map/ppermute | solution.py:216
  21.9 3.8 %collective-permute-start.1 = (bf16[2,768,512]{2,1,0:T(8,128)(2,1)}, bf16[2,768,512]{2,1,0:T(8,128)(2,1)}, u32[]{:S(2)}, u32[]{:S(2)}) collective-permute-start(bf16[2,768,512]{2,1,0:T(8,128)(2,1)} %operators.1.mine_ref), channel_id=1, source_target_pairs={{0,4},{4,0},{8,12},{12,8},{16,20},{20,16},{24,28},{28,24},{1,5},{5... | collective-permute-start | bytes 4718600 | tf_op jit(solution)/shard_map/ppermute | solution.py:212
  31.3 15.4 %collective-permute-start.4 = (bf16[2,256,512]{2,1,0:T(8,128)(2,1)}, bf16[2,256,512]{2,1,0:T(8,128)(2,1)}, u32[]{:S(2)}, u32[]{:S(2)}) collective-permute-start(bf16[2,256,512]{2,1,0:T(8,128)(2,1)} %constant_dynamic-slice_fusion.4), channel_id=1, source_target_pairs={{0,8},{4,12},{8,0},{12,4},{16,24},{20,28},{24,16},{28,20},{1,9},{5... | collective-permute-start | bytes 1572872 | tf_op jit(solution)/shard_map/ppermute | solution.py:240
  34.0 59.6 %collective-permute-start.20 = (f32[4,4,128]{2,1,0:T(4,128)S(1)}, f32[4,4,128]{2,1,0:T(4,128)S(1)}, u32[]{:S(2)}, u32[]{:S(2)}) collective-permute-start(f32[4,4,128]{2,1,0:T(4,128)S(1)} %broadcast_multiply_fusion), channel_id=1, source_target_pairs={{0,4},{4,0},{8,12},{12,8},{16,20},{20,16},{24,28},{28,24},{1,5},{5... | collective-permute-start | bytes 24584 | tf_op jit(solution)/shard_map/ppermute | solution.py:214
  46.7 24.3 %collective-permute-start.5 = (bf16[2,256,512]{2,1,0:T(8,128)(2,1)}, bf16[2,256,512]{2,1,0:T(8,128)(2,1)}, u32[]{:S(2)}, u32[]{:S(2)}) collective-permute-start(bf16[2,256,512]{2,1,0:T(8,128)(2,1)} %collective-permute-done.4), channel_id=1, source_target_pairs={{0,4},{4,0},{8,12},{12,8},{16,20},{20,16},{24,28},{28,24},{1,5},{5... | collective-permute-start | bytes 1572872 | tf_op jit(solution)/shard_map/ppermute | solution.py:241
  69.2 10.5 %collective-permute-start.7 = (bf16[512,256]{1,0:T(8,128)(2,1)}, bf16[512,256]{1,0:T(8,128)(2,1)S(1)}, u32[]{:S(2)}, u32[]{:S(2)}) collective-permute-start(bf16[512,256]{1,0:T(8,128)(2,1)} %get-tuple-element.47.mine_ref), channel_id=1, source_target_pairs={{0,8},{4,12},{8,0},{12,4},{16,24},{20,28},{24,16},{28,20},{1,9},{5... | collective-permute-start | bytes 786440 | tf_op jit(solution)/shard_map/ppermute | solution.py:341
  72.3 15.8 %collective-permute-start.2 = (bf16[512,256]{1,0:T(8,128)(2,1)}, bf16[512,256]{1,0:T(8,128)(2,1)}, u32[]{:S(2)}, u32[]{:S(2)}) collective-permute-start(bf16[512,256]{1,0:T(8,128)(2,1)} %get-tuple-element.37.mine_ref), channel_id=1, source_target_pairs={{0,8},{4,12},{8,0},{12,4},{16,24},{20,28},{24,16},{28,20},{1,9},{5... | collective-permute-start | bytes 786440 | tf_op jit(solution)/shard_map/ppermute | solution.py:341
  72.6 19.2 %collective-permute-start.10 = (bf16[512,256]{1,0:T(8,128)(2,1)}, bf16[512,256]{1,0:T(8,128)(2,1)S(1)}, u32[]{:S(2)}, u32[]{:S(2)}) collective-permute-start(bf16[512,256]{1,0:T(8,128)(2,1)} %get-tuple-element.54.mine_ref), channel_id=1, source_target_pairs={{0,8},{4,12},{8,0},{12,4},{16,24},{20,28},{24,16},{28,20},{1,9},{5... | collective-permute-start | bytes 786440 | tf_op jit(solution)/shard_map/ppermute | solution.py:341
  79.7 17.7 %collective-permute-start.8 = (bf16[512,256]{1,0:T(8,128)(2,1)}, bf16[512,256]{1,0:T(8,128)(2,1)S(1)}, u32[]{:S(2)}, u32[]{:S(2)}) collective-permute-start(bf16[512,256]{1,0:T(8,128)(2,1)} %get-tuple-element.50.mine_ref), channel_id=1, source_target_pairs={{0,8},{4,12},{8,0},{12,4},{16,24},{20,28},{24,16},{28,20},{1,9},{5... | collective-permute-start | bytes 786440 | tf_op jit(solution)/shard_map/ppermute | solution.py:341
  84.5 17.0 %collective-permute-start.9 = (bf16[512,256]{1,0:T(8,128)(2,1)}, bf16[512,256]{1,0:T(8,128)(2,1)S(1)}, u32[]{:S(2)}, u32[]{:S(2)}) collective-permute-start(bf16[512,256]{1,0:T(8,128)(2,1)} %stage.11), channel_id=1, source_target_pairs={{0,16},{4,20},{8,24},{12,28},{1,17},{5,21},{9,25},{13,29},{2,18},{... | collective-permute-start | bytes 786440 | tf_op jit(solution)/shard_map/ppermute | solution.py:341
  88.1 14.9 %collective-permute-start.3 = (bf16[512,256]{1,0:T(8,128)(2,1)}, bf16[512,256]{1,0:T(8,128)(2,1)S(1)}, u32[]{:S(2)}, u32[]{:S(2)}) collective-permute-start(bf16[512,256]{1,0:T(8,128)(2,1)} %get-tuple-element.40.mine_ref), channel_id=1, source_target_pairs={{0,8},{4,12},{8,0},{12,4},{16,24},{20,28},{24,16},{28,20},{1,9},{5... | collective-permute-start | bytes 786440 | tf_op jit(solution)/shard_map/ppermute | solution.py:341
  91.8 15.2 %collective-permute-start.6 = (bf16[512,256]{1,0:T(8,128)(2,1)}, bf16[512,256]{1,0:T(8,128)(2,1)S(1)}, u32[]{:S(2)}, u32[]{:S(2)}) collective-permute-start(bf16[512,256]{1,0:T(8,128)(2,1)} %stage.9), channel_id=1, source_target_pairs={{0,16},{4,20},{8,24},{12,28},{1,17},{5,21},{9,25},{13,29},{2,18},{... | collective-permute-start | bytes 786440 | tf_op jit(solution)/shard_map/ppermute | solution.py:341
  93.6 15.0 %collective-permute-start.11 = (bf16[512,256]{1,0:T(8,128)(2,1)S(1)}, bf16[512,256]{1,0:T(8,128)(2,1)S(1)}, u32[]{:S(2)}, u32[]{:S(2)}) collective-permute-start(bf16[512,256]{1,0:T(8,128)(2,1)S(1)} %copy-done.19), channel_id=1, source_target_pairs={{0,8},{4,12},{8,0},{12,4},{16,24},{20,28},{24,16},{28,20},{1,9},{5... | collective-permute-start | bytes 786440 | tf_op jit(solution)/shard_map/ppermute | solution.py:341
  97.4 15.2 %collective-permute-start.12 = (bf16[512,256]{1,0:T(8,128)(2,1)}, bf16[512,256]{1,0:T(8,128)(2,1)S(1)}, u32[]{:S(2)}, u32[]{:S(2)}) collective-permute-start(bf16[512,256]{1,0:T(8,128)(2,1)} %stage.13), channel_id=1, source_target_pairs={{0,16},{4,20},{8,24},{12,28},{1,17},{5,21},{9,25},{13,29},{2,18},{... | collective-permute-start | bytes 786440 | tf_op jit(solution)/shard_map/ppermute | solution.py:341
  101.5 23.0 %collective-permute-start.15 = (bf16[512,256]{1,0:T(8,128)(2,1)}, bf16[512,256]{1,0:T(8,128)(2,1)S(1)}, u32[]{:S(2)}, u32[]{:S(2)}) collective-permute-start(bf16[512,256]{1,0:T(8,128)(2,1)} %get-tuple-element.61.mine_ref), channel_id=1, source_target_pairs={{0,8},{4,12},{8,0},{12,4},{16,24},{20,28},{24,16},{28,20},{1,9},{5... | collective-permute-start | bytes 786440 | tf_op jit(solution)/shard_map/ppermute | solution.py:341
  103.0 24.4 %collective-permute-start.16 = (bf16[512,256]{1,0:T(8,128)(2,1)}, bf16[512,256]{1,0:T(8,128)(2,1)S(1)}, u32[]{:S(2)}, u32[]{:S(2)}) collective-permute-start(bf16[512,256]{1,0:T(8,128)(2,1)} %stage.10), channel_id=1, source_target_pairs={{0,16},{4,20},{8,24},{12,28},{1,17},{5,21},{9,25},{13,29},{2,18},{... | collective-permute-start | bytes 786440 | tf_op jit(solution)/shard_map/ppermute | solution.py:341
  107.0 21.7 %collective-permute-start.13 = (bf16[512,256]{1,0:T(8,128)(2,1)S(1)}, bf16[512,256]{1,0:T(8,128)(2,1)S(1)}, u32[]{:S(2)}, u32[]{:S(2)}) collective-permute-start(bf16[512,256]{1,0:T(8,128)(2,1)S(1)} %copy-done.18), channel_id=1, source_target_pairs={{0,8},{4,12},{8,0},{12,4},{16,24},{20,28},{24,16},{28,20},{1,9},{5... | collective-permute-start | bytes 786440 | tf_op jit(solution)/shard_map/ppermute | solution.py:341
  108.6 23.1 %collective-permute-start.14 = (bf16[512,256]{1,0:T(8,128)(2,1)}, bf16[512,256]{1,0:T(8,128)(2,1)S(1)}, u32[]{:S(2)}, u32[]{:S(2)}) collective-permute-start(bf16[512,256]{1,0:T(8,128)(2,1)} %stage.8), channel_id=1, source_target_pairs={{0,16},{4,20},{8,24},{12,28},{1,17},{5,21},{9,25},{13,29},{2,18},{... | collective-permute-start | bytes 786440 | tf_op jit(solution)/shard_map/ppermute | solution.py:341
  112.6 28.1 %collective-permute-start.17 = (bf16[512,256]{1,0:T(8,128)(2,1)}, bf16[512,256]{1,0:T(8,128)(2,1)S(1)}, u32[]{:S(2)}, u32[]{:S(2)}) collective-permute-start(bf16[512,256]{1,0:T(8,128)(2,1)} %stage.12), channel_id=1, source_target_pairs={{0,16},{4,20},{8,24},{12,28},{1,17},{5,21},{9,25},{13,29},{2,18},{... | collective-permute-start | bytes 786440 | tf_op jit(solution)/shard_map/ppermute | solution.py:341
  127.5 22.3 %collective-permute-start.19 = (bf16[512,256]{1,0:T(8,128)(2,1)}, bf16[512,256]{1,0:T(8,128)(2,1)S(1)}, u32[]{:S(2)}, u32[]{:S(2)}) collective-permute-start(bf16[512,256]{1,0:T(8,128)(2,1)} %stage.15), channel_id=1, source_target_pairs={{0,16},{4,20},{8,24},{12,28},{1,17},{5,21},{9,25},{13,29},{2,18},{... | collective-permute-start | bytes 786440 | tf_op jit(solution)/shard_map/ppermute | solution.py:341
  131.7 13.5 %collective-permute-start.18 = (bf16[512,256]{1,0:T(8,128)(2,1)}, bf16[512,256]{1,0:T(8,128)(2,1)S(1)}, u32[]{:S(2)}, u32[]{:S(2)}) collective-permute-start(bf16[512,256]{1,0:T(8,128)(2,1)} %stage.14), channel_id=1, source_target_pairs={{0,16},{4,20},{8,24},{12,28},{1,17},{5,21},{9,25},{13,29},{2,18},{... | collective-permute-start | bytes 786440 | tf_op jit(solution)/shard_map/ppermute | solution.py:341
  154.4 7.2 %collective-permute-start.21 = (f32[224,128]{1,0:T(8,128)S(1)}, f32[224,128]{1,0:T(8,128)S(1)}, u32[]{:S(2)}, u32[]{:S(2)}) collective-permute-start(f32[224,128]{1,0:T(8,128)S(1)} %pad_maximum_fusion.1), channel_id=1, source_target_pairs={{0,3},{1,0},{2,1},{3,2},{4,7},{5,4},{6,5},{7,6},{8,11},{9,8},{10,9... | collective-permute-start | bytes 344072 | tf_op jit(solution)/shard_map/ppermute | solution.py:370
  158.1 9.5 %collective-permute-start.22 = (f32[224,128]{1,0:T(8,128)S(1)}, f32[224,128]{1,0:T(8,128)S(1)}, u32[]{:S(2)}, u32[]{:S(2)}) collective-permute-start(f32[224,128]{1,0:T(8,128)S(1)} %pad_maximum_fusion.1), channel_id=1, source_target_pairs={{0,2},{1,3},{2,0},{3,1},{4,6},{5,7},{6,4},{7,5},{8,10},{9,11},{10,... | collective-permute-start | bytes 344072 | tf_op jit(solution)/shard_map/ppermute | solution.py:370
  158.1 9.5 %collective-permute-start.23 = (f32[224,128]{1,0:T(8,128)S(1)}, f32[224,128]{1,0:T(8,128)S(1)}, u32[]{:S(2)}, u32[]{:S(2)}) collective-permute-start(f32[224,128]{1,0:T(8,128)S(1)} %pad_maximum_fusion.1), channel_id=1, source_target_pairs={{0,1},{1,2},{2,3},{3,0},{4,5},{5,6},{6,7},{7,4},{8,9},{9,10},{10,1... | collective-permute-start | bytes 344072 | tf_op jit(solution)/shard_map/ppermute | solution.py:370
  (28 other events, 167.1 us)

commit v3 on v2

--- a/solution.py
+++ b/solution.py
@@ -12,6 +12,7 @@
 bf16 = jnp.bfloat16
 pair = 2
 flight = 3
+lag = 2
 
 
 def dot(a, b):
@@ -89,44 +90,43 @@
     late_ref[0] = late
 
 
-def join_state_kernel(core_ref, mine_ref, other_ref, late_ref, seen_ref, *end_refs):
+def join_state_kernel(b, core_ref, mine_ref, other_ref, late_ref, seen_ref, *end_refs):
     features = late_ref.shape[2]
     first = core_ref[0] == 0
-    mine, other = mine_ref[0, 0], other_ref[0, 0]
-    early = jnp.where(first, mine, other)
-    late = jnp.where(first, other, mine)
-    joined = dot(late_ref[0], early[:features]) + late.astype(f32)
-    seen = late.shape[0] - features
-    seen_ref[0, :seen, :] = early[features:].astype(f32)
-    seen_ref[0, seen:, :] = joined[features:]
-    end = joined[:features].astype(bf16)
+    late_operator = late_ref[b]
     for q, end_ref in enumerate(end_refs):
-
-        @pl.when(pl.program_id(0) == q)
-        def _():
-            end_ref[...] = end
-
-
-def stage_kernel(up_ref, mine_ref, other_ref, a_ref, out_ref):
+        mine, other = mine_ref[0, q], other_ref[0, q]
+        early = jnp.where(first, mine, other)
+        late = jnp.where(first, other, mine)
+        joined = dot(late_operator, early[:features]) + late.astype(f32)
+        seen = late.shape[0] - features
+        seen_ref[q, :seen, :] = early[features:].astype(f32)
+        seen_ref[q, seen:, :] = joined[features:]
+        end_ref[...] = joined[:features].astype(bf16)
+
+
+def stage_kernel(b, up_ref, mine_ref, other_ref, a_ref, out_ref):
     up = up_ref[0] == 1
     mine, other = mine_ref[...], other_ref[...]
     early = jnp.where(up, other, mine)
     late = jnp.where(up, mine, other)
-    out_ref[...] = (dot(a_ref[0], early) + late.astype(f32)).astype(bf16)
-
-
-def final_kernel(dates, up_ref, first_ref, last_ref, phi_ref, q_ref, seen_ref, rw_ref, c_ref, out_ref):
+    out_ref[...] = (dot(a_ref[b], early) + late.astype(f32)).astype(bf16)
+
+
+def final_kernel(
+    b, q, dates, up_ref, first_ref, last_ref, phi_ref, q_ref, seen_ref, rw_ref, c_ref, out_ref
+):
     sens = rw_ref.shape[1]
     width = first_ref.shape[1]
     first = first_ref[...].astype(f32)
     first = jnp.where(up_ref[0] == 1, first, jnp.zeros_like(first))
-    entering = (first + dot(phi_ref[0], last_ref[...])).astype(bf16)
-    seen = seen_ref[0] + dot(q_ref[0], entering)
-    weight = rw_ref[0]
+    entering = (first + dot(phi_ref[b], last_ref[...])).astype(bf16)
+    seen = seen_ref[q] + dot(q_ref[b], entering)
+    weight = rw_ref[b]
     ws = jnp.concatenate(
         [weight * seen[t * sens : (t + 1) * sens] for t in range(dates)], axis=1
     )
-    c_high, c_low = split(c_ref[0])
+    c_high, c_low = split(c_ref[b])
     w_high, w_low = split(ws)
     mixed = dot(
         jnp.concatenate([c_high, c_low, c_high], axis=1),
@@ -138,6 +138,65 @@
     for t in range(dates):
         out_ref[0, t : t + 1, :] = within[:, t * width : (t + 1) * width]
         out_ref[1, t : t + 1, :] = net[:, t * width : (t + 1) * width]
+
+
+def pack_kernel(buckets, pieces, *refs):
+    stats, discount_ref, out_ref = refs[:-2], refs[-2], refs[-1]
+    dates = stats[0].shape[1]
+    lanes = out_ref.shape[1]
+    block = pair * dates
+    for q in range(pieces):
+        own = [stats[b * pieces + q] for b in range(buckets)]
+        within = sum(ref[0] for ref in own)
+        for r, value in enumerate([within] + [ref[1] for ref in own]):
+            rows = jnp.concatenate(
+                [value[:, i * lanes : (i + 1) * lanes] for i in range(pair)], axis=0
+            )
+            row = (r * pieces + q) * block
+            out_ref[row : row + block, :] = rows.astype(bf16)
+    out_ref[(buckets + 1) * pieces * block :, :] = discount_ref[...]
+
+
+def margin_kernel(
+    buckets, dates, local_micro, half, place_ref, gamma_ref, count_ref, *refs
+):
+    messages, (out_ref, spread_ref, margin_ref) = refs[:-3], refs[-3:]
+    zs = len(messages)
+    lanes = out_ref.shape[2]
+    body = half * dates
+    shard, core = place_ref[0], place_ref[1]
+    origin = [lax.rem(shard - k + zs, zs) for k in range(zs)]
+    within = 0.0
+    nets = []
+    for k, ref in enumerate(messages):
+        within = within + ref[:body, :].astype(f32)
+        for b in range(buckets):
+            row = (b + 1) * body
+            nets.append((origin[k] * buckets + b, ref[row : row + body, :].astype(f32)))
+        row = (buckets + 1) * body
+        size = local_micro * dates
+        rest = ref[row : row + 2 * size, :].astype(f32)
+        spread_ref[pl.ds(origin[k] * local_micro, local_micro)] = (
+            rest[:size] + rest[size:]
+        ).reshape(local_micro, dates, lanes)
+    squares = within
+    for i, (at, net) in enumerate(nets):
+        coupled = 0.0
+        for k, (other_at, other) in enumerate(nets):
+            if k != i:
+                coupled = coupled + gamma_ref[at, other_at] * other
+        squares = squares + net * coupled
+    root = jnp.sqrt(squares).reshape(half, dates, lanes)
+    lane = lax.broadcasted_iota(jnp.int32, (dates, lanes), 1)
+    total = jnp.zeros((dates, lanes), f32)
+    for m in range(half):
+        live = count_ref[core * half + m]
+        margin = jnp.where(lane < live, root[m], f32(0.0))
+        margin_ref[m] = margin
+        total = total + spread_ref[core * half + m] * margin / live.astype(f32)
+    total = jnp.sum(jnp.sum(total, axis=0, keepdims=True), axis=1, keepdims=True)
+    out_ref[:local_micro] = margin_ref[pl.ds(place_ref[2], local_micro)]
+    out_ref[local_micro] = jnp.broadcast_to(total, (dates, lanes))
 
 
 def shards(
@@ -180,10 +239,11 @@
         ],
         out_specs=pl.BlockSpec((1, rows, features), lambda b: (b, 0, 0)),
         cost_estimate=cost(2 * buckets * dates * features**3, 2**23),
+        compiler_params=pltpu.CompilerParams(vmem_limit_bytes=24 * 2**20),
         name="operators",
     )(transition, readout)
 
-    def local(octet):
+    def local(octet, scales):
         return pl.pallas_call(
             local_kernel,
             out_shape=jax.ShapeDtypeStruct((buckets, pieces, rows, width), bf16),
@@ -205,14 +265,17 @@
                     pltpu.VMEM((features, half * lanes), bf16),
                 ],
             ),
+            compiler_params=pltpu.CompilerParams(vmem_limit_bytes=24 * 2**20),
             cost_estimate=cost(2 * buckets * dates * rows * features * half * lanes // 2, 2**24),
             name="local",
         )(scales, octet, shocks, transition, readout)
 
+    scales, operators = lax.optimization_barrier((scales, operators))
     operators_other = lax.ppermute(operators, "date", swap)
     discount = (step_days.astype(f32) / 365.0)[:, None, None] * discount
     discount_other = lax.ppermute(discount, "date", swap)
-    sent = local(1 - core_flag)
+    sent = local(1 - core_flag, scales)
+    operators_other, sent = lax.optimization_barrier((operators_other, sent))
     late_half = lax.ppermute(sent, "date", swap)
 
     block3 = lambda r: pl.BlockSpec((1, r, features), lambda b: (b, 0, 0))
@@ -227,6 +290,7 @@
         in_specs=[smem, block3(rows), block3(rows)],
         out_specs=(block3(features), block3(2 * seen_rows), block3(rows)),
         cost_estimate=cost(2 * buckets * rows * features**2, 2**22),
+        compiler_params=pltpu.CompilerParams(vmem_limit_bytes=24 * 2**20),
         name="join_operators",
     )(core_flag, operators, operators_other)
 
@@ -237,7 +301,12 @@
         far = [(i, i ^ (2 << s)) for i in range(segments)]
         rows_half = features // 2
         part = lax.dynamic_slice_in_dim(block, core * rows_half, rows_half, 1)
+        if s == 0:
+            scales, part = lax.optimization_barrier((scales, part))
         part = lax.ppermute(part, "date", far)
+        if s == 0:
+            own = local(core_flag, scales)
+            part, own = lax.optimization_barrier((part, own))
         part_other = lax.ppermute(part, "date", swap)
         first = core == 0
         other = jnp.concatenate(
@@ -257,25 +326,23 @@
                 "bij,bjk->bik", above, below, preferred_element_type=f32
             ).astype(bf16)
 
-    own = local(core_flag)
+    if stages < 2:
+        own = local(core_flag, scales)
 
     ends = []
     seens = []
+    vmem = pl.BlockSpec(memory_space=pltpu.VMEM)
+    small = pltpu.CompilerParams(vmem_limit_bytes=16 * 2**20)
     for b in range(buckets):
-        piece = pl.BlockSpec((1, 1, rows, width), lambda q, b=b: (b, q, 0, 0))
+        piece = pl.BlockSpec((1, pieces, rows, width), lambda i, b=b: (b, 0, 0, 0))
         result = pl.pallas_call(
-            join_state_kernel,
+            functools.partial(join_state_kernel, b),
             out_shape=(jax.ShapeDtypeStruct((pieces, 2 * seen_rows, width), f32),)
             + (jax.ShapeDtypeStruct((features, width), bf16),) * pieces,
-            grid=(pieces,),
-            in_specs=[
-                smem,
-                piece,
-                piece,
-                pl.BlockSpec((1, rows, features), lambda q, b=b: (b, 0, 0)),
-            ],
-            out_specs=(pl.BlockSpec((1, 2 * seen_rows, width), lambda q: (q, 0, 0)),)
-            + (pl.BlockSpec((features, width), lambda q: (0, 0)),) * pieces,
+            grid=(1,),
+            in_specs=[smem, piece, piece, vmem],
+            out_specs=(vmem,) * (pieces + 1),
+            compiler_params=small,
             cost_estimate=cost(2 * rows * features * half * lanes, 2**22),
             name="join_states",
         )(core_flag, own, late_half, late)
@@ -283,22 +350,15 @@
         ends.extend(result[1:])
 
     weight_column = risk_weight[:, :, None]
-    flat = pl.BlockSpec((features, width), lambda i: (0, 0))
     count = buckets * pieces
 
     def stage(j, up, mine, other, combiner):
-        b = j // pieces
         return pl.pallas_call(
-            stage_kernel,
+            functools.partial(stage_kernel, j // pieces),
             out_shape=jax.ShapeDtypeStruct((features, width), bf16),
-            grid=(1,),
-            in_specs=[
-                smem,
-                flat,
-                flat,
-                pl.BlockSpec((1, features, features), lambda i: (b, 0, 0)),
-            ],
-            out_specs=flat,
+            in_specs=[smem, vmem, vmem, vmem],
+            out_specs=vmem,
+            compiler_params=small,
             cost_estimate=cost(2 * features**2 * width, 2**20),
             name="stage",
         )(up, mine, other, combiner)
@@ -306,102 +366,105 @@
     def final(j, up, first, last, operator):
         b, q = divmod(j, pieces)
         return pl.pallas_call(
-            functools.partial(final_kernel, 2 * dates),
+            functools.partial(final_kernel, b, q, 2 * dates),
             out_shape=jax.ShapeDtypeStruct((2, 2 * dates, width), f32),
-            grid=(1,),
-            in_specs=[
-                smem,
-                flat,
-                flat,
-                pl.BlockSpec((1, features, features), lambda i: (b, 0, 0)),
-                pl.BlockSpec((1, 2 * seen_rows, features), lambda i: (b, 0, 0)),
-                pl.BlockSpec((1, 2 * seen_rows, width), lambda i: (q, 0, 0)),
-                pl.BlockSpec((1, sens, 1), lambda i: (b, 0, 0)),
-                pl.BlockSpec((1, sens, sens), lambda i: (b, 0, 0)),
-            ],
-            out_specs=pl.BlockSpec((2, 2 * dates, width), lambda i: (0, 0, 0)),
+            in_specs=[smem] + [vmem] * 7,
+            out_specs=vmem,
+            compiler_params=small,
             cost_estimate=cost(4 * features**2 * width, 2**21),
             name="final",
         )(up, first, last, operator, seer, seens[b], weight_column, correlation)
 
-    always = jnp.ones((1,), jnp.int32)
     hold = [jnp.zeros((features, width), bf16)] * count
-    hold_flag = always
+    hold_flag = jnp.ones((1,), jnp.int32)
+    come = None
     for s in range(stages):
         last = s == stages - 1
         bit = 2 << s
         link = [(i, i ^ bit) for i in range(segments) if not (last and i & bit)]
         arrived = []
+        results = []
+        leaving_list = []
         for j in range(count):
-            leaving = ends[j]
+            if come is None:
+                leaving = ends[j]
+            else:
+                near = come[j]
+                if last and j > lag:
+                    near, results[j - lag - 1] = lax.optimization_barrier(
+                        (near, results[j - lag - 1])
+                    )
+                leaving = stage(j, ups[s - 1], ends[j], near, combiners[s - 1])
             if j >= flight:
                 leaving, arrived[j - flight] = lax.optimization_barrier(
                     (leaving, arrived[j - flight])
                 )
+            leaving_list.append(leaving)
             arrived.append(lax.ppermute(leaving, "date", link))
+            if last and j >= lag:
+                i = j - lag
+                results.append(final(i, hold_flag, hold[i], arrived[i], prefix))
         if last:
-            results = [final(j, hold_flag, hold[j], arrived[j], prefix) for j in range(count)]
+            for i in range(len(results), count):
+                results.append(final(i, hold_flag, hold[i], arrived[i], prefix))
         else:
             if s == 0:
                 hold = arrived
                 hold_flag = ups[0]
             else:
-                raise_by = [
-                    hold[j].astype(f32)
-                    + dot(prefix[j // pieces], arrived[j])
+                raised = [
+                    hold[j].astype(f32) + dot(prefix[j // pieces], arrived[j])
                     for j in range(count)
                 ]
-                hold = [jnp.where(ups[s][0] == 1, r, h).astype(bf16) for r, h in zip(raise_by, hold)]
-            ends = [stage(j, ups[s], ends[j], arrived[j], combiners[s]) for j in range(count)]
-
-    stats = jnp.stack(results).reshape(buckets, pieces, 2, 2 * dates, pair, lanes)
-    stats = jnp.moveaxis(stats, 2, 0)
-    stats = jnp.moveaxis(stats, 3, 2).reshape(2, buckets, 2 * dates, half, lanes)
+                hold = [jnp.where(ups[s][0] == 1, r, h).astype(bf16) for r, h in zip(raised, hold)]
+            ends = leaving_list
+            come = arrived
+
     local_micro = discount.shape[1]
     both = jnp.where(
         core == 0,
         jnp.stack([discount, discount_other]),
         jnp.stack([discount_other, discount]),
-    )
-    body = jnp.concatenate([jnp.sum(stats[0], axis=0, keepdims=True), stats[1]], axis=0)
-    message = jnp.concatenate([body.reshape(-1, lanes), both.reshape(-1, lanes)], axis=0)
+    ).reshape(2 * dates, local_micro, lanes)
+    high, low = split(jnp.swapaxes(both, 0, 1))
+    carried = jnp.concatenate([high.reshape(-1, lanes), low.reshape(-1, lanes)], axis=0)
+    body_rows = (buckets + 1) * half * 2 * dates
+    message = pl.pallas_call(
+        functools.partial(pack_kernel, buckets, pieces),
+        out_shape=jax.ShapeDtypeStruct((body_rows + carried.shape[0], lanes), bf16),
+        in_specs=[vmem] * (count + 1),
+        out_specs=vmem,
+        compiler_params=small,
+        name="pack",
+    )(*results, carried)
     gathered = [message]
     for k in range(1, zs):
         gathered.append(lax.ppermute(message, "bucket", [(i, (i + k) % zs) for i in range(zs)]))
-    gathered = jnp.roll(jnp.stack(gathered[::-1]), z + 1, axis=0)
-    body_rows = body.size // lanes
-    parts = gathered[:, :body_rows].reshape(zs, buckets + 1, 2 * dates, half, lanes)
-    discounts = gathered[:, body_rows:].reshape(zs, 2 * dates, local_micro, lanes)
-    discounts = jnp.swapaxes(discounts, 0, 1).reshape(2 * dates, batches, lanes)
-    discounts = lax.dynamic_slice_in_dim(discounts, core * half, half, 1)
-    within = jnp.sum(parts[:, 0], axis=0)
-    nets = parts[:, 1:].reshape(zs * buckets, 2 * dates, half, lanes)
     gamma = (
         0.5
         * (cross_gamma + cross_gamma.T)
         * (1.0 - jnp.eye(cross_gamma.shape[0], dtype=f32))
     )
-    coupled = jnp.sum(gamma[:, :, None, None, None] * nets[None], axis=1)
-    squares = within + jnp.sum(nets * coupled, axis=0)
-    counts = lax.dynamic_slice_in_dim(path_counts, core * half, half)
-    alive = jnp.arange(lanes, dtype=jnp.int32)[None, :] < counts[:, None]
-    margins = jnp.where(alive[None], jnp.sqrt(squares), f32(0.0))
-    total = jnp.sum(discounts * margins / counts.astype(f32)[None, :, None])
     start = z * local_micro
     holder = start // half
-    inside = start - holder * half
-    block_of = lambda section: lax.dynamic_slice(
-        margins, (section * dates, inside, 0), (dates, local_micro, lanes)
-    )
-    out = jnp.concatenate(
-        [block_of(1 - core).reshape(-1, lanes), jnp.full((8, lanes), total)], axis=0
-    )
+    place = jnp.stack([z, core, start - holder * half]).astype(jnp.int32)
+    out = pl.pallas_call(
+        functools.partial(margin_kernel, buckets, 2 * dates, local_micro, half),
+        out_shape=jax.ShapeDtypeStruct((local_micro + 1, 2 * dates, lanes), f32),
+        in_specs=[smem] * 3 + [vmem] * zs,
+        out_specs=vmem,
+        scratch_shapes=[
+            pltpu.VMEM((batches, 2 * dates, lanes), f32),
+            pltpu.VMEM((half, 2 * dates, lanes), f32),
+        ],
+        compiler_params=small,
+        name="margins",
+    )(place, gamma, path_counts, *gathered)
     came = lax.ppermute(out, "date", swap)
-    split_row = dates * local_micro
-    margin = jnp.where(
-        holder == core, block_of(core), came[:split_row].reshape(dates, local_micro, lanes)
-    )
-    total = jnp.full((8, lanes), total) + came[split_row:]
+    margin = jnp.where(holder == core, out[:local_micro], came[:local_micro])
+    margin = lax.dynamic_slice_in_dim(margin, core * dates, dates, 1)
+    margin = jnp.swapaxes(margin, 0, 1)
+    total = out[local_micro] + came[local_micro]
     step = 2
     while step < segments:
         total = total + lax.ppermute(total, "date", [(i, i ^ step) for i in range(segments)])

time: 182 us -> 154 us (0.85)
  Pallas kernels: 90.1 us -> 54 us
  local copies, waits for them, and re-layouts: 14.4 us -> 31.6 us
  waiting for transfers between devices: 31 us -> 24.5 us
  other arithmetic: 8.34 us -> 4.54 us
  starting transfers between devices: 35 us -> 37.3 us
    pallas_call x18 -> x20, Pallas kernels: 52.8 us -> 25.7 us  [the longest x8 12.1 us: final(): pl.pallas_call(functools.partial(final_kernel, b, q, 2 * dates), out_shap...]
    unnamed x64 -> x80, local copies, waits for them, and re-layouts: 9.77 us -> 30.9 us
    ppermute x16, waiting for transfers between devices: 0.04 us -> 15.5 us  [shards(): arrived.append(lax.ppermute(leaving, 'date', link))]
    ppermute x1, waiting for transfers between devices: 12.5 us -> 0.01 us  [shards(): part = lax.ppermute(part, 'date', far)]
    ppermute x3, waiting for transfers between devices: 8.48 us -> 2.84 us  [shards(): lax.ppermute(message, 'bucket', [(i, (i + k) % zs) for i in range(zs)])]
    pallas_call x2, Pallas kernels: 27.8 us -> 23.7 us  [local(): pl.pallas_call(local_kernel, out_shape=jax.ShapeDtypeStruct((buckets, pie...]
    ppermute x1, waiting for transfers between devices: 3.73 us -> 0.01 us  [shards(): operators_other = lax.ppermute(operators, 'date', swap)]
    pallas_call x1, Pallas kernels: 3.81 us -> 1.18 us  [shards(): pl.pallas_call(join_operator_kernel, out_shape=(jax.ShapeDtypeStruct((buc...]
  transfers between devices with their start and end apart: 27 -> 27, of which waited for: 7 -> 13; matrix products, arithmetic and copies ran while one was open for 7% -> 3% of each run, Pallas kernels for 41% -> 30%
where the time goes in v3:
time: 154 us; the launch traced here: 153 us
  Pallas kernels  54 us (35%)
  starting transfers between devices  37.3 us (24%)
  local copies, waits for them, and re-layouts  31.6 us (21%)
  waiting for transfers between devices  24.5 us (16%)
  other arithmetic  4.54 us (3%)
    unnamed x80, local copies, waits for them, and re-layouts  30.9 us
    ppermute x16, starting transfers between devices, shards(): arrived.append(lax.ppermute(leaving, 'date', link))  25 us
    pallas_call x2, Pallas kernels, local(): pl.pallas_call(local_kernel, out_shape=jax.ShapeDtypeStruct((buckets, pie...  23.7 us
    ppermute x16, waiting for transfers between devices, shards(): arrived.append(lax.ppermute(leaving, 'date', link))  15.5 us
    pallas_call x8, Pallas kernels, final(): pl.pallas_call(functools.partial(final_kernel, b, q, 2 * dates), out_shap...  12.1 us
    pallas_call x8, Pallas kernels, stage(): pl.pallas_call(functools.partial(stage_kernel, j // pieces), out_shape=ja...  6.92 us
    pallas_call x2, Pallas kernels, shards(): pl.pallas_call(functools.partial(join_state_kernel, b), out_shape=(jax.Sh...  5.82 us
    ppermute x3, starting transfers between devices, shards(): lax.ppermute(message, 'bucket', [(i, (i + k) % zs) for i in range(zs)])  5.55 us
  transfers between devices with their start and end apart: 27, of which 13 were waited for; matrix products, arithmetic and copies ran while one was open for 3% of the time, Pallas kernels for 30%

profile of v3, /device:TPU:0, one launch (start us, length us, event | category | flops | bytes accessed | tf_op | source)
XLA Modules:
  0.0 153.2 jit_solution(8955128114814400545)
XLA Ops:
  1.3 2.2 %copy-done.10 = bf16[4,2,512,512]{3,2,1,0:T(8,128)(2,1)S(1)} copy-done((bf16[4,2,512,512]{3,2,1,0:T(8,128)(2,1)S(1)}, bf16[4,2,512,512]{3,2,1,0:T(8,128)(2,1)}, u32[]{:S(2)}) %copy-start.10) | copy-done | bytes 4194328
  4.4 3.5 %operators.1.mine_ref = bf16[2,768,512]{2,1,0:T(8,128)(2,1)S(1)} custom-call(bf16[4,2,512,512]{3,2,1,0:T(8,128)(2,1)S(1)} %copy-done.10, bf16[2,64,512]{2,1,0:T(8,128)(2,1)S(1)} %copy-done.26), custom_call_target="tpu_custom_call" | custom-call | flops 2147483648 | bytes 8388608 | tf_op jit(solution)/shard_map/operators/pallas_call | solution.py:232
  8.4 5.8 %copy-done = bf16[4,2,512,16,128]{4,3,2,1,0:T(8,128)(2,1)S(1)} copy-done((bf16[4,2,512,16,128]{4,3,2,1,0:T(8,128)(2,1)S(1)}, bf16[4,2,512,16,128]{4,3,2,1,0:T(8,128)(2,1)}, u32[]{:S(2)}) %copy-start) | copy-done | bytes 16777240
  14.2 2.2 %copy-done.11 = bf16[4,2,512,512]{3,2,1,0:T(8,128)(2,1)S(1)} copy-done((bf16[4,2,512,512]{3,2,1,0:T(8,128)(2,1)S(1)}, bf16[4,2,512,512]{3,2,1,0:T(8,128)(2,1)}, u32[]{:S(2)}) %copy-start.11) | copy-done | bytes 4194328
  16.4 12.6 %local.2 = bf16[2,4,768,256]{3,2,1,0:T(8,128)(2,1)} custom-call(f32[4]{0:T(128)S(1)} %get-tuple-element.53.scale_ref, s32[1]{0:T(128)S(6)} %sub.26.octet_ref, bf16[4,2,512,16,128]{4,3,2,1,0:T(8,128)(2,1)S(1)} %copy-done, bf16[4,2,512,512]{3,2,1,0:T(8,128)(2,1)S(1)} %copy-done.11, bf16[2,64,512]{2,1,0:T(8,128)(2,1)S(1)} %copy-done.27), custom_call_target="tpu_custom_call" | custom-call | flops 3221225472 | bytes 16777216 | tf_op jit(solution)/shard_map/local/pallas_call | solution.py:247
  35.7 2.5 %collective-permute-start.1 = (bf16[2,256,512]{2,1,0:T(8,128)(2,1)S(1)}, bf16[2,256,512]{2,1,0:T(8,128)(2,1)S(1)}, u32[]{:S(2)}, u32[]{:S(2)}) collective-permute-start(bf16[2,256,512]{2,1,0:T(8,128)(2,1)S(1)} %constant_dynamic-slice_fusion), channel_id=1, source_target_pairs={{0,8},{4,12},{8,0},{12,4},{16,24},{20,28},{24,16},{28,20},{1,9},{5... | collective-permute-start | bytes 1572872 | tf_op jit(solution)/shard_map/ppermute | solution.py:306
  38.2 5.8 %copy-done.1 = bf16[4,2,512,16,128]{4,3,2,1,0:T(8,128)(2,1)S(1)} copy-done((bf16[4,2,512,16,128]{4,3,2,1,0:T(8,128)(2,1)S(1)}, bf16[4,2,512,16,128]{4,3,2,1,0:T(8,128)(2,1)}, u32[]{:S(2)}) %copy-start.1) | copy-done | bytes 16777240
  43.9 11.1 %local.3.mine_ref = bf16[2,4,768,256]{3,2,1,0:T(8,128)(2,1)S(1)} custom-call(f32[4]{0:T(128)S(1)} %get-tuple-element.53.scale_ref, s32[1]{0:T(128)} %bitcast.1.core_ref.octet_ref, bf16[4,2,512,16,128]{4,3,2,1,0:T(8,128)(2,1)S(1)} %copy-done.1, bf16[4,2,512,512]{3,2,1,0:T(8,128)(2,1)S(1)} %copy-done.12, bf16[2,64,512]{2,1,0:T(8,128)(2,1)S(1)} %copy-done.27), custom_call_target="tpu_custom_call" | custom-call | flops 3221225472 | bytes 16777216 | tf_op jit(solution)/shard_map/local/pallas_call | solution.py:247
  60.0 1.9 %copy-done.8 = bf16[2,4,768,256]{3,2,1,0:T(8,128)(2,1)S(1)} copy-done((bf16[2,4,768,256]{3,2,1,0:T(8,128)(2,1)S(1)}, bf16[2,4,768,256]{3,2,1,0:T(8,128)(2,1)}, u32[]{:S(2)}) %copy-start.8) | copy-done | bytes 3145752
  61.8 2.6 %join_states.3 = (f32[4,512,256]{2,1,0:T(8,128)S(1)}, bf16[512,256]{1,0:T(8,128)(2,1)S(1)}, bf16[512,256]{1,0:T(8,128)(2,1)S(1)}, bf16[512,256]{1,0:T(8,128)(2,1)S(1)}, bf16[512,256]{1,0:T(8,128)(2,1)S(1)}) custom-call(s32[1]{0:T(128)} %bitcast.1.core_ref.octet_ref, bf16[2,4,768,256]{3,2,1,0:T(8,128)(2,1)S(1)} %copy-done.8, ...), custom_call_target="tpu_custom_call" | custom-call | flops 805306368 | bytes 4194304 | tf_op jit(solution)/shard_map/join_states/pallas_call | solution.py:338
  67.3 6.4 %collective-permute-done.3.other_ref.first_ref = bf16[512,256]{1,0:T(8,128)(2,1)S(1)} collective-permute-done((bf16[512,256]{1,0:T(8,128)(2,1)S(1)}, bf16[512,256]{1,0:T(8,128)(2,1)S(1)}, u32[]{:S(2)}, u32[]{:S(2)}) %collective-permute-start.3) | collective-permute-done | bytes 262176 | tf_op jit(solution)/shard_map/ppermute | solution.py:403
  74.2 3.8 %collective-permute-start.6 = (bf16[512,256]{1,0:T(8,128)(2,1)S(1)}, bf16[512,256]{1,0:T(8,128)(2,1)S(1)}, u32[]{:S(2)}, u32[]{:S(2)}) collective-permute-start(bf16[512,256]{1,0:T(8,128)(2,1)S(1)} %stage.8), channel_id=1, source_target_pairs={{0,16},{4,20},{8,24},{12,28},{1,17},{5,21},{9,25},{13,29},{2,18},{... | collective-permute-start | bytes 786440 | tf_op jit(solution)/shard_map/ppermute | solution.py:403
  78.0 3.2 %join_states.2 = (f32[4,512,256]{2,1,0:T(8,128)S(1)}, bf16[512,256]{1,0:T(8,128)(2,1)S(1)}, bf16[512,256]{1,0:T(8,128)(2,1)}, bf16[512,256]{1,0:T(8,128)(2,1)}, bf16[512,256]{1,0:T(8,128)(2,1)}) custom-call(s32[1]{0:T(128)} %bitcast.1.core_ref.octet_ref, bf16[2,4,768,256]{3,2,1,0:T(8,128)(2,1)S(1)} %copy-done.9, ...), custom_call_target="tpu_custom_call" | custom-call | flops 805306368 | bytes 4194304 | tf_op jit(solution)/shard_map/join_states/pallas_call | solution.py:338
  85.2 3.4 %collective-permute-start.12 = (bf16[512,256]{1,0:T(8,128)(2,1)S(1)}, bf16[512,256]{1,0:T(8,128)(2,1)S(1)}, u32[]{:S(2)}, u32[]{:S(2)}) collective-permute-start(bf16[512,256]{1,0:T(8,128)(2,1)S(1)} %stage.10), channel_id=1, source_target_pairs={{0,16},{4,20},{8,24},{12,28},{1,17},{5,21},{9,25},{13,29},{2,18},{... | collective-permute-start | bytes 786440 | tf_op jit(solution)/shard_map/ppermute | solution.py:403
  91.7 4.5 %collective-permute-done.8.other_ref.first_ref = bf16[512,256]{1,0:T(8,128)(2,1)S(1)} collective-permute-done((bf16[512,256]{1,0:T(8,128)(2,1)S(1)}, bf16[512,256]{1,0:T(8,128)(2,1)S(1)}, u32[]{:S(2)}, u32[]{:S(2)}) %collective-permute-start.8) | collective-permute-done | bytes 262176 | tf_op jit(solution)/shard_map/ppermute | solution.py:403
  98.5 4.4 %collective-permute-start.14 = (bf16[512,256]{1,0:T(8,128)(2,1)}, bf16[512,256]{1,0:T(8,128)(2,1)}, u32[]{:S(2)}, u32[]{:S(2)}) collective-permute-start(bf16[512,256]{1,0:T(8,128)(2,1)} %stage.11), channel_id=1, source_target_pairs={{0,16},{4,20},{8,24},{12,28},{1,17},{5,21},{9,25},{13,29},{2,18},{... | collective-permute-start | bytes 786440 | tf_op jit(solution)/shard_map/ppermute | solution.py:403
  106.1 2.0 %collective-permute-start.16 = (bf16[512,256]{1,0:T(8,128)(2,1)}, bf16[512,256]{1,0:T(8,128)(2,1)}, u32[]{:S(2)}, u32[]{:S(2)}) collective-permute-start(bf16[512,256]{1,0:T(8,128)(2,1)} %stage.12), channel_id=1, source_target_pairs={{0,16},{4,20},{8,24},{12,28},{1,17},{5,21},{9,25},{13,29},{2,18},{... | collective-permute-start | bytes 786440 | tf_op jit(solution)/shard_map/ppermute | solution.py:403
  116.7 1.9 %final.11.refs_3_ = f32[2,8,256]{2,1,0:T(8,128)S(1)} custom-call(s32[1]{0:T(128)} %bitcast.4.up_ref, bf16[512,256]{1,0:T(8,128)(2,1)S(1)} %collective-permute-done.4.other_ref.first_ref, bf16[512,256]{1,0:T(8,128)(2,1)} %collective-permute-done.14.last_ref, bf16[2,512,512]{2,1,0:T(8,128)(2,1)S(1)} %get-tuple-element.96.phi_ref, ...), custom_call_target="tpu_custom_call" | custom-call | flops 268435456 | bytes 2097152 | tf_op jit(solution)/shard_map/final/pallas_call | solution.py:368
  118.7 1.9 %final.12.refs_4_ = f32[2,8,256]{2,1,0:T(8,128)S(1)} custom-call(s32[1]{0:T(128)} %bitcast.4.up_ref, bf16[512,256]{1,0:T(8,128)(2,1)S(1)} %copy-done.25, bf16[512,256]{1,0:T(8,128)(2,1)} %collective-permute-done.16.last_ref, bf16[2,512,512]{2,1,0:T(8,128)(2,1)S(1)} %get-tuple-element.96.phi_ref, bf16[2,512,512]{2,1,0:T(8,128)(2,1)S(1)} %get-tuple-element.64.q_ref, ...), custom_call_target="tpu_custom_call" | custom-call | flops 268435456 | bytes 2097152 | tf_op jit(solution)/shard_map/final/pallas_call | solution.py:368
  125.9 1.9 %final.13.refs_5_ = f32[2,8,256]{2,1,0:T(8,128)S(1)} custom-call(s32[1]{0:T(128)} %bitcast.4.up_ref, bf16[512,256]{1,0:T(8,128)(2,1)} %collective-permute-done.11.other_ref.first_ref, bf16[512,256]{1,0:T(8,128)(2,1)S(1)} %collective-permute-done.17.last_ref, bf16[2,512,512]{2,1,0:T(8,128)(2,1)S(1)} %get-tuple-element.96.phi_ref, ...), custom_call_target="tpu_custom_call" | custom-call | flops 268435456 | bytes 2097152 | tf_op jit(solution)/shard_map/final/pallas_call | solution.py:368
  127.7 2.0 %collective-permute-done.18.last_ref = bf16[512,256]{1,0:T(8,128)(2,1)S(1)} collective-permute-done((bf16[512,256]{1,0:T(8,128)(2,1)S(1)}, bf16[512,256]{1,0:T(8,128)(2,1)S(1)}, u32[]{:S(2)}, u32[]{:S(2)}) %collective-permute-start.18) | collective-permute-done | bytes 262176 | tf_op jit(solution)/shard_map/ppermute | solution.py:403
  136.1 2.6 %collective-permute-start.22 = (bf16[256,128]{1,0:T(8,128)(2,1)S(1)}, bf16[256,128]{1,0:T(8,128)(2,1)S(1)}, u32[]{:S(2)}, u32[]{:S(2)}) collective-permute-start(bf16[256,128]{1,0:T(8,128)(2,1)S(1)} %pack.1.refs_0_), channel_id=1, source_target_pairs={{0,2},{1,3},{2,0},{3,1},{4,6},{5,7},{6,4},{7,5},{8,10},{9,11},{10,... | collective-permute-start | bytes 196616 | tf_op jit(solution)/shard_map/ppermute | solution.py:442
  145.5 3.1 %collective-permute-done.25 = f32[8,128]{1,0:T(8,128)S(1)} collective-permute-done((f32[8,128]{1,0:T(8,128)S(1)}, f32[8,128]{1,0:T(8,128)S(1)}, u32[]{:S(2)}, u32[]{:S(2)}) %collective-permute-start.25) | collective-permute-done | bytes 4128 | tf_op jit(solution)/shard_map/ppermute | solution.py:470
  148.6 2.5 %collective-permute-start.26 = (f32[8,128]{1,0:T(8,128)S(1)}, f32[8,128]{1,0:T(8,128)S(1)}, u32[]{:S(2)}, u32[]{:S(2)}) collective-permute-start(f32[8,128]{1,0:T(8,128)S(1)} %add.28), channel_id=1, source_target_pairs={{0,16},{4,20},{8,24},{12,28},{16,0},{20,4},{24,8},{28,12},{1,17},{... | collective-permute-start | bytes 12296 | tf_op jit(solution)/shard_map/ppermute | solution.py:470
  (155 shorter events, 58.5 us)
Async XLA Ops:
  7.9 21.1 %collective-permute-start = (bf16[2,768,512]{2,1,0:T(8,128)(2,1)S(1)}, bf16[2,768,512]{2,1,0:T(8,128)(2,1)S(1)}, u32[]{:S(2)}, u32[]{:S(2)}) collective-permute-start(bf16[2,768,512]{2,1,0:T(8,128)(2,1)S(1)} %operators.1.mine_ref), channel_id=1, source_target_pairs={{0,4},{4,0},{8,12},{12,8},{16,20},{20,16},{24,28},{28,24},{1,5},{5... | collective-permute-start | bytes 4718600 | tf_op jit(solution)/shard_map/ppermute | solution.py:274
  30.1 29.8 %collective-permute-start.2 = (bf16[2,4,768,256]{3,2,1,0:T(8,128)(2,1)}, bf16[2,4,768,256]{3,2,1,0:T(8,128)(2,1)}, u32[]{:S(2)}, u32[]{:S(2)}) collective-permute-start(bf16[2,4,768,256]{3,2,1,0:T(8,128)(2,1)} %local.2), channel_id=1, source_target_pairs={{0,4},{4,0},{8,12},{12,8},{16,20},{20,16},{24,28},{28,24},{1,5},{5... | collective-permute-start | bytes 9437192 | tf_op jit(solution)/shard_map/ppermute | solution.py:279
  35.7 21.1 %collective-permute-start.1 = (bf16[2,256,512]{2,1,0:T(8,128)(2,1)S(1)}, bf16[2,256,512]{2,1,0:T(8,128)(2,1)S(1)}, u32[]{:S(2)}, u32[]{:S(2)}) collective-permute-start(bf16[2,256,512]{2,1,0:T(8,128)(2,1)S(1)} %constant_dynamic-slice_fusion), channel_id=1, source_target_pairs={{0,8},{4,12},{8,0},{12,4},{16,24},{20,28},{24,16},{28,20},{1,9},{5... | collective-permute-start | bytes 1572872 | tf_op jit(solution)/shard_map/ppermute | solution.py:306
  64.4 9.2 %collective-permute-start.3 = (bf16[512,256]{1,0:T(8,128)(2,1)S(1)}, bf16[512,256]{1,0:T(8,128)(2,1)S(1)}, u32[]{:S(2)}, u32[]{:S(2)}) collective-permute-start(bf16[512,256]{1,0:T(8,128)(2,1)S(1)} %get-tuple-element.59.mine_ref), channel_id=1, source_target_pairs={{0,8},{4,12},{8,0},{12,4},{16,24},{20,28},{24,16},{28,20},{1,9},{5... | collective-permute-start | bytes 786440 | tf_op jit(solution)/shard_map/ppermute | solution.py:403
  64.7 16.5 %collective-permute-start.7 = (bf16[512,256]{1,0:T(8,128)(2,1)S(1)}, bf16[512,256]{1,0:T(8,128)(2,1)S(1)}, u32[]{:S(2)}, u32[]{:S(2)}) collective-permute-start(bf16[512,256]{1,0:T(8,128)(2,1)S(1)} %get-tuple-element.69.mine_ref), channel_id=1, source_target_pairs={{0,8},{4,12},{8,0},{12,4},{16,24},{20,28},{24,16},{28,20},{1,9},{5... | collective-permute-start | bytes 786440 | tf_op jit(solution)/shard_map/ppermute | solution.py:403
  66.5 18.4 %collective-permute-start.10 = (bf16[512,256]{1,0:T(8,128)(2,1)S(1)}, bf16[512,256]{1,0:T(8,128)(2,1)S(1)}, u32[]{:S(2)}, u32[]{:S(2)}) collective-permute-start(bf16[512,256]{1,0:T(8,128)(2,1)S(1)} %get-tuple-element.75.mine_ref), channel_id=1, source_target_pairs={{0,8},{4,12},{8,0},{12,4},{16,24},{20,28},{24,16},{28,20},{1,9},{5... | collective-permute-start | bytes 786440 | tf_op jit(solution)/shard_map/ppermute | solution.py:403
  73.7 16.9 %collective-permute-start.4 = (bf16[512,256]{1,0:T(8,128)(2,1)S(1)}, bf16[512,256]{1,0:T(8,128)(2,1)S(1)}, u32[]{:S(2)}, u32[]{:S(2)}) collective-permute-start(bf16[512,256]{1,0:T(8,128)(2,1)S(1)} %get-tuple-element.60.mine_ref), channel_id=1, source_target_pairs={{0,8},{4,12},{8,0},{12,4},{16,24},{20,28},{24,16},{28,20},{1,9},{5... | collective-permute-start | bytes 786440 | tf_op jit(solution)/shard_map/ppermute | solution.py:403
  74.2 16.4 %collective-permute-start.6 = (bf16[512,256]{1,0:T(8,128)(2,1)S(1)}, bf16[512,256]{1,0:T(8,128)(2,1)S(1)}, u32[]{:S(2)}, u32[]{:S(2)}) collective-permute-start(bf16[512,256]{1,0:T(8,128)(2,1)S(1)} %stage.8), channel_id=1, source_target_pairs={{0,16},{4,20},{8,24},{12,28},{1,17},{5,21},{9,25},{13,29},{2,18},{... | collective-permute-start | bytes 786440 | tf_op jit(solution)/shard_map/ppermute | solution.py:403
  81.2 14.9 %collective-permute-start.8 = (bf16[512,256]{1,0:T(8,128)(2,1)S(1)}, bf16[512,256]{1,0:T(8,128)(2,1)S(1)}, u32[]{:S(2)}, u32[]{:S(2)}) collective-permute-start(bf16[512,256]{1,0:T(8,128)(2,1)S(1)} %get-tuple-element.70.mine_ref), channel_id=1, source_target_pairs={{0,8},{4,12},{8,0},{12,4},{16,24},{20,28},{24,16},{28,20},{1,9},{5... | collective-permute-start | bytes 786440 | tf_op jit(solution)/shard_map/ppermute | solution.py:403
  83.1 13.1 %collective-permute-start.9 = (bf16[512,256]{1,0:T(8,128)(2,1)S(1)}, bf16[512,256]{1,0:T(8,128)(2,1)S(1)}, u32[]{:S(2)}, u32[]{:S(2)}) collective-permute-start(bf16[512,256]{1,0:T(8,128)(2,1)S(1)} %stage.9), channel_id=1, source_target_pairs={{0,16},{4,20},{8,24},{12,28},{1,17},{5,21},{9,25},{13,29},{2,18},{... | collective-permute-start | bytes 786440 | tf_op jit(solution)/shard_map/ppermute | solution.py:403
  85.2 20.2 %collective-permute-start.12 = (bf16[512,256]{1,0:T(8,128)(2,1)S(1)}, bf16[512,256]{1,0:T(8,128)(2,1)S(1)}, u32[]{:S(2)}, u32[]{:S(2)}) collective-permute-start(bf16[512,256]{1,0:T(8,128)(2,1)S(1)} %stage.10), channel_id=1, source_target_pairs={{0,16},{4,20},{8,24},{12,28},{1,17},{5,21},{9,25},{13,29},{2,18},{... | collective-permute-start | bytes 786440 | tf_op jit(solution)/shard_map/ppermute | solution.py:403
  90.5 13.3 %collective-permute-start.20 = (f32[4,4,128]{2,1,0:T(4,128)S(1)}, f32[4,4,128]{2,1,0:T(4,128)}, u32[]{:S(2)}, u32[]{:S(2)}) collective-permute-start(f32[4,4,128]{2,1,0:T(4,128)S(1)} %broadcast_multiply_fusion), channel_id=1, source_target_pairs={{0,4},{4,0},{8,12},{12,8},{16,20},{20,16},{24,28},{28,24},{1,5},{5... | collective-permute-start | bytes 24584 | tf_op jit(solution)/shard_map/ppermute | solution.py:276
  90.6 23.4 %collective-permute-start.11 = (bf16[512,256]{1,0:T(8,128)(2,1)}, bf16[512,256]{1,0:T(8,128)(2,1)}, u32[]{:S(2)}, u32[]{:S(2)}) collective-permute-start(bf16[512,256]{1,0:T(8,128)(2,1)} %get-tuple-element.76.mine_ref), channel_id=1, source_target_pairs={{0,8},{4,12},{8,0},{12,4},{16,24},{20,28},{24,16},{28,20},{1,9},{5... | collective-permute-start | bytes 786440 | tf_op jit(solution)/shard_map/ppermute | solution.py:403
  97.1 21.5 %collective-permute-start.13 = (bf16[512,256]{1,0:T(8,128)(2,1)}, bf16[512,256]{1,0:T(8,128)(2,1)}, u32[]{:S(2)}, u32[]{:S(2)}) collective-permute-start(bf16[512,256]{1,0:T(8,128)(2,1)} %get-tuple-element.79.mine_ref), channel_id=1, source_target_pairs={{0,8},{4,12},{8,0},{12,4},{16,24},{20,28},{24,16},{28,20},{1,9},{5... | collective-permute-start | bytes 786440 | tf_op jit(solution)/shard_map/ppermute | solution.py:403
  98.5 18.3 %collective-permute-start.14 = (bf16[512,256]{1,0:T(8,128)(2,1)}, bf16[512,256]{1,0:T(8,128)(2,1)}, u32[]{:S(2)}, u32[]{:S(2)}) collective-permute-start(bf16[512,256]{1,0:T(8,128)(2,1)} %stage.11), channel_id=1, source_target_pairs={{0,16},{4,20},{8,24},{12,28},{1,17},{5,21},{9,25},{13,29},{2,18},{... | collective-permute-start | bytes 786440 | tf_op jit(solution)/shard_map/ppermute | solution.py:403
  103.9 16.6 %collective-permute-start.15 = (bf16[512,256]{1,0:T(8,128)(2,1)}, bf16[512,256]{1,0:T(8,128)(2,1)}, u32[]{:S(2)}, u32[]{:S(2)}) collective-permute-start(bf16[512,256]{1,0:T(8,128)(2,1)} %get-tuple-element.83.mine_ref), channel_id=1, source_target_pairs={{0,8},{4,12},{8,0},{12,4},{16,24},{20,28},{24,16},{28,20},{1,9},{5... | collective-permute-start | bytes 786440 | tf_op jit(solution)/shard_map/ppermute | solution.py:403
  106.1 12.5 %collective-permute-start.16 = (bf16[512,256]{1,0:T(8,128)(2,1)}, bf16[512,256]{1,0:T(8,128)(2,1)}, u32[]{:S(2)}, u32[]{:S(2)}) collective-permute-start(bf16[512,256]{1,0:T(8,128)(2,1)} %stage.12), channel_id=1, source_target_pairs={{0,16},{4,20},{8,24},{12,28},{1,17},{5,21},{9,25},{13,29},{2,18},{... | collective-permute-start | bytes 786440 | tf_op jit(solution)/shard_map/ppermute | solution.py:403
  115.3 10.6 %collective-permute-start.17 = (bf16[512,256]{1,0:T(8,128)(2,1)S(1)}, bf16[512,256]{1,0:T(8,128)(2,1)S(1)}, u32[]{:S(2)}, u32[]{:S(2)}) collective-permute-start(bf16[512,256]{1,0:T(8,128)(2,1)S(1)} %stage.13), channel_id=1, source_target_pairs={{0,16},{4,20},{8,24},{12,28},{1,17},{5,21},{9,25},{13,29},{2,18},{... | collective-permute-start | bytes 786440 | tf_op jit(solution)/shard_map/ppermute | solution.py:403
  121.9 7.9 %collective-permute-start.18 = (bf16[512,256]{1,0:T(8,128)(2,1)S(1)}, bf16[512,256]{1,0:T(8,128)(2,1)S(1)}, u32[]{:S(2)}, u32[]{:S(2)}) collective-permute-start(bf16[512,256]{1,0:T(8,128)(2,1)S(1)} %stage.14), channel_id=1, source_target_pairs={{0,16},{4,20},{8,24},{12,28},{1,17},{5,21},{9,25},{13,29},{2,18},{... | collective-permute-start | bytes 786440 | tf_op jit(solution)/shard_map/ppermute | solution.py:403
  124.5 8.0 %collective-permute-start.19 = (bf16[512,256]{1,0:T(8,128)(2,1)S(1)}, bf16[512,256]{1,0:T(8,128)(2,1)S(1)}, u32[]{:S(2)}, u32[]{:S(2)}) collective-permute-start(bf16[512,256]{1,0:T(8,128)(2,1)S(1)} %stage.15), channel_id=1, source_target_pairs={{0,16},{4,20},{8,24},{12,28},{1,17},{5,21},{9,25},{13,29},{2,18},{... | collective-permute-start | bytes 786440 | tf_op jit(solution)/shard_map/ppermute | solution.py:403
  134.4 6.1 %collective-permute-start.21 = (bf16[256,128]{1,0:T(8,128)(2,1)S(1)}, bf16[256,128]{1,0:T(8,128)(2,1)S(1)}, u32[]{:S(2)}, u32[]{:S(2)}) collective-permute-start(bf16[256,128]{1,0:T(8,128)(2,1)S(1)} %pack.1.refs_0_), channel_id=1, source_target_pairs={{0,1},{1,2},{2,3},{3,0},{4,5},{5,6},{6,7},{7,4},{8,9},{9,10},{10,1... | collective-permute-start | bytes 196616 | tf_op jit(solution)/shard_map/ppermute | solution.py:442
  136.1 5.2 %collective-permute-start.22 = (bf16[256,128]{1,0:T(8,128)(2,1)S(1)}, bf16[256,128]{1,0:T(8,128)(2,1)S(1)}, u32[]{:S(2)}, u32[]{:S(2)}) collective-permute-start(bf16[256,128]{1,0:T(8,128)(2,1)S(1)} %pack.1.refs_0_), channel_id=1, source_target_pairs={{0,2},{1,3},{2,0},{3,1},{4,6},{5,7},{6,4},{7,5},{8,10},{9,11},{10,... | collective-permute-start | bytes 196616 | tf_op jit(solution)/shard_map/ppermute | solution.py:442
  138.6 4.3 %collective-permute-start.23 = (bf16[256,128]{1,0:T(8,128)(2,1)S(1)}, bf16[256,128]{1,0:T(8,128)(2,1)S(1)}, u32[]{:S(2)}, u32[]{:S(2)}) collective-permute-start(bf16[256,128]{1,0:T(8,128)(2,1)S(1)} %pack.1.refs_0_), channel_id=1, source_target_pairs={{0,3},{1,0},{2,1},{3,2},{4,7},{5,4},{6,5},{7,6},{8,11},{9,8},{10,9... | collective-permute-start | bytes 196616 | tf_op jit(solution)/shard_map/ppermute | solution.py:442
  148.6 4.1 %collective-permute-start.26 = (f32[8,128]{1,0:T(8,128)S(1)}, f32[8,128]{1,0:T(8,128)S(1)}, u32[]{:S(2)}, u32[]{:S(2)}) collective-permute-start(f32[8,128]{1,0:T(8,128)S(1)} %add.28), channel_id=1, source_target_pairs={{0,16},{4,20},{8,24},{12,28},{16,0},{20,4},{24,8},{28,12},{1,17},{... | collective-permute-start | bytes 12296 | tf_op jit(solution)/shard_map/ppermute | solution.py:470
  (42 other events, 290.5 us)

commit v4 on v3

--- a/solution.py
+++ b/solution.py
@@ -7,12 +7,14 @@
 from jax.experimental.pallas import tpu as pltpu
 from jax.sharding import PartitionSpec as P
 
+
 epsilon = 1e-06
 f32 = jnp.float32
 bf16 = jnp.bfloat16
 pair = 2
-flight = 3
+flight = 4
 lag = 2
+early = 2
 
 
 def dot(a, b):
@@ -40,40 +42,65 @@
     w_ref[0, :features, :] = product
 
 
-def local_kernel(scale_ref, octet_ref, x_ref, a_ref, r_ref, out_ref, rows_ref, state_ref):
+def local_kernel(
+    dates, scale_ref, octet_ref, x_ref, a_ref, r_ref, out_ref, even_ref, odd_ref, state_ref
+):
     features, micro, lanes = x_ref.shape[2:]
     sens = r_ref.shape[1]
-    t = pl.program_id(1)
-    rows_ref[...] = x_ref[0, 0].astype(f32).reshape(features * micro, lanes)
-    scale = scale_ref[t]
+    step = pl.program_id(0)
     width = pair * lanes
-
-    def shock(q):
-        return scale * jnp.concatenate(
+    pieces = micro // pair
+    chunk = features // pieces
+    buffers = (even_ref, odd_ref)
+
+    def lay_out(into, q):
+        part = slice(q * chunk, (q + 1) * chunk)
+        into[q * chunk * micro : (q + 1) * chunk * micro, :] = (
+            x_ref[0, 0, part].astype(f32).reshape(chunk * micro, lanes)
+        )
+
+    def advance(rows_ref, q, first):
+        cols = slice(q * width, (q + 1) * width)
+        total = scale_ref[jnp.maximum(step - 1, 0)] * jnp.concatenate(
             [rows_ref[pl.ds(q * pair + i, features, stride=micro), :] for i in range(pair)],
             axis=1,
         )
-
-    @pl.when(t == 0)
+        if not first:
+            total = total + dot(a_ref[0, 0], state_ref[:, cols])
+        state = total.astype(bf16)
+        state_ref[:, cols] = state
+        row = pl.multiple_of(features + (step - 1) * sens, sens)
+        out_ref[q, pl.ds(row, sens), :] = dot(r_ref[0], state).astype(bf16)
+        return state
+
+    def both(parity, ahead, first, last):
+        for q in range(pieces):
+            state = advance(buffers[1 - parity], q, first)
+            if ahead:
+                lay_out(buffers[parity], q)
+            if last:
+                out_ref[q, :features, :] = state
+
+    @pl.when(step == 0)
     def _():
-        for q in range(micro // pair):
-            state_ref[:, q * width : (q + 1) * width] = shock(q).astype(bf16)
-
-    @pl.when(t > 0)
+        for q in range(pieces):
+            lay_out(buffers[0], q)
+
+    @pl.when(step == 1)
     def _():
-        for q in range(micro // pair):
-            cols = slice(q * width, (q + 1) * width)
-            state_ref[:, cols] = (shock(q) + dot(a_ref[0, 0], state_ref[:, cols])).astype(bf16)
-
-    row = pl.multiple_of(features + t * sens, sens)
-    for q in range(micro // pair):
-        state = state_ref[:, q * width : (q + 1) * width]
-        out_ref[0, q, pl.ds(row, sens), :] = dot(r_ref[0], state).astype(bf16)
-
-    @pl.when(t == pl.num_programs(1) - 1)
-    def _():
-        for q in range(micro // pair):
-            out_ref[0, q, :features, :] = state_ref[:, q * width : (q + 1) * width]
+        both(1, dates > 1, True, dates == 1)
+
+    for parity in range(2):
+
+        @pl.when((lax.rem(step, 2) == parity) & (step > 1) & (step < dates))
+        def _():
+            both(parity, True, False, False)
+
+    if dates > 1:
+
+        @pl.when(step == dates)
+        def _():
+            both(dates % 2, False, False, True)
 
 
 def join_operator_kernel(core_ref, mine_ref, other_ref, p_ref, q_ref, late_ref):
@@ -95,7 +122,7 @@
     first = core_ref[0] == 0
     late_operator = late_ref[b]
     for q, end_ref in enumerate(end_refs):
-        mine, other = mine_ref[0, q], other_ref[0, q]
+        mine, other = mine_ref[q], other_ref[q]
         early = jnp.where(first, mine, other)
         late = jnp.where(first, other, mine)
         joined = dot(late_operator, early[:features]) + late.astype(f32)
@@ -239,34 +266,37 @@
         ],
         out_specs=pl.BlockSpec((1, rows, features), lambda b: (b, 0, 0)),
         cost_estimate=cost(2 * buckets * dates * features**3, 2**23),
-        compiler_params=pltpu.CompilerParams(vmem_limit_bytes=24 * 2**20),
+        compiler_params=pltpu.CompilerParams(vmem_limit_bytes=50 * 2**20),
         name="operators",
     )(transition, readout)
 
-    def local(octet, scales):
+    def local(b, octet, scales):
         return pl.pallas_call(
-            local_kernel,
-            out_shape=jax.ShapeDtypeStruct((buckets, pieces, rows, width), bf16),
+            functools.partial(local_kernel, dates),
+            out_shape=jax.ShapeDtypeStruct((pieces, rows, width), bf16),
             grid_spec=pltpu.PrefetchScalarGridSpec(
                 num_scalar_prefetch=2,
-                grid=(buckets, dates),
+                grid=(dates + 1,),
                 in_specs=[
                     pl.BlockSpec(
-                        (1, 1, features, half, lanes), lambda b, t, s, o: (t, b, 0, o[0], 0)
+                        (1, 1, features, half, lanes),
+                        lambda i, s, o: (jnp.minimum(i, dates - 1), b, 0, o[0], 0),
                     ),
-                    pl.BlockSpec((1, 1, features, features), lambda b, t, s, o: (t, b, 0, 0)),
-                    pl.BlockSpec((1, sens, features), lambda b, t, s, o: (b, 0, 0)),
+                    pl.BlockSpec(
+                        (1, 1, features, features),
+                        lambda i, s, o: (jnp.maximum(i - 1, 0), b, 0, 0),
+                    ),
+                    pl.BlockSpec((1, sens, features), lambda i, s, o: (b, 0, 0)),
                 ],
-                out_specs=pl.BlockSpec(
-                    (1, pieces, rows, width), lambda b, t, s, o: (b, 0, 0, 0)
-                ),
+                out_specs=pl.BlockSpec((pieces, rows, width), lambda i, s, o: (0, 0, 0)),
                 scratch_shapes=[
+                    pltpu.VMEM((features * half, lanes), f32),
                     pltpu.VMEM((features * half, lanes), f32),
                     pltpu.VMEM((features, half * lanes), bf16),
                 ],
             ),
-            compiler_params=pltpu.CompilerParams(vmem_limit_bytes=24 * 2**20),
-            cost_estimate=cost(2 * buckets * dates * rows * features * half * lanes // 2, 2**24),
+            compiler_params=pltpu.CompilerParams(vmem_limit_bytes=50 * 2**20),
+            cost_estimate=cost(2 * dates * rows * features * half * lanes // 2, 2**23),
             name="local",
         )(scales, octet, shocks, transition, readout)
 
@@ -274,7 +304,7 @@
     operators_other = lax.ppermute(operators, "date", swap)
     discount = (step_days.astype(f32) / 365.0)[:, None, None] * discount
     discount_other = lax.ppermute(discount, "date", swap)
-    sent = local(1 - core_flag, scales)
+    sent = local(0, 1 - core_flag, scales)
     operators_other, sent = lax.optimization_barrier((operators_other, sent))
     late_half = lax.ppermute(sent, "date", swap)
 
@@ -290,13 +320,14 @@
         in_specs=[smem, block3(rows), block3(rows)],
         out_specs=(block3(features), block3(2 * seen_rows), block3(rows)),
         cost_estimate=cost(2 * buckets * rows * features**2, 2**22),
-        compiler_params=pltpu.CompilerParams(vmem_limit_bytes=24 * 2**20),
+        compiler_params=pltpu.CompilerParams(vmem_limit_bytes=50 * 2**20),
         name="join_operators",
     )(core_flag, operators, operators_other)
 
     combiners = []
     eye = jnp.broadcast_to(jnp.eye(features, dtype=bf16), (buckets, features, features))
     prefix = eye
+    prefixes = [eye]
     for s in range(stages - 1):
         far = [(i, i ^ (2 << s)) for i in range(segments)]
         rows_half = features // 2
@@ -305,7 +336,7 @@
             scales, part = lax.optimization_barrier((scales, part))
         part = lax.ppermute(part, "date", far)
         if s == 0:
-            own = local(core_flag, scales)
+            own = local(0, core_flag, scales)
             part, own = lax.optimization_barrier((part, own))
         part_other = lax.ppermute(part, "date", swap)
         first = core == 0
@@ -319,6 +350,7 @@
         else:
             moved = jnp.einsum("bij,bjk->bik", prefix, other, preferred_element_type=f32)
             prefix = jnp.where(up, moved.astype(bf16), prefix)
+        prefixes.append(prefix)
         if s < stages - 2:
             above = jnp.where(up, block, other)
             below = jnp.where(up, other, block)
@@ -327,20 +359,19 @@
             ).astype(bf16)
 
     if stages < 2:
-        own = local(core_flag, scales)
+        own = local(0, core_flag, scales)
 
     ends = []
     seens = []
     vmem = pl.BlockSpec(memory_space=pltpu.VMEM)
     small = pltpu.CompilerParams(vmem_limit_bytes=16 * 2**20)
-    for b in range(buckets):
-        piece = pl.BlockSpec((1, pieces, rows, width), lambda i, b=b: (b, 0, 0, 0))
+
+    def join_states(b, own, late_half):
         result = pl.pallas_call(
             functools.partial(join_state_kernel, b),
             out_shape=(jax.ShapeDtypeStruct((pieces, 2 * seen_rows, width), f32),)
             + (jax.ShapeDtypeStruct((features, width), bf16),) * pieces,
-            grid=(1,),
-            in_specs=[smem, piece, piece, vmem],
+            in_specs=[smem, vmem, vmem, vmem],
             out_specs=(vmem,) * (pieces + 1),
             compiler_params=small,
             cost_estimate=cost(2 * rows * features * half * lanes, 2**22),
@@ -375,50 +406,74 @@
             name="final",
         )(up, first, last, operator, seer, seens[b], weight_column, correlation)
 
-    hold = [jnp.zeros((features, width), bf16)] * count
-    hold_flag = jnp.ones((1,), jnp.int32)
-    come = None
-    for s in range(stages):
+    arrived = [[] for _ in range(stages)]
+    leaving = [[] for _ in range(stages)]
+    holds = {}
+    results = []
+
+    def held(s, j):
+        if s == 0:
+            return jnp.zeros((features, width), bf16), jnp.ones((1,), jnp.int32)
+        if s == 1:
+            return arrived[0][j], ups[0]
+        if (s, j) not in holds:
+            before, flag = held(s - 1, j)
+            before = jnp.where(flag[0] == 1, before, jnp.zeros_like(before)).astype(f32)
+            moved = dot(prefixes[s - 1][j // pieces], arrived[s - 1][j])
+            value = jnp.where(ups[s - 1][0] == 1, before + moved, before)
+            holds[s, j] = value.astype(bf16)
+        return holds[s, j], jnp.ones((1,), jnp.int32)
+
+    def advance(s, after=None):
+        j = len(arrived[s])
         last = s == stages - 1
         bit = 2 << s
         link = [(i, i ^ bit) for i in range(segments) if not (last and i & bit)]
-        arrived = []
-        results = []
-        leaving_list = []
-        for j in range(count):
-            if come is None:
-                leaving = ends[j]
+        if s == 0:
+            out = ends[j]
+        else:
+            near = arrived[s - 1][j]
+            if after is not None:
+                near, results[after] = lax.optimization_barrier((near, results[after]))
+            out = stage(j, ups[s - 1], leaving[s - 1][j], near, combiners[s - 1])
+        if j >= flight:
+            out, arrived[s][j - flight] = lax.optimization_barrier((out, arrived[s][j - flight]))
+        leaving[s].append(out)
+        arrived[s].append(lax.ppermute(out, "date", link))
+
+    def finish():
+        i = len(results)
+        before, flag = held(stages - 1, i)
+        results.append(final(i, flag, before, arrived[-1][i], prefixes[stages - 1]))
+
+    join_states(0, own, late_half)
+    for b in range(buckets):
+        for _ in range(pieces):
+            advance(0)
+        if b + 1 < buckets:
+            scales, ends[-1] = lax.optimization_barrier((scales, ends[-1]))
+            sent = local(b + 1, 1 - core_flag, scales)
+            late_half = lax.ppermute(sent, "date", swap)
+            if stages > 1:
+                for _ in range(early):
+                    arrived[0][len(arrived[1])], sent = lax.optimization_barrier(
+                        (arrived[0][len(arrived[1])], sent)
+                    )
+                    advance(1)
+                    scales, leaving[1][-1] = lax.optimization_barrier((scales, leaving[1][-1]))
             else:
-                near = come[j]
-                if last and j > lag:
-                    near, results[j - lag - 1] = lax.optimization_barrier(
-                        (near, results[j - lag - 1])
-                    )
-                leaving = stage(j, ups[s - 1], ends[j], near, combiners[s - 1])
-            if j >= flight:
-                leaving, arrived[j - flight] = lax.optimization_barrier(
-                    (leaving, arrived[j - flight])
-                )
-            leaving_list.append(leaving)
-            arrived.append(lax.ppermute(leaving, "date", link))
-            if last and j >= lag:
-                i = j - lag
-                results.append(final(i, hold_flag, hold[i], arrived[i], prefix))
-        if last:
-            for i in range(len(results), count):
-                results.append(final(i, hold_flag, hold[i], arrived[i], prefix))
-        else:
-            if s == 0:
-                hold = arrived
-                hold_flag = ups[0]
-            else:
-                raised = [
-                    hold[j].astype(f32) + dot(prefix[j // pieces], arrived[j])
-                    for j in range(count)
-                ]
-                hold = [jnp.where(ups[s][0] == 1, r, h).astype(bf16) for r, h in zip(raised, hold)]
-            ends = leaving_list
-            come = arrived
+                scales, sent = lax.optimization_barrier((scales, sent))
+            own = local(b + 1, core_flag, scales)
+            join_states(b + 1, own, late_half)
+    for s in range(1, stages):
+        last = s == stages - 1
+        while len(arrived[s]) < count:
+            j = len(arrived[s])
+            while last and len(results) < j - lag:
+                finish()
+            advance(s, j - lag - 1 if last and j > lag else None)
+    while len(results) < count:
+        finish()
 
     local_micro = discount.shape[1]
     both = jnp.where(
@@ -485,4 +540,6 @@
         P(),
     )
     out_specs = (P("date", "bucket", None), P())
+
+
     return jax.shard_map(shards, mesh=mesh, in_specs=in_specs, out_specs=out_specs, check_vma=False)

time: 154 us -> 161 us (1.045)
  Pallas kernels: 54 us -> 75.7 us
  local copies, waits for them, and re-layouts: 31.6 us -> 11.6 us
  waiting for transfers between devices: 24.5 us -> 29 us
    unnamed x80 -> x74, local copies, waits for them, and re-layouts: 30.9 us -> 10.9 us
    pallas_call x4 -> x6, Pallas kernels: 29.5 us -> 43.8 us  [the longest x4 39.3 us: local(): pl.pallas_call(functools.partial(local_kernel, dates), out_shape=jax.Shap...]
    pallas_call x8, Pallas kernels: 6.92 us -> 10.4 us  [stage(): pl.pallas_call(functools.partial(stage_kernel, j // pieces), out_shape=ja...]
    ppermute x1, waiting for transfers between devices: 0.01 us -> 3.01 us  [shards(): part = lax.ppermute(part, 'date', far)]
    ppermute x1, waiting for transfers between devices: 0.94 us -> 3.82 us  [shards(): part_other = lax.ppermute(part, 'date', swap)]
  transfers between devices with their start and end apart: 27 -> 28, of which waited for: 13 -> 11; matrix products, arithmetic and copies ran while one was open for 3% -> 4% of each run, Pallas kernels for 30% -> 36%
where the time goes in v4:
time: 161 us; the launch traced here: 160 us
  Pallas kernels  75.7 us (47%)
  starting transfers between devices  37.1 us (23%)
  waiting for transfers between devices  29 us (18%)
  local copies, waits for them, and re-layouts  11.6 us (7%)
  other arithmetic  5.11 us (3%)
    pallas_call x4, Pallas kernels, local(): pl.pallas_call(functools.partial(local_kernel, dates), out_shape=jax.Shap...  39.3 us
    ppermute x16, starting transfers between devices, advance(): arrived[s].append(lax.ppermute(out, 'date', link))  23.4 us
    ppermute x16, waiting for transfers between devices, advance(): arrived[s].append(lax.ppermute(out, 'date', link))  14.6 us
    pallas_call x8, Pallas kernels, final(): pl.pallas_call(functools.partial(final_kernel, b, q, 2 * dates), out_shap...  13.2 us
    unnamed x74, local copies, waits for them, and re-layouts  10.9 us
    pallas_call x8, Pallas kernels, stage(): pl.pallas_call(functools.partial(stage_kernel, j // pieces), out_shape=ja...  10.4 us
    ppermute x3, starting transfers between devices, shards(): lax.ppermute(message, 'bucket', [(i, (i + k) % zs) for i in range(zs)])  5.57 us
    pallas_call x1, Pallas kernels, shards(): pl.pallas_call(functools.partial(operator_kernel, dates), out_shape=jax.S...  4.78 us
  transfers between devices with their start and end apart: 28, of which 11 were waited for; matrix products, arithmetic and copies ran while one was open for 4% of the time, Pallas kernels for 36%

profile of v4, /device:TPU:0, one launch (start us, length us, event | category | flops | bytes accessed | tf_op | source)
XLA Modules:
  0.0 159.6 jit_solution(10645483193546587024)
XLA Ops:
  2.2 4.8 %operators.1.mine_ref = bf16[2,768,512]{2,1,0:T(8,128)(2,1)S(1)} custom-call(bf16[4,2,512,512]{3,2,1,0:T(8,128)(2,1)} %a_ref.9, bf16[2,64,512]{2,1,0:T(8,128)(2,1)S(1)} %copy-done.10), custom_call_target="tpu_custom_call" | custom-call | flops 2147483648 | bytes 8388608 | tf_op jit(solution)/shard_map/operators/pallas_call | solution.py:259
  7.6 10.4 %local.4 = bf16[4,768,256]{2,1,0:T(8,128)(2,1)} custom-call(f32[4]{0:T(128)S(1)} %get-tuple-element.65.scale_ref, s32[1]{0:T(128)S(6)} %sub.27.octet_ref, bf16[4,2,512,16,128]{4,3,2,1,0:T(8,128)(2,1)} %x_ref.7, bf16[4,2,512,512]{3,2,1,0:T(8,128)(2,1)} %a_ref.9, bf16[2,64,512]{2,1,0:T(8,128)(2,1)S(1)} %copy-done.10), custom_call_target="tpu_custom_call" | custom-call | flops 1610612736 | bytes 8388608 | tf_op jit(solution)/shard_map/local/pallas_call | solution.py:274
  18.0 2.6 %join_operators.1 = (bf16[2,512,512]{2,1,0:T(8,128)(2,1)S(1)}, bf16[2,512,512]{2,1,0:T(8,128)(2,1)S(1)}, bf16[2,768,512]{2,1,0:T(8,128)(2,1)S(1)}) custom-call(s32[1]{0:T(128)} %bitcast.1.core_ref.octet_ref, bf16[2,768,512]{2,1,0:T(8,128)(2,1)} %copy-done.12, bf16[2,768,512]{2,1,0:T(8,128)(2,1)} %collective-permute-done.other_ref), custom_call_target="tpu_custom_call" | custom-call | flops 805306368 | bytes 4194304 | tf_op jit(solution)/shard_map/join_operators/pallas_call | solution.py:312
  21.7 2.9 %collective-permute-start.1 = (bf16[2,256,512]{2,1,0:T(8,128)(2,1)S(1)}, bf16[2,256,512]{2,1,0:T(8,128)(2,1)}, u32[]{:S(2)}, u32[]{:S(2)}) collective-permute-start(bf16[2,256,512]{2,1,0:T(8,128)(2,1)S(1)} %constant_dynamic-slice_fusion), channel_id=1, source_target_pairs={{0,8},{4,12},{8,0},{12,4},{16,24},{20,28},{24,16},{28,20},{1,9},{5... | collective-permute-start | bytes 1572872 | tf_op jit(solution)/shard_map/ppermute | solution.py:337
  24.7 9.2 %local.5.mine_ref = bf16[4,768,256]{2,1,0:T(8,128)(2,1)S(1)} custom-call(f32[4]{0:T(128)S(1)} %get-tuple-element.65.scale_ref, s32[1]{0:T(128)} %bitcast.1.core_ref.octet_ref, bf16[4,2,512,16,128]{4,3,2,1,0:T(8,128)(2,1)} %x_ref.7, bf16[4,2,512,512]{3,2,1,0:T(8,128)(2,1)} %a_ref.9, bf16[2,64,512]{2,1,0:T(8,128)(2,1)S(1)} %copy-done.11), custom_call_target="tpu_custom_call" | custom-call | flops 1610612736 | bytes 8388608 | tf_op jit(solution)/shard_map/local/pallas_call | solution.py:274
  33.9 3.0 %collective-permute-done.1 = bf16[2,256,512]{2,1,0:T(8,128)(2,1)} collective-permute-done((bf16[2,256,512]{2,1,0:T(8,128)(2,1)S(1)}, bf16[2,256,512]{2,1,0:T(8,128)(2,1)}, u32[]{:S(2)}, u32[]{:S(2)}) %collective-permute-start.1) | collective-permute-done | bytes 524320 | tf_op jit(solution)/shard_map/ppermute | solution.py:337
  39.6 10.5 %local.6 = bf16[4,768,256]{2,1,0:T(8,128)(2,1)} custom-call(f32[4]{0:T(128)S(1)} %get-tuple-element.65.scale_ref, s32[1]{0:T(128)S(6)} %sub.27.octet_ref, bf16[4,2,512,16,128]{4,3,2,1,0:T(8,128)(2,1)} %x_ref.7, bf16[4,2,512,512]{3,2,1,0:T(8,128)(2,1)} %a_ref.9, bf16[2,64,512]{2,1,0:T(8,128)(2,1)S(1)} %copy-done.11), custom_call_target="tpu_custom_call" | custom-call | flops 1610612736 | bytes 8388608 | tf_op jit(solution)/shard_map/local/pallas_call | solution.py:274
  50.7 3.8 %collective-permute-done.4 = bf16[2,256,512]{2,1,0:T(8,128)(2,1)S(1)} collective-permute-done((bf16[2,256,512]{2,1,0:T(8,128)(2,1)}, bf16[2,256,512]{2,1,0:T(8,128)(2,1)S(1)}, u32[]{:S(2)}, u32[]{:S(2)}) %collective-permute-start.4) | collective-permute-done | bytes 524320 | tf_op jit(solution)/shard_map/ppermute | solution.py:341
  58.2 11.6 %collective-permute-done.3.other_ref.first_ref = bf16[512,256]{1,0:T(8,128)(2,1)S(1)} collective-permute-done((bf16[512,256]{1,0:T(8,128)(2,1)}, bf16[512,256]{1,0:T(8,128)(2,1)S(1)}, u32[]{:S(2)}, u32[]{:S(2)}) %collective-permute-start.3) | collective-permute-done | bytes 262176 | tf_op jit(solution)/shard_map/ppermute | solution.py:442
  69.9 2.1 %stage.8 = bf16[512,256]{1,0:T(8,128)(2,1)} custom-call(s32[1]{0:T(128)} %bitcast.4.up_ref, bf16[512,256]{1,0:T(8,128)(2,1)} %get-tuple-element.60.mine_ref, bf16[512,256]{1,0:T(8,128)(2,1)S(1)} %collective-permute-done.3.other_ref.first_ref, bf16[2,512,512]{2,1,0:T(8,128)(2,1)S(1)} %get-tuple-element.99.a_ref), custom_call_target="tpu_custom_call" | custom-call | flops 134217728 | bytes 1048576 | tf_op jit(solution)/shard_map/stage/pallas_call | solution.py:387
  72.0 4.4 %collective-permute-start.8 = (bf16[512,256]{1,0:T(8,128)(2,1)}, bf16[512,256]{1,0:T(8,128)(2,1)}, u32[]{:S(2)}, u32[]{:S(2)}) collective-permute-start(bf16[512,256]{1,0:T(8,128)(2,1)} %stage.8), channel_id=1, source_target_pairs={{0,16},{4,20},{8,24},{12,28},{1,17},{5,21},{9,25},{13,29},{2,18},{... | collective-permute-start | bytes 786440 | tf_op jit(solution)/shard_map/ppermute | solution.py:442
  79.8 2.0 %stage.9 = bf16[512,256]{1,0:T(8,128)(2,1)} custom-call(s32[1]{0:T(128)} %bitcast.4.up_ref, bf16[512,256]{1,0:T(8,128)(2,1)} %get-tuple-element.64.mine_ref, bf16[512,256]{1,0:T(8,128)(2,1)} %collective-permute-done.5.other_ref.first_ref, bf16[2,512,512]{2,1,0:T(8,128)(2,1)S(1)} %get-tuple-element.99.a_ref), custom_call_target="tpu_custom_call" | custom-call | flops 134217728 | bytes 1048576 | tf_op jit(solution)/shard_map/stage/pallas_call | solution.py:387
  81.9 9.2 %local.7.mine_ref = bf16[4,768,256]{2,1,0:T(8,128)(2,1)S(1)} custom-call(f32[4]{0:T(128)S(1)} %get-tuple-element.65.scale_ref, s32[1]{0:T(128)} %bitcast.1.core_ref.octet_ref, bf16[4,2,512,16,128]{4,3,2,1,0:T(8,128)(2,1)} %x_ref.7, bf16[4,2,512,512]{3,2,1,0:T(8,128)(2,1)} %a_ref.9, bf16[2,64,512]{2,1,0:T(8,128)(2,1)S(1)} %copy-done.11), custom_call_target="tpu_custom_call" | custom-call | flops 1610612736 | bytes 8388608 | tf_op jit(solution)/shard_map/local/pallas_call | solution.py:274
  92.6 3.2 %join_states.3 = (f32[4,512,256]{2,1,0:T(8,128)S(1)}, bf16[512,256]{1,0:T(8,128)(2,1)S(1)}, bf16[512,256]{1,0:T(8,128)(2,1)}, bf16[512,256]{1,0:T(8,128)(2,1)}, bf16[512,256]{1,0:T(8,128)(2,1)}) custom-call(s32[1]{0:T(128)} %bitcast.1.core_ref.octet_ref, bf16[4,768,256]{2,1,0:T(8,128)(2,1)S(1)} %local.7.mine_ref, ...), custom_call_target="tpu_custom_call" | custom-call | flops 805306368 | bytes 4194304 | tf_op jit(solution)/shard_map/join_states/pallas_call | solution.py:370
  98.6 1.9 %final.8.refs_0_ = f32[2,8,256]{2,1,0:T(8,128)S(1)} custom-call(s32[1]{0:T(128)} %bitcast.4.up_ref, bf16[512,256]{1,0:T(8,128)(2,1)S(1)} %copy-done.20, bf16[512,256]{1,0:T(8,128)(2,1)} %collective-permute-done.8.last_ref, bf16[2,512,512]{2,1,0:T(8,128)(2,1)S(1)} %get-tuple-element.98.phi_ref, bf16[2,512,512]{2,1,0:T(8,128)(2,1)S(1)} %get-tuple-element.70.q_ref, ...), custom_call_target="tpu_custom_call" | custom-call | flops 268435456 | bytes 2097152 | tf_op jit(solution)/shard_map/final/pallas_call | solution.py:399
  108.0 2.0 %collective-permute-start.13 = (bf16[512,256]{1,0:T(8,128)(2,1)}, bf16[512,256]{1,0:T(8,128)(2,1)}, u32[]{:S(2)}, u32[]{:S(2)}) collective-permute-start(bf16[512,256]{1,0:T(8,128)(2,1)} %stage.10), channel_id=1, source_target_pairs={{0,16},{4,20},{8,24},{12,28},{1,17},{5,21},{9,25},{13,29},{2,18},{... | collective-permute-start | bytes 786440 | tf_op jit(solution)/shard_map/ppermute | solution.py:442
  113.0 2.0 %collective-permute-start.17 = (bf16[512,256]{1,0:T(8,128)(2,1)}, bf16[512,256]{1,0:T(8,128)(2,1)}, u32[]{:S(2)}, u32[]{:S(2)}) collective-permute-start(bf16[512,256]{1,0:T(8,128)(2,1)} %stage.12), channel_id=1, source_target_pairs={{0,16},{4,20},{8,24},{12,28},{1,17},{5,21},{9,25},{13,29},{2,18},{... | collective-permute-start | bytes 786440 | tf_op jit(solution)/shard_map/ppermute | solution.py:442
  123.6 2.0 %final.10.refs_2_ = f32[2,8,256]{2,1,0:T(8,128)S(1)} custom-call(s32[1]{0:T(128)} %bitcast.4.up_ref, bf16[512,256]{1,0:T(8,128)(2,1)S(1)} %copy-done.14, bf16[512,256]{1,0:T(8,128)(2,1)} %collective-permute-done.13.last_ref, bf16[2,512,512]{2,1,0:T(8,128)(2,1)S(1)} %get-tuple-element.98.phi_ref, bf16[2,512,512]{2,1,0:T(8,128)(2,1)S(1)} %get-tuple-element.70.q_ref, ...), custom_call_target="tpu_custom_call" | custom-call | flops 268435456 | bytes 2097152 | tf_op jit(solution)/shard_map/final/pallas_call | solution.py:399
  128.3 1.9 %final.12.refs_4_ = f32[2,8,256]{2,1,0:T(8,128)S(1)} custom-call(s32[1]{0:T(128)} %bitcast.4.up_ref, bf16[512,256]{1,0:T(8,128)(2,1)S(1)} %copy-done.18, bf16[512,256]{1,0:T(8,128)(2,1)} %collective-permute-done.17.last_ref, bf16[2,512,512]{2,1,0:T(8,128)(2,1)S(1)} %get-tuple-element.98.phi_ref, bf16[2,512,512]{2,1,0:T(8,128)(2,1)S(1)} %get-tuple-element.70.q_ref, ...), custom_call_target="tpu_custom_call" | custom-call | flops 268435456 | bytes 2097152 | tf_op jit(solution)/shard_map/final/pallas_call | solution.py:399
  132.8 1.9 %final.14.refs_6_ = f32[2,8,256]{2,1,0:T(8,128)S(1)} custom-call(s32[1]{0:T(128)} %bitcast.4.up_ref, bf16[512,256]{1,0:T(8,128)(2,1)} %collective-permute-done.14.other_ref.first_ref, bf16[512,256]{1,0:T(8,128)(2,1)S(1)} %collective-permute-done.19.last_ref, bf16[2,512,512]{2,1,0:T(8,128)(2,1)S(1)} %get-tuple-element.98.phi_ref, ...), custom_call_target="tpu_custom_call" | custom-call | flops 268435456 | bytes 2097152 | tf_op jit(solution)/shard_map/final/pallas_call | solution.py:399
  136.9 2.7 %collective-permute-done.20.last_ref = bf16[512,256]{1,0:T(8,128)(2,1)S(1)} collective-permute-done((bf16[512,256]{1,0:T(8,128)(2,1)S(1)}, bf16[512,256]{1,0:T(8,128)(2,1)S(1)}, u32[]{:S(2)}, u32[]{:S(2)}) %collective-permute-start.20) | collective-permute-done | bytes 262176 | tf_op jit(solution)/shard_map/ppermute | solution.py:442
  142.1 2.6 %collective-permute-start.23 = (bf16[256,128]{1,0:T(8,128)(2,1)S(1)}, bf16[256,128]{1,0:T(8,128)(2,1)S(1)}, u32[]{:S(2)}, u32[]{:S(2)}) collective-permute-start(bf16[256,128]{1,0:T(8,128)(2,1)S(1)} %pack.1.refs_0_), channel_id=1, source_target_pairs={{0,2},{1,3},{2,0},{3,1},{4,6},{5,7},{6,4},{7,5},{8,10},{9,11},{10,... | collective-permute-start | bytes 196616 | tf_op jit(solution)/shard_map/ppermute | solution.py:497
  152.9 2.1 %collective-permute-done.26 = f32[8,128]{1,0:T(8,128)S(1)} collective-permute-done((f32[8,128]{1,0:T(8,128)S(1)}, f32[8,128]{1,0:T(8,128)S(1)}, u32[]{:S(2)}, u32[]{:S(2)}) %collective-permute-start.26) | collective-permute-done | bytes 4128 | tf_op jit(solution)/shard_map/ppermute | solution.py:525
  155.1 2.5 %collective-permute-start.27 = (f32[8,128]{1,0:T(8,128)S(1)}, f32[8,128]{1,0:T(8,128)S(1)}, u32[]{:S(2)}, u32[]{:S(2)}) collective-permute-start(f32[8,128]{1,0:T(8,128)S(1)} %add.28), channel_id=1, source_target_pairs={{0,16},{4,20},{8,24},{12,28},{16,0},{20,4},{24,8},{28,12},{1,17},{... | collective-permute-start | bytes 12296 | tf_op jit(solution)/shard_map/ppermute | solution.py:525
  (153 shorter events, 57.1 us)
Async XLA Ops:
  7.0 10.9 %collective-permute-start = (bf16[2,768,512]{2,1,0:T(8,128)(2,1)S(1)}, bf16[2,768,512]{2,1,0:T(8,128)(2,1)}, u32[]{:S(2)}, u32[]{:S(2)}) collective-permute-start(bf16[2,768,512]{2,1,0:T(8,128)(2,1)S(1)} %operators.1.mine_ref), channel_id=1, source_target_pairs={{0,4},{4,0},{8,12},{12,8},{16,20},{20,16},{24,28},{28,24},{1,5},{5... | collective-permute-start | bytes 4718600 | tf_op jit(solution)/shard_map/ppermute | solution.py:304
  17.9 19.0 %collective-permute-start.2 = (bf16[4,768,256]{2,1,0:T(8,128)(2,1)}, bf16[4,768,256]{2,1,0:T(8,128)(2,1)S(1)}, u32[]{:S(2)}, u32[]{:S(2)}) collective-permute-start(bf16[4,768,256]{2,1,0:T(8,128)(2,1)} %local.4), channel_id=1, source_target_pairs={{0,4},{4,0},{8,12},{12,8},{16,20},{20,16},{24,28},{28,24},{1,5},{5... | collective-permute-start | bytes 4718600 | tf_op jit(solution)/shard_map/ppermute | solution.py:309
  21.7 15.2 %collective-permute-start.1 = (bf16[2,256,512]{2,1,0:T(8,128)(2,1)S(1)}, bf16[2,256,512]{2,1,0:T(8,128)(2,1)}, u32[]{:S(2)}, u32[]{:S(2)}) collective-permute-start(bf16[2,256,512]{2,1,0:T(8,128)(2,1)S(1)} %constant_dynamic-slice_fusion), channel_id=1, source_target_pairs={{0,8},{4,12},{8,0},{12,4},{16,24},{20,28},{24,16},{28,20},{1,9},{5... | collective-permute-start | bytes 1572872 | tf_op jit(solution)/shard_map/ppermute | solution.py:337
  50.1 41.0 %collective-permute-start.6 = (bf16[4,768,256]{2,1,0:T(8,128)(2,1)}, bf16[4,768,256]{2,1,0:T(8,128)(2,1)}, u32[]{:S(2)}, u32[]{:S(2)}) collective-permute-start(bf16[4,768,256]{2,1,0:T(8,128)(2,1)} %local.6), channel_id=1, source_target_pairs={{0,4},{4,0},{8,12},{12,8},{16,20},{20,16},{24,28},{28,24},{1,5},{5... | collective-permute-start | bytes 4718600 | tf_op jit(solution)/shard_map/ppermute | solution.py:456
  55.6 23.7 %collective-permute-start.5 = (bf16[512,256]{1,0:T(8,128)(2,1)}, bf16[512,256]{1,0:T(8,128)(2,1)}, u32[]{:S(2)}, u32[]{:S(2)}) collective-permute-start(bf16[512,256]{1,0:T(8,128)(2,1)} %get-tuple-element.64.mine_ref), channel_id=1, source_target_pairs={{0,8},{4,12},{8,0},{12,4},{16,24},{20,28},{24,16},{28,20},{1,9},{5... | collective-permute-start | bytes 786440 | tf_op jit(solution)/shard_map/ppermute | solution.py:442
  57.4 12.4 %collective-permute-start.3 = (bf16[512,256]{1,0:T(8,128)(2,1)}, bf16[512,256]{1,0:T(8,128)(2,1)S(1)}, u32[]{:S(2)}, u32[]{:S(2)}) collective-permute-start(bf16[512,256]{1,0:T(8,128)(2,1)} %get-tuple-element.60.mine_ref), channel_id=1, source_target_pairs={{0,8},{4,12},{8,0},{12,4},{16,24},{20,28},{24,16},{28,20},{1,9},{5... | collective-permute-start | bytes 786440 | tf_op jit(solution)/shard_map/ppermute | solution.py:442
  72.0 25.1 %collective-permute-start.8 = (bf16[512,256]{1,0:T(8,128)(2,1)}, bf16[512,256]{1,0:T(8,128)(2,1)}, u32[]{:S(2)}, u32[]{:S(2)}) collective-permute-start(bf16[512,256]{1,0:T(8,128)(2,1)} %stage.8), channel_id=1, source_target_pairs={{0,16},{4,20},{8,24},{12,28},{1,17},{5,21},{9,25},{13,29},{2,18},{... | collective-permute-start | bytes 786440 | tf_op jit(solution)/shard_map/ppermute | solution.py:442
  77.0 34.7 %collective-permute-start.21 = (f32[4,4,128]{2,1,0:T(4,128)}, f32[4,4,128]{2,1,0:T(4,128)}, u32[]{:S(2)}, u32[]{:S(2)}) collective-permute-start(f32[4,4,128]{2,1,0:T(4,128)} %broadcast_multiply_fusion), channel_id=1, source_target_pairs={{0,4},{4,0},{8,12},{12,8},{16,20},{20,16},{24,28},{28,24},{1,5},{5... | collective-permute-start | bytes 24584 | tf_op jit(solution)/shard_map/ppermute | solution.py:306
  77.8 22.7 %collective-permute-start.7 = (bf16[512,256]{1,0:T(8,128)(2,1)}, bf16[512,256]{1,0:T(8,128)(2,1)S(1)}, u32[]{:S(2)}, u32[]{:S(2)}) collective-permute-start(bf16[512,256]{1,0:T(8,128)(2,1)} %copy-done.25), channel_id=1, source_target_pairs={{0,8},{4,12},{8,0},{12,4},{16,24},{20,28},{24,16},{28,20},{1,9},{5... | collective-permute-start | bytes 786440 | tf_op jit(solution)/shard_map/ppermute | solution.py:442
  79.3 23.8 %collective-permute-start.12 = (bf16[512,256]{1,0:T(8,128)(2,1)}, bf16[512,256]{1,0:T(8,128)(2,1)S(1)}, u32[]{:S(2)}, u32[]{:S(2)}) collective-permute-start(bf16[512,256]{1,0:T(8,128)(2,1)} %copy-done.23), channel_id=1, source_target_pairs={{0,8},{4,12},{8,0},{12,4},{16,24},{20,28},{24,16},{28,20},{1,9},{5... | collective-permute-start | bytes 786440 | tf_op jit(solution)/shard_map/ppermute | solution.py:442
  91.1 13.5 %collective-permute-start.10 = (bf16[512,256]{1,0:T(8,128)(2,1)}, bf16[512,256]{1,0:T(8,128)(2,1)S(1)}, u32[]{:S(2)}, u32[]{:S(2)}) collective-permute-start(bf16[512,256]{1,0:T(8,128)(2,1)} %stage.9), channel_id=1, source_target_pairs={{0,16},{4,20},{8,24},{12,28},{1,17},{5,21},{9,25},{13,29},{2,18},{... | collective-permute-start | bytes 786440 | tf_op jit(solution)/shard_map/ppermute | solution.py:442
  97.1 10.9 %collective-permute-start.9 = (bf16[512,256]{1,0:T(8,128)(2,1)S(1)}, bf16[512,256]{1,0:T(8,128)(2,1)S(1)}, u32[]{:S(2)}, u32[]{:S(2)}) collective-permute-start(bf16[512,256]{1,0:T(8,128)(2,1)S(1)} %get-tuple-element.73.mine_ref), channel_id=1, source_target_pairs={{0,8},{4,12},{8,0},{12,4},{16,24},{20,28},{24,16},{28,20},{1,9},{5... | collective-permute-start | bytes 786440 | tf_op jit(solution)/shard_map/ppermute | solution.py:442
  100.9 11.4 %collective-permute-start.15 = (bf16[512,256]{1,0:T(8,128)(2,1)S(1)}, bf16[512,256]{1,0:T(8,128)(2,1)S(1)}, u32[]{:S(2)}, u32[]{:S(2)}) collective-permute-start(bf16[512,256]{1,0:T(8,128)(2,1)S(1)} %stage.11), channel_id=1, source_target_pairs={{0,16},{4,20},{8,24},{12,28},{1,17},{5,21},{9,25},{13,29},{2,18},{... | collective-permute-start | bytes 786440 | tf_op jit(solution)/shard_map/ppermute | solution.py:442
  103.1 27.1 %collective-permute-start.16 = (bf16[512,256]{1,0:T(8,128)(2,1)}, bf16[512,256]{1,0:T(8,128)(2,1)S(1)}, u32[]{:S(2)}, u32[]{:S(2)}) collective-permute-start(bf16[512,256]{1,0:T(8,128)(2,1)} %get-tuple-element.85.mine_ref), channel_id=1, source_target_pairs={{0,8},{4,12},{8,0},{12,4},{16,24},{20,28},{24,16},{28,20},{1,9},{5... | collective-permute-start | bytes 786440 | tf_op jit(solution)/shard_map/ppermute | solution.py:442
  104.6 16.2 %collective-permute-start.14 = (bf16[512,256]{1,0:T(8,128)(2,1)}, bf16[512,256]{1,0:T(8,128)(2,1)}, u32[]{:S(2)}, u32[]{:S(2)}) collective-permute-start(bf16[512,256]{1,0:T(8,128)(2,1)} %get-tuple-element.82.mine_ref), channel_id=1, source_target_pairs={{0,8},{4,12},{8,0},{12,4},{16,24},{20,28},{24,16},{28,20},{1,9},{5... | collective-permute-start | bytes 786440 | tf_op jit(solution)/shard_map/ppermute | solution.py:442
  108.0 14.2 %collective-permute-start.13 = (bf16[512,256]{1,0:T(8,128)(2,1)}, bf16[512,256]{1,0:T(8,128)(2,1)}, u32[]{:S(2)}, u32[]{:S(2)}) collective-permute-start(bf16[512,256]{1,0:T(8,128)(2,1)} %stage.10), channel_id=1, source_target_pairs={{0,16},{4,20},{8,24},{12,28},{1,17},{5,21},{9,25},{13,29},{2,18},{... | collective-permute-start | bytes 786440 | tf_op jit(solution)/shard_map/ppermute | solution.py:442
  111.7 13.9 %collective-permute-start.11 = (bf16[512,256]{1,0:T(8,128)(2,1)}, bf16[512,256]{1,0:T(8,128)(2,1)}, u32[]{:S(2)}, u32[]{:S(2)}) collective-permute-start(bf16[512,256]{1,0:T(8,128)(2,1)} %get-tuple-element.77.mine_ref), channel_id=1, source_target_pairs={{0,8},{4,12},{8,0},{12,4},{16,24},{20,28},{24,16},{28,20},{1,9},{5... | collective-permute-start | bytes 786440 | tf_op jit(solution)/shard_map/ppermute | solution.py:442
  113.0 15.3 %collective-permute-start.17 = (bf16[512,256]{1,0:T(8,128)(2,1)}, bf16[512,256]{1,0:T(8,128)(2,1)}, u32[]{:S(2)}, u32[]{:S(2)}) collective-permute-start(bf16[512,256]{1,0:T(8,128)(2,1)} %stage.12), channel_id=1, source_target_pairs={{0,16},{4,20},{8,24},{12,28},{1,17},{5,21},{9,25},{13,29},{2,18},{... | collective-permute-start | bytes 786440 | tf_op jit(solution)/shard_map/ppermute | solution.py:442
  122.2 10.6 %collective-permute-start.19 = (bf16[512,256]{1,0:T(8,128)(2,1)S(1)}, bf16[512,256]{1,0:T(8,128)(2,1)S(1)}, u32[]{:S(2)}, u32[]{:S(2)}) collective-permute-start(bf16[512,256]{1,0:T(8,128)(2,1)S(1)} %stage.14), channel_id=1, source_target_pairs={{0,16},{4,20},{8,24},{12,28},{1,17},{5,21},{9,25},{13,29},{2,18},{... | collective-permute-start | bytes 786440 | tf_op jit(solution)/shard_map/ppermute | solution.py:442
  127.0 8.0 %collective-permute-start.18 = (bf16[512,256]{1,0:T(8,128)(2,1)S(1)}, bf16[512,256]{1,0:T(8,128)(2,1)S(1)}, u32[]{:S(2)}, u32[]{:S(2)}) collective-permute-start(bf16[512,256]{1,0:T(8,128)(2,1)S(1)} %stage.13), channel_id=1, source_target_pairs={{0,16},{4,20},{8,24},{12,28},{1,17},{5,21},{9,25},{13,29},{2,18},{... | collective-permute-start | bytes 786440 | tf_op jit(solution)/shard_map/ppermute | solution.py:442
  131.5 8.1 %collective-permute-start.20 = (bf16[512,256]{1,0:T(8,128)(2,1)S(1)}, bf16[512,256]{1,0:T(8,128)(2,1)S(1)}, u32[]{:S(2)}, u32[]{:S(2)}) collective-permute-start(bf16[512,256]{1,0:T(8,128)(2,1)S(1)} %stage.15), channel_id=1, source_target_pairs={{0,16},{4,20},{8,24},{12,28},{1,17},{5,21},{9,25},{13,29},{2,18},{... | collective-permute-start | bytes 786440 | tf_op jit(solution)/shard_map/ppermute | solution.py:442
  140.5 6.8 %collective-permute-start.22 = (bf16[256,128]{1,0:T(8,128)(2,1)S(1)}, bf16[256,128]{1,0:T(8,128)(2,1)S(1)}, u32[]{:S(2)}, u32[]{:S(2)}) collective-permute-start(bf16[256,128]{1,0:T(8,128)(2,1)S(1)} %pack.1.refs_0_), channel_id=1, source_target_pairs={{0,1},{1,2},{2,3},{3,0},{4,5},{5,6},{6,7},{7,4},{8,9},{9,10},{10,1... | collective-permute-start | bytes 196616 | tf_op jit(solution)/shard_map/ppermute | solution.py:497
  142.1 7.0 %collective-permute-start.23 = (bf16[256,128]{1,0:T(8,128)(2,1)S(1)}, bf16[256,128]{1,0:T(8,128)(2,1)S(1)}, u32[]{:S(2)}, u32[]{:S(2)}) collective-permute-start(bf16[256,128]{1,0:T(8,128)(2,1)S(1)} %pack.1.refs_0_), channel_id=1, source_target_pairs={{0,2},{1,3},{2,0},{3,1},{4,6},{5,7},{6,4},{7,5},{8,10},{9,11},{10,... | collective-permute-start | bytes 196616 | tf_op jit(solution)/shard_map/ppermute | solution.py:497
  144.7 4.6 %collective-permute-start.24 = (bf16[256,128]{1,0:T(8,128)(2,1)S(1)}, bf16[256,128]{1,0:T(8,128)(2,1)S(1)}, u32[]{:S(2)}, u32[]{:S(2)}) collective-permute-start(bf16[256,128]{1,0:T(8,128)(2,1)S(1)} %pack.1.refs_0_), channel_id=1, source_target_pairs={{0,3},{1,0},{2,1},{3,2},{4,7},{5,4},{6,5},{7,6},{8,11},{9,8},{10,9... | collective-permute-start | bytes 196616 | tf_op jit(solution)/shard_map/ppermute | solution.py:497
  (40 other events, 249.0 us)

commit v5 on v4

--- a/solution.py
+++ b/solution.py
@@ -30,77 +30,107 @@
     return pl.CostEstimate(flops=flops, bytes_accessed=read, transcendentals=0)
 
 
-def operator_kernel(dates, a_ref, r_ref, w_ref):
-    features = a_ref.shape[-1]
-    sens = r_ref.shape[1]
-    product = a_ref[0, 0]
+def after(x, y):
+    return lax.optimization_barrier((x, y))[0]
+
+
+def operator_kernel(dates, buckets, a_hbm, r_hbm, w_ref, a_ref, r_ref, a_sem, r_sem):
+    features = a_hbm.shape[-1]
+    sens = r_hbm.shape[1]
+    fetch_r = pltpu.make_async_copy(r_hbm, r_ref, r_sem)
+    fetch = [
+        [pltpu.make_async_copy(a_hbm.at[t, b], a_ref.at[t, b], a_sem.at[t, b]) for b in range(buckets)]
+        for t in range(dates)
+    ]
     for t in range(dates):
-        if t:
-            product = dot(a_ref[t, 0], product).astype(bf16)
-        row = features + t * sens
-        w_ref[0, row : row + sens, :] = dot(r_ref[0], product).astype(bf16)
-    w_ref[0, :features, :] = product
+        for b in range(buckets):
+            fetch[t][b].start()
+        if t == 0:
+            fetch_r.start()
+    products = [None] * buckets
+    fetch_r.wait()
+    for t in range(dates):
+        for b in range(buckets):
+            fetch[t][b].wait()
+            if t:
+                products[b] = dot(a_ref[t, b], products[b]).astype(bf16)
+            else:
+                products[b] = a_ref[t, b]
+            row = features + t * sens
+            w_ref[b, row : row + sens, :] = dot(r_ref[b], products[b]).astype(bf16)
+    for b in range(buckets):
+        w_ref[b, :features, :] = products[b]
 
 
 def local_kernel(
-    dates, scale_ref, octet_ref, x_ref, a_ref, r_ref, out_ref, even_ref, odd_ref, state_ref
+    dates,
+    b,
+    scale_ref,
+    octet_ref,
+    x_hbm,
+    a_hbm,
+    r_hbm,
+    out_ref,
+    x_ref,
+    a_ref,
+    r_ref,
+    rows_ref,
+    state_ref,
+    x_sem,
+    a_sem,
+    r_sem,
 ):
-    features, micro, lanes = x_ref.shape[2:]
-    sens = r_ref.shape[1]
-    step = pl.program_id(0)
+    features, micro, lanes = x_ref.shape[1:]
+    sens = r_hbm.shape[1]
     width = pair * lanes
     pieces = micro // pair
-    chunk = features // pieces
-    buffers = (even_ref, odd_ref)
-
-    def lay_out(into, q):
-        part = slice(q * chunk, (q + 1) * chunk)
-        into[q * chunk * micro : (q + 1) * chunk * micro, :] = (
-            x_ref[0, 0, part].astype(f32).reshape(chunk * micro, lanes)
+    begin = pl.multiple_of(octet_ref[0] * micro, micro)
+
+    def fetch_x(t):
+        return pltpu.make_async_copy(
+            x_hbm.at[t, b, :, pl.ds(begin, micro), :], x_ref.at[t], x_sem.at[t]
         )
 
-    def advance(rows_ref, q, first):
-        cols = slice(q * width, (q + 1) * width)
-        total = scale_ref[jnp.maximum(step - 1, 0)] * jnp.concatenate(
-            [rows_ref[pl.ds(q * pair + i, features, stride=micro), :] for i in range(pair)],
-            axis=1,
-        )
-        if not first:
-            total = total + dot(a_ref[0, 0], state_ref[:, cols])
-        state = total.astype(bf16)
-        state_ref[:, cols] = state
-        row = pl.multiple_of(features + (step - 1) * sens, sens)
-        out_ref[q, pl.ds(row, sens), :] = dot(r_ref[0], state).astype(bf16)
-        return state
-
-    def both(parity, ahead, first, last):
+    def fetch_a(t):
+        return pltpu.make_async_copy(a_hbm.at[t, b], a_ref.at[t], a_sem.at[t])
+
+    fetch_r = pltpu.make_async_copy(r_hbm.at[b], r_ref, r_sem)
+    for t in range(dates):
+        fetch_x(t).start()
+        if t:
+            fetch_a(t).start()
+        else:
+            fetch_r.start()
+
+    def one_date(t, first):
+        fetch_x(t).wait()
+        rows_ref[...] = x_ref[t].astype(f32).reshape(features * micro, lanes)
+        if first:
+            fetch_r.wait()
+        else:
+            fetch_a(t).wait()
+        row = pl.multiple_of(features + t * sens, sens)
         for q in range(pieces):
-            state = advance(buffers[1 - parity], q, first)
-            if ahead:
-                lay_out(buffers[parity], q)
-            if last:
-                out_ref[q, :features, :] = state
-
-    @pl.when(step == 0)
-    def _():
-        for q in range(pieces):
-            lay_out(buffers[0], q)
-
-    @pl.when(step == 1)
-    def _():
-        both(1, dates > 1, True, dates == 1)
-
-    for parity in range(2):
-
-        @pl.when((lax.rem(step, 2) == parity) & (step > 1) & (step < dates))
-        def _():
-            both(parity, True, False, False)
-
-    if dates > 1:
-
-        @pl.when(step == dates)
-        def _():
-            both(dates % 2, False, False, True)
+            cols = slice(q * width, (q + 1) * width)
+            total = scale_ref[t] * jnp.concatenate(
+                [rows_ref[pl.ds(q * pair + i, features, stride=micro), :] for i in range(pair)],
+                axis=1,
+            )
+            if not first:
+                total = total + dot(a_ref[t], state_ref[:, cols])
+            state = total.astype(bf16)
+            state_ref[:, cols] = state
+            out_ref[q, pl.ds(row, sens), :] = dot(r_ref[...], state).astype(bf16)
+
+    one_date(0, True)
+
+    def body(t, carry):
+        one_date(t, False)
+        return carry
+
+    lax.fori_loop(1, dates, body, 0)
+    for q in range(pieces):
+        out_ref[q, :features, :] = state_ref[:, q * width : (q + 1) * width]
 
 
 def join_operator_kernel(core_ref, mine_ref, other_ref, p_ref, q_ref, late_ref):
@@ -256,56 +286,52 @@
     swap = [(i, i ^ 1) for i in range(segments)]
     smem = pl.BlockSpec(memory_space=pltpu.SMEM)
 
+    vmem = pl.BlockSpec(memory_space=pltpu.VMEM)
+    hbm = pl.BlockSpec(memory_space=pltpu.HBM)
+    small = pltpu.CompilerParams(vmem_limit_bytes=16 * 2**20)
     operators = pl.pallas_call(
-        functools.partial(operator_kernel, dates),
+        functools.partial(operator_kernel, dates, buckets),
         out_shape=jax.ShapeDtypeStruct((buckets, rows, features), bf16),
-        grid=(buckets,),
-        in_specs=[
-            pl.BlockSpec((dates, 1, features, features), lambda b: (0, b, 0, 0)),
-            pl.BlockSpec((1, sens, features), lambda b: (b, 0, 0)),
+        in_specs=[hbm, hbm],
+        out_specs=vmem,
+        scratch_shapes=[
+            pltpu.VMEM((dates, buckets, features, features), bf16),
+            pltpu.VMEM((buckets, sens, features), bf16),
+            pltpu.SemaphoreType.DMA((dates, buckets)),
+            pltpu.SemaphoreType.DMA,
         ],
-        out_specs=pl.BlockSpec((1, rows, features), lambda b: (b, 0, 0)),
+        compiler_params=small,
         cost_estimate=cost(2 * buckets * dates * features**3, 2**23),
-        compiler_params=pltpu.CompilerParams(vmem_limit_bytes=50 * 2**20),
         name="operators",
     )(transition, readout)
 
     def local(b, octet, scales):
         return pl.pallas_call(
-            functools.partial(local_kernel, dates),
+            functools.partial(local_kernel, dates, b),
             out_shape=jax.ShapeDtypeStruct((pieces, rows, width), bf16),
-            grid_spec=pltpu.PrefetchScalarGridSpec(
-                num_scalar_prefetch=2,
-                grid=(dates + 1,),
-                in_specs=[
-                    pl.BlockSpec(
-                        (1, 1, features, half, lanes),
-                        lambda i, s, o: (jnp.minimum(i, dates - 1), b, 0, o[0], 0),
-                    ),
-                    pl.BlockSpec(
-                        (1, 1, features, features),
-                        lambda i, s, o: (jnp.maximum(i - 1, 0), b, 0, 0),
-                    ),
-                    pl.BlockSpec((1, sens, features), lambda i, s, o: (b, 0, 0)),
-                ],
-                out_specs=pl.BlockSpec((pieces, rows, width), lambda i, s, o: (0, 0, 0)),
-                scratch_shapes=[
-                    pltpu.VMEM((features * half, lanes), f32),
-                    pltpu.VMEM((features * half, lanes), f32),
-                    pltpu.VMEM((features, half * lanes), bf16),
-                ],
-            ),
-            compiler_params=pltpu.CompilerParams(vmem_limit_bytes=50 * 2**20),
+            in_specs=[smem, smem, hbm, hbm, hbm],
+            out_specs=vmem,
+            scratch_shapes=[
+                pltpu.VMEM((dates, features, half, lanes), bf16),
+                pltpu.VMEM((dates, features, features), bf16),
+                pltpu.VMEM((sens, features), bf16),
+                pltpu.VMEM((features * half, lanes), f32),
+                pltpu.VMEM((features, half * lanes), bf16),
+                pltpu.SemaphoreType.DMA((dates,)),
+                pltpu.SemaphoreType.DMA((dates,)),
+                pltpu.SemaphoreType.DMA,
+            ],
+            compiler_params=small,
             cost_estimate=cost(2 * dates * rows * features * half * lanes // 2, 2**23),
             name="local",
         )(scales, octet, shocks, transition, readout)
 
-    scales, operators = lax.optimization_barrier((scales, operators))
+    scales = after(scales, operators)
     operators_other = lax.ppermute(operators, "date", swap)
     discount = (step_days.astype(f32) / 365.0)[:, None, None] * discount
     discount_other = lax.ppermute(discount, "date", swap)
     sent = local(0, 1 - core_flag, scales)
-    operators_other, sent = lax.optimization_barrier((operators_other, sent))
+    operators_other = after(operators_other, sent)
     late_half = lax.ppermute(sent, "date", swap)
 
     block3 = lambda r: pl.BlockSpec((1, r, features), lambda b: (b, 0, 0))
@@ -320,7 +346,7 @@
         in_specs=[smem, block3(rows), block3(rows)],
         out_specs=(block3(features), block3(2 * seen_rows), block3(rows)),
         cost_estimate=cost(2 * buckets * rows * features**2, 2**22),
-        compiler_params=pltpu.CompilerParams(vmem_limit_bytes=50 * 2**20),
+        compiler_params=pltpu.CompilerParams(vmem_limit_bytes=16 * 2**20),
         name="join_operators",
     )(core_flag, operators, operators_other)
 
@@ -333,11 +359,11 @@
         rows_half = features // 2
         part = lax.dynamic_slice_in_dim(block, core * rows_half, rows_half, 1)
         if s == 0:
-            scales, part = lax.optimization_barrier((scales, part))
+            scales = after(scales, part)
         part = lax.ppermute(part, "date", far)
         if s == 0:
             own = local(0, core_flag, scales)
-            part, own = lax.optimization_barrier((part, own))
+            part = after(part, own)
         part_other = lax.ppermute(part, "date", swap)
         first = core == 0
         other = jnp.concatenate(
@@ -363,8 +389,6 @@
 
     ends = []
     seens = []
-    vmem = pl.BlockSpec(memory_space=pltpu.VMEM)
-    small = pltpu.CompilerParams(vmem_limit_bytes=16 * 2**20)
 
     def join_states(b, own, late_half):
         result = pl.pallas_call(
@@ -424,7 +448,7 @@
             holds[s, j] = value.astype(bf16)
         return holds[s, j], jnp.ones((1,), jnp.int32)
 
-    def advance(s, after=None):
+    def advance(s, behind=None):
         j = len(arrived[s])
         last = s == stages - 1
         bit = 2 << s
@@ -433,11 +457,11 @@
             out = ends[j]
         else:
             near = arrived[s - 1][j]
-            if after is not None:
-                near, results[after] = lax.optimization_barrier((near, results[after]))
+            if behind is not None:
+                near = after(near, results[behind])
             out = stage(j, ups[s - 1], leaving[s - 1][j], near, combiners[s - 1])
         if j >= flight:
-            out, arrived[s][j - flight] = lax.optimization_barrier((out, arrived[s][j - flight]))
+            out = after(out, arrived[s][j - flight])
         leaving[s].append(out)
         arrived[s].append(lax.ppermute(out, "date", link))
 
@@ -451,18 +475,17 @@
         for _ in range(pieces):
             advance(0)
         if b + 1 < buckets:
-            scales, ends[-1] = lax.optimization_barrier((scales, ends[-1]))
+            scales = after(scales, ends[-1])
             sent = local(b + 1, 1 - core_flag, scales)
             late_half = lax.ppermute(sent, "date", swap)
             if stages > 1:
                 for _ in range(early):
-                    arrived[0][len(arrived[1])], sent = lax.optimization_barrier(
-                        (arrived[0][len(arrived[1])], sent)
-                    )
+                    at = len(arrived[1])
+                    arrived[0][at] = after(arrived[0][at], sent)
                     advance(1)
-                    scales, leaving[1][-1] = lax.optimization_barrier((scales, leaving[1][-1]))
+                    scales = after(scales, leaving[1][-1])
             else:
-                scales, sent = lax.optimization_barrier((scales, sent))
+                scales = after(scales, sent)
             own = local(b + 1, core_flag, scales)
             join_states(b + 1, own, late_half)
     for s in range(1, stages):

time: 161 us -> 172 us (1.068)
  local copies, waits for them, and re-layouts: 11.6 us -> 31.8 us
  Pallas kernels: 75.7 us -> 70.7 us
  waiting for transfers between devices: 29 us -> 27 us
  starting transfers between devices: 37.1 us -> 35.2 us
    unnamed x74 -> x98, local copies, waits for them, and re-layouts: 10.9 us -> 31.1 us
    ppermute x16, waiting for transfers between devices: 14.6 us -> 18.5 us  [advance(): arrived[s].append(lax.ppermute(out, 'date', link))]
    ppermute x1, waiting for transfers between devices: 3.82 us -> 0.01 us  [shards(): part_other = lax.ppermute(part, 'date', swap)]
    pallas_call x5, Pallas kernels: 44.1 us -> 40.8 us  [the longest x4 35.2 us: local(): pl.pallas_call(functools.partial(local_kernel, dates, b), out_shape=jax.S...]
    ppermute x1, waiting for transfers between devices: 3.01 us -> 0.01 us  [shards(): part = lax.ppermute(part, 'date', far)]
    pallas_call x8, Pallas kernels: 10.4 us -> 8.18 us  [stage(): pl.pallas_call(functools.partial(stage_kernel, j // pieces), out_shape=ja...]
where the time goes in v5:
time: 172 us; the launch traced here: 171 us
  Pallas kernels  70.7 us (41%)
  starting transfers between devices  35.2 us (20%)
  local copies, waits for them, and re-layouts  31.8 us (18%)
  waiting for transfers between devices  27 us (16%)
  other arithmetic  4.76 us (3%)
    pallas_call x4, Pallas kernels, local(): pl.pallas_call(functools.partial(local_kernel, dates, b), out_shape=jax.S...  35.2 us
    unnamed x98, local copies, waits for them, and re-layouts  31.1 us
    ppermute x16, starting transfers between devices, advance(): arrived[s].append(lax.ppermute(out, 'date', link))  22.5 us
    ppermute x16, waiting for transfers between devices, advance(): arrived[s].append(lax.ppermute(out, 'date', link))  18.5 us
    pallas_call x8, Pallas kernels, final(): pl.pallas_call(functools.partial(final_kernel, b, q, 2 * dates), out_shap...  12.1 us
    pallas_call x8, Pallas kernels, stage(): pl.pallas_call(functools.partial(stage_kernel, j // pieces), out_shape=ja...  8.18 us
    pallas_call x2, Pallas kernels, join_states(): pl.pallas_call(functools.partial(join_state_kernel, b), out_shape=(jax.Sh...  6.01 us
    pallas_call x1, Pallas kernels, shards(): pl.pallas_call(functools.partial(operator_kernel, dates, buckets), out_sh...  5.62 us
  transfers between devices with their start and end apart: 28, of which 11 were waited for; matrix products, arithmetic and copies ran while one was open for 4% of the time, Pallas kernels for 36%

profile of v5, /device:TPU:0, one launch (start us, length us, event | category | flops | bytes accessed | tf_op | source)
XLA Modules:
  0.0 170.9 jit_solution(7057997305921500518)
XLA Ops:
  0.6 2.2 %copy-done.4 = bf16[4,2,512,512]{3,2,1,0:T(8,128)(2,1)S(1)} copy-done((bf16[4,2,512,512]{3,2,1,0:T(8,128)(2,1)S(1)}, bf16[4,2,512,512]{3,2,1,0:T(8,128)(2,1)}, u32[]{:S(2)}) %copy-start.4) | copy-done | bytes 4194328
  3.7 5.6 %operators.1.mine_ref = bf16[2,768,512]{2,1,0:T(8,128)(2,1)} custom-call(bf16[4,2,512,512]{3,2,1,0:T(8,128)(2,1)S(1)} %copy-done.4, bf16[2,64,512]{2,1,0:T(8,128)(2,1)S(1)} %copy-done.17), custom_call_target="tpu_custom_call" | custom-call | flops 2147483648 | bytes 8388608 | tf_op jit(solution)/shard_map/operators/pallas_call | solution.py:292
  9.9 5.8 %copy-done = bf16[4,2,512,16,128]{4,3,2,1,0:T(8,128)(2,1)S(1)} copy-done((bf16[4,2,512,16,128]{4,3,2,1,0:T(8,128)(2,1)S(1)}, bf16[4,2,512,16,128]{4,3,2,1,0:T(8,128)(2,1)}, u32[]{:S(2)}) %copy-start) | copy-done | bytes 16777240
  15.7 2.2 %copy-done.5 = bf16[4,2,512,512]{3,2,1,0:T(8,128)(2,1)S(1)} copy-done((bf16[4,2,512,512]{3,2,1,0:T(8,128)(2,1)S(1)}, bf16[4,2,512,512]{3,2,1,0:T(8,128)(2,1)}, u32[]{:S(2)}) %copy-start.5) | copy-done | bytes 4194328
  17.9 9.4 %local.4 = bf16[4,768,256]{2,1,0:T(8,128)(2,1)} custom-call(f32[4]{0:T(128)S(1)} %get-tuple-element.54.scale_ref, s32[1]{0:T(128)S(6)} %sub.28.octet_ref, bf16[4,2,512,16,128]{4,3,2,1,0:T(8,128)(2,1)S(1)} %copy-done, bf16[4,2,512,512]{3,2,1,0:T(8,128)(2,1)S(1)} %copy-done.5, bf16[2,64,512]{2,1,0:T(8,128)(2,1)S(1)} %copy-done.17), custom_call_target="tpu_custom_call" | custom-call | flops 1610612736 | bytes 8388608 | tf_op jit(solution)/shard_map/local/pallas_call | solution.py:309
  27.4 2.7 %join_operators.1 = (bf16[2,512,512]{2,1,0:T(8,128)(2,1)S(1)}, bf16[2,512,512]{2,1,0:T(8,128)(2,1)S(1)}, bf16[2,768,512]{2,1,0:T(8,128)(2,1)S(1)}) custom-call(s32[1]{0:T(128)} %bitcast.1.core_ref.octet_ref, bf16[2,768,512]{2,1,0:T(8,128)(2,1)} %operators.1.mine_ref, bf16[2,768,512]{2,1,0:T(8,128)(2,1)} %collective-permute-done.other_ref), custom_call_target="tpu_custom_call" | custom-call | flops 805306368 | bytes 4194304 | tf_op jit(solution)/shard_map/join_operators/pallas_call | solution.py:338
  31.2 2.9 %collective-permute-start.3 = (bf16[2,256,512]{2,1,0:T(8,128)(2,1)S(1)}, bf16[2,256,512]{2,1,0:T(8,128)(2,1)}, u32[]{:S(2)}, u32[]{:S(2)}) collective-permute-start(bf16[2,256,512]{2,1,0:T(8,128)(2,1)S(1)} %constant_dynamic-slice_fusion), channel_id=1, source_target_pairs={{0,8},{4,12},{8,0},{12,4},{16,24},{20,28},{24,16},{28,20},{1,9},{5... | collective-permute-start | bytes 1572872 | tf_op jit(solution)/shard_map/ppermute | solution.py:363
  34.1 5.8 %copy-done.1 = bf16[4,2,512,16,128]{4,3,2,1,0:T(8,128)(2,1)S(1)} copy-done((bf16[4,2,512,16,128]{4,3,2,1,0:T(8,128)(2,1)S(1)}, bf16[4,2,512,16,128]{4,3,2,1,0:T(8,128)(2,1)}, u32[]{:S(2)}) %copy-start.1) | copy-done | bytes 16777240
  39.9 8.2 %local.5.mine_ref = bf16[4,768,256]{2,1,0:T(8,128)(2,1)S(1)} custom-call(f32[4]{0:T(128)S(1)} %get-tuple-element.54.scale_ref, s32[1]{0:T(128)} %bitcast.1.core_ref.octet_ref, bf16[4,2,512,16,128]{4,3,2,1,0:T(8,128)(2,1)S(1)} %copy-done.1, bf16[4,2,512,512]{3,2,1,0:T(8,128)(2,1)S(1)} %copy-done.6, bf16[2,64,512]{2,1,0:T(8,128)(2,1)S(1)} %copy-done.18), custom_call_target="tpu_custom_call" | custom-call | flops 1610612736 | bytes 8388608 | tf_op jit(solution)/shard_map/local/pallas_call | solution.py:309
  48.1 2.7 %join_states.2 = (f32[4,512,256]{2,1,0:T(8,128)S(1)}, bf16[512,256]{1,0:T(8,128)(2,1)}, bf16[512,256]{1,0:T(8,128)(2,1)S(1)}, bf16[512,256]{1,0:T(8,128)(2,1)S(1)}, bf16[512,256]{1,0:T(8,128)(2,1)S(1)}) custom-call(s32[1]{0:T(128)} %bitcast.1.core_ref.octet_ref, bf16[4,768,256]{2,1,0:T(8,128)(2,1)S(1)} %local.5.mine_ref, ...), custom_call_target="tpu_custom_call" | custom-call | flops 805306368 | bytes 4194304 | tf_op jit(solution)/shard_map/join_states/pallas_call | solution.py:394
  50.8 9.5 %local.6 = bf16[4,768,256]{2,1,0:T(8,128)(2,1)} custom-call(f32[4]{0:T(128)S(1)} %get-tuple-element.54.scale_ref, s32[1]{0:T(128)S(6)} %sub.28.octet_ref, bf16[4,2,512,16,128]{4,3,2,1,0:T(8,128)(2,1)S(1)} %copy-done.2, bf16[4,2,512,512]{3,2,1,0:T(8,128)(2,1)S(1)} %copy-done.6, bf16[2,64,512]{2,1,0:T(8,128)(2,1)S(1)} %copy-done.18), custom_call_target="tpu_custom_call" | custom-call | flops 1610612736 | bytes 8388608 | tf_op jit(solution)/shard_map/local/pallas_call | solution.py:309
  60.9 2.0 %collective-permute-start.6 = (bf16[512,256]{1,0:T(8,128)(2,1)S(1)}, bf16[512,256]{1,0:T(8,128)(2,1)S(1)}, u32[]{:S(2)}, u32[]{:S(2)}) collective-permute-start(bf16[512,256]{1,0:T(8,128)(2,1)S(1)} %get-tuple-element.49.mine_ref), channel_id=1, source_target_pairs={{0,8},{4,12},{8,0},{12,4},{16,24},{20,28},{24,16},{28,20},{1,9},{5... | collective-permute-start | bytes 786440 | tf_op jit(solution)/shard_map/ppermute | solution.py:466
  64.7 5.6 %collective-permute-done.2.other_ref.first_ref = bf16[512,256]{1,0:T(8,128)(2,1)S(1)} collective-permute-done((bf16[512,256]{1,0:T(8,128)(2,1)}, bf16[512,256]{1,0:T(8,128)(2,1)S(1)}, u32[]{:S(2)}, u32[]{:S(2)}) %collective-permute-start.2) | collective-permute-done | bytes 262176 | tf_op jit(solution)/shard_map/ppermute | solution.py:466
  70.3 5.6 %collective-permute-done.6.other_ref.first_ref = bf16[512,256]{1,0:T(8,128)(2,1)S(1)} collective-permute-done((bf16[512,256]{1,0:T(8,128)(2,1)S(1)}, bf16[512,256]{1,0:T(8,128)(2,1)S(1)}, u32[]{:S(2)}, u32[]{:S(2)}) %collective-permute-start.6) | collective-permute-done | bytes 262176 | tf_op jit(solution)/shard_map/ppermute | solution.py:466
  79.5 3.4 %collective-permute-start.5 = (bf16[512,256]{1,0:T(8,128)(2,1)S(1)}, bf16[512,256]{1,0:T(8,128)(2,1)S(1)}, u32[]{:S(2)}, u32[]{:S(2)}) collective-permute-start(bf16[512,256]{1,0:T(8,128)(2,1)S(1)} %stage.8), channel_id=1, source_target_pairs={{0,16},{4,20},{8,24},{12,28},{1,17},{5,21},{9,25},{13,29},{2,18},{... | collective-permute-start | bytes 786440 | tf_op jit(solution)/shard_map/ppermute | solution.py:466
  87.0 3.4 %collective-permute-start.9 = (bf16[512,256]{1,0:T(8,128)(2,1)S(1)}, bf16[512,256]{1,0:T(8,128)(2,1)S(1)}, u32[]{:S(2)}, u32[]{:S(2)}) collective-permute-start(bf16[512,256]{1,0:T(8,128)(2,1)S(1)} %stage.10), channel_id=1, source_target_pairs={{0,16},{4,20},{8,24},{12,28},{1,17},{5,21},{9,25},{13,29},{2,18},{... | collective-permute-start | bytes 786440 | tf_op jit(solution)/shard_map/ppermute | solution.py:466
  90.5 5.8 %copy-done.3 = bf16[4,2,512,16,128]{4,3,2,1,0:T(8,128)(2,1)S(1)} copy-done((bf16[4,2,512,16,128]{4,3,2,1,0:T(8,128)(2,1)S(1)}, bf16[4,2,512,16,128]{4,3,2,1,0:T(8,128)(2,1)}, u32[]{:S(2)}) %copy-start.3) | copy-done | bytes 16777240
  96.2 8.2 %local.7.mine_ref = bf16[4,768,256]{2,1,0:T(8,128)(2,1)S(1)} custom-call(f32[4]{0:T(128)S(1)} %get-tuple-element.54.scale_ref, s32[1]{0:T(128)} %bitcast.1.core_ref.octet_ref, bf16[4,2,512,16,128]{4,3,2,1,0:T(8,128)(2,1)S(1)} %copy-done.3, bf16[4,2,512,512]{3,2,1,0:T(8,128)(2,1)S(1)} %copy-done.7, bf16[2,64,512]{2,1,0:T(8,128)(2,1)S(1)} %copy-done.18), custom_call_target="tpu_custom_call" | custom-call | flops 1610612736 | bytes 8388608 | tf_op jit(solution)/shard_map/local/pallas_call | solution.py:309
  104.4 3.3 %join_states.3 = (f32[4,512,256]{2,1,0:T(8,128)S(1)}, bf16[512,256]{1,0:T(8,128)(2,1)S(1)}, bf16[512,256]{1,0:T(8,128)(2,1)}, bf16[512,256]{1,0:T(8,128)(2,1)}, bf16[512,256]{1,0:T(8,128)(2,1)}) custom-call(s32[1]{0:T(128)} %bitcast.1.core_ref.octet_ref, bf16[4,768,256]{2,1,0:T(8,128)(2,1)S(1)} %local.7.mine_ref, ...), custom_call_target="tpu_custom_call" | custom-call | flops 805306368 | bytes 4194304 | tf_op jit(solution)/shard_map/join_states/pallas_call | solution.py:394
  142.3 2.9 %collective-permute-done.18.last_ref = bf16[512,256]{1,0:T(8,128)(2,1)S(1)} collective-permute-done((bf16[512,256]{1,0:T(8,128)(2,1)S(1)}, bf16[512,256]{1,0:T(8,128)(2,1)S(1)}, u32[]{:S(2)}, u32[]{:S(2)}) %collective-permute-start.18) | collective-permute-done | bytes 262176 | tf_op jit(solution)/shard_map/ppermute | solution.py:466
  147.1 2.7 %collective-permute-done.20.last_ref = bf16[512,256]{1,0:T(8,128)(2,1)S(1)} collective-permute-done((bf16[512,256]{1,0:T(8,128)(2,1)S(1)}, bf16[512,256]{1,0:T(8,128)(2,1)S(1)}, u32[]{:S(2)}, u32[]{:S(2)}) %collective-permute-start.20) | collective-permute-done | bytes 262176 | tf_op jit(solution)/shard_map/ppermute | solution.py:466
  153.4 2.6 %collective-permute-start.23 = (bf16[256,128]{1,0:T(8,128)(2,1)S(1)}, bf16[256,128]{1,0:T(8,128)(2,1)S(1)}, u32[]{:S(2)}, u32[]{:S(2)}) collective-permute-start(bf16[256,128]{1,0:T(8,128)(2,1)S(1)} %pack.1.refs_0_), channel_id=1, source_target_pairs={{0,2},{1,3},{2,0},{3,1},{4,6},{5,7},{6,4},{7,5},{8,10},{9,11},{10,... | collective-permute-start | bytes 196616 | tf_op jit(solution)/shard_map/ppermute | solution.py:520
  163.2 3.1 %collective-permute-done.26 = f32[8,128]{1,0:T(8,128)S(1)} collective-permute-done((f32[8,128]{1,0:T(8,128)S(1)}, f32[8,128]{1,0:T(8,128)S(1)}, u32[]{:S(2)}, u32[]{:S(2)}) %collective-permute-start.26) | collective-permute-done | bytes 4128 | tf_op jit(solution)/shard_map/ppermute | solution.py:548
  166.3 2.5 %collective-permute-start.27 = (f32[8,128]{1,0:T(8,128)S(1)}, f32[8,128]{1,0:T(8,128)S(1)}, u32[]{:S(2)}, u32[]{:S(2)}) collective-permute-start(f32[8,128]{1,0:T(8,128)S(1)} %add.28), channel_id=1, source_target_pairs={{0,16},{4,20},{8,24},{12,28},{16,0},{20,4},{24,8},{28,12},{1,17},{... | collective-permute-start | bytes 12296 | tf_op jit(solution)/shard_map/ppermute | solution.py:548
  (177 shorter events, 61.5 us)
Async XLA Ops:
  9.4 18.0 %collective-permute-start = (bf16[2,768,512]{2,1,0:T(8,128)(2,1)}, bf16[2,768,512]{2,1,0:T(8,128)(2,1)}, u32[]{:S(2)}, u32[]{:S(2)}) collective-permute-start(bf16[2,768,512]{2,1,0:T(8,128)(2,1)} %operators.1.mine_ref), channel_id=1, source_target_pairs={{0,4},{4,0},{8,12},{12,8},{16,20},{20,16},{24,28},{28,24},{1,5},{5... | collective-permute-start | bytes 4718600 | tf_op jit(solution)/shard_map/ppermute | solution.py:330
  27.3 20.8 %collective-permute-start.1 = (bf16[4,768,256]{2,1,0:T(8,128)(2,1)}, bf16[4,768,256]{2,1,0:T(8,128)(2,1)}, u32[]{:S(2)}, u32[]{:S(2)}) collective-permute-start(bf16[4,768,256]{2,1,0:T(8,128)(2,1)} %local.4), channel_id=1, source_target_pairs={{0,4},{4,0},{8,12},{12,8},{16,20},{20,16},{24,28},{28,24},{1,5},{5... | collective-permute-start | bytes 4718600 | tf_op jit(solution)/shard_map/ppermute | solution.py:335
  31.2 29.3 %collective-permute-start.3 = (bf16[2,256,512]{2,1,0:T(8,128)(2,1)S(1)}, bf16[2,256,512]{2,1,0:T(8,128)(2,1)}, u32[]{:S(2)}, u32[]{:S(2)}) collective-permute-start(bf16[2,256,512]{2,1,0:T(8,128)(2,1)S(1)} %constant_dynamic-slice_fusion), channel_id=1, source_target_pairs={{0,8},{4,12},{8,0},{12,4},{16,24},{20,28},{24,16},{28,20},{1,9},{5... | collective-permute-start | bytes 1572872 | tf_op jit(solution)/shard_map/ppermute | solution.py:363
  60.3 44.1 %collective-permute-start.12 = (bf16[4,768,256]{2,1,0:T(8,128)(2,1)}, bf16[4,768,256]{2,1,0:T(8,128)(2,1)}, u32[]{:S(2)}, u32[]{:S(2)}) collective-permute-start(bf16[4,768,256]{2,1,0:T(8,128)(2,1)} %local.6), channel_id=1, source_target_pairs={{0,4},{4,0},{8,12},{12,8},{16,20},{20,16},{24,28},{28,24},{1,5},{5... | collective-permute-start | bytes 4718600 | tf_op jit(solution)/shard_map/ppermute | solution.py:480
  60.4 15.5 %collective-permute-start.4 = (bf16[2,256,512]{2,1,0:T(8,128)(2,1)}, bf16[2,256,512]{2,1,0:T(8,128)(2,1)S(1)}, u32[]{:S(2)}, u32[]{:S(2)}) collective-permute-start(bf16[2,256,512]{2,1,0:T(8,128)(2,1)} %collective-permute-done.3), channel_id=1, source_target_pairs={{0,4},{4,0},{8,12},{12,8},{16,20},{20,16},{24,28},{28,24},{1,5},{5... | collective-permute-start | bytes 1572872 | tf_op jit(solution)/shard_map/ppermute | solution.py:367
  60.9 9.4 %collective-permute-start.2 = (bf16[512,256]{1,0:T(8,128)(2,1)}, bf16[512,256]{1,0:T(8,128)(2,1)S(1)}, u32[]{:S(2)}, u32[]{:S(2)}) collective-permute-start(bf16[512,256]{1,0:T(8,128)(2,1)} %get-tuple-element.42.mine_ref), channel_id=1, source_target_pairs={{0,8},{4,12},{8,0},{12,4},{16,24},{20,28},{24,16},{28,20},{1,9},{5... | collective-permute-start | bytes 786440 | tf_op jit(solution)/shard_map/ppermute | solution.py:466
  60.9 15.0 %collective-permute-start.6 = (bf16[512,256]{1,0:T(8,128)(2,1)S(1)}, bf16[512,256]{1,0:T(8,128)(2,1)S(1)}, u32[]{:S(2)}, u32[]{:S(2)}) collective-permute-start(bf16[512,256]{1,0:T(8,128)(2,1)S(1)} %get-tuple-element.49.mine_ref), channel_id=1, source_target_pairs={{0,8},{4,12},{8,0},{12,4},{16,24},{20,28},{24,16},{28,20},{1,9},{5... | collective-permute-start | bytes 786440 | tf_op jit(solution)/shard_map/ppermute | solution.py:466
  64.6 46.6 %collective-permute-start.10 = (bf16[512,256]{1,0:T(8,128)(2,1)}, bf16[512,256]{1,0:T(8,128)(2,1)S(1)}, u32[]{:S(2)}, u32[]{:S(2)}) collective-permute-start(bf16[512,256]{1,0:T(8,128)(2,1)} %copy-done.31), channel_id=1, source_target_pairs={{0,8},{4,12},{8,0},{12,4},{16,24},{20,28},{24,16},{28,20},{1,9},{5... | collective-permute-start | bytes 786440 | tf_op jit(solution)/shard_map/ppermute | solution.py:466
  70.3 16.0 %collective-permute-start.8 = (bf16[512,256]{1,0:T(8,128)(2,1)}, bf16[512,256]{1,0:T(8,128)(2,1)S(1)}, u32[]{:S(2)}, u32[]{:S(2)}) collective-permute-start(bf16[512,256]{1,0:T(8,128)(2,1)} %copy-done.33), channel_id=1, source_target_pairs={{0,8},{4,12},{8,0},{12,4},{16,24},{20,28},{24,16},{28,20},{1,9},{5... | collective-permute-start | bytes 786440 | tf_op jit(solution)/shard_map/ppermute | solution.py:466
  79.5 30.8 %collective-permute-start.5 = (bf16[512,256]{1,0:T(8,128)(2,1)S(1)}, bf16[512,256]{1,0:T(8,128)(2,1)S(1)}, u32[]{:S(2)}, u32[]{:S(2)}) collective-permute-start(bf16[512,256]{1,0:T(8,128)(2,1)S(1)} %stage.8), channel_id=1, source_target_pairs={{0,16},{4,20},{8,24},{12,28},{1,17},{5,21},{9,25},{13,29},{2,18},{... | collective-permute-start | bytes 786440 | tf_op jit(solution)/shard_map/ppermute | solution.py:466
  83.3 31.0 %collective-permute-start.7 = (bf16[512,256]{1,0:T(8,128)(2,1)S(1)}, bf16[512,256]{1,0:T(8,128)(2,1)S(1)}, u32[]{:S(2)}, u32[]{:S(2)}) collective-permute-start(bf16[512,256]{1,0:T(8,128)(2,1)S(1)} %stage.9), channel_id=1, source_target_pairs={{0,16},{4,20},{8,24},{12,28},{1,17},{5,21},{9,25},{13,29},{2,18},{... | collective-permute-start | bytes 786440 | tf_op jit(solution)/shard_map/ppermute | solution.py:466
  87.0 33.7 %collective-permute-start.9 = (bf16[512,256]{1,0:T(8,128)(2,1)S(1)}, bf16[512,256]{1,0:T(8,128)(2,1)S(1)}, u32[]{:S(2)}, u32[]{:S(2)}) collective-permute-start(bf16[512,256]{1,0:T(8,128)(2,1)S(1)} %stage.10), channel_id=1, source_target_pairs={{0,16},{4,20},{8,24},{12,28},{1,17},{5,21},{9,25},{13,29},{2,18},{... | collective-permute-start | bytes 786440 | tf_op jit(solution)/shard_map/ppermute | solution.py:466
  109.1 7.7 %collective-permute-start.13 = (bf16[512,256]{1,0:T(8,128)(2,1)S(1)}, bf16[512,256]{1,0:T(8,128)(2,1)S(1)}, u32[]{:S(2)}, u32[]{:S(2)}) collective-permute-start(bf16[512,256]{1,0:T(8,128)(2,1)S(1)} %get-tuple-element.56.mine_ref), channel_id=1, source_target_pairs={{0,8},{4,12},{8,0},{12,4},{16,24},{20,28},{24,16},{28,20},{1,9},{5... | collective-permute-start | bytes 786440 | tf_op jit(solution)/shard_map/ppermute | solution.py:466
  110.3 8.8 %collective-permute-start.21 = (f32[4,4,128]{2,1,0:T(4,128)S(1)}, f32[4,4,128]{2,1,0:T(4,128)}, u32[]{:S(2)}, u32[]{:S(2)}) collective-permute-start(f32[4,4,128]{2,1,0:T(4,128)S(1)} %broadcast_multiply_fusion), channel_id=1, source_target_pairs={{0,4},{4,0},{8,12},{12,8},{16,20},{20,16},{24,28},{28,24},{1,5},{5... | collective-permute-start | bytes 24584 | tf_op jit(solution)/shard_map/ppermute | solution.py:332
  112.3 15.9 %collective-permute-start.11 = (bf16[512,256]{1,0:T(8,128)(2,1)}, bf16[512,256]{1,0:T(8,128)(2,1)}, u32[]{:S(2)}, u32[]{:S(2)}) collective-permute-start(bf16[512,256]{1,0:T(8,128)(2,1)} %stage.11), channel_id=1, source_target_pairs={{0,16},{4,20},{8,24},{12,28},{1,17},{5,21},{9,25},{13,29},{2,18},{... | collective-permute-start | bytes 786440 | tf_op jit(solution)/shard_map/ppermute | solution.py:466
  115.3 14.8 %collective-permute-start.15 = (bf16[512,256]{1,0:T(8,128)(2,1)}, bf16[512,256]{1,0:T(8,128)(2,1)}, u32[]{:S(2)}, u32[]{:S(2)}) collective-permute-start(bf16[512,256]{1,0:T(8,128)(2,1)} %get-tuple-element.61.mine_ref), channel_id=1, source_target_pairs={{0,8},{4,12},{8,0},{12,4},{16,24},{20,28},{24,16},{28,20},{1,9},{5... | collective-permute-start | bytes 786440 | tf_op jit(solution)/shard_map/ppermute | solution.py:466
  116.9 16.1 %collective-permute-start.17 = (bf16[512,256]{1,0:T(8,128)(2,1)}, bf16[512,256]{1,0:T(8,128)(2,1)}, u32[]{:S(2)}, u32[]{:S(2)}) collective-permute-start(bf16[512,256]{1,0:T(8,128)(2,1)} %get-tuple-element.65.mine_ref), channel_id=1, source_target_pairs={{0,8},{4,12},{8,0},{12,4},{16,24},{20,28},{24,16},{28,20},{1,9},{5... | collective-permute-start | bytes 786440 | tf_op jit(solution)/shard_map/ppermute | solution.py:466
  119.2 18.4 %collective-permute-start.19 = (bf16[512,256]{1,0:T(8,128)(2,1)}, bf16[512,256]{1,0:T(8,128)(2,1)}, u32[]{:S(2)}, u32[]{:S(2)}) collective-permute-start(bf16[512,256]{1,0:T(8,128)(2,1)} %get-tuple-element.69.mine_ref), channel_id=1, source_target_pairs={{0,8},{4,12},{8,0},{12,4},{16,24},{20,28},{24,16},{28,20},{1,9},{5... | collective-permute-start | bytes 786440 | tf_op jit(solution)/shard_map/ppermute | solution.py:466
  121.4 14.2 %collective-permute-start.14 = (bf16[512,256]{1,0:T(8,128)(2,1)}, bf16[512,256]{1,0:T(8,128)(2,1)}, u32[]{:S(2)}, u32[]{:S(2)}) collective-permute-start(bf16[512,256]{1,0:T(8,128)(2,1)} %stage.12), channel_id=1, source_target_pairs={{0,16},{4,20},{8,24},{12,28},{1,17},{5,21},{9,25},{13,29},{2,18},{... | collective-permute-start | bytes 786440 | tf_op jit(solution)/shard_map/ppermute | solution.py:466
  131.6 8.8 %collective-permute-start.16 = (bf16[512,256]{1,0:T(8,128)(2,1)S(1)}, bf16[512,256]{1,0:T(8,128)(2,1)S(1)}, u32[]{:S(2)}, u32[]{:S(2)}) collective-permute-start(bf16[512,256]{1,0:T(8,128)(2,1)S(1)} %stage.13), channel_id=1, source_target_pairs={{0,16},{4,20},{8,24},{12,28},{1,17},{5,21},{9,25},{13,29},{2,18},{... | collective-permute-start | bytes 786440 | tf_op jit(solution)/shard_map/ppermute | solution.py:466
  134.3 10.9 %collective-permute-start.18 = (bf16[512,256]{1,0:T(8,128)(2,1)S(1)}, bf16[512,256]{1,0:T(8,128)(2,1)S(1)}, u32[]{:S(2)}, u32[]{:S(2)}) collective-permute-start(bf16[512,256]{1,0:T(8,128)(2,1)S(1)} %stage.14), channel_id=1, source_target_pairs={{0,16},{4,20},{8,24},{12,28},{1,17},{5,21},{9,25},{13,29},{2,18},{... | collective-permute-start | bytes 786440 | tf_op jit(solution)/shard_map/ppermute | solution.py:466
  138.9 11.0 %collective-permute-start.20 = (bf16[512,256]{1,0:T(8,128)(2,1)S(1)}, bf16[512,256]{1,0:T(8,128)(2,1)S(1)}, u32[]{:S(2)}, u32[]{:S(2)}) collective-permute-start(bf16[512,256]{1,0:T(8,128)(2,1)S(1)} %stage.15), channel_id=1, source_target_pairs={{0,16},{4,20},{8,24},{12,28},{1,17},{5,21},{9,25},{13,29},{2,18},{... | collective-permute-start | bytes 786440 | tf_op jit(solution)/shard_map/ppermute | solution.py:466
  151.7 6.8 %collective-permute-start.22 = (bf16[256,128]{1,0:T(8,128)(2,1)S(1)}, bf16[256,128]{1,0:T(8,128)(2,1)S(1)}, u32[]{:S(2)}, u32[]{:S(2)}) collective-permute-start(bf16[256,128]{1,0:T(8,128)(2,1)S(1)} %pack.1.refs_0_), channel_id=1, source_target_pairs={{0,1},{1,2},{2,3},{3,0},{4,5},{5,6},{6,7},{7,4},{8,9},{9,10},{10,1... | collective-permute-start | bytes 196616 | tf_op jit(solution)/shard_map/ppermute | solution.py:520
  153.4 7.0 %collective-permute-start.23 = (bf16[256,128]{1,0:T(8,128)(2,1)S(1)}, bf16[256,128]{1,0:T(8,128)(2,1)S(1)}, u32[]{:S(2)}, u32[]{:S(2)}) collective-permute-start(bf16[256,128]{1,0:T(8,128)(2,1)S(1)} %pack.1.refs_0_), channel_id=1, source_target_pairs={{0,2},{1,3},{2,0},{3,1},{4,6},{5,7},{6,4},{7,5},{8,10},{9,11},{10,... | collective-permute-start | bytes 196616 | tf_op jit(solution)/shard_map/ppermute | solution.py:520
  (52 other events, 333.2 us)

commit v6 on v5

--- a/solution.py
+++ b/solution.py
@@ -11,10 +11,10 @@
 epsilon = 1e-06
 f32 = jnp.float32
 bf16 = jnp.bfloat16
-pair = 2
-flight = 4
-lag = 2
-early = 2
+pair = 4
+flight = 2
+lag = 1
+early = 1
 
 
 def dot(a, b):
@@ -34,32 +34,16 @@
     return lax.optimization_barrier((x, y))[0]
 
 
-def operator_kernel(dates, buckets, a_hbm, r_hbm, w_ref, a_ref, r_ref, a_sem, r_sem):
-    features = a_hbm.shape[-1]
-    sens = r_hbm.shape[1]
-    fetch_r = pltpu.make_async_copy(r_hbm, r_ref, r_sem)
-    fetch = [
-        [pltpu.make_async_copy(a_hbm.at[t, b], a_ref.at[t, b], a_sem.at[t, b]) for b in range(buckets)]
-        for t in range(dates)
-    ]
+def operator_kernel(dates, a_ref, r_ref, w_ref):
+    features = a_ref.shape[-1]
+    sens = r_ref.shape[1]
+    product = a_ref[0, 0]
     for t in range(dates):
-        for b in range(buckets):
-            fetch[t][b].start()
-        if t == 0:
-            fetch_r.start()
-    products = [None] * buckets
-    fetch_r.wait()
-    for t in range(dates):
-        for b in range(buckets):
-            fetch[t][b].wait()
-            if t:
-                products[b] = dot(a_ref[t, b], products[b]).astype(bf16)
-            else:
-                products[b] = a_ref[t, b]
-            row = features + t * sens
-            w_ref[b, row : row + sens, :] = dot(r_ref[b], products[b]).astype(bf16)
-    for b in range(buckets):
-        w_ref[b, :features, :] = products[b]
+        if t:
+            product = dot(a_ref[t, 0], product).astype(bf16)
+        row = features + t * sens
+        w_ref[0, row : row + sens, :] = dot(r_ref[0], product).astype(bf16)
+    w_ref[0, :features, :] = product
 
 
 def local_kernel(
@@ -101,34 +85,26 @@
             fetch_a(t).start()
         else:
             fetch_r.start()
-
-    def one_date(t, first):
+    for t in range(dates):
         fetch_x(t).wait()
         rows_ref[...] = x_ref[t].astype(f32).reshape(features * micro, lanes)
-        if first:
+        if t:
+            fetch_a(t).wait()
+        else:
             fetch_r.wait()
-        else:
-            fetch_a(t).wait()
-        row = pl.multiple_of(features + t * sens, sens)
         for q in range(pieces):
             cols = slice(q * width, (q + 1) * width)
             total = scale_ref[t] * jnp.concatenate(
                 [rows_ref[pl.ds(q * pair + i, features, stride=micro), :] for i in range(pair)],
                 axis=1,
             )
-            if not first:
+            if t:
                 total = total + dot(a_ref[t], state_ref[:, cols])
-            state = total.astype(bf16)
-            state_ref[:, cols] = state
-            out_ref[q, pl.ds(row, sens), :] = dot(r_ref[...], state).astype(bf16)
-
-    one_date(0, True)
-
-    def body(t, carry):
-        one_date(t, False)
-        return carry
-
-    lax.fori_loop(1, dates, body, 0)
+            state_ref[:, cols] = total.astype(bf16)
+        row = features + t * sens
+        for q in range(pieces):
+            state = state_ref[:, q * width : (q + 1) * width]
+            out_ref[q, row : row + sens, :] = dot(r_ref[...], state).astype(bf16)
     for q in range(pieces):
         out_ref[q, :features, :] = state_ref[:, q * width : (q + 1) * width]
 
@@ -289,19 +265,18 @@
     vmem = pl.BlockSpec(memory_space=pltpu.VMEM)
     hbm = pl.BlockSpec(memory_space=pltpu.HBM)
     small = pltpu.CompilerParams(vmem_limit_bytes=16 * 2**20)
+    large = pltpu.CompilerParams(vmem_limit_bytes=50 * 2**20)
     operators = pl.pallas_call(
-        functools.partial(operator_kernel, dates, buckets),
+        functools.partial(operator_kernel, dates),
         out_shape=jax.ShapeDtypeStruct((buckets, rows, features), bf16),
-        in_specs=[hbm, hbm],
-        out_specs=vmem,
-        scratch_shapes=[
-            pltpu.VMEM((dates, buckets, features, features), bf16),
-            pltpu.VMEM((buckets, sens, features), bf16),
-            pltpu.SemaphoreType.DMA((dates, buckets)),
-            pltpu.SemaphoreType.DMA,
+        grid=(buckets,),
+        in_specs=[
+            pl.BlockSpec((dates, 1, features, features), lambda b: (0, b, 0, 0)),
+            pl.BlockSpec((1, sens, features), lambda b: (b, 0, 0)),
         ],
-        compiler_params=small,
+        out_specs=pl.BlockSpec((1, rows, features), lambda b: (b, 0, 0)),
         cost_estimate=cost(2 * buckets * dates * features**3, 2**23),
+        compiler_params=pltpu.CompilerParams(vmem_limit_bytes=50 * 2**20),
         name="operators",
     )(transition, readout)
 
@@ -321,7 +296,7 @@
                 pltpu.SemaphoreType.DMA((dates,)),
                 pltpu.SemaphoreType.DMA,
             ],
-            compiler_params=small,
+            compiler_params=large,
             cost_estimate=cost(2 * dates * rows * features * half * lanes // 2, 2**23),
             name="local",
         )(scales, octet, shocks, transition, readout)

time: 172 us -> 141 us (0.82)
  local copies, waits for them, and re-layouts: 31.8 us -> 10.9 us
  Pallas kernels: 70.7 us -> 57.5 us
  waiting for transfers between devices: 27 us -> 40 us
  starting transfers between devices: 35.2 us -> 28.6 us
  other arithmetic: 4.76 us -> 2.09 us
    unnamed x98 -> x46, local copies, waits for them, and re-layouts: 31.1 us -> 10.2 us
    ppermute x16 -> x8, waiting for transfers between devices: 18.5 us -> 31.9 us  [advance(): arrived[s].append(lax.ppermute(out, 'date', link))]
    pallas_call x4, Pallas kernels: 35.2 us -> 25.5 us  [local(): pl.pallas_call(functools.partial(local_kernel, dates, b), out_shape=jax.S...]
    ppermute x16 -> x8, starting transfers between devices: 22.5 us -> 16.1 us  [advance(): arrived[s].append(lax.ppermute(out, 'date', link))]
    pallas_call x8 -> x4, Pallas kernels: 12.1 us -> 9.12 us  [final(): pl.pallas_call(functools.partial(final_kernel, b, q, 2 * dates), out_shap...]
    pallas_call x8 -> x4, Pallas kernels: 8.18 us -> 8.72 us  [stage(): pl.pallas_call(functools.partial(stage_kernel, j // pieces), out_shape=ja...]
  transfers between devices with their start and end apart: 28 -> 20, of which waited for: 11 -> 11; matrix products, arithmetic and copies ran while one was open for 4% -> 2% of each run, Pallas kernels for 36% -> 35%
where the time goes in v6:
time: 141 us; the launch traced here: 140 us
  Pallas kernels  57.5 us (41%)
  waiting for transfers between devices  40 us (28%)
  starting transfers between devices  28.6 us (20%)
  local copies, waits for them, and re-layouts  10.9 us (8%)
  other arithmetic  2.09 us (1%)
    ppermute x8, waiting for transfers between devices, advance(): arrived[s].append(lax.ppermute(out, 'date', link))  31.9 us
    pallas_call x4, Pallas kernels, local(): pl.pallas_call(functools.partial(local_kernel, dates, b), out_shape=jax.S...  25.5 us
    ppermute x8, starting transfers between devices, advance(): arrived[s].append(lax.ppermute(out, 'date', link))  16.1 us
    unnamed x46, local copies, waits for them, and re-layouts  10.2 us
    pallas_call x4, Pallas kernels, final(): pl.pallas_call(functools.partial(final_kernel, b, q, 2 * dates), out_shap...  9.12 us
    pallas_call x4, Pallas kernels, stage(): pl.pallas_call(functools.partial(stage_kernel, j // pieces), out_shape=ja...  8.72 us
    pallas_call x1, Pallas kernels, shards(): pl.pallas_call(functools.partial(operator_kernel, dates), out_shape=jax.S...  5.65 us
    ppermute x3, starting transfers between devices, shards(): lax.ppermute(message, 'bucket', [(i, (i + k) % zs) for i in range(zs)])  5.57 us
  transfers between devices with their start and end apart: 20, of which 11 were waited for; matrix products, arithmetic and copies ran while one was open for 2% of the time, Pallas kernels for 35%

profile of v6, /device:TPU:0, one launch (start us, length us, event | category | flops | bytes accessed | tf_op | source)
XLA Modules:
  0.0 140.1 jit_solution(5464598091005895937)
XLA Ops:
  1.5 5.7 %operators.1.mine_ref = bf16[2,768,512]{2,1,0:T(8,128)(2,1)} custom-call(bf16[4,2,512,512]{3,2,1,0:T(8,128)(2,1)} %a_hbm.7, bf16[2,64,512]{2,1,0:T(8,128)(2,1)S(1)} %copy-done.7), custom_call_target="tpu_custom_call" | custom-call | flops 2147483648 | bytes 8388608 | tf_op jit(solution)/shard_map/operators/pallas_call | solution.py:269
  7.7 7.0 %local.4 = bf16[2,768,512]{2,1,0:T(8,128)(2,1)} custom-call(f32[4]{0:T(128)S(1)} %get-tuple-element.36.scale_ref, s32[1]{0:T(128)S(6)} %sub.28.octet_ref, bf16[4,2,512,16,128]{4,3,2,1,0:T(8,128)(2,1)} %x_hbm.7, bf16[4,2,512,512]{3,2,1,0:T(8,128)(2,1)} %a_hbm.7, bf16[2,64,512]{2,1,0:T(8,128)(2,1)S(1)} %copy-done.7), custom_call_target="tpu_custom_call" | custom-call | flops 1610612736 | bytes 8388608 | tf_op jit(solution)/shard_map/local/pallas_call | solution.py:284
  14.8 2.6 %join_operators.1 = (bf16[2,512,512]{2,1,0:T(8,128)(2,1)S(1)}, bf16[2,512,512]{2,1,0:T(8,128)(2,1)S(1)}, bf16[2,768,512]{2,1,0:T(8,128)(2,1)S(1)}) custom-call(s32[1]{0:T(128)} %bitcast.1.core_ref.octet_ref, bf16[2,768,512]{2,1,0:T(8,128)(2,1)} %operators.1.mine_ref, bf16[2,768,512]{2,1,0:T(8,128)(2,1)} %collective-permute-done.other_ref), custom_call_target="tpu_custom_call" | custom-call | flops 805306368 | bytes 4194304 | tf_op jit(solution)/shard_map/join_operators/pallas_call | solution.py:313
  18.4 2.9 %collective-permute-start.3 = (bf16[2,256,512]{2,1,0:T(8,128)(2,1)S(1)}, bf16[2,256,512]{2,1,0:T(8,128)(2,1)}, u32[]{:S(2)}, u32[]{:S(2)}) collective-permute-start(bf16[2,256,512]{2,1,0:T(8,128)(2,1)S(1)} %constant_dynamic-slice_fusion), channel_id=1, source_target_pairs={{0,8},{4,12},{8,0},{12,4},{16,24},{20,28},{24,16},{28,20},{1,9},{5... | collective-permute-start | bytes 1572872 | tf_op jit(solution)/shard_map/ppermute | solution.py:338
  21.4 5.8 %local.5.mine_ref = bf16[2,768,512]{2,1,0:T(8,128)(2,1)S(1)} custom-call(f32[4]{0:T(128)S(1)} %get-tuple-element.36.scale_ref, s32[1]{0:T(128)} %bitcast.1.core_ref.octet_ref, bf16[4,2,512,16,128]{4,3,2,1,0:T(8,128)(2,1)} %x_hbm.7, bf16[4,2,512,512]{3,2,1,0:T(8,128)(2,1)} %a_hbm.7, bf16[2,64,512]{2,1,0:T(8,128)(2,1)S(1)} %copy-done.8), custom_call_target="tpu_custom_call" | custom-call | flops 1610612736 | bytes 8388608 | tf_op jit(solution)/shard_map/local/pallas_call | solution.py:284
  30.3 7.0 %local.6 = bf16[2,768,512]{2,1,0:T(8,128)(2,1)} custom-call(f32[4]{0:T(128)S(1)} %get-tuple-element.36.scale_ref, s32[1]{0:T(128)S(6)} %sub.28.octet_ref, bf16[4,2,512,16,128]{4,3,2,1,0:T(8,128)(2,1)} %x_hbm.7, bf16[4,2,512,512]{3,2,1,0:T(8,128)(2,1)} %a_hbm.7, bf16[2,64,512]{2,1,0:T(8,128)(2,1)S(1)} %copy-done.8), custom_call_target="tpu_custom_call" | custom-call | flops 1610612736 | bytes 8388608 | tf_op jit(solution)/shard_map/local/pallas_call | solution.py:284
  39.7 12.5 %collective-permute-done.2.other_ref.first_ref = bf16[512,512]{1,0:T(8,128)(2,1)S(1)} collective-permute-done((bf16[512,512]{1,0:T(8,128)(2,1)S(1)}, bf16[512,512]{1,0:T(8,128)(2,1)S(1)}, u32[]{:S(2)}, u32[]{:S(2)}) %collective-permute-start.2) | collective-permute-done | bytes 524320 | tf_op jit(solution)/shard_map/ppermute | solution.py:441
  56.0 4.3 %collective-permute-start.5 = (bf16[512,512]{1,0:T(8,128)(2,1)}, bf16[512,512]{1,0:T(8,128)(2,1)}, u32[]{:S(2)}, u32[]{:S(2)}) collective-permute-start(bf16[512,512]{1,0:T(8,128)(2,1)} %stage.4), channel_id=1, source_target_pairs={{0,16},{4,20},{8,24},{12,28},{1,17},{5,21},{9,25},{13,29},{2,18},{... | collective-permute-start | bytes 1572872 | tf_op jit(solution)/shard_map/ppermute | solution.py:441
  60.3 2.6 %collective-permute-done.6.other_ref.first_ref = bf16[512,512]{1,0:T(8,128)(2,1)S(1)} collective-permute-done((bf16[512,512]{1,0:T(8,128)(2,1)}, bf16[512,512]{1,0:T(8,128)(2,1)S(1)}, u32[]{:S(2)}, u32[]{:S(2)}) %collective-permute-start.6) | collective-permute-done | bytes 524320 | tf_op jit(solution)/shard_map/ppermute | solution.py:441
  62.9 2.5 %stage.5 = bf16[512,512]{1,0:T(8,128)(2,1)} custom-call(s32[1]{0:T(128)} %bitcast.4.up_ref, bf16[512,512]{1,0:T(8,128)(2,1)} %get-tuple-element.30.mine_ref, bf16[512,512]{1,0:T(8,128)(2,1)S(1)} %collective-permute-done.6.other_ref.first_ref, bf16[2,512,512]{2,1,0:T(8,128)(2,1)S(1)} %get-tuple-element.49.a_ref), custom_call_target="tpu_custom_call" | custom-call | flops 268435456 | bytes 1048576 | tf_op jit(solution)/shard_map/stage/pallas_call | solution.py:386
  65.4 4.4 %collective-permute-start.7 = (bf16[512,512]{1,0:T(8,128)(2,1)}, bf16[512,512]{1,0:T(8,128)(2,1)}, u32[]{:S(2)}, u32[]{:S(2)}) collective-permute-start(bf16[512,512]{1,0:T(8,128)(2,1)} %stage.5), channel_id=1, source_target_pairs={{0,16},{4,20},{8,24},{12,28},{1,17},{5,21},{9,25},{13,29},{2,18},{... | collective-permute-start | bytes 1572872 | tf_op jit(solution)/shard_map/ppermute | solution.py:441
  69.8 5.8 %local.7.mine_ref = bf16[2,768,512]{2,1,0:T(8,128)(2,1)S(1)} custom-call(f32[4]{0:T(128)S(1)} %get-tuple-element.36.scale_ref, s32[1]{0:T(128)} %bitcast.1.core_ref.octet_ref, bf16[4,2,512,16,128]{4,3,2,1,0:T(8,128)(2,1)} %x_hbm.7, bf16[4,2,512,512]{3,2,1,0:T(8,128)(2,1)} %a_hbm.7, bf16[2,64,512]{2,1,0:T(8,128)(2,1)S(1)} %copy-done.8), custom_call_target="tpu_custom_call" | custom-call | flops 1610612736 | bytes 8388608 | tf_op jit(solution)/shard_map/local/pallas_call | solution.py:284
  75.7 3.2 %join_states.3 = (f32[2,512,512]{2,1,0:T(8,128)S(1)}, bf16[512,512]{1,0:T(8,128)(2,1)}, bf16[512,512]{1,0:T(8,128)(2,1)}) custom-call(s32[1]{0:T(128)} %bitcast.1.core_ref.octet_ref, bf16[2,768,512]{2,1,0:T(8,128)(2,1)S(1)} %local.7.mine_ref, bf16[2,768,512]{2,1,0:T(8,128)(2,1)} %collective-permute-done.8.other_ref, bf16[2,768,512]{2,1,0:T(8,128)(2,1)S(1)} %copy-done.5), custom_call_target="tpu_custom_call" | custom-call | flops 805306368 | bytes 4194304 | tf_op jit(solution)/shard_map/join_states/pallas_call | solution.py:369
  85.2 2.3 %final.4.refs_0_ = f32[2,8,512]{2,1,0:T(8,128)S(1)} custom-call(s32[1]{0:T(128)} %bitcast.4.up_ref, bf16[512,512]{1,0:T(8,128)(2,1)S(1)} %copy-done.11, bf16[512,512]{1,0:T(8,128)(2,1)} %collective-permute-done.5.last_ref, bf16[2,512,512]{2,1,0:T(8,128)(2,1)S(1)} %get-tuple-element.48.phi_ref, bf16[2,512,512]{2,1,0:T(8,128)(2,1)S(1)} %get-tuple-element.34.q_ref, ...), custom_call_target="tpu_custom_call" | custom-call | flops 536870912 | bytes 2097152 | tf_op jit(solution)/shard_map/final/pallas_call | solution.py:398
  87.5 2.2 %final.5.refs_1_ = f32[2,8,512]{2,1,0:T(8,128)S(1)} custom-call(s32[1]{0:T(128)} %bitcast.4.up_ref, bf16[512,512]{1,0:T(8,128)(2,1)S(1)} %copy-done.13, bf16[512,512]{1,0:T(8,128)(2,1)} %collective-permute-done.7.last_ref, bf16[2,512,512]{2,1,0:T(8,128)(2,1)S(1)} %get-tuple-element.48.phi_ref, bf16[2,512,512]{2,1,0:T(8,128)(2,1)S(1)} %get-tuple-element.34.q_ref, ...), custom_call_target="tpu_custom_call" | custom-call | flops 536870912 | bytes 2097152 | tf_op jit(solution)/shard_map/final/pallas_call | solution.py:398
  89.8 5.5 %collective-permute-done.9.other_ref.first_ref = bf16[512,512]{1,0:T(8,128)(2,1)} collective-permute-done((bf16[512,512]{1,0:T(8,128)(2,1)}, bf16[512,512]{1,0:T(8,128)(2,1)}, u32[]{:S(2)}, u32[]{:S(2)}) %collective-permute-start.9) | collective-permute-done | bytes 524320 | tf_op jit(solution)/shard_map/ppermute | solution.py:441
  95.3 2.5 %stage.6 = bf16[512,512]{1,0:T(8,128)(2,1)} custom-call(s32[1]{0:T(128)} %bitcast.4.up_ref, bf16[512,512]{1,0:T(8,128)(2,1)} %get-tuple-element.38.mine_ref, bf16[512,512]{1,0:T(8,128)(2,1)} %collective-permute-done.9.other_ref.first_ref, bf16[2,512,512]{2,1,0:T(8,128)(2,1)S(1)} %get-tuple-element.49.a_ref), custom_call_target="tpu_custom_call" | custom-call | flops 268435456 | bytes 1048576 | tf_op jit(solution)/shard_map/stage/pallas_call | solution.py:386
  99.9 5.1 %collective-permute-done.11.other_ref.first_ref = bf16[512,512]{1,0:T(8,128)(2,1)} collective-permute-done((bf16[512,512]{1,0:T(8,128)(2,1)}, bf16[512,512]{1,0:T(8,128)(2,1)}, u32[]{:S(2)}, u32[]{:S(2)}) %collective-permute-start.11) | collective-permute-done | bytes 524320 | tf_op jit(solution)/shard_map/ppermute | solution.py:441
  105.0 2.5 %stage.7 = bf16[512,512]{1,0:T(8,128)(2,1)} custom-call(s32[1]{0:T(128)} %bitcast.4.up_ref, bf16[512,512]{1,0:T(8,128)(2,1)} %get-tuple-element.43.mine_ref, bf16[512,512]{1,0:T(8,128)(2,1)} %collective-permute-done.11.other_ref.first_ref, bf16[2,512,512]{2,1,0:T(8,128)(2,1)S(1)} %get-tuple-element.49.a_ref), custom_call_target="tpu_custom_call" | custom-call | flops 268435456 | bytes 1048576 | tf_op jit(solution)/shard_map/stage/pallas_call | solution.py:386
  110.7 2.4 %final.6.refs_2_ = f32[2,8,512]{2,1,0:T(8,128)S(1)} custom-call(s32[1]{0:T(128)} %bitcast.4.up_ref, bf16[512,512]{1,0:T(8,128)(2,1)} %collective-permute-done.9.other_ref.first_ref, bf16[512,512]{1,0:T(8,128)(2,1)} %collective-permute-done.10.last_ref, bf16[2,512,512]{2,1,0:T(8,128)(2,1)S(1)} %get-tuple-element.48.phi_ref, ...), custom_call_target="tpu_custom_call" | custom-call | flops 536870912 | bytes 2097152 | tf_op jit(solution)/shard_map/final/pallas_call | solution.py:398
  113.1 6.1 %collective-permute-done.12.last_ref = bf16[512,512]{1,0:T(8,128)(2,1)S(1)} collective-permute-done((bf16[512,512]{1,0:T(8,128)(2,1)}, bf16[512,512]{1,0:T(8,128)(2,1)S(1)}, u32[]{:S(2)}, u32[]{:S(2)}) %collective-permute-start.12) | collective-permute-done | bytes 524320 | tf_op jit(solution)/shard_map/ppermute | solution.py:441
  123.1 2.6 %collective-permute-start.15 = (bf16[256,128]{1,0:T(8,128)(2,1)S(1)}, bf16[256,128]{1,0:T(8,128)(2,1)S(1)}, u32[]{:S(2)}, u32[]{:S(2)}) collective-permute-start(bf16[256,128]{1,0:T(8,128)(2,1)S(1)} %pack.1.refs_0_), channel_id=1, source_target_pairs={{0,2},{1,3},{2,0},{3,1},{4,6},{5,7},{6,4},{7,5},{8,10},{9,11},{10,... | collective-permute-start | bytes 196616 | tf_op jit(solution)/shard_map/ppermute | solution.py:495
  132.5 3.1 %collective-permute-done.18 = f32[8,128]{1,0:T(8,128)S(1)} collective-permute-done((f32[8,128]{1,0:T(8,128)S(1)}, f32[8,128]{1,0:T(8,128)S(1)}, u32[]{:S(2)}, u32[]{:S(2)}) %collective-permute-start.18) | collective-permute-done | bytes 4128 | tf_op jit(solution)/shard_map/ppermute | solution.py:523
  135.6 2.4 %collective-permute-start.19 = (f32[8,128]{1,0:T(8,128)S(1)}, f32[8,128]{1,0:T(8,128)S(1)}, u32[]{:S(2)}, u32[]{:S(2)}) collective-permute-start(f32[8,128]{1,0:T(8,128)S(1)} %add.28), channel_id=1, source_target_pairs={{0,16},{4,20},{8,24},{12,28},{16,0},{20,4},{24,8},{28,12},{1,17},{... | collective-permute-start | bytes 12296 | tf_op jit(solution)/shard_map/ppermute | solution.py:523
  (101 shorter events, 36.2 us)
Async XLA Ops:
  7.2 7.6 %collective-permute-start = (bf16[2,768,512]{2,1,0:T(8,128)(2,1)}, bf16[2,768,512]{2,1,0:T(8,128)(2,1)}, u32[]{:S(2)}, u32[]{:S(2)}) collective-permute-start(bf16[2,768,512]{2,1,0:T(8,128)(2,1)} %operators.1.mine_ref), channel_id=1, source_target_pairs={{0,4},{4,0},{8,12},{12,8},{16,20},{20,16},{24,28},{28,24},{1,5},{5... | collective-permute-start | bytes 4718600 | tf_op jit(solution)/shard_map/ppermute | solution.py:305
  14.7 12.5 %collective-permute-start.1 = (bf16[2,768,512]{2,1,0:T(8,128)(2,1)}, bf16[2,768,512]{2,1,0:T(8,128)(2,1)S(1)}, u32[]{:S(2)}, u32[]{:S(2)}) collective-permute-start(bf16[2,768,512]{2,1,0:T(8,128)(2,1)} %local.4), channel_id=1, source_target_pairs={{0,4},{4,0},{8,12},{12,8},{16,20},{20,16},{24,28},{28,24},{1,5},{5... | collective-permute-start | bytes 4718600 | tf_op jit(solution)/shard_map/ppermute | solution.py:310
  17.4 9.8 %copy-start.4 = (bf16[2,768,512]{2,1,0:T(8,128)(2,1)}, bf16[2,768,512]{2,1,0:T(8,128)(2,1)S(1)}, u32[]{:S(2)}) copy-start(bf16[2,768,512]{2,1,0:T(8,128)(2,1)S(1)} %get-tuple-element.28.late_ref) | copy-start | bytes 4718596
  18.4 19.0 %collective-permute-start.3 = (bf16[2,256,512]{2,1,0:T(8,128)(2,1)S(1)}, bf16[2,256,512]{2,1,0:T(8,128)(2,1)}, u32[]{:S(2)}, u32[]{:S(2)}) collective-permute-start(bf16[2,256,512]{2,1,0:T(8,128)(2,1)S(1)} %constant_dynamic-slice_fusion), channel_id=1, source_target_pairs={{0,8},{4,12},{8,0},{12,4},{16,24},{20,28},{24,16},{28,20},{1,9},{5... | collective-permute-start | bytes 1572872 | tf_op jit(solution)/shard_map/ppermute | solution.py:338
  30.3 7.0 %copy-start.15 = (bf16[512,512]{1,0:T(8,128)(2,1)}, bf16[512,512]{1,0:T(8,128)(2,1)S(1)}, u32[]{:S(2)}) copy-start(bf16[512,512]{1,0:T(8,128)(2,1)S(1)} %get-tuple-element.29.mine_ref) | copy-start | bytes 1572868
  37.3 38.4 %collective-permute-start.8 = (bf16[2,768,512]{2,1,0:T(8,128)(2,1)}, bf16[2,768,512]{2,1,0:T(8,128)(2,1)}, u32[]{:S(2)}, u32[]{:S(2)}) collective-permute-start(bf16[2,768,512]{2,1,0:T(8,128)(2,1)} %local.6), channel_id=1, source_target_pairs={{0,4},{4,0},{8,12},{12,8},{16,20},{20,16},{24,28},{28,24},{1,5},{5... | collective-permute-start | bytes 4718600 | tf_op jit(solution)/shard_map/ppermute | solution.py:455
  37.4 14.9 %collective-permute-start.2 = (bf16[512,512]{1,0:T(8,128)(2,1)S(1)}, bf16[512,512]{1,0:T(8,128)(2,1)S(1)}, u32[]{:S(2)}, u32[]{:S(2)}) collective-permute-start(bf16[512,512]{1,0:T(8,128)(2,1)S(1)} %get-tuple-element.29.mine_ref), channel_id=1, source_target_pairs={{0,8},{4,12},{8,0},{12,4},{16,24},{20,28},{24,16},{28,20},{1,9},{5... | collective-permute-start | bytes 1572872 | tf_op jit(solution)/shard_map/ppermute | solution.py:441
  37.4 14.8 %collective-permute-start.4 = (bf16[2,256,512]{2,1,0:T(8,128)(2,1)}, bf16[2,256,512]{2,1,0:T(8,128)(2,1)S(1)}, u32[]{:S(2)}, u32[]{:S(2)}) collective-permute-start(bf16[2,256,512]{2,1,0:T(8,128)(2,1)} %collective-permute-done.3), channel_id=1, source_target_pairs={{0,4},{4,0},{8,12},{12,8},{16,20},{20,16},{24,28},{28,24},{1,5},{5... | collective-permute-start | bytes 1572872 | tf_op jit(solution)/shard_map/ppermute | solution.py:342
  38.0 24.9 %collective-permute-start.6 = (bf16[512,512]{1,0:T(8,128)(2,1)}, bf16[512,512]{1,0:T(8,128)(2,1)S(1)}, u32[]{:S(2)}, u32[]{:S(2)}) collective-permute-start(bf16[512,512]{1,0:T(8,128)(2,1)} %get-tuple-element.30.mine_ref), channel_id=1, source_target_pairs={{0,8},{4,12},{8,0},{12,4},{16,24},{20,28},{24,16},{28,20},{1,9},{5... | collective-permute-start | bytes 1572872 | tf_op jit(solution)/shard_map/ppermute | solution.py:441
  56.0 26.6 %collective-permute-start.5 = (bf16[512,512]{1,0:T(8,128)(2,1)}, bf16[512,512]{1,0:T(8,128)(2,1)}, u32[]{:S(2)}, u32[]{:S(2)}) collective-permute-start(bf16[512,512]{1,0:T(8,128)(2,1)} %stage.4), channel_id=1, source_target_pairs={{0,16},{4,20},{8,24},{12,28},{1,17},{5,21},{9,25},{13,29},{2,18},{... | collective-permute-start | bytes 1572872 | tf_op jit(solution)/shard_map/ppermute | solution.py:441
  65.4 10.2 %copy-start.5 = (bf16[2,768,512]{2,1,0:T(8,128)(2,1)S(1)}, bf16[2,768,512]{2,1,0:T(8,128)(2,1)}, u32[]{:S(2)}) copy-start(bf16[2,768,512]{2,1,0:T(8,128)(2,1)} %copy-done.4) | copy-start | bytes 4718596
  65.4 22.1 %collective-permute-start.7 = (bf16[512,512]{1,0:T(8,128)(2,1)}, bf16[512,512]{1,0:T(8,128)(2,1)}, u32[]{:S(2)}, u32[]{:S(2)}) collective-permute-start(bf16[512,512]{1,0:T(8,128)(2,1)} %stage.5), channel_id=1, source_target_pairs={{0,16},{4,20},{8,24},{12,28},{1,17},{5,21},{9,25},{13,29},{2,18},{... | collective-permute-start | bytes 1572872 | tf_op jit(solution)/shard_map/ppermute | solution.py:441
  80.2 15.1 %collective-permute-start.9 = (bf16[512,512]{1,0:T(8,128)(2,1)}, bf16[512,512]{1,0:T(8,128)(2,1)}, u32[]{:S(2)}, u32[]{:S(2)}) collective-permute-start(bf16[512,512]{1,0:T(8,128)(2,1)} %get-tuple-element.38.mine_ref), channel_id=1, source_target_pairs={{0,8},{4,12},{8,0},{12,4},{16,24},{20,28},{24,16},{28,20},{1,9},{5... | collective-permute-start | bytes 1572872 | tf_op jit(solution)/shard_map/ppermute | solution.py:441
  80.7 24.2 %collective-permute-start.11 = (bf16[512,512]{1,0:T(8,128)(2,1)}, bf16[512,512]{1,0:T(8,128)(2,1)}, u32[]{:S(2)}, u32[]{:S(2)}) collective-permute-start(bf16[512,512]{1,0:T(8,128)(2,1)} %get-tuple-element.43.mine_ref), channel_id=1, source_target_pairs={{0,8},{4,12},{8,0},{12,4},{16,24},{20,28},{24,16},{28,20},{1,9},{5... | collective-permute-start | bytes 1572872 | tf_op jit(solution)/shard_map/ppermute | solution.py:441
  82.3 26.7 %collective-permute-start.13 = (f32[4,4,128]{2,1,0:T(4,128)S(1)}, f32[4,4,128]{2,1,0:T(4,128)S(1)}, u32[]{:S(2)}, u32[]{:S(2)}) collective-permute-start(f32[4,4,128]{2,1,0:T(4,128)S(1)} %broadcast_multiply_fusion), channel_id=1, source_target_pairs={{0,4},{4,0},{8,12},{12,8},{16,20},{20,16},{24,28},{28,24},{1,5},{5... | collective-permute-start | bytes 24584 | tf_op jit(solution)/shard_map/ppermute | solution.py:307
  97.8 11.3 %collective-permute-start.10 = (bf16[512,512]{1,0:T(8,128)(2,1)}, bf16[512,512]{1,0:T(8,128)(2,1)}, u32[]{:S(2)}, u32[]{:S(2)}) collective-permute-start(bf16[512,512]{1,0:T(8,128)(2,1)} %stage.6), channel_id=1, source_target_pairs={{0,16},{4,20},{8,24},{12,28},{1,17},{5,21},{9,25},{13,29},{2,18},{... | collective-permute-start | bytes 1572872 | tf_op jit(solution)/shard_map/ppermute | solution.py:441
  107.4 11.7 %collective-permute-start.12 = (bf16[512,512]{1,0:T(8,128)(2,1)}, bf16[512,512]{1,0:T(8,128)(2,1)S(1)}, u32[]{:S(2)}, u32[]{:S(2)}) collective-permute-start(bf16[512,512]{1,0:T(8,128)(2,1)} %stage.7), channel_id=1, source_target_pairs={{0,16},{4,20},{8,24},{12,28},{1,17},{5,21},{9,25},{13,29},{2,18},{... | collective-permute-start | bytes 1572872 | tf_op jit(solution)/shard_map/ppermute | solution.py:441
  113.1 16.9 %copy-start.17 = (s32[16]{0:T(128)S(1)}, s32[16]{0:T(128)}, u32[]{:S(2)}) copy-start(s32[16]{0:T(128)} %count_ref.1) | copy-start | bytes 196
  121.4 6.1 %collective-permute-start.14 = (bf16[256,128]{1,0:T(8,128)(2,1)S(1)}, bf16[256,128]{1,0:T(8,128)(2,1)S(1)}, u32[]{:S(2)}, u32[]{:S(2)}) collective-permute-start(bf16[256,128]{1,0:T(8,128)(2,1)S(1)} %pack.1.refs_0_), channel_id=1, source_target_pairs={{0,1},{1,2},{2,3},{3,0},{4,5},{5,6},{6,7},{7,4},{8,9},{9,10},{10,1... | collective-permute-start | bytes 196616 | tf_op jit(solution)/shard_map/ppermute | solution.py:495
  123.1 5.2 %collective-permute-start.15 = (bf16[256,128]{1,0:T(8,128)(2,1)S(1)}, bf16[256,128]{1,0:T(8,128)(2,1)S(1)}, u32[]{:S(2)}, u32[]{:S(2)}) collective-permute-start(bf16[256,128]{1,0:T(8,128)(2,1)S(1)} %pack.1.refs_0_), channel_id=1, source_target_pairs={{0,2},{1,3},{2,0},{3,1},{4,6},{5,7},{6,4},{7,5},{8,10},{9,11},{10,... | collective-permute-start | bytes 196616 | tf_op jit(solution)/shard_map/ppermute | solution.py:495
  125.7 4.3 %collective-permute-start.16 = (bf16[256,128]{1,0:T(8,128)(2,1)S(1)}, bf16[256,128]{1,0:T(8,128)(2,1)S(1)}, u32[]{:S(2)}, u32[]{:S(2)}) collective-permute-start(bf16[256,128]{1,0:T(8,128)(2,1)S(1)} %pack.1.refs_0_), channel_id=1, source_target_pairs={{0,3},{1,0},{2,1},{3,2},{4,7},{5,4},{6,5},{7,6},{8,11},{9,8},{10,9... | collective-permute-start | bytes 196616 | tf_op jit(solution)/shard_map/ppermute | solution.py:495
  130.8 1.2 collective-permute-start.17
  132.0 3.6 %collective-permute-start.18 = (f32[8,128]{1,0:T(8,128)S(1)}, f32[8,128]{1,0:T(8,128)S(1)}, u32[]{:S(2)}, u32[]{:S(2)}) collective-permute-start(f32[8,128]{1,0:T(8,128)S(1)} %fusion.5), channel_id=1, source_target_pairs={{0,8},{4,12},{8,0},{12,4},{16,24},{20,28},{24,16},{28,20},{1,9},{5... | collective-permute-start | bytes 12296 | tf_op jit(solution)/shard_map/ppermute | solution.py:523
  135.6 4.0 %collective-permute-start.19 = (f32[8,128]{1,0:T(8,128)S(1)}, f32[8,128]{1,0:T(8,128)S(1)}, u32[]{:S(2)}, u32[]{:S(2)}) collective-permute-start(f32[8,128]{1,0:T(8,128)S(1)} %add.28), channel_id=1, source_target_pairs={{0,16},{4,20},{8,24},{12,28},{16,0},{20,4},{24,8},{28,12},{1,17},{... | collective-permute-start | bytes 12296 | tf_op jit(solution)/shard_map/ppermute | solution.py:523
  (18 other events, 57.1 us)

commit v7 on v6

--- a/solution.py
+++ b/solution.py
@@ -11,10 +11,17 @@
 epsilon = 1e-06
 f32 = jnp.float32
 bf16 = jnp.bfloat16
-pair = 4
-flight = 2
+pair = 2
+flight = 8
 lag = 1
 early = 1
+
+
+def chunks(units, bucket, buckets):
+    sizes = [2] * (units // 2) + [1] * (units % 2)
+    if bucket == buckets - 1 and units % 2 == 0:
+        sizes[-1:] = [1, 1]
+    return sizes
 
 
 def dot(a, b):
@@ -109,7 +116,7 @@
         out_ref[q, :features, :] = state_ref[:, q * width : (q + 1) * width]
 
 
-def join_operator_kernel(core_ref, mine_ref, other_ref, p_ref, q_ref, late_ref):
+def join_operator_kernel(core_ref, mine_ref, other_ref, p_ref, q_ref, late_ref, part_ref):
     features = mine_ref.shape[2]
     first = core_ref[0] == 0
     mine, other = mine_ref[0], other_ref[0]
@@ -117,25 +124,91 @@
     late = jnp.where(first, other, mine)
     joined = dot(late, early[:features]).astype(bf16)
     p_ref[0] = joined[:features]
+    part_ref[0] = jnp.where(first, joined[: features // 2], joined[features // 2 : features])
     seen = late.shape[0] - features
     q_ref[0, :seen, :] = early[features:]
     q_ref[0, seen:, :] = joined[features:]
     late_ref[0] = late
 
 
-def join_state_kernel(b, core_ref, mine_ref, other_ref, late_ref, seen_ref, *end_refs):
-    features = late_ref.shape[2]
+def join_state_kernel(
+    b,
+    sizes,
+    core_ref,
+    mine_hbm,
+    other_hbm,
+    late_hbm,
+    seen_ref,
+    *refs,
+):
+    end_refs = refs[:-6]
+    mine_ref, other_ref, late_ref, mine_sem, other_sem, late_sem = refs[-6:]
+    features = late_ref.shape[1]
+    width = mine_ref.shape[2]
     first = core_ref[0] == 0
-    late_operator = late_ref[b]
-    for q, end_ref in enumerate(end_refs):
-        mine, other = mine_ref[q], other_ref[q]
-        early = jnp.where(first, mine, other)
-        late = jnp.where(first, other, mine)
-        joined = dot(late_operator, early[:features]) + late.astype(f32)
-        seen = late.shape[0] - features
-        seen_ref[q, :seen, :] = early[features:].astype(f32)
-        seen_ref[q, seen:, :] = joined[features:]
-        end_ref[...] = joined[:features].astype(bf16)
+    fetch = pltpu.make_async_copy(late_hbm.at[b], late_ref, late_sem)
+    fetch.start()
+    pieces = [
+        (
+            pltpu.make_async_copy(mine_hbm.at[q], mine_ref.at[q], mine_sem.at[q]),
+            pltpu.make_async_copy(other_hbm.at[q], other_ref.at[q], other_sem.at[q]),
+        )
+        for q in range(sum(sizes))
+    ]
+    for one, two in pieces:
+        one.start()
+        two.start()
+    fetch.wait()
+    late_operator = late_ref[...]
+    q = 0
+    for end_ref, size in zip(end_refs, sizes):
+        for i in range(size):
+            for piece in pieces[q]:
+                piece.wait()
+            mine, other = mine_ref[q], other_ref[q]
+            early = jnp.where(first, mine, other)
+            late = jnp.where(first, other, mine)
+            joined = dot(late_operator, early[:features]) + late.astype(f32)
+            seen = late.shape[0] - features
+            seen_ref[q, :seen, :] = early[features:]
+            seen_ref[q, seen:, :] = joined[features:].astype(bf16)
+            end_ref[:, i * width : (i + 1) * width] = joined[:features].astype(bf16)
+            q += 1
+
+
+def far_copies(b, core, part_hbm, part_other_hbm, a_ref, sem):
+    half = part_hbm.shape[1]
+    near = pl.ds(pl.multiple_of(core * half, half), half)
+    away = pl.ds(pl.multiple_of((1 - core) * half, half), half)
+    return (
+        pltpu.make_async_copy(part_hbm.at[b], a_ref.at[near], sem.at[0]),
+        pltpu.make_async_copy(part_other_hbm.at[b], a_ref.at[away], sem.at[1]),
+    )
+
+
+def first_stage_kernel(
+    b, flag_ref, mine_ref, other_ref, block_hbm, part_hbm, part_other_hbm, out_ref, a_ref, sem
+):
+    up = flag_ref[1] == 1
+
+    @pl.when(up)
+    def _():
+        copy = pltpu.make_async_copy(block_hbm.at[b], a_ref, sem.at[0])
+        copy.start()
+        copy.wait()
+
+    @pl.when(flag_ref[1] == 0)
+    def _():
+        copies = far_copies(b, flag_ref[0], part_hbm, part_other_hbm, a_ref, sem)
+        for copy in copies:
+            copy.start()
+        for copy in copies:
+            copy.wait()
+
+    mine, other = mine_ref[...], other_ref[...]
+    early = jnp.where(up, other, mine)
+    late = jnp.where(up, mine, other)
+    out_ref[...] = (dot(a_ref[...], early) + late.astype(f32)).astype(bf16)
 
 
 def stage_kernel(b, up_ref, mine_ref, other_ref, a_ref, out_ref):
@@ -146,15 +219,32 @@
     out_ref[...] = (dot(a_ref[b], early) + late.astype(f32)).astype(bf16)
 
 
-def final_kernel(
-    b, q, dates, up_ref, first_ref, last_ref, phi_ref, q_ref, seen_ref, rw_ref, c_ref, out_ref
-):
+def final_kernel(b, q, dates, halves, flag_ref, first_ref, last_ref, *refs):
+    prefix, (q_hbm, seen_hbm, rw_ref, c_ref, out_ref) = refs[:-9], refs[-9:-4]
+    a_ref, q_ref, seen_ref, sem = refs[-4:]
     sens = rw_ref.shape[1]
     width = first_ref.shape[1]
-    first = first_ref[...].astype(f32)
-    first = jnp.where(up_ref[0] == 1, first, jnp.zeros_like(first))
-    entering = (first + dot(phi_ref[b], last_ref[...])).astype(bf16)
-    seen = seen_ref[q] + dot(q_ref[b], entering)
+    units = seen_ref.shape[0]
+    fetch_q = pltpu.make_async_copy(q_hbm.at[b], q_ref, sem.at[2])
+    fetch_seen = pltpu.make_async_copy(seen_hbm.at[pl.ds(q, units)], seen_ref, sem.at[3])
+    if halves:
+        copies = far_copies(b, flag_ref[0], *prefix, a_ref, sem)
+    else:
+        copies = (pltpu.make_async_copy(prefix[0].at[b], a_ref, sem.at[0]),)
+    for copy in copies:
+        copy.start()
+    fetch_q.start()
+    fetch_seen.start()
+    for copy in copies:
+        copy.wait()
+    up = flag_ref[1] == 1
+    last = last_ref[...]
+    moved = first_ref[...].astype(f32) + dot(a_ref[...], last)
+    entering = jnp.where(up, moved.astype(bf16), last)
+    fetch_q.wait()
+    seen = dot(q_ref[...], entering)
+    fetch_seen.wait()
+    seen = seen + jnp.concatenate([seen_ref[i] for i in range(units)], axis=1).astype(f32)
     weight = rw_ref[b]
     ws = jnp.concatenate(
         [weight * seen[t * sens : (t + 1) * sens] for t in range(dates)], axis=1
@@ -173,21 +263,22 @@
         out_ref[1, t : t + 1, :] = net[:, t * width : (t + 1) * width]
 
 
-def pack_kernel(buckets, pieces, *refs):
+def pack_kernel(places, buckets, half, *refs):
     stats, discount_ref, out_ref = refs[:-2], refs[-2], refs[-1]
     dates = stats[0].shape[1]
     lanes = out_ref.shape[1]
-    block = pair * dates
-    for q in range(pieces):
-        own = [stats[b * pieces + q] for b in range(buckets)]
-        within = sum(ref[0] for ref in own)
-        for r, value in enumerate([within] + [ref[1] for ref in own]):
-            rows = jnp.concatenate(
-                [value[:, i * lanes : (i + 1) * lanes] for i in range(pair)], axis=0
-            )
-            row = (r * pieces + q) * block
-            out_ref[row : row + block, :] = rows.astype(bf16)
-    out_ref[(buckets + 1) * pieces * block :, :] = discount_ref[...]
+
+    def value(kind, b, m):
+        j, lane = places[b, m]
+        return stats[j][kind, :, lane * lanes : (lane + 1) * lanes]
+
+    for m in range(0, half, 2):
+        block = [[value(1, b, m + i) for i in range(2)] for b in range(buckets)]
+        block.insert(0, [sum(value(0, b, m + i) for b in range(buckets)) for i in range(2)])
+        for r, parts in enumerate(block):
+            row = (r * half + m) * dates
+            out_ref[row : row + 2 * dates, :] = jnp.concatenate(parts, axis=0).astype(bf16)
+    out_ref[(buckets + 1) * half * dates :, :] = discount_ref[...]
 
 
 def margin_kernel(
@@ -264,7 +355,8 @@
 
     vmem = pl.BlockSpec(memory_space=pltpu.VMEM)
     hbm = pl.BlockSpec(memory_space=pltpu.HBM)
-    small = pltpu.CompilerParams(vmem_limit_bytes=16 * 2**20)
+    anywhere = pl.BlockSpec(memory_space=pl.ANY)
+    small = pltpu.CompilerParams(vmem_limit_bytes=50 * 2**20)
     large = pltpu.CompilerParams(vmem_limit_bytes=50 * 2**20)
     operators = pl.pallas_call(
         functools.partial(operator_kernel, dates),
@@ -303,28 +395,33 @@
 
     scales = after(scales, operators)
     operators_other = lax.ppermute(operators, "date", swap)
-    discount = (step_days.astype(f32) / 365.0)[:, None, None] * discount
-    discount_other = lax.ppermute(discount, "date", swap)
     sent = local(0, 1 - core_flag, scales)
     operators_other = after(operators_other, sent)
     late_half = lax.ppermute(sent, "date", swap)
 
     block3 = lambda r: pl.BlockSpec((1, r, features), lambda b: (b, 0, 0))
-    block, seer, late = pl.pallas_call(
+    block, seer, late, part = pl.pallas_call(
         join_operator_kernel,
         out_shape=(
             jax.ShapeDtypeStruct((buckets, features, features), bf16),
             jax.ShapeDtypeStruct((buckets, 2 * seen_rows, features), bf16),
             jax.ShapeDtypeStruct((buckets, rows, features), bf16),
+            jax.ShapeDtypeStruct((buckets, features // 2, features), bf16),
         ),
         grid=(buckets,),
         in_specs=[smem, block3(rows), block3(rows)],
-        out_specs=(block3(features), block3(2 * seen_rows), block3(rows)),
+        out_specs=(
+            block3(features),
+            block3(2 * seen_rows),
+            block3(rows),
+            block3(features // 2),
+        ),
         cost_estimate=cost(2 * buckets * rows * features**2, 2**22),
-        compiler_params=pltpu.CompilerParams(vmem_limit_bytes=16 * 2**20),
+        compiler_params=pltpu.CompilerParams(vmem_limit_bytes=60 * 2**20),
         name="join_operators",
     )(core_flag, operators, operators_other)
 
+    joined_block = block
     combiners = []
     eye = jnp.broadcast_to(jnp.eye(features, dtype=bf16), (buckets, features, features))
     prefix = eye
@@ -332,7 +429,8 @@
     for s in range(stages - 1):
         far = [(i, i ^ (2 << s)) for i in range(segments)]
         rows_half = features // 2
-        part = lax.dynamic_slice_in_dim(block, core * rows_half, rows_half, 1)
+        if s > 0:
+            part = lax.dynamic_slice_in_dim(block, core * rows_half, rows_half, 1)
         if s == 0:
             scales = after(scales, part)
         part = lax.ppermute(part, "date", far)
@@ -340,6 +438,11 @@
             own = local(0, core_flag, scales)
             part = after(part, own)
         part_other = lax.ppermute(part, "date", swap)
+        if s == 0:
+            flags = jnp.concatenate([core_flag, ups[0]])
+            straight, crossed = part, part_other
+            if stages == 2:
+                continue
         first = core == 0
         other = jnp.concatenate(
             [jnp.where(first, part, part_other), jnp.where(first, part_other, part)], axis=1
@@ -348,10 +451,11 @@
         combiners.append(jnp.where(up, block, other))
         if s == 0:
             prefix = jnp.where(up, other, eye)
+            prefixes.append(prefix)
         else:
             moved = jnp.einsum("bij,bjk->bik", prefix, other, preferred_element_type=f32)
             prefix = jnp.where(up, moved.astype(bf16), prefix)
-        prefixes.append(prefix)
+            prefixes.append(prefix)
         if s < stages - 2:
             above = jnp.where(up, block, other)
             below = jnp.where(up, other, block)
@@ -364,28 +468,61 @@
 
     ends = []
     seens = []
+    table = []
+    places = {}
+    for b in range(buckets):
+        unit = 0
+        for size in chunks(pieces, b, buckets):
+            for i in range(size * pair):
+                places[b, unit * pair + i] = (len(table), i)
+            table.append((b, unit, size))
+            unit += size
+    count = len(table)
 
     def join_states(b, own, late_half):
-        result = pl.pallas_call(
-            functools.partial(join_state_kernel, b),
-            out_shape=(jax.ShapeDtypeStruct((pieces, 2 * seen_rows, width), f32),)
-            + (jax.ShapeDtypeStruct((features, width), bf16),) * pieces,
-            in_specs=[smem, vmem, vmem, vmem],
-            out_specs=(vmem,) * (pieces + 1),
+        sizes = [size for at, _, size in table if at == b]
+        call = pl.pallas_call(
+            functools.partial(join_state_kernel, b, sizes),
+            out_shape=(jax.ShapeDtypeStruct((pieces, 2 * seen_rows, width), bf16),)
+            + tuple(jax.ShapeDtypeStruct((features, size * width), bf16) for size in sizes),
+            in_specs=[smem, anywhere, anywhere, anywhere],
+            out_specs=(vmem,) * (len(sizes) + 1),
+            scratch_shapes=[
+                pltpu.VMEM((pieces, rows, width), bf16),
+                pltpu.VMEM((pieces, rows, width), bf16),
+                pltpu.VMEM((rows, features), bf16),
+                pltpu.SemaphoreType.DMA((pieces,)),
+                pltpu.SemaphoreType.DMA((pieces,)),
+                pltpu.SemaphoreType.DMA,
+            ],
             compiler_params=small,
             cost_estimate=cost(2 * rows * features * half * lanes, 2**22),
             name="join_states",
-        )(core_flag, own, late_half, late)
+        )
+        result = call(core_flag, own, late_half, late)
         seens.append(result[0])
         ends.extend(result[1:])
 
     weight_column = risk_weight[:, :, None]
-    count = buckets * pieces
+
+    square = pltpu.VMEM((features, features), bf16)
+
+    def first_stage(j, mine, other):
+        return pl.pallas_call(
+            functools.partial(first_stage_kernel, table[j][0]),
+            out_shape=jax.ShapeDtypeStruct(mine.shape, bf16),
+            in_specs=[smem, vmem, vmem] + [anywhere] * 3,
+            out_specs=vmem,
+            scratch_shapes=[square, pltpu.SemaphoreType.DMA((2,))],
+            compiler_params=small,
+            cost_estimate=cost(2 * features**2 * width, 2**20),
+            name="stage",
+        )(flags, mine, other, joined_block, straight, crossed)
 
     def stage(j, up, mine, other, combiner):
         return pl.pallas_call(
-            functools.partial(stage_kernel, j // pieces),
-            out_shape=jax.ShapeDtypeStruct((features, width), bf16),
+            functools.partial(stage_kernel, table[j][0]),
+            out_shape=jax.ShapeDtypeStruct(mine.shape, bf16),
             in_specs=[smem, vmem, vmem, vmem],
             out_specs=vmem,
             compiler_params=small,
@@ -393,17 +530,28 @@
             name="stage",
         )(up, mine, other, combiner)
 
-    def final(j, up, first, last, operator):
-        b, q = divmod(j, pieces)
+    def final(j, up, first, last):
+        b, q, size = table[j]
+        halves = stages == 2
+        prefix = (straight, crossed) if halves else (prefixes[-1],)
+        flag = flags if halves else jnp.concatenate([core_flag, jnp.ones((1,), jnp.int32)])
+        if not halves:
+            first = jnp.where(up[0] == 1, first, jnp.zeros_like(first))
         return pl.pallas_call(
-            functools.partial(final_kernel, b, q, 2 * dates),
-            out_shape=jax.ShapeDtypeStruct((2, 2 * dates, width), f32),
-            in_specs=[smem] + [vmem] * 7,
+            functools.partial(final_kernel, b, q, 2 * dates, halves),
+            out_shape=jax.ShapeDtypeStruct((2, 2 * dates, size * width), f32),
+            in_specs=[smem, vmem, vmem] + [anywhere] * (len(prefix) + 2) + [vmem] * 2,
             out_specs=vmem,
+            scratch_shapes=[
+                square,
+                pltpu.VMEM((2 * seen_rows, features), bf16),
+                pltpu.VMEM((size, 2 * seen_rows, width), bf16),
+                pltpu.SemaphoreType.DMA((4,)),
+            ],
             compiler_params=small,
             cost_estimate=cost(4 * features**2 * width, 2**21),
             name="final",
-        )(up, first, last, operator, seer, seens[b], weight_column, correlation)
+        )(flag, first, last, *prefix, seer, seens[b], weight_column, correlation)
 
     arrived = [[] for _ in range(stages)]
     leaving = [[] for _ in range(stages)]
@@ -412,13 +560,13 @@
 
     def held(s, j):
         if s == 0:
-            return jnp.zeros((features, width), bf16), jnp.ones((1,), jnp.int32)
+            return jnp.zeros(arrived[0][j].shape, bf16), jnp.ones((1,), jnp.int32)
         if s == 1:
             return arrived[0][j], ups[0]
         if (s, j) not in holds:
             before, flag = held(s - 1, j)
             before = jnp.where(flag[0] == 1, before, jnp.zeros_like(before)).astype(f32)
-            moved = dot(prefixes[s - 1][j // pieces], arrived[s - 1][j])
+            moved = dot(prefixes[s - 1][table[j][0]], arrived[s - 1][j])
             value = jnp.where(ups[s - 1][0] == 1, before + moved, before)
             holds[s, j] = value.astype(bf16)
         return holds[s, j], jnp.ones((1,), jnp.int32)
@@ -434,7 +582,10 @@
             near = arrived[s - 1][j]
             if behind is not None:
                 near = after(near, results[behind])
-            out = stage(j, ups[s - 1], leaving[s - 1][j], near, combiners[s - 1])
+            if s == 1:
+                out = first_stage(j, leaving[0][j], near)
+            else:
+                out = stage(j, ups[s - 1], leaving[s - 1][j], near, combiners[s - 1])
         if j >= flight:
             out = after(out, arrived[s][j - flight])
         leaving[s].append(out)
@@ -443,28 +594,35 @@
     def finish():
         i = len(results)
         before, flag = held(stages - 1, i)
-        results.append(final(i, flag, before, arrived[-1][i], prefixes[stages - 1]))
+        results.append(final(i, flag, before, arrived[-1][i]))
 
     join_states(0, own, late_half)
     for b in range(buckets):
-        for _ in range(pieces):
-            advance(0)
+        for at, _, _ in table:
+            if at == b:
+                advance(0)
         if b + 1 < buckets:
             scales = after(scales, ends[-1])
             sent = local(b + 1, 1 - core_flag, scales)
             late_half = lax.ppermute(sent, "date", swap)
-            if stages > 1:
-                for _ in range(early):
-                    at = len(arrived[1])
-                    arrived[0][at] = after(arrived[0][at], sent)
-                    advance(1)
-                    scales = after(scales, leaving[1][-1])
-            else:
-                scales = after(scales, sent)
+            scales = after(scales, sent)
+            for _ in range(early if stages > 1 else 0):
+                at = len(arrived[1])
+                arrived[0][at] = after(arrived[0][at], sent)
+                advance(1)
+                scales = after(scales, leaving[1][-1])
             own = local(b + 1, core_flag, scales)
             join_states(b + 1, own, late_half)
     for s in range(1, stages):
         last = s == stages - 1
+        if last:
+            while len(arrived[s]) < 2:
+                advance(s)
+            discount, cross_gamma, step_days = lax.optimization_barrier(
+                (discount, cross_gamma, step_days, leaving[s][-1])
+            )[:3]
+            discount = (step_days.astype(f32) / 365.0)[:, None, None] * discount
+            discount_other = lax.ppermute(discount, "date", swap)
         while len(arrived[s]) < count:
             j = len(arrived[s])
             while last and len(results) < j - lag:
@@ -483,7 +641,7 @@
     carried = jnp.concatenate([high.reshape(-1, lanes), low.reshape(-1, lanes)], axis=0)
     body_rows = (buckets + 1) * half * 2 * dates
     message = pl.pallas_call(
-        functools.partial(pack_kernel, buckets, pieces),
+        functools.partial(pack_kernel, places, buckets, half),
         out_shape=jax.ShapeDtypeStruct((body_rows + carried.shape[0], lanes), bf16),
         in_specs=[vmem] * (count + 1),
         out_specs=vmem,

time: 141 us -> 143 us (1.014)
  Pallas kernels: 57.5 us -> 66.2 us
  waiting for transfers between devices: 40 us -> 35.8 us
  local copies, waits for them, and re-layouts: 10.9 us -> 6.71 us
  starting transfers between devices: 28.6 us -> 31.1 us
    ppermute x8 -> x10, waiting for transfers between devices: 31.9 us -> 16 us  [advance(): arrived[s].append(lax.ppermute(out, 'date', link))]
    ppermute x1, waiting for transfers between devices: 0.01 us -> 12.7 us  [shards(): part = lax.ppermute(part, 'date', far)]
    pallas_call x11 -> x13, Pallas kernels: 22.8 us -> 32.1 us  [the longest x5 13.4 us: final(): pl.pallas_call(functools.partial(final_kernel, b, q, 2 * dates, halves),...]
    unnamed x46 -> x45, local copies, waits for them, and re-layouts: 10.2 us -> 4.74 us
    select_n x2 -> x0, other arithmetic: 1.78 us -> none  [the longest x1 1.3 us: shards(): jnp.where(first, part, part_other)]
    ppermute x8 -> x10, starting transfers between devices: 16.1 us -> 17.7 us  [advance(): arrived[s].append(lax.ppermute(out, 'date', link))]
  transfers between devices with their start and end apart: 20 -> 22, of which waited for: 11 -> 11; matrix products, arithmetic and copies ran while one was open for 2% -> 3% of each run, Pallas kernels for 35% -> 34%
where the time goes in v7:
time: 143 us
  Pallas kernels  66.2 us (46%)
  waiting for transfers between devices  35.8 us (25%)
  starting transfers between devices  31.1 us (22%)
  local copies, waits for them, and re-layouts  6.71 us (5%)
  other arithmetic  1.72 us (1%)
    pallas_call x4, Pallas kernels, local(): pl.pallas_call(functools.partial(local_kernel, dates, b), out_shape=jax.S...  24.5 us
    ppermute x10, starting transfers between devices, advance(): arrived[s].append(lax.ppermute(out, 'date', link))  17.7 us
    ppermute x10, waiting for transfers between devices, advance(): arrived[s].append(lax.ppermute(out, 'date', link))  16 us
    pallas_call x5, Pallas kernels, final(): pl.pallas_call(functools.partial(final_kernel, b, q, 2 * dates, halves),...  13.4 us
    ppermute x1, waiting for transfers between devices, shards(): part = lax.ppermute(part, 'date', far)  12.7 us
    pallas_call x5, Pallas kernels, first_stage(): pl.pallas_call(functools.partial(first_stage_kernel, table[j][0]), out_sh...  10.5 us
    pallas_call x2, Pallas kernels, join_states(): result = call(core_flag, own, late_half, late)  8.11 us
    ppermute x3, starting transfers between devices, shards(): lax.ppermute(message, 'bucket', [(i, (i + k) % zs) for i in range(zs)])  5.56 us
  transfers between devices with their start and end apart: 22, of which 11 were waited for; matrix products, arithmetic and copies ran while one was open for 3% of the time, Pallas kernels for 34%

profile of v7, /device:TPU:0, one launch (start us, length us, event | category | flops | bytes accessed | tf_op | source)
XLA Modules:
  0.0 142.6 jit_solution(3476103422574085923)
XLA Ops:
  1.5 4.8 %operators.1.mine_ref = bf16[2,768,512]{2,1,0:T(8,128)(2,1)S(1)} custom-call(bf16[4,2,512,512]{3,2,1,0:T(8,128)(2,1)} %a_hbm.7, bf16[2,64,512]{2,1,0:T(8,128)(2,1)S(1)} %copy-done.5), custom_call_target="tpu_custom_call" | custom-call | flops 2147483648 | bytes 8388608 | tf_op jit(solution)/shard_map/operators/pallas_call | solution.py:361
  7.0 5.8 %local.4 = bf16[4,768,256]{2,1,0:T(8,128)(2,1)S(1)} custom-call(f32[4]{0:T(128)S(1)} %multiply_sqrt_fusion.scale_ref, s32[1]{0:T(128)S(6)} %sub.26.octet_ref, bf16[4,2,512,16,128]{4,3,2,1,0:T(8,128)(2,1)} %x_hbm.7, bf16[4,2,512,512]{3,2,1,0:T(8,128)(2,1)} %a_hbm.7, bf16[2,64,512]{2,1,0:T(8,128)(2,1)S(1)} %copy-done.6), custom_call_target="tpu_custom_call" | custom-call | flops 1610612736 | bytes 8388608 | tf_op jit(solution)/shard_map/local/pallas_call | solution.py:376
  12.9 3.9 %join_operators.1 = (bf16[2,512,512]{2,1,0:T(8,128)(2,1)}, bf16[2,512,512]{2,1,0:T(8,128)(2,1)}, bf16[2,768,512]{2,1,0:T(8,128)(2,1)}, bf16[2,256,512]{2,1,0:T(8,128)(2,1)}) custom-call(s32[1]{0:T(128)} %bitcast.1.core_ref.octet_ref, bf16[2,768,512]{2,1,0:T(8,128)(2,1)} %copy-done.10, bf16[2,768,512]{2,1,0:T(8,128)(2,1)} %collective-permute-done.other_ref), custom_call_target="tpu_custom_call" | custom-call | flops 805306368 | bytes 4194304 | tf_op jit(solution)/shard_map/join_operators/pallas_call | solution.py:403
  16.8 5.8 %local.5.mine_hbm = bf16[4,768,256]{2,1,0:T(8,128)(2,1)S(1)} custom-call(f32[4]{0:T(128)S(1)} %multiply_sqrt_fusion.scale_ref, s32[1]{0:T(128)} %bitcast.1.core_ref.octet_ref, bf16[4,2,512,16,128]{4,3,2,1,0:T(8,128)(2,1)} %x_hbm.7, bf16[4,2,512,512]{3,2,1,0:T(8,128)(2,1)} %a_hbm.7, bf16[2,64,512]{2,1,0:T(8,128)(2,1)S(1)} %copy-done.6), custom_call_target="tpu_custom_call" | custom-call | flops 1610612736 | bytes 8388608 | tf_op jit(solution)/shard_map/local/pallas_call | solution.py:376
  22.6 3.8 %join_states.2 = (bf16[4,512,256]{2,1,0:T(8,128)(2,1)S(1)}, bf16[512,512]{1,0:T(8,128)(2,1)}, bf16[512,512]{1,0:T(8,128)(2,1)S(1)}) custom-call(s32[1]{0:T(128)} %bitcast.1.core_ref.octet_ref, bf16[4,768,256]{2,1,0:T(8,128)(2,1)S(1)} %local.5.mine_hbm, bf16[4,768,256]{2,1,0:T(8,128)(2,1)} %collective-permute-done.1.other_hbm, ...), custom_call_target="tpu_custom_call" | custom-call | flops 805306368 | bytes 4194304 | tf_op jit(solution)/shard_map/join_states/pallas_call | solution.py:502
  27.5 7.1 %local.6 = bf16[4,768,256]{2,1,0:T(8,128)(2,1)} custom-call(f32[4]{0:T(128)S(1)} %multiply_sqrt_fusion.scale_ref, s32[1]{0:T(128)S(6)} %sub.26.octet_ref, bf16[4,2,512,16,128]{4,3,2,1,0:T(8,128)(2,1)} %x_hbm.7, bf16[4,2,512,512]{3,2,1,0:T(8,128)(2,1)} %a_hbm.7, bf16[2,64,512]{2,1,0:T(8,128)(2,1)S(1)} %copy-done.6), custom_call_target="tpu_custom_call" | custom-call | flops 1610612736 | bytes 8388608 | tf_op jit(solution)/shard_map/local/pallas_call | solution.py:376
  35.1 2.6 %collective-permute-start.3 = (bf16[2,256,512]{2,1,0:T(8,128)(2,1)S(1)}, bf16[2,256,512]{2,1,0:T(8,128)(2,1)S(1)}, u32[]{:S(2)}, u32[]{:S(2)}) collective-permute-start(bf16[2,256,512]{2,1,0:T(8,128)(2,1)S(1)} %copy-done.20), channel_id=1, source_target_pairs={{0,8},{4,12},{8,0},{12,4},{16,24},{20,28},{24,16},{28,20},{1,9},{5... | collective-permute-start | bytes 1572872 | tf_op jit(solution)/shard_map/ppermute | solution.py:436
  37.8 12.7 %collective-permute-done.3.part_hbm.refs_0_ = bf16[2,256,512]{2,1,0:T(8,128)(2,1)S(1)} collective-permute-done((bf16[2,256,512]{2,1,0:T(8,128)(2,1)S(1)}, bf16[2,256,512]{2,1,0:T(8,128)(2,1)S(1)}, u32[]{:S(2)}, u32[]{:S(2)}) %collective-permute-start.3) | collective-permute-done | bytes 524320 | tf_op jit(solution)/shard_map/ppermute | solution.py:436
  52.6 9.1 %collective-permute-done.5.other_ref.first_ref = bf16[512,512]{1,0:T(8,128)(2,1)S(1)} collective-permute-done((bf16[512,512]{1,0:T(8,128)(2,1)}, bf16[512,512]{1,0:T(8,128)(2,1)S(1)}, u32[]{:S(2)}, u32[]{:S(2)}) %collective-permute-start.5) | collective-permute-done | bytes 524320 | tf_op jit(solution)/shard_map/ppermute | solution.py:592
  61.7 2.6 %stage.6 = bf16[512,512]{1,0:T(8,128)(2,1)} custom-call(s32[2]{0:T(128)S(1)} %pad_add_fusion.1.flag_ref, bf16[512,512]{1,0:T(8,128)(2,1)} %get-tuple-element.36.mine_ref, bf16[512,512]{1,0:T(8,128)(2,1)S(1)} %collective-permute-done.5.other_ref.first_ref, bf16[2,512,512]{2,1,0:T(8,128)(2,1)S(1)} %copy-done.1, ...), custom_call_target="tpu_custom_call" | custom-call | flops 134217728 | bytes 1048576 | tf_op jit(solution)/shard_map/stage/pallas_call | solution.py:511
  64.3 4.8 %collective-permute-start.6 = (bf16[512,512]{1,0:T(8,128)(2,1)}, bf16[512,512]{1,0:T(8,128)(2,1)}, u32[]{:S(2)}, u32[]{:S(2)}) collective-permute-start(bf16[512,512]{1,0:T(8,128)(2,1)} %stage.6), channel_id=1, source_target_pairs={{0,16},{4,20},{8,24},{12,28},{1,17},{5,21},{9,25},{13,29},{2,18},{... | collective-permute-start | bytes 1572872 | tf_op jit(solution)/shard_map/ppermute | solution.py:592
  69.1 5.8 %local.7.mine_hbm = bf16[4,768,256]{2,1,0:T(8,128)(2,1)S(1)} custom-call(f32[4]{0:T(128)S(1)} %multiply_sqrt_fusion.scale_ref, s32[1]{0:T(128)} %bitcast.1.core_ref.octet_ref, bf16[4,2,512,16,128]{4,3,2,1,0:T(8,128)(2,1)} %x_hbm.7, bf16[4,2,512,512]{3,2,1,0:T(8,128)(2,1)} %a_hbm.7, bf16[2,64,512]{2,1,0:T(8,128)(2,1)S(1)} %copy-done.6), custom_call_target="tpu_custom_call" | custom-call | flops 1610612736 | bytes 8388608 | tf_op jit(solution)/shard_map/local/pallas_call | solution.py:376
  74.9 4.3 %join_states.3 = (bf16[4,512,256]{2,1,0:T(8,128)(2,1)S(1)}, bf16[512,512]{1,0:T(8,128)(2,1)}, bf16[512,256]{1,0:T(8,128)(2,1)}, bf16[512,256]{1,0:T(8,128)(2,1)}) custom-call(s32[1]{0:T(128)} %bitcast.1.core_ref.octet_ref, bf16[4,768,256]{2,1,0:T(8,128)(2,1)S(1)} %local.7.mine_hbm, bf16[4,768,256]{2,1,0:T(8,128)(2,1)} %collective-permute-done.8.other_hbm, ...), custom_call_target="tpu_custom_call" | custom-call | flops 805306368 | bytes 4194304 | tf_op jit(solution)/shard_map/join_states/pallas_call | solution.py:502
  83.0 2.4 %stage.5 = bf16[512,512]{1,0:T(8,128)(2,1)} custom-call(s32[2]{0:T(128)S(1)} %pad_add_fusion.1.flag_ref, bf16[512,512]{1,0:T(8,128)(2,1)S(1)} %copy-done.12, bf16[512,512]{1,0:T(8,128)(2,1)} %collective-permute-done.2.other_ref.first_ref, bf16[2,512,512]{2,1,0:T(8,128)(2,1)S(1)} %copy-done.1, ...), custom_call_target="tpu_custom_call" | custom-call | flops 134217728 | bytes 1048576 | tf_op jit(solution)/shard_map/stage/pallas_call | solution.py:511
  85.4 2.1 %collective-permute-start.7 = (bf16[512,512]{1,0:T(8,128)(2,1)}, bf16[512,512]{1,0:T(8,128)(2,1)}, u32[]{:S(2)}, u32[]{:S(2)}) collective-permute-start(bf16[512,512]{1,0:T(8,128)(2,1)} %stage.5), channel_id=1, source_target_pairs={{0,16},{4,20},{8,24},{12,28},{1,17},{5,21},{9,25},{13,29},{2,18},{... | collective-permute-start | bytes 1572872 | tf_op jit(solution)/shard_map/ppermute | solution.py:592
  87.6 3.1 %final.5.refs_0_ = f32[2,8,512]{2,1,0:T(8,128)S(1)} custom-call(s32[2]{0:T(128)S(1)} %pad_add_fusion.1.flag_ref, bf16[512,512]{1,0:T(8,128)(2,1)S(1)} %copy-done.8, bf16[512,512]{1,0:T(8,128)(2,1)} %collective-permute-done.6.last_ref, bf16[2,256,512]{2,1,0:T(8,128)(2,1)S(1)} %collective-permute-done.3.part_hbm.refs_0_, ...), custom_call_target="tpu_custom_call" | custom-call | flops 268435456 | bytes 2097152 | tf_op jit(solution)/shard_map/final/pallas_call | solution.py:540
  90.7 2.4 %collective-permute-done.9.other_ref.first_ref = bf16[512,512]{1,0:T(8,128)(2,1)} collective-permute-done((bf16[512,512]{1,0:T(8,128)(2,1)}, bf16[512,512]{1,0:T(8,128)(2,1)}, u32[]{:S(2)}, u32[]{:S(2)}) %collective-permute-start.9) | collective-permute-done | bytes 524320 | tf_op jit(solution)/shard_map/ppermute | solution.py:592
  93.1 2.6 %stage.7 = bf16[512,512]{1,0:T(8,128)(2,1)} custom-call(s32[2]{0:T(128)S(1)} %pad_add_fusion.1.flag_ref, bf16[512,512]{1,0:T(8,128)(2,1)} %get-tuple-element.43.mine_ref, bf16[512,512]{1,0:T(8,128)(2,1)} %collective-permute-done.9.other_ref.first_ref, bf16[2,512,512]{2,1,0:T(8,128)(2,1)S(1)} %copy-done.1, ...), custom_call_target="tpu_custom_call" | custom-call | flops 134217728 | bytes 1048576 | tf_op jit(solution)/shard_map/stage/pallas_call | solution.py:511
  102.7 3.2 %final.6.refs_1_ = f32[2,8,512]{2,1,0:T(8,128)S(1)} custom-call(s32[2]{0:T(128)S(1)} %pad_add_fusion.1.flag_ref, bf16[512,512]{1,0:T(8,128)(2,1)} %collective-permute-done.2.other_ref.first_ref, bf16[512,512]{1,0:T(8,128)(2,1)} %collective-permute-done.7.last_ref, bf16[2,256,512]{2,1,0:T(8,128)(2,1)S(1)} %collective-permute-done.3.part_hbm.refs_0_, ...), custom_call_target="tpu_custom_call" | custom-call | flops 268435456 | bytes 2097152 | tf_op jit(solution)/shard_map/final/pallas_call | solution.py:540
  110.9 3.2 %final.7.refs_2_ = f32[2,8,512]{2,1,0:T(8,128)S(1)} custom-call(s32[2]{0:T(128)S(1)} %pad_add_fusion.1.flag_ref, bf16[512,512]{1,0:T(8,128)(2,1)} %collective-permute-done.9.other_ref.first_ref, bf16[512,512]{1,0:T(8,128)(2,1)} %collective-permute-done.10.last_ref, bf16[2,256,512]{2,1,0:T(8,128)(2,1)S(1)} %collective-permute-done.3.part_hbm.refs_0_, ...), custom_call_target="tpu_custom_call" | custom-call | flops 268435456 | bytes 2097152 | tf_op jit(solution)/shard_map/final/pallas_call | solution.py:540
  117.5 2.1 %final.8.refs_3_ = f32[2,8,256]{2,1,0:T(8,128)S(1)} custom-call(s32[2]{0:T(128)S(1)} %pad_add_fusion.1.flag_ref, bf16[512,256]{1,0:T(8,128)(2,1)} %collective-permute-done.11.other_ref.first_ref, bf16[512,256]{1,0:T(8,128)(2,1)S(1)} %collective-permute-done.12.last_ref, bf16[2,256,512]{2,1,0:T(8,128)(2,1)S(1)} %collective-permute-done.3.part_hbm.refs_0_, ...), custom_call_target="tpu_custom_call" | custom-call | flops 268435456 | bytes 2097152 | tf_op jit(solution)/shard_map/final/pallas_call | solution.py:540
  119.7 2.4 %collective-permute-done.14.last_ref = bf16[512,256]{1,0:T(8,128)(2,1)S(1)} collective-permute-done((bf16[512,256]{1,0:T(8,128)(2,1)S(1)}, bf16[512,256]{1,0:T(8,128)(2,1)S(1)}, u32[]{:S(2)}, u32[]{:S(2)}) %collective-permute-start.14) | collective-permute-done | bytes 262176 | tf_op jit(solution)/shard_map/ppermute | solution.py:592
  125.5 2.6 %collective-permute-start.17 = (bf16[256,128]{1,0:T(8,128)(2,1)S(1)}, bf16[256,128]{1,0:T(8,128)(2,1)S(1)}, u32[]{:S(2)}, u32[]{:S(2)}) collective-permute-start(bf16[256,128]{1,0:T(8,128)(2,1)S(1)} %pack.1.refs_0_), channel_id=1, source_target_pairs={{0,2},{1,3},{2,0},{3,1},{4,6},{5,7},{6,4},{7,5},{8,10},{9,11},{10,... | collective-permute-start | bytes 196616 | tf_op jit(solution)/shard_map/ppermute | solution.py:653
  138.0 2.5 %collective-permute-start.21 = (f32[8,128]{1,0:T(8,128)S(1)}, f32[8,128]{1,0:T(8,128)S(1)}, u32[]{:S(2)}, u32[]{:S(2)}) collective-permute-start(f32[8,128]{1,0:T(8,128)S(1)} %add.24), channel_id=1, source_target_pairs={{0,16},{4,20},{8,24},{12,28},{16,0},{20,4},{24,8},{28,12},{1,17},{... | collective-permute-start | bytes 12296 | tf_op jit(solution)/shard_map/ppermute | solution.py:681
  (105 shorter events, 39.8 us)
Async XLA Ops:
  6.4 6.5 %collective-permute-start = (bf16[2,768,512]{2,1,0:T(8,128)(2,1)S(1)}, bf16[2,768,512]{2,1,0:T(8,128)(2,1)}, u32[]{:S(2)}, u32[]{:S(2)}) collective-permute-start(bf16[2,768,512]{2,1,0:T(8,128)(2,1)S(1)} %operators.1.mine_ref), channel_id=1, source_target_pairs={{0,4},{4,0},{8,12},{12,8},{16,20},{20,16},{24,28},{28,24},{1,5},{5... | collective-permute-start | bytes 4718600 | tf_op jit(solution)/shard_map/ppermute | solution.py:397
  12.8 9.8 %collective-permute-start.1 = (bf16[4,768,256]{2,1,0:T(8,128)(2,1)S(1)}, bf16[4,768,256]{2,1,0:T(8,128)(2,1)}, u32[]{:S(2)}, u32[]{:S(2)}) collective-permute-start(bf16[4,768,256]{2,1,0:T(8,128)(2,1)S(1)} %local.4), channel_id=1, source_target_pairs={{0,4},{4,0},{8,12},{12,8},{16,20},{20,16},{24,28},{28,24},{1,5},{5... | collective-permute-start | bytes 4718600 | tf_op jit(solution)/shard_map/ppermute | solution.py:400
  27.5 34.2 %copy-start.1 = (bf16[2,512,512]{2,1,0:T(8,128)(2,1)S(1)}, bf16[2,512,512]{2,1,0:T(8,128)(2,1)}, u32[]{:S(2)}) copy-start(bf16[2,512,512]{2,1,0:T(8,128)(2,1)} %get-tuple-element.33.block_hbm) | copy-start | bytes 3145732
  34.6 40.3 %collective-permute-start.8 = (bf16[4,768,256]{2,1,0:T(8,128)(2,1)}, bf16[4,768,256]{2,1,0:T(8,128)(2,1)}, u32[]{:S(2)}, u32[]{:S(2)}) collective-permute-start(bf16[4,768,256]{2,1,0:T(8,128)(2,1)} %local.6), channel_id=1, source_target_pairs={{0,4},{4,0},{8,12},{12,8},{16,20},{20,16},{24,28},{28,24},{1,5},{5... | collective-permute-start | bytes 4718600 | tf_op jit(solution)/shard_map/ppermute | solution.py:607
  35.1 15.3 %collective-permute-start.3 = (bf16[2,256,512]{2,1,0:T(8,128)(2,1)S(1)}, bf16[2,256,512]{2,1,0:T(8,128)(2,1)S(1)}, u32[]{:S(2)}, u32[]{:S(2)}) collective-permute-start(bf16[2,256,512]{2,1,0:T(8,128)(2,1)S(1)} %copy-done.20), channel_id=1, source_target_pairs={{0,8},{4,12},{8,0},{12,4},{16,24},{20,28},{24,16},{28,20},{1,9},{5... | collective-permute-start | bytes 1572872 | tf_op jit(solution)/shard_map/ppermute | solution.py:436
  37.7 24.0 %collective-permute-start.5 = (bf16[512,512]{1,0:T(8,128)(2,1)}, bf16[512,512]{1,0:T(8,128)(2,1)S(1)}, u32[]{:S(2)}, u32[]{:S(2)}) collective-permute-start(bf16[512,512]{1,0:T(8,128)(2,1)} %get-tuple-element.36.mine_ref), channel_id=1, source_target_pairs={{0,8},{4,12},{8,0},{12,4},{16,24},{20,28},{24,16},{28,20},{1,9},{5... | collective-permute-start | bytes 1572872 | tf_op jit(solution)/shard_map/ppermute | solution.py:592
  50.5 11.2 %collective-permute-start.4 = (bf16[2,256,512]{2,1,0:T(8,128)(2,1)S(1)}, bf16[2,256,512]{2,1,0:T(8,128)(2,1)S(1)}, u32[]{:S(2)}, u32[]{:S(2)}) collective-permute-start(bf16[2,256,512]{2,1,0:T(8,128)(2,1)S(1)} %collective-permute-done.3.part_hbm.refs_0_), channel_id=1, source_target_pairs={{0,4},{4,0},{8,12},{12,8},{16,20},{20,16},{24,28},{28,24},{1,5},{5... | collective-permute-start | bytes 1572872 | tf_op jit(solution)/shard_map/ppermute | solution.py:440
  50.5 31.4 %collective-permute-start.2 = (bf16[512,512]{1,0:T(8,128)(2,1)}, bf16[512,512]{1,0:T(8,128)(2,1)}, u32[]{:S(2)}, u32[]{:S(2)}) collective-permute-start(bf16[512,512]{1,0:T(8,128)(2,1)} %copy-done.11), channel_id=1, source_target_pairs={{0,8},{4,12},{8,0},{12,4},{16,24},{20,28},{24,16},{28,20},{1,9},{5... | collective-permute-start | bytes 1572872 | tf_op jit(solution)/shard_map/ppermute | solution.py:592
  64.3 23.2 %collective-permute-start.6 = (bf16[512,512]{1,0:T(8,128)(2,1)}, bf16[512,512]{1,0:T(8,128)(2,1)}, u32[]{:S(2)}, u32[]{:S(2)}) collective-permute-start(bf16[512,512]{1,0:T(8,128)(2,1)} %stage.6), channel_id=1, source_target_pairs={{0,16},{4,20},{8,24},{12,28},{1,17},{5,21},{9,25},{13,29},{2,18},{... | collective-permute-start | bytes 1572872 | tf_op jit(solution)/shard_map/ppermute | solution.py:592
  80.2 12.9 %collective-permute-start.9 = (bf16[512,512]{1,0:T(8,128)(2,1)}, bf16[512,512]{1,0:T(8,128)(2,1)}, u32[]{:S(2)}, u32[]{:S(2)}) collective-permute-start(bf16[512,512]{1,0:T(8,128)(2,1)} %get-tuple-element.43.mine_ref), channel_id=1, source_target_pairs={{0,8},{4,12},{8,0},{12,4},{16,24},{20,28},{24,16},{28,20},{1,9},{5... | collective-permute-start | bytes 1572872 | tf_op jit(solution)/shard_map/ppermute | solution.py:592
  85.4 17.3 %collective-permute-start.7 = (bf16[512,512]{1,0:T(8,128)(2,1)}, bf16[512,512]{1,0:T(8,128)(2,1)}, u32[]{:S(2)}, u32[]{:S(2)}) collective-permute-start(bf16[512,512]{1,0:T(8,128)(2,1)} %stage.5), channel_id=1, source_target_pairs={{0,16},{4,20},{8,24},{12,28},{1,17},{5,21},{9,25},{13,29},{2,18},{... | collective-permute-start | bytes 1572872 | tf_op jit(solution)/shard_map/ppermute | solution.py:592
  95.6 15.3 %collective-permute-start.10 = (bf16[512,512]{1,0:T(8,128)(2,1)}, bf16[512,512]{1,0:T(8,128)(2,1)}, u32[]{:S(2)}, u32[]{:S(2)}) collective-permute-start(bf16[512,512]{1,0:T(8,128)(2,1)} %stage.7), channel_id=1, source_target_pairs={{0,16},{4,20},{8,24},{12,28},{1,17},{5,21},{9,25},{13,29},{2,18},{... | collective-permute-start | bytes 1572872 | tf_op jit(solution)/shard_map/ppermute | solution.py:592
  98.4 3.4 %collective-permute-start.15 = (f32[4,4,128]{2,1,0:T(4,128)}, f32[4,4,128]{2,1,0:T(4,128)}, u32[]{:S(2)}, u32[]{:S(2)}) collective-permute-start(f32[4,4,128]{2,1,0:T(4,128)} %broadcast_multiply_fusion), channel_id=1, source_target_pairs={{0,4},{4,0},{8,12},{12,8},{16,20},{20,16},{24,28},{28,24},{1,5},{5... | collective-permute-start | bytes 24584 | tf_op jit(solution)/shard_map/ppermute | solution.py:625
  98.4 9.5 %collective-permute-start.11 = (bf16[512,256]{1,0:T(8,128)(2,1)}, bf16[512,256]{1,0:T(8,128)(2,1)}, u32[]{:S(2)}, u32[]{:S(2)}) collective-permute-start(bf16[512,256]{1,0:T(8,128)(2,1)} %get-tuple-element.46.mine_ref), channel_id=1, source_target_pairs={{0,8},{4,12},{8,0},{12,4},{16,24},{20,28},{24,16},{28,20},{1,9},{5... | collective-permute-start | bytes 786440 | tf_op jit(solution)/shard_map/ppermute | solution.py:592
  99.9 14.2 %collective-permute-start.13 = (bf16[512,256]{1,0:T(8,128)(2,1)}, bf16[512,256]{1,0:T(8,128)(2,1)S(1)}, u32[]{:S(2)}, u32[]{:S(2)}) collective-permute-start(bf16[512,256]{1,0:T(8,128)(2,1)} %get-tuple-element.48.mine_ref), channel_id=1, source_target_pairs={{0,8},{4,12},{8,0},{12,4},{16,24},{20,28},{24,16},{28,20},{1,9},{5... | collective-permute-start | bytes 786440 | tf_op jit(solution)/shard_map/ppermute | solution.py:592
  109.6 7.9 %collective-permute-start.12 = (bf16[512,256]{1,0:T(8,128)(2,1)S(1)}, bf16[512,256]{1,0:T(8,128)(2,1)S(1)}, u32[]{:S(2)}, u32[]{:S(2)}) collective-permute-start(bf16[512,256]{1,0:T(8,128)(2,1)S(1)} %stage.8), channel_id=1, source_target_pairs={{0,16},{4,20},{8,24},{12,28},{1,17},{5,21},{9,25},{13,29},{2,18},{... | collective-permute-start | bytes 786440 | tf_op jit(solution)/shard_map/ppermute | solution.py:592
  115.6 6.5 %collective-permute-start.14 = (bf16[512,256]{1,0:T(8,128)(2,1)S(1)}, bf16[512,256]{1,0:T(8,128)(2,1)S(1)}, u32[]{:S(2)}, u32[]{:S(2)}) collective-permute-start(bf16[512,256]{1,0:T(8,128)(2,1)S(1)} %stage.9), channel_id=1, source_target_pairs={{0,16},{4,20},{8,24},{12,28},{1,17},{5,21},{9,25},{13,29},{2,18},{... | collective-permute-start | bytes 786440 | tf_op jit(solution)/shard_map/ppermute | solution.py:592
  119.7 12.7 %copy-start.15 = (s32[16]{0:T(128)S(1)}, s32[16]{0:T(128)}, u32[]{:S(2)}) copy-start(s32[16]{0:T(128)} %count_ref.1) | copy-start | bytes 196
  123.8 6.1 %collective-permute-start.16 = (bf16[256,128]{1,0:T(8,128)(2,1)S(1)}, bf16[256,128]{1,0:T(8,128)(2,1)S(1)}, u32[]{:S(2)}, u32[]{:S(2)}) collective-permute-start(bf16[256,128]{1,0:T(8,128)(2,1)S(1)} %pack.1.refs_0_), channel_id=1, source_target_pairs={{0,1},{1,2},{2,3},{3,0},{4,5},{5,6},{6,7},{7,4},{8,9},{9,10},{10,1... | collective-permute-start | bytes 196616 | tf_op jit(solution)/shard_map/ppermute | solution.py:653
  125.5 5.2 %collective-permute-start.17 = (bf16[256,128]{1,0:T(8,128)(2,1)S(1)}, bf16[256,128]{1,0:T(8,128)(2,1)S(1)}, u32[]{:S(2)}, u32[]{:S(2)}) collective-permute-start(bf16[256,128]{1,0:T(8,128)(2,1)S(1)} %pack.1.refs_0_), channel_id=1, source_target_pairs={{0,2},{1,3},{2,0},{3,1},{4,6},{5,7},{6,4},{7,5},{8,10},{9,11},{10,... | collective-permute-start | bytes 196616 | tf_op jit(solution)/shard_map/ppermute | solution.py:653
  128.1 4.3 %collective-permute-start.18 = (bf16[256,128]{1,0:T(8,128)(2,1)S(1)}, bf16[256,128]{1,0:T(8,128)(2,1)S(1)}, u32[]{:S(2)}, u32[]{:S(2)}) collective-permute-start(bf16[256,128]{1,0:T(8,128)(2,1)S(1)} %pack.1.refs_0_), channel_id=1, source_target_pairs={{0,3},{1,0},{2,1},{3,2},{4,7},{5,4},{6,5},{7,6},{8,11},{9,8},{10,9... | collective-permute-start | bytes 196616 | tf_op jit(solution)/shard_map/ppermute | solution.py:653
  133.2 1.2 collective-permute-start.19
  134.4 3.6 %collective-permute-start.20 = (f32[8,128]{1,0:T(8,128)S(1)}, f32[8,128]{1,0:T(8,128)S(1)}, u32[]{:S(2)}, u32[]{:S(2)}) collective-permute-start(f32[8,128]{1,0:T(8,128)S(1)} %fusion.4), channel_id=1, source_target_pairs={{0,8},{4,12},{8,0},{12,4},{16,24},{20,28},{24,16},{28,20},{1,9},{5... | collective-permute-start | bytes 12296 | tf_op jit(solution)/shard_map/ppermute | solution.py:681
  138.0 4.1 %collective-permute-start.21 = (f32[8,128]{1,0:T(8,128)S(1)}, f32[8,128]{1,0:T(8,128)S(1)}, u32[]{:S(2)}, u32[]{:S(2)}) collective-permute-start(f32[8,128]{1,0:T(8,128)S(1)} %add.24), channel_id=1, source_target_pairs={{0,16},{4,20},{8,24},{12,28},{16,0},{20,4},{24,8},{28,12},{1,17},{... | collective-permute-start | bytes 12296 | tf_op jit(solution)/shard_map/ppermute | solution.py:681
  (20 other events, 101.6 us)

commit v8 on v7

--- a/solution.py
+++ b/solution.py
@@ -19,8 +19,11 @@
 
 def chunks(units, bucket, buckets):
     sizes = [2] * (units // 2) + [1] * (units % 2)
-    if bucket == buckets - 1 and units % 2 == 0:
-        sizes[-1:] = [1, 1]
+    if units % 2 == 0:
+        if bucket == 0:
+            sizes[:1] = [1, 1]
+        elif bucket == buckets - 1:
+            sizes[-1:] = [1, 1]
     return sizes
 
 
@@ -46,10 +49,14 @@
     sens = r_ref.shape[1]
     product = a_ref[0, 0]
     for t in range(dates):
-        if t:
-            product = dot(a_ref[t, 0], product).astype(bf16)
+        upper = r_ref[0]
+        if t + 1 < dates:
+            upper = jnp.concatenate([a_ref[t + 1, 0], upper], axis=0)
+        moved = dot(upper, product).astype(bf16)
         row = features + t * sens
-        w_ref[0, row : row + sens, :] = dot(r_ref[0], product).astype(bf16)
+        w_ref[0, row : row + sens, :] = moved[-sens:]
+        if t + 1 < dates:
+            product = moved[:features]
     w_ref[0, :features, :] = product
 
 
@@ -593,6 +600,8 @@
 
     def finish():
         i = len(results)
+        if results:
+            arrived[-1][i] = after(arrived[-1][i], results[-1])
         before, flag = held(stages - 1, i)
         results.append(final(i, flag, before, arrived[-1][i]))
 
@@ -627,7 +636,7 @@
             j = len(arrived[s])
             while last and len(results) < j - lag:
                 finish()
-            advance(s, j - lag - 1 if last and j > lag else None)
+            advance(s)
     while len(results) < count:
         finish()
 

time: 143 us -> 152 us (1.063)
  waiting for transfers between devices: 35.8 us -> 47.6 us
  local copies, waits for them, and re-layouts: 6.71 us -> 4.31 us
    ppermute x10 -> x12, waiting for transfers between devices: 16 us -> 27.4 us  [advance(): arrived[s].append(lax.ppermute(out, 'date', link))]
    pallas_call x5 -> x6, Pallas kernels: 13.4 us -> 14.7 us  [final(): pl.pallas_call(functools.partial(final_kernel, b, q, 2 * dates, halves),...]
    unnamed x45 -> x39, local copies, waits for them, and re-layouts: 4.74 us -> 3.61 us
    pallas_call x5 -> x6, Pallas kernels: 10.5 us -> 9.75 us  [first_stage(): pl.pallas_call(functools.partial(first_stage_kernel, table[j][0]), out_sh...]
    ppermute x10 -> x12, starting transfers between devices: 17.7 us -> 18.3 us  [advance(): arrived[s].append(lax.ppermute(out, 'date', link))]
  transfers between devices with their start and end apart: 22 -> 24, of which waited for: 11 -> 13; matrix products, arithmetic and copies ran while one was open for 3% -> 1% of each run, Pallas kernels for 34% -> 32%
where the time goes in v8:
time: 152 us; the launch traced here: 151 us
  Pallas kernels  66.5 us (44%)
  waiting for transfers between devices  47.6 us (31%)
  starting transfers between devices  31.6 us (21%)
  local copies, waits for them, and re-layouts  4.31 us (3%)
    ppermute x12, waiting for transfers between devices, advance(): arrived[s].append(lax.ppermute(out, 'date', link))  27.4 us
    pallas_call x4, Pallas kernels, local(): pl.pallas_call(functools.partial(local_kernel, dates, b), out_shape=jax.S...  24.8 us
    ppermute x12, starting transfers between devices, advance(): arrived[s].append(lax.ppermute(out, 'date', link))  18.3 us
    pallas_call x6, Pallas kernels, final(): pl.pallas_call(functools.partial(final_kernel, b, q, 2 * dates, halves),...  14.7 us
    ppermute x1, waiting for transfers between devices, shards(): part = lax.ppermute(part, 'date', far)  12.5 us
    pallas_call x6, Pallas kernels, first_stage(): pl.pallas_call(functools.partial(first_stage_kernel, table[j][0]), out_sh...  9.75 us
    pallas_call x2, Pallas kernels, join_states(): result = call(core_flag, own, late_half, late)  8.07 us
    ppermute x3, starting transfers between devices, shards(): lax.ppermute(message, 'bucket', [(i, (i + k) % zs) for i in range(zs)])  5.56 us
  transfers between devices with their start and end apart: 24, of which 13 were waited for; matrix products, arithmetic and copies ran while one was open for 1% of the time, Pallas kernels for 32%

profile of v8, /device:TPU:0, one launch (start us, length us, event | category | flops | bytes accessed | tf_op | source)
XLA Modules:
  0.0 151.5 jit_solution(17242321762152360066)
XLA Ops:
  1.5 4.3 %operators.1.mine_ref = bf16[2,768,512]{2,1,0:T(8,128)(2,1)S(1)} custom-call(bf16[4,2,512,512]{3,2,1,0:T(8,128)(2,1)} %a_hbm.7, bf16[2,64,512]{2,1,0:T(8,128)(2,1)S(1)} %copy-done.6), custom_call_target="tpu_custom_call" | custom-call | flops 2147483648 | bytes 8388608 | tf_op jit(solution)/shard_map/operators/pallas_call | solution.py:368
  6.5 5.8 %local.4 = bf16[4,768,256]{2,1,0:T(8,128)(2,1)S(1)} custom-call(f32[4]{0:T(128)S(1)} %multiply_sqrt_fusion.scale_ref, s32[1]{0:T(128)S(6)} %sub.26.octet_ref, bf16[4,2,512,16,128]{4,3,2,1,0:T(8,128)(2,1)} %x_hbm.7, bf16[4,2,512,512]{3,2,1,0:T(8,128)(2,1)} %a_hbm.7, bf16[2,64,512]{2,1,0:T(8,128)(2,1)S(1)} %copy-done.7), custom_call_target="tpu_custom_call" | custom-call | flops 1610612736 | bytes 8388608 | tf_op jit(solution)/shard_map/local/pallas_call | solution.py:383
  12.4 3.9 %join_operators.1 = (bf16[2,512,512]{2,1,0:T(8,128)(2,1)}, bf16[2,512,512]{2,1,0:T(8,128)(2,1)}, bf16[2,768,512]{2,1,0:T(8,128)(2,1)}, bf16[2,256,512]{2,1,0:T(8,128)(2,1)}) custom-call(s32[1]{0:T(128)} %bitcast.1.core_ref.octet_ref, bf16[2,768,512]{2,1,0:T(8,128)(2,1)} %copy-done.8, bf16[2,768,512]{2,1,0:T(8,128)(2,1)} %collective-permute-done.other_ref), custom_call_target="tpu_custom_call" | custom-call | flops 805306368 | bytes 4194304 | tf_op jit(solution)/shard_map/join_operators/pallas_call | solution.py:410
  16.3 5.8 %local.5.mine_hbm = bf16[4,768,256]{2,1,0:T(8,128)(2,1)S(1)} custom-call(f32[4]{0:T(128)S(1)} %multiply_sqrt_fusion.scale_ref, s32[1]{0:T(128)} %bitcast.1.core_ref.octet_ref, bf16[4,2,512,16,128]{4,3,2,1,0:T(8,128)(2,1)} %x_hbm.7, bf16[4,2,512,512]{3,2,1,0:T(8,128)(2,1)} %a_hbm.7, bf16[2,64,512]{2,1,0:T(8,128)(2,1)S(1)} %copy-done.7), custom_call_target="tpu_custom_call" | custom-call | flops 1610612736 | bytes 8388608 | tf_op jit(solution)/shard_map/local/pallas_call | solution.py:383
  22.1 3.8 %join_states.2 = (bf16[4,512,256]{2,1,0:T(8,128)(2,1)S(1)}, bf16[512,256]{1,0:T(8,128)(2,1)}, bf16[512,256]{1,0:T(8,128)(2,1)}, bf16[512,512]{1,0:T(8,128)(2,1)S(1)}) custom-call(s32[1]{0:T(128)} %bitcast.1.core_ref.octet_ref, bf16[4,768,256]{2,1,0:T(8,128)(2,1)S(1)} %local.5.mine_hbm, bf16[4,768,256]{2,1,0:T(8,128)(2,1)} %collective-permute-done.1.other_hbm, ...), custom_call_target="tpu_custom_call" | custom-call | flops 805306368 | bytes 4194304 | tf_op jit(solution)/shard_map/join_states/pallas_call | solution.py:509
  26.0 7.4 %local.6 = bf16[4,768,256]{2,1,0:T(8,128)(2,1)} custom-call(f32[4]{0:T(128)S(1)} %multiply_sqrt_fusion.scale_ref, s32[1]{0:T(128)S(6)} %sub.26.octet_ref, bf16[4,2,512,16,128]{4,3,2,1,0:T(8,128)(2,1)} %x_hbm.7, bf16[4,2,512,512]{3,2,1,0:T(8,128)(2,1)} %a_hbm.7, bf16[2,64,512]{2,1,0:T(8,128)(2,1)S(1)} %copy-done.7), custom_call_target="tpu_custom_call" | custom-call | flops 1610612736 | bytes 8388608 | tf_op jit(solution)/shard_map/local/pallas_call | solution.py:383
  34.0 2.6 %collective-permute-start.3 = (bf16[2,256,512]{2,1,0:T(8,128)(2,1)S(1)}, bf16[2,256,512]{2,1,0:T(8,128)(2,1)S(1)}, u32[]{:S(2)}, u32[]{:S(2)}) collective-permute-start(bf16[2,256,512]{2,1,0:T(8,128)(2,1)S(1)} %copy-done.17), channel_id=1, source_target_pairs={{0,8},{4,12},{8,0},{12,4},{16,24},{20,28},{24,16},{28,20},{1,9},{5... | collective-permute-start | bytes 1572872 | tf_op jit(solution)/shard_map/ppermute | solution.py:443
  36.6 12.5 %collective-permute-done.3.part_hbm.refs_0_ = bf16[2,256,512]{2,1,0:T(8,128)(2,1)S(1)} collective-permute-done((bf16[2,256,512]{2,1,0:T(8,128)(2,1)S(1)}, bf16[2,256,512]{2,1,0:T(8,128)(2,1)S(1)}, u32[]{:S(2)}, u32[]{:S(2)}) %collective-permute-start.3) | collective-permute-done | bytes 524320 | tf_op jit(solution)/shard_map/ppermute | solution.py:443
  53.2 5.5 %collective-permute-done.5.other_ref.first_ref = bf16[512,256]{1,0:T(8,128)(2,1)} collective-permute-done((bf16[512,256]{1,0:T(8,128)(2,1)}, bf16[512,256]{1,0:T(8,128)(2,1)}, u32[]{:S(2)}, u32[]{:S(2)}) %collective-permute-start.5) | collective-permute-done | bytes 262176 | tf_op jit(solution)/shard_map/ppermute | solution.py:599
  58.6 5.6 %collective-permute-done.2.other_ref.first_ref = bf16[512,256]{1,0:T(8,128)(2,1)} collective-permute-done((bf16[512,256]{1,0:T(8,128)(2,1)}, bf16[512,256]{1,0:T(8,128)(2,1)}, u32[]{:S(2)}, u32[]{:S(2)}) %collective-permute-start.2) | collective-permute-done | bytes 262176 | tf_op jit(solution)/shard_map/ppermute | solution.py:599
  65.7 2.2 %stage.7 = bf16[512,256]{1,0:T(8,128)(2,1)} custom-call(s32[2]{0:T(128)S(1)} %pad_add_fusion.1.flag_ref, bf16[512,256]{1,0:T(8,128)(2,1)} %get-tuple-element.39.mine_ref, bf16[512,256]{1,0:T(8,128)(2,1)} %collective-permute-done.5.other_ref.first_ref, bf16[2,512,512]{2,1,0:T(8,128)(2,1)S(1)} %copy-done, ...), custom_call_target="tpu_custom_call" | custom-call | flops 134217728 | bytes 1048576 | tf_op jit(solution)/shard_map/stage/pallas_call | solution.py:518
  67.9 4.4 %collective-permute-start.6 = (bf16[512,256]{1,0:T(8,128)(2,1)}, bf16[512,256]{1,0:T(8,128)(2,1)}, u32[]{:S(2)}, u32[]{:S(2)}) collective-permute-start(bf16[512,256]{1,0:T(8,128)(2,1)} %stage.7), channel_id=1, source_target_pairs={{0,16},{4,20},{8,24},{12,28},{1,17},{5,21},{9,25},{13,29},{2,18},{... | collective-permute-start | bytes 786440 | tf_op jit(solution)/shard_map/ppermute | solution.py:599
  72.3 5.8 %local.7.mine_hbm = bf16[4,768,256]{2,1,0:T(8,128)(2,1)S(1)} custom-call(f32[4]{0:T(128)S(1)} %multiply_sqrt_fusion.scale_ref, s32[1]{0:T(128)} %bitcast.1.core_ref.octet_ref, bf16[4,2,512,16,128]{4,3,2,1,0:T(8,128)(2,1)} %x_hbm.7, bf16[4,2,512,512]{3,2,1,0:T(8,128)(2,1)} %a_hbm.7, bf16[2,64,512]{2,1,0:T(8,128)(2,1)S(1)} %copy-done.7), custom_call_target="tpu_custom_call" | custom-call | flops 1610612736 | bytes 8388608 | tf_op jit(solution)/shard_map/local/pallas_call | solution.py:383
  78.2 4.2 %join_states.3 = (bf16[4,512,256]{2,1,0:T(8,128)(2,1)S(1)}, bf16[512,512]{1,0:T(8,128)(2,1)}, bf16[512,256]{1,0:T(8,128)(2,1)}, bf16[512,256]{1,0:T(8,128)(2,1)}) custom-call(s32[1]{0:T(128)} %bitcast.1.core_ref.octet_ref, bf16[4,768,256]{2,1,0:T(8,128)(2,1)S(1)} %local.7.mine_hbm, bf16[4,768,256]{2,1,0:T(8,128)(2,1)} %collective-permute-done.10.other_hbm, ...), custom_call_target="tpu_custom_call" | custom-call | flops 805306368 | bytes 4194304 | tf_op jit(solution)/shard_map/join_states/pallas_call | solution.py:509
  91.2 7.3 %collective-permute-done.11.other_ref.first_ref = bf16[512,512]{1,0:T(8,128)(2,1)} collective-permute-done((bf16[512,512]{1,0:T(8,128)(2,1)}, bf16[512,512]{1,0:T(8,128)(2,1)}, u32[]{:S(2)}, u32[]{:S(2)}) %collective-permute-start.11) | collective-permute-done | bytes 524320 | tf_op jit(solution)/shard_map/ppermute | solution.py:599
  101.6 2.5 %collective-permute-done.13.other_ref.first_ref = bf16[512,256]{1,0:T(8,128)(2,1)} collective-permute-done((bf16[512,256]{1,0:T(8,128)(2,1)}, bf16[512,256]{1,0:T(8,128)(2,1)}, u32[]{:S(2)}, u32[]{:S(2)}) %collective-permute-start.13) | collective-permute-done | bytes 262176 | tf_op jit(solution)/shard_map/ppermute | solution.py:599
  111.6 2.4 %final.6.refs_0_ = f32[2,8,256]{2,1,0:T(8,128)S(1)} custom-call(s32[2]{0:T(128)S(1)} %pad_add_fusion.1.flag_ref, bf16[512,256]{1,0:T(8,128)(2,1)} %collective-permute-done.5.other_ref.first_ref, bf16[512,256]{1,0:T(8,128)(2,1)} %collective-permute-done.6.last_ref, bf16[2,256,512]{2,1,0:T(8,128)(2,1)S(1)} %collective-permute-done.3.part_hbm.refs_0_, ...), custom_call_target="tpu_custom_call" | custom-call | flops 268435456 | bytes 2097152 | tf_op jit(solution)/shard_map/final/pallas_call | solution.py:547
  114.1 5.4 %collective-permute-done.7.last_ref = bf16[512,256]{1,0:T(8,128)(2,1)S(1)} collective-permute-done((bf16[512,256]{1,0:T(8,128)(2,1)S(1)}, bf16[512,256]{1,0:T(8,128)(2,1)S(1)}, u32[]{:S(2)}, u32[]{:S(2)}) %collective-permute-start.7) | collective-permute-done | bytes 262176 | tf_op jit(solution)/shard_map/ppermute | solution.py:599
  121.6 3.1 %final.8.refs_2_ = f32[2,8,512]{2,1,0:T(8,128)S(1)} custom-call(s32[2]{0:T(128)S(1)} %pad_add_fusion.1.flag_ref, bf16[512,512]{1,0:T(8,128)(2,1)} %collective-permute-done.8.other_ref.first_ref, bf16[512,512]{1,0:T(8,128)(2,1)S(1)} %collective-permute-done.9.last_ref, bf16[2,256,512]{2,1,0:T(8,128)(2,1)S(1)} %collective-permute-done.3.part_hbm.refs_0_, ...), custom_call_target="tpu_custom_call" | custom-call | flops 268435456 | bytes 2097152 | tf_op jit(solution)/shard_map/final/pallas_call | solution.py:547
  124.7 3.2 %final.9.refs_3_ = f32[2,8,512]{2,1,0:T(8,128)S(1)} custom-call(s32[2]{0:T(128)S(1)} %pad_add_fusion.1.flag_ref, bf16[512,512]{1,0:T(8,128)(2,1)} %collective-permute-done.11.other_ref.first_ref, bf16[512,512]{1,0:T(8,128)(2,1)S(1)} %collective-permute-done.12.last_ref, bf16[2,256,512]{2,1,0:T(8,128)(2,1)S(1)} %collective-permute-done.3.part_hbm.refs_0_, ...), custom_call_target="tpu_custom_call" | custom-call | flops 268435456 | bytes 2097152 | tf_op jit(solution)/shard_map/final/pallas_call | solution.py:547
  127.9 2.1 %final.10.refs_4_ = f32[2,8,256]{2,1,0:T(8,128)S(1)} custom-call(s32[2]{0:T(128)S(1)} %pad_add_fusion.1.flag_ref, bf16[512,256]{1,0:T(8,128)(2,1)} %collective-permute-done.13.other_ref.first_ref, bf16[512,256]{1,0:T(8,128)(2,1)S(1)} %collective-permute-done.14.last_ref, bf16[2,256,512]{2,1,0:T(8,128)(2,1)S(1)} %collective-permute-done.3.part_hbm.refs_0_, ...), custom_call_target="tpu_custom_call" | custom-call | flops 268435456 | bytes 2097152 | tf_op jit(solution)/shard_map/final/pallas_call | solution.py:547
  133.9 2.6 %collective-permute-start.19 = (bf16[256,128]{1,0:T(8,128)(2,1)S(1)}, bf16[256,128]{1,0:T(8,128)(2,1)S(1)}, u32[]{:S(2)}, u32[]{:S(2)}) collective-permute-start(bf16[256,128]{1,0:T(8,128)(2,1)S(1)} %pack.1.refs_0_), channel_id=1, source_target_pairs={{0,2},{1,3},{2,0},{3,1},{4,6},{5,7},{6,4},{7,5},{8,10},{9,11},{10,... | collective-permute-start | bytes 196616 | tf_op jit(solution)/shard_map/ppermute | solution.py:662
  138.7 2.5 %collective-permute-done.19.refs_2_ = bf16[256,128]{1,0:T(8,128)(2,1)S(1)} collective-permute-done((bf16[256,128]{1,0:T(8,128)(2,1)S(1)}, bf16[256,128]{1,0:T(8,128)(2,1)S(1)}, u32[]{:S(2)}, u32[]{:S(2)}) %collective-permute-start.19) | collective-permute-done | bytes 65568 | tf_op jit(solution)/shard_map/ppermute | solution.py:662
  146.9 2.5 %collective-permute-start.23 = (f32[8,128]{1,0:T(8,128)S(1)}, f32[8,128]{1,0:T(8,128)S(1)}, u32[]{:S(2)}, u32[]{:S(2)}) collective-permute-start(f32[8,128]{1,0:T(8,128)S(1)} %add.24), channel_id=1, source_target_pairs={{0,16},{4,20},{8,24},{12,28},{16,0},{20,4},{24,8},{28,12},{1,17},{... | collective-permute-start | bytes 12296 | tf_op jit(solution)/shard_map/ppermute | solution.py:690
  (105 shorter events, 42.9 us)
Async XLA Ops:
  5.9 6.5 %collective-permute-start = (bf16[2,768,512]{2,1,0:T(8,128)(2,1)S(1)}, bf16[2,768,512]{2,1,0:T(8,128)(2,1)}, u32[]{:S(2)}, u32[]{:S(2)}) collective-permute-start(bf16[2,768,512]{2,1,0:T(8,128)(2,1)S(1)} %operators.1.mine_ref), channel_id=1, source_target_pairs={{0,4},{4,0},{8,12},{12,8},{16,20},{20,16},{24,28},{28,24},{1,5},{5... | collective-permute-start | bytes 4718600 | tf_op jit(solution)/shard_map/ppermute | solution.py:404
  12.3 9.8 %collective-permute-start.1 = (bf16[4,768,256]{2,1,0:T(8,128)(2,1)S(1)}, bf16[4,768,256]{2,1,0:T(8,128)(2,1)}, u32[]{:S(2)}, u32[]{:S(2)}) collective-permute-start(bf16[4,768,256]{2,1,0:T(8,128)(2,1)S(1)} %local.4), channel_id=1, source_target_pairs={{0,4},{4,0},{8,12},{12,8},{16,20},{20,16},{24,28},{28,24},{1,5},{5... | collective-permute-start | bytes 4718600 | tf_op jit(solution)/shard_map/ppermute | solution.py:407
  33.5 44.7 %collective-permute-start.10 = (bf16[4,768,256]{2,1,0:T(8,128)(2,1)}, bf16[4,768,256]{2,1,0:T(8,128)(2,1)}, u32[]{:S(2)}, u32[]{:S(2)}) collective-permute-start(bf16[4,768,256]{2,1,0:T(8,128)(2,1)} %local.6), channel_id=1, source_target_pairs={{0,4},{4,0},{8,12},{12,8},{16,20},{20,16},{24,28},{28,24},{1,5},{5... | collective-permute-start | bytes 4718600 | tf_op jit(solution)/shard_map/ppermute | solution.py:616
  34.0 15.1 %collective-permute-start.3 = (bf16[2,256,512]{2,1,0:T(8,128)(2,1)S(1)}, bf16[2,256,512]{2,1,0:T(8,128)(2,1)S(1)}, u32[]{:S(2)}, u32[]{:S(2)}) collective-permute-start(bf16[2,256,512]{2,1,0:T(8,128)(2,1)S(1)} %copy-done.17), channel_id=1, source_target_pairs={{0,8},{4,12},{8,0},{12,4},{16,24},{20,28},{24,16},{28,20},{1,9},{5... | collective-permute-start | bytes 1572872 | tf_op jit(solution)/shard_map/ppermute | solution.py:443
  49.1 15.1 %collective-permute-start.4 = (bf16[2,256,512]{2,1,0:T(8,128)(2,1)S(1)}, bf16[2,256,512]{2,1,0:T(8,128)(2,1)S(1)}, u32[]{:S(2)}, u32[]{:S(2)}) collective-permute-start(bf16[2,256,512]{2,1,0:T(8,128)(2,1)S(1)} %collective-permute-done.3.part_hbm.refs_0_), channel_id=1, source_target_pairs={{0,4},{4,0},{8,12},{12,8},{16,20},{20,16},{24,28},{28,24},{1,5},{5... | collective-permute-start | bytes 1572872 | tf_op jit(solution)/shard_map/ppermute | solution.py:447
  49.1 9.5 %collective-permute-start.5 = (bf16[512,256]{1,0:T(8,128)(2,1)}, bf16[512,256]{1,0:T(8,128)(2,1)}, u32[]{:S(2)}, u32[]{:S(2)}) collective-permute-start(bf16[512,256]{1,0:T(8,128)(2,1)} %get-tuple-element.39.mine_ref), channel_id=1, source_target_pairs={{0,8},{4,12},{8,0},{12,4},{16,24},{20,28},{24,16},{28,20},{1,9},{5... | collective-permute-start | bytes 786440 | tf_op jit(solution)/shard_map/ppermute | solution.py:599
  50.9 13.4 %collective-permute-start.2 = (bf16[512,256]{1,0:T(8,128)(2,1)}, bf16[512,256]{1,0:T(8,128)(2,1)}, u32[]{:S(2)}, u32[]{:S(2)}) collective-permute-start(bf16[512,256]{1,0:T(8,128)(2,1)} %get-tuple-element.35.mine_ref), channel_id=1, source_target_pairs={{0,8},{4,12},{8,0},{12,4},{16,24},{20,28},{24,16},{28,20},{1,9},{5... | collective-permute-start | bytes 786440 | tf_op jit(solution)/shard_map/ppermute | solution.py:599
  51.4 35.7 %collective-permute-start.8 = (bf16[512,512]{1,0:T(8,128)(2,1)}, bf16[512,512]{1,0:T(8,128)(2,1)}, u32[]{:S(2)}, u32[]{:S(2)}) collective-permute-start(bf16[512,512]{1,0:T(8,128)(2,1)} %copy-done.9), channel_id=1, source_target_pairs={{0,8},{4,12},{8,0},{12,4},{16,24},{20,28},{24,16},{28,20},{1,9},{5... | collective-permute-start | bytes 1572872 | tf_op jit(solution)/shard_map/ppermute | solution.py:599
  67.9 42.3 %collective-permute-start.6 = (bf16[512,256]{1,0:T(8,128)(2,1)}, bf16[512,256]{1,0:T(8,128)(2,1)}, u32[]{:S(2)}, u32[]{:S(2)}) collective-permute-start(bf16[512,256]{1,0:T(8,128)(2,1)} %stage.7), channel_id=1, source_target_pairs={{0,16},{4,20},{8,24},{12,28},{1,17},{5,21},{9,25},{13,29},{2,18},{... | collective-permute-start | bytes 786440 | tf_op jit(solution)/shard_map/ppermute | solution.py:599
  83.4 15.1 %collective-permute-start.11 = (bf16[512,512]{1,0:T(8,128)(2,1)}, bf16[512,512]{1,0:T(8,128)(2,1)}, u32[]{:S(2)}, u32[]{:S(2)}) collective-permute-start(bf16[512,512]{1,0:T(8,128)(2,1)} %get-tuple-element.49.mine_ref), channel_id=1, source_target_pairs={{0,8},{4,12},{8,0},{12,4},{16,24},{20,28},{24,16},{28,20},{1,9},{5... | collective-permute-start | bytes 1572872 | tf_op jit(solution)/shard_map/ppermute | solution.py:599
  84.9 19.2 %collective-permute-start.13 = (bf16[512,256]{1,0:T(8,128)(2,1)}, bf16[512,256]{1,0:T(8,128)(2,1)}, u32[]{:S(2)}, u32[]{:S(2)}) collective-permute-start(bf16[512,256]{1,0:T(8,128)(2,1)} %get-tuple-element.52.mine_ref), channel_id=1, source_target_pairs={{0,8},{4,12},{8,0},{12,4},{16,24},{20,28},{24,16},{28,20},{1,9},{5... | collective-permute-start | bytes 786440 | tf_op jit(solution)/shard_map/ppermute | solution.py:599
  85.5 22.1 %collective-permute-start.15 = (bf16[512,256]{1,0:T(8,128)(2,1)}, bf16[512,256]{1,0:T(8,128)(2,1)S(1)}, u32[]{:S(2)}, u32[]{:S(2)}) collective-permute-start(bf16[512,256]{1,0:T(8,128)(2,1)} %get-tuple-element.54.mine_ref), channel_id=1, source_target_pairs={{0,8},{4,12},{8,0},{12,4},{16,24},{20,28},{24,16},{28,20},{1,9},{5... | collective-permute-start | bytes 786440 | tf_op jit(solution)/shard_map/ppermute | solution.py:599
  89.8 31.8 %collective-permute-start.9 = (bf16[512,512]{1,0:T(8,128)(2,1)S(1)}, bf16[512,512]{1,0:T(8,128)(2,1)S(1)}, u32[]{:S(2)}, u32[]{:S(2)}) collective-permute-start(bf16[512,512]{1,0:T(8,128)(2,1)S(1)} %stage.8), channel_id=1, source_target_pairs={{0,16},{4,20},{8,24},{12,28},{1,17},{5,21},{9,25},{13,29},{2,18},{... | collective-permute-start | bytes 1572872 | tf_op jit(solution)/shard_map/ppermute | solution.py:599
  98.5 1.7 %collective-permute-start.17 = (f32[4,4,128]{2,1,0:T(4,128)S(1)}, f32[4,4,128]{2,1,0:T(4,128)S(1)}, u32[]{:S(2)}, u32[]{:S(2)}) collective-permute-start(f32[4,4,128]{2,1,0:T(4,128)S(1)} %broadcast_multiply_fusion), channel_id=1, source_target_pairs={{0,4},{4,0},{8,12},{12,8},{16,20},{20,16},{24,28},{28,24},{1,5},{5... | collective-permute-start | bytes 24584 | tf_op jit(solution)/shard_map/ppermute | solution.py:634
  100.2 24.5 %collective-permute-start.12 = (bf16[512,512]{1,0:T(8,128)(2,1)S(1)}, bf16[512,512]{1,0:T(8,128)(2,1)S(1)}, u32[]{:S(2)}, u32[]{:S(2)}) collective-permute-start(bf16[512,512]{1,0:T(8,128)(2,1)S(1)} %stage.9), channel_id=1, source_target_pairs={{0,16},{4,20},{8,24},{12,28},{1,17},{5,21},{9,25},{13,29},{2,18},{... | collective-permute-start | bytes 1572872 | tf_op jit(solution)/shard_map/ppermute | solution.py:599
  104.1 15.3 %collective-permute-start.7 = (bf16[512,256]{1,0:T(8,128)(2,1)S(1)}, bf16[512,256]{1,0:T(8,128)(2,1)S(1)}, u32[]{:S(2)}, u32[]{:S(2)}) collective-permute-start(bf16[512,256]{1,0:T(8,128)(2,1)S(1)} %copy-done.12), channel_id=1, source_target_pairs={{0,16},{4,20},{8,24},{12,28},{1,17},{5,21},{9,25},{13,29},{2,18},{... | collective-permute-start | bytes 786440 | tf_op jit(solution)/shard_map/ppermute | solution.py:599
  107.6 20.3 %collective-permute-start.14 = (bf16[512,256]{1,0:T(8,128)(2,1)S(1)}, bf16[512,256]{1,0:T(8,128)(2,1)S(1)}, u32[]{:S(2)}, u32[]{:S(2)}) collective-permute-start(bf16[512,256]{1,0:T(8,128)(2,1)S(1)} %stage.10), channel_id=1, source_target_pairs={{0,16},{4,20},{8,24},{12,28},{1,17},{5,21},{9,25},{13,29},{2,18},{... | collective-permute-start | bytes 786440 | tf_op jit(solution)/shard_map/ppermute | solution.py:599
  110.2 20.3 %collective-permute-start.16 = (bf16[512,256]{1,0:T(8,128)(2,1)S(1)}, bf16[512,256]{1,0:T(8,128)(2,1)S(1)}, u32[]{:S(2)}, u32[]{:S(2)}) collective-permute-start(bf16[512,256]{1,0:T(8,128)(2,1)S(1)} %stage.11), channel_id=1, source_target_pairs={{0,16},{4,20},{8,24},{12,28},{1,17},{5,21},{9,25},{13,29},{2,18},{... | collective-permute-start | bytes 786440 | tf_op jit(solution)/shard_map/ppermute | solution.py:599
  132.3 6.5 %collective-permute-start.18 = (bf16[256,128]{1,0:T(8,128)(2,1)S(1)}, bf16[256,128]{1,0:T(8,128)(2,1)S(1)}, u32[]{:S(2)}, u32[]{:S(2)}) collective-permute-start(bf16[256,128]{1,0:T(8,128)(2,1)S(1)} %pack.1.refs_0_), channel_id=1, source_target_pairs={{0,1},{1,2},{2,3},{3,0},{4,5},{5,6},{6,7},{7,4},{8,9},{9,10},{10,1... | collective-permute-start | bytes 196616 | tf_op jit(solution)/shard_map/ppermute | solution.py:662
  133.9 7.3 %collective-permute-start.19 = (bf16[256,128]{1,0:T(8,128)(2,1)S(1)}, bf16[256,128]{1,0:T(8,128)(2,1)S(1)}, u32[]{:S(2)}, u32[]{:S(2)}) collective-permute-start(bf16[256,128]{1,0:T(8,128)(2,1)S(1)} %pack.1.refs_0_), channel_id=1, source_target_pairs={{0,2},{1,3},{2,0},{3,1},{4,6},{5,7},{6,4},{7,5},{8,10},{9,11},{10,... | collective-permute-start | bytes 196616 | tf_op jit(solution)/shard_map/ppermute | solution.py:662
  136.4 4.8 %collective-permute-start.20 = (bf16[256,128]{1,0:T(8,128)(2,1)S(1)}, bf16[256,128]{1,0:T(8,128)(2,1)S(1)}, u32[]{:S(2)}, u32[]{:S(2)}) collective-permute-start(bf16[256,128]{1,0:T(8,128)(2,1)S(1)} %pack.1.refs_0_), channel_id=1, source_target_pairs={{0,3},{1,0},{2,1},{3,2},{4,7},{5,4},{6,5},{7,6},{8,11},{9,8},{10,9... | collective-permute-start | bytes 196616 | tf_op jit(solution)/shard_map/ppermute | solution.py:662
  142.1 1.2 collective-permute-start.21
  143.3 3.6 %collective-permute-start.22 = (f32[8,128]{1,0:T(8,128)S(1)}, f32[8,128]{1,0:T(8,128)S(1)}, u32[]{:S(2)}, u32[]{:S(2)}) collective-permute-start(f32[8,128]{1,0:T(8,128)S(1)} %fusion.4), channel_id=1, source_target_pairs={{0,8},{4,12},{8,0},{12,4},{16,24},{20,28},{24,16},{28,20},{1,9},{5... | collective-permute-start | bytes 12296 | tf_op jit(solution)/shard_map/ppermute | solution.py:690
  146.9 4.1 %collective-permute-start.23 = (f32[8,128]{1,0:T(8,128)S(1)}, f32[8,128]{1,0:T(8,128)S(1)}, u32[]{:S(2)}, u32[]{:S(2)}) collective-permute-start(f32[8,128]{1,0:T(8,128)S(1)} %add.24), channel_id=1, source_target_pairs={{0,16},{4,20},{8,24},{12,28},{16,0},{20,4},{24,8},{28,12},{1,17},{... | collective-permute-start | bytes 12296 | tf_op jit(solution)/shard_map/ppermute | solution.py:690
  (19 other events, 247.5 us)

commit v9 on v8

--- a/solution.py
+++ b/solution.py
@@ -123,7 +123,7 @@
         out_ref[q, :features, :] = state_ref[:, q * width : (q + 1) * width]
 
 
-def join_operator_kernel(core_ref, mine_ref, other_ref, p_ref, q_ref, late_ref, part_ref):
+def join_operator_kernel(core_ref, mine_ref, other_ref, p_ref, q_ref, part_ref):
     features = mine_ref.shape[2]
     first = core_ref[0] == 0
     mine, other = mine_ref[0], other_ref[0]
@@ -135,16 +135,17 @@
     seen = late.shape[0] - features
     q_ref[0, :seen, :] = early[features:]
     q_ref[0, seen:, :] = joined[features:]
-    late_ref[0] = late
 
 
 def join_state_kernel(
     b,
+    begin,
     sizes,
     core_ref,
     mine_hbm,
     other_hbm,
-    late_hbm,
+    operator_hbm,
+    operator_other_hbm,
     seen_ref,
     *refs,
 ):
@@ -153,19 +154,26 @@
     features = late_ref.shape[1]
     width = mine_ref.shape[2]
     first = core_ref[0] == 0
-    fetch = pltpu.make_async_copy(late_hbm.at[b], late_ref, late_sem)
-    fetch.start()
+
+    @pl.when(first)
+    def _():
+        pltpu.make_async_copy(operator_other_hbm.at[b], late_ref, late_sem).start()
+
+    @pl.when(core_ref[0] != 0)
+    def _():
+        pltpu.make_async_copy(operator_hbm.at[b], late_ref, late_sem).start()
+
     pieces = [
         (
-            pltpu.make_async_copy(mine_hbm.at[q], mine_ref.at[q], mine_sem.at[q]),
-            pltpu.make_async_copy(other_hbm.at[q], other_ref.at[q], other_sem.at[q]),
+            pltpu.make_async_copy(mine_hbm.at[begin + q], mine_ref.at[q], mine_sem.at[q]),
+            pltpu.make_async_copy(other_hbm.at[begin + q], other_ref.at[q], other_sem.at[q]),
         )
         for q in range(sum(sizes))
     ]
     for one, two in pieces:
         one.start()
         two.start()
-    fetch.wait()
+    pltpu.make_async_copy(operator_hbm.at[b], late_ref, late_sem).wait()
     late_operator = late_ref[...]
     q = 0
     for end_ref, size in zip(end_refs, sizes):
@@ -407,12 +415,11 @@
     late_half = lax.ppermute(sent, "date", swap)
 
     block3 = lambda r: pl.BlockSpec((1, r, features), lambda b: (b, 0, 0))
-    block, seer, late, part = pl.pallas_call(
+    block, seer, part = pl.pallas_call(
         join_operator_kernel,
         out_shape=(
             jax.ShapeDtypeStruct((buckets, features, features), bf16),
             jax.ShapeDtypeStruct((buckets, 2 * seen_rows, features), bf16),
-            jax.ShapeDtypeStruct((buckets, rows, features), bf16),
             jax.ShapeDtypeStruct((buckets, features // 2, features), bf16),
         ),
         grid=(buckets,),
@@ -420,7 +427,6 @@
         out_specs=(
             block3(features),
             block3(2 * seen_rows),
-            block3(rows),
             block3(features // 2),
         ),
         cost_estimate=cost(2 * buckets * rows * features**2, 2**22),
@@ -488,27 +494,34 @@
 
     def join_states(b, own, late_half):
         sizes = [size for at, _, size in table if at == b]
-        call = pl.pallas_call(
-            functools.partial(join_state_kernel, b, sizes),
-            out_shape=(jax.ShapeDtypeStruct((pieces, 2 * seen_rows, width), bf16),)
-            + tuple(jax.ShapeDtypeStruct((features, size * width), bf16) for size in sizes),
-            in_specs=[smem, anywhere, anywhere, anywhere],
-            out_specs=(vmem,) * (len(sizes) + 1),
-            scratch_shapes=[
-                pltpu.VMEM((pieces, rows, width), bf16),
-                pltpu.VMEM((pieces, rows, width), bf16),
-                pltpu.VMEM((rows, features), bf16),
-                pltpu.SemaphoreType.DMA((pieces,)),
-                pltpu.SemaphoreType.DMA((pieces,)),
-                pltpu.SemaphoreType.DMA,
-            ],
-            compiler_params=small,
-            cost_estimate=cost(2 * rows * features * half * lanes, 2**22),
-            name="join_states",
-        )
-        result = call(core_flag, own, late_half, late)
-        seens.append(result[0])
-        ends.extend(result[1:])
+        begin = 0
+        for group in [sizes] if b == 0 else [sizes[:1], sizes[1:]]:
+            units = sum(group)
+            call = pl.pallas_call(
+                functools.partial(join_state_kernel, b, begin, group),
+                out_shape=(jax.ShapeDtypeStruct((units, 2 * seen_rows, width), bf16),)
+                + tuple(jax.ShapeDtypeStruct((features, size * width), bf16) for size in group),
+                in_specs=[smem] + [anywhere] * 4,
+                out_specs=(vmem,) * (len(group) + 1),
+                scratch_shapes=[
+                    pltpu.VMEM((units, rows, width), bf16),
+                    pltpu.VMEM((units, rows, width), bf16),
+                    pltpu.VMEM((rows, features), bf16),
+                    pltpu.SemaphoreType.DMA((units,)),
+                    pltpu.SemaphoreType.DMA((units,)),
+                    pltpu.SemaphoreType.DMA,
+                ],
+                compiler_params=small,
+                cost_estimate=cost(2 * rows * features * units * width, 2**21),
+                name="join_states",
+            )
+            result = call(core_flag, own, late_half, operators, operators_other)
+            ends.extend(result[1:])
+            unit = 0
+            for size in group:
+                seens.append((result[0], unit))
+                unit += size
+            begin += units
 
     weight_column = risk_weight[:, :, None]
 
@@ -538,14 +551,14 @@
         )(up, mine, other, combiner)
 
     def final(j, up, first, last):
-        b, q, size = table[j]
+        b, _, size = table[j]
         halves = stages == 2
         prefix = (straight, crossed) if halves else (prefixes[-1],)
         flag = flags if halves else jnp.concatenate([core_flag, jnp.ones((1,), jnp.int32)])
         if not halves:
             first = jnp.where(up[0] == 1, first, jnp.zeros_like(first))
         return pl.pallas_call(
-            functools.partial(final_kernel, b, q, 2 * dates, halves),
+            functools.partial(final_kernel, b, seens[j][1], 2 * dates, halves),
             out_shape=jax.ShapeDtypeStruct((2, 2 * dates, size * width), f32),
             in_specs=[smem, vmem, vmem] + [anywhere] * (len(prefix) + 2) + [vmem] * 2,
             out_specs=vmem,
@@ -558,7 +571,7 @@
             compiler_params=small,
             cost_estimate=cost(4 * features**2 * width, 2**21),
             name="final",
-        )(flag, first, last, *prefix, seer, seens[b], weight_column, correlation)
+        )(flag, first, last, *prefix, seer, seens[j][0], weight_column, correlation)
 
     arrived = [[] for _ in range(stages)]
     leaving = [[] for _ in range(stages)]

time: 152 us -> 154 us (1.013)
    pallas_call x8 -> x9, Pallas kernels: 22.8 us -> 24.4 us  [the longest x6 14.2 us: final(): pl.pallas_call(functools.partial(final_kernel, b, seens[j][1], 2 * dates,...]
    unnamed x39 -> x43, local copies, waits for them, and re-layouts: 3.61 us -> 4.21 us
where the time goes in v9:
time: 154 us; the launch traced here: 153 us
  Pallas kernels  67.7 us (44%)
  waiting for transfers between devices  48.8 us (32%)
  starting transfers between devices  30.2 us (20%)
  local copies, waits for them, and re-layouts  4.91 us (3%)
    ppermute x12, waiting for transfers between devices, advance(): arrived[s].append(lax.ppermute(out, 'date', link))  27.6 us
    pallas_call x4, Pallas kernels, local(): pl.pallas_call(functools.partial(local_kernel, dates, b), out_shape=jax.S...  24.9 us
    ppermute x12, starting transfers between devices, advance(): arrived[s].append(lax.ppermute(out, 'date', link))  18.3 us
    pallas_call x6, Pallas kernels, final(): pl.pallas_call(functools.partial(final_kernel, b, seens[j][1], 2 * dates,...  14.2 us
    ppermute x1, waiting for transfers between devices, shards(): part = lax.ppermute(part, 'date', far)  12.5 us
    pallas_call x3, Pallas kernels, join_states(): result = call(core_flag, own, late_half, operators, operators_other)  10.1 us
    pallas_call x6, Pallas kernels, first_stage(): pl.pallas_call(functools.partial(first_stage_kernel, table[j][0]), out_sh...  9.73 us
    ppermute x3, starting transfers between devices, shards(): lax.ppermute(message, 'bucket', [(i, (i + k) % zs) for i in range(zs)])  5.58 us
  transfers between devices with their start and end apart: 24, of which 13 were waited for; matrix products, arithmetic and copies ran while one was open for 1% of the time, Pallas kernels for 32%

profile of v9, /device:TPU:0, one launch (start us, length us, event | category | flops | bytes accessed | tf_op | source)
XLA Modules:
  0.0 153.1 jit_solution(14434089430422740429)
XLA Ops:
  1.5 4.3 %operators.1.mine_ref.operator_hbm = bf16[2,768,512]{2,1,0:T(8,128)(2,1)S(1)} custom-call(bf16[4,2,512,512]{3,2,1,0:T(8,128)(2,1)} %a_hbm.7, bf16[2,64,512]{2,1,0:T(8,128)(2,1)S(1)} %copy-done.5), custom_call_target="tpu_custom_call" | custom-call | flops 2147483648 | bytes 8388608 | tf_op jit(solution)/shard_map/operators/pallas_call | solution.py:376
  6.5 5.8 %local.4 = bf16[4,768,256]{2,1,0:T(8,128)(2,1)S(1)} custom-call(f32[4]{0:T(128)S(1)} %multiply_sqrt_fusion.scale_ref, s32[1]{0:T(128)S(6)} %sub.26.octet_ref, bf16[4,2,512,16,128]{4,3,2,1,0:T(8,128)(2,1)} %x_hbm.7, bf16[4,2,512,512]{3,2,1,0:T(8,128)(2,1)} %a_hbm.7, bf16[2,64,512]{2,1,0:T(8,128)(2,1)S(1)} %copy-done.6), custom_call_target="tpu_custom_call" | custom-call | flops 1610612736 | bytes 8388608 | tf_op jit(solution)/shard_map/local/pallas_call | solution.py:391
  12.4 3.6 %join_operators.1 = (bf16[2,512,512]{2,1,0:T(8,128)(2,1)}, bf16[2,512,512]{2,1,0:T(8,128)(2,1)}, bf16[2,256,512]{2,1,0:T(8,128)(2,1)}) custom-call(s32[1]{0:T(128)} %bitcast.1.core_ref.octet_ref, bf16[2,768,512]{2,1,0:T(8,128)(2,1)} %copy-done.2, bf16[2,768,512]{2,1,0:T(8,128)(2,1)} %collective-permute-done.other_ref.operator_other_hbm), custom_call_target="tpu_custom_call" | custom-call | flops 805306368 | bytes 4194304 | tf_op jit(solution)/shard_map/join_operators/pallas_call | solution.py:418
  15.9 5.8 %local.5.mine_hbm = bf16[4,768,256]{2,1,0:T(8,128)(2,1)S(1)} custom-call(f32[4]{0:T(128)S(1)} %multiply_sqrt_fusion.scale_ref, s32[1]{0:T(128)} %bitcast.1.core_ref.octet_ref, bf16[4,2,512,16,128]{4,3,2,1,0:T(8,128)(2,1)} %x_hbm.7, bf16[4,2,512,512]{3,2,1,0:T(8,128)(2,1)} %a_hbm.7, bf16[2,64,512]{2,1,0:T(8,128)(2,1)S(1)} %copy-done.6), custom_call_target="tpu_custom_call" | custom-call | flops 1610612736 | bytes 8388608 | tf_op jit(solution)/shard_map/local/pallas_call | solution.py:391
  21.8 3.9 %join_states.3 = (bf16[4,512,256]{2,1,0:T(8,128)(2,1)S(1)}, bf16[512,256]{1,0:T(8,128)(2,1)}, bf16[512,256]{1,0:T(8,128)(2,1)}, bf16[512,512]{1,0:T(8,128)(2,1)S(1)}) custom-call(s32[1]{0:T(128)} %bitcast.1.core_ref.octet_ref, bf16[4,768,256]{2,1,0:T(8,128)(2,1)S(1)} %local.5.mine_hbm, bf16[4,768,256]{2,1,0:T(8,128)(2,1)} %collective-permute-done.1.other_hbm, ...), custom_call_target="tpu_custom_call" | custom-call | flops 805306368 | bytes 2097152 | tf_op jit(solution)/shard_map/join_states/pallas_call | solution.py:518
  25.7 7.4 %local.6 = bf16[4,768,256]{2,1,0:T(8,128)(2,1)} custom-call(f32[4]{0:T(128)S(1)} %multiply_sqrt_fusion.scale_ref, s32[1]{0:T(128)S(6)} %sub.26.octet_ref, bf16[4,2,512,16,128]{4,3,2,1,0:T(8,128)(2,1)} %x_hbm.7, bf16[4,2,512,512]{3,2,1,0:T(8,128)(2,1)} %a_hbm.7, bf16[2,64,512]{2,1,0:T(8,128)(2,1)S(1)} %copy-done.6), custom_call_target="tpu_custom_call" | custom-call | flops 1610612736 | bytes 8388608 | tf_op jit(solution)/shard_map/local/pallas_call | solution.py:391
  33.7 2.6 %collective-permute-start.3 = (bf16[2,256,512]{2,1,0:T(8,128)(2,1)S(1)}, bf16[2,256,512]{2,1,0:T(8,128)(2,1)S(1)}, u32[]{:S(2)}, u32[]{:S(2)}) collective-permute-start(bf16[2,256,512]{2,1,0:T(8,128)(2,1)S(1)} %copy-done.19), channel_id=1, source_target_pairs={{0,8},{4,12},{8,0},{12,4},{16,24},{20,28},{24,16},{28,20},{1,9},{5... | collective-permute-start | bytes 1572872 | tf_op jit(solution)/shard_map/ppermute | solution.py:449
  36.2 12.5 %collective-permute-done.3.part_hbm.refs_0_ = bf16[2,256,512]{2,1,0:T(8,128)(2,1)S(1)} collective-permute-done((bf16[2,256,512]{2,1,0:T(8,128)(2,1)S(1)}, bf16[2,256,512]{2,1,0:T(8,128)(2,1)S(1)}, u32[]{:S(2)}, u32[]{:S(2)}) %collective-permute-start.3) | collective-permute-done | bytes 524320 | tf_op jit(solution)/shard_map/ppermute | solution.py:449
  52.8 5.5 %collective-permute-done.5.other_ref.first_ref = bf16[512,256]{1,0:T(8,128)(2,1)} collective-permute-done((bf16[512,256]{1,0:T(8,128)(2,1)}, bf16[512,256]{1,0:T(8,128)(2,1)}, u32[]{:S(2)}, u32[]{:S(2)}) %collective-permute-start.5) | collective-permute-done | bytes 262176 | tf_op jit(solution)/shard_map/ppermute | solution.py:612
  58.3 5.6 %collective-permute-done.2.other_ref.first_ref = bf16[512,256]{1,0:T(8,128)(2,1)} collective-permute-done((bf16[512,256]{1,0:T(8,128)(2,1)}, bf16[512,256]{1,0:T(8,128)(2,1)}, u32[]{:S(2)}, u32[]{:S(2)}) %collective-permute-start.2) | collective-permute-done | bytes 262176 | tf_op jit(solution)/shard_map/ppermute | solution.py:612
  65.3 2.2 %stage.7 = bf16[512,256]{1,0:T(8,128)(2,1)} custom-call(s32[2]{0:T(128)S(1)} %pad_add_fusion.1.flag_ref, bf16[512,256]{1,0:T(8,128)(2,1)} %get-tuple-element.38.mine_ref, bf16[512,256]{1,0:T(8,128)(2,1)} %collective-permute-done.5.other_ref.first_ref, bf16[2,512,512]{2,1,0:T(8,128)(2,1)S(1)} %copy-done, ...), custom_call_target="tpu_custom_call" | custom-call | flops 134217728 | bytes 1048576 | tf_op jit(solution)/shard_map/stage/pallas_call | solution.py:531
  67.5 4.4 %collective-permute-start.6 = (bf16[512,256]{1,0:T(8,128)(2,1)}, bf16[512,256]{1,0:T(8,128)(2,1)}, u32[]{:S(2)}, u32[]{:S(2)}) collective-permute-start(bf16[512,256]{1,0:T(8,128)(2,1)} %stage.7), channel_id=1, source_target_pairs={{0,16},{4,20},{8,24},{12,28},{1,17},{5,21},{9,25},{13,29},{2,18},{... | collective-permute-start | bytes 786440 | tf_op jit(solution)/shard_map/ppermute | solution.py:612
  71.9 5.8 %local.7.mine_hbm = bf16[4,768,256]{2,1,0:T(8,128)(2,1)S(1)} custom-call(f32[4]{0:T(128)S(1)} %multiply_sqrt_fusion.scale_ref, s32[1]{0:T(128)} %bitcast.1.core_ref.octet_ref, bf16[4,2,512,16,128]{4,3,2,1,0:T(8,128)(2,1)} %x_hbm.7, bf16[4,2,512,512]{3,2,1,0:T(8,128)(2,1)} %a_hbm.7, bf16[2,64,512]{2,1,0:T(8,128)(2,1)S(1)} %copy-done.6), custom_call_target="tpu_custom_call" | custom-call | flops 1610612736 | bytes 8388608 | tf_op jit(solution)/shard_map/local/pallas_call | solution.py:391
  77.8 3.2 %join_states.4 = (bf16[2,512,256]{2,1,0:T(8,128)(2,1)S(1)}, bf16[512,512]{1,0:T(8,128)(2,1)}) custom-call(s32[1]{0:T(128)} %bitcast.1.core_ref.octet_ref, bf16[4,768,256]{2,1,0:T(8,128)(2,1)S(1)} %local.7.mine_hbm, bf16[4,768,256]{2,1,0:T(8,128)(2,1)} %collective-permute-done.10.other_hbm, bf16[2,768,512]{2,1,0:T(8,128)(2,1)} %copy-done.2, ...), custom_call_target="tpu_custom_call" | custom-call | flops 402653184 | bytes 2097152 | tf_op jit(solution)/shard_map/join_states/pallas_call | solution.py:518
  83.3 3.1 %join_states.5 = (bf16[2,512,256]{2,1,0:T(8,128)(2,1)S(1)}, bf16[512,256]{1,0:T(8,128)(2,1)}, bf16[512,256]{1,0:T(8,128)(2,1)}) custom-call(s32[1]{0:T(128)} %bitcast.1.core_ref.octet_ref, bf16[4,768,256]{2,1,0:T(8,128)(2,1)S(1)} %local.7.mine_hbm, bf16[4,768,256]{2,1,0:T(8,128)(2,1)} %collective-permute-done.10.other_hbm, bf16[2,768,512]{2,1,0:T(8,128)(2,1)} %copy-done.2, ...), custom_call_target="tpu_custom_call" | custom-call | flops 402653184 | bytes 2097152 | tf_op jit(solution)/shard_map/join_states/pallas_call | solution.py:518
  93.5 3.4 %collective-permute-done.11.other_ref.first_ref = bf16[512,512]{1,0:T(8,128)(2,1)} collective-permute-done((bf16[512,512]{1,0:T(8,128)(2,1)}, bf16[512,512]{1,0:T(8,128)(2,1)}, u32[]{:S(2)}, u32[]{:S(2)}) %collective-permute-start.11) | collective-permute-done | bytes 524320 | tf_op jit(solution)/shard_map/ppermute | solution.py:612
  100.0 2.5 %collective-permute-done.13.other_ref.first_ref = bf16[512,256]{1,0:T(8,128)(2,1)} collective-permute-done((bf16[512,256]{1,0:T(8,128)(2,1)}, bf16[512,256]{1,0:T(8,128)(2,1)}, u32[]{:S(2)}, u32[]{:S(2)}) %collective-permute-start.13) | collective-permute-done | bytes 262176 | tf_op jit(solution)/shard_map/ppermute | solution.py:612
  110.0 2.4 %final.6.refs_0_ = f32[2,8,256]{2,1,0:T(8,128)S(1)} custom-call(s32[2]{0:T(128)S(1)} %pad_add_fusion.1.flag_ref, bf16[512,256]{1,0:T(8,128)(2,1)} %collective-permute-done.5.other_ref.first_ref, bf16[512,256]{1,0:T(8,128)(2,1)} %collective-permute-done.6.last_ref, bf16[2,256,512]{2,1,0:T(8,128)(2,1)S(1)} %collective-permute-done.3.part_hbm.refs_0_, ...), custom_call_target="tpu_custom_call" | custom-call | flops 268435456 | bytes 2097152 | tf_op jit(solution)/shard_map/final/pallas_call | solution.py:560
  112.5 10.0 %collective-permute-done.7.last_ref = bf16[512,256]{1,0:T(8,128)(2,1)S(1)} collective-permute-done((bf16[512,256]{1,0:T(8,128)(2,1)S(1)}, bf16[512,256]{1,0:T(8,128)(2,1)S(1)}, u32[]{:S(2)}, u32[]{:S(2)}) %collective-permute-start.7) | collective-permute-done | bytes 262176 | tf_op jit(solution)/shard_map/ppermute | solution.py:612
  124.6 3.1 %final.8.refs_2_ = f32[2,8,512]{2,1,0:T(8,128)S(1)} custom-call(s32[2]{0:T(128)S(1)} %pad_add_fusion.1.flag_ref, bf16[512,512]{1,0:T(8,128)(2,1)} %collective-permute-done.8.other_ref.first_ref, bf16[512,512]{1,0:T(8,128)(2,1)S(1)} %collective-permute-done.9.last_ref, bf16[2,256,512]{2,1,0:T(8,128)(2,1)S(1)} %collective-permute-done.3.part_hbm.refs_0_, ...), custom_call_target="tpu_custom_call" | custom-call | flops 268435456 | bytes 2097152 | tf_op jit(solution)/shard_map/final/pallas_call | solution.py:560
  127.8 2.6 %final.9.refs_3_ = f32[2,8,512]{2,1,0:T(8,128)S(1)} custom-call(s32[2]{0:T(128)S(1)} %pad_add_fusion.1.flag_ref, bf16[512,512]{1,0:T(8,128)(2,1)} %collective-permute-done.11.other_ref.first_ref, bf16[512,512]{1,0:T(8,128)(2,1)S(1)} %collective-permute-done.12.last_ref, bf16[2,256,512]{2,1,0:T(8,128)(2,1)S(1)} %collective-permute-done.3.part_hbm.refs_0_, ...), custom_call_target="tpu_custom_call" | custom-call | flops 268435456 | bytes 2097152 | tf_op jit(solution)/shard_map/final/pallas_call | solution.py:560
  136.0 2.6 %collective-permute-start.19 = (bf16[256,128]{1,0:T(8,128)(2,1)S(1)}, bf16[256,128]{1,0:T(8,128)(2,1)S(1)}, u32[]{:S(2)}, u32[]{:S(2)}) collective-permute-start(bf16[256,128]{1,0:T(8,128)(2,1)S(1)} %pack.1.refs_0_), channel_id=1, source_target_pairs={{0,2},{1,3},{2,0},{3,1},{4,6},{5,7},{6,4},{7,5},{8,10},{9,11},{10,... | collective-permute-start | bytes 196616 | tf_op jit(solution)/shard_map/ppermute | solution.py:675
  144.9 3.6 %collective-permute-done.22 = f32[8,128]{1,0:T(8,128)S(1)} collective-permute-done((f32[8,128]{1,0:T(8,128)S(1)}, f32[8,128]{1,0:T(8,128)S(1)}, u32[]{:S(2)}, u32[]{:S(2)}) %collective-permute-start.22) | collective-permute-done | bytes 4128 | tf_op jit(solution)/shard_map/ppermute | solution.py:703
  148.5 2.5 %collective-permute-start.23 = (f32[8,128]{1,0:T(8,128)S(1)}, f32[8,128]{1,0:T(8,128)S(1)}, u32[]{:S(2)}, u32[]{:S(2)}) collective-permute-start(f32[8,128]{1,0:T(8,128)S(1)} %add.24), channel_id=1, source_target_pairs={{0,16},{4,20},{8,24},{12,28},{16,0},{20,4},{24,8},{28,12},{1,17},{... | collective-permute-start | bytes 12296 | tf_op jit(solution)/shard_map/ppermute | solution.py:703
  (110 shorter events, 43.6 us)
Async XLA Ops:
  5.9 6.5 %collective-permute-start = (bf16[2,768,512]{2,1,0:T(8,128)(2,1)S(1)}, bf16[2,768,512]{2,1,0:T(8,128)(2,1)}, u32[]{:S(2)}, u32[]{:S(2)}) collective-permute-start(bf16[2,768,512]{2,1,0:T(8,128)(2,1)S(1)} %operators.1.mine_ref.operator_hbm), channel_id=1, source_target_pairs={{0,4},{4,0},{8,12},{12,8},{16,20},{20,16},{24,28},{28,24},{1,5},{5... | collective-permute-start | bytes 4718600 | tf_op jit(solution)/shard_map/ppermute | solution.py:412
  12.3 9.5 %collective-permute-start.1 = (bf16[4,768,256]{2,1,0:T(8,128)(2,1)S(1)}, bf16[4,768,256]{2,1,0:T(8,128)(2,1)}, u32[]{:S(2)}, u32[]{:S(2)}) collective-permute-start(bf16[4,768,256]{2,1,0:T(8,128)(2,1)S(1)} %local.4), channel_id=1, source_target_pairs={{0,4},{4,0},{8,12},{12,8},{16,20},{20,16},{24,28},{28,24},{1,5},{5... | collective-permute-start | bytes 4718600 | tf_op jit(solution)/shard_map/ppermute | solution.py:415
  33.1 44.6 %collective-permute-start.10 = (bf16[4,768,256]{2,1,0:T(8,128)(2,1)}, bf16[4,768,256]{2,1,0:T(8,128)(2,1)}, u32[]{:S(2)}, u32[]{:S(2)}) collective-permute-start(bf16[4,768,256]{2,1,0:T(8,128)(2,1)} %local.6), channel_id=1, source_target_pairs={{0,4},{4,0},{8,12},{12,8},{16,20},{20,16},{24,28},{28,24},{1,5},{5... | collective-permute-start | bytes 4718600 | tf_op jit(solution)/shard_map/ppermute | solution.py:629
  33.7 15.1 %collective-permute-start.3 = (bf16[2,256,512]{2,1,0:T(8,128)(2,1)S(1)}, bf16[2,256,512]{2,1,0:T(8,128)(2,1)S(1)}, u32[]{:S(2)}, u32[]{:S(2)}) collective-permute-start(bf16[2,256,512]{2,1,0:T(8,128)(2,1)S(1)} %copy-done.19), channel_id=1, source_target_pairs={{0,8},{4,12},{8,0},{12,4},{16,24},{20,28},{24,16},{28,20},{1,9},{5... | collective-permute-start | bytes 1572872 | tf_op jit(solution)/shard_map/ppermute | solution.py:449
  48.8 15.1 %collective-permute-start.4 = (bf16[2,256,512]{2,1,0:T(8,128)(2,1)S(1)}, bf16[2,256,512]{2,1,0:T(8,128)(2,1)S(1)}, u32[]{:S(2)}, u32[]{:S(2)}) collective-permute-start(bf16[2,256,512]{2,1,0:T(8,128)(2,1)S(1)} %collective-permute-done.3.part_hbm.refs_0_), channel_id=1, source_target_pairs={{0,4},{4,0},{8,12},{12,8},{16,20},{20,16},{24,28},{28,24},{1,5},{5... | collective-permute-start | bytes 1572872 | tf_op jit(solution)/shard_map/ppermute | solution.py:453
  48.8 9.5 %collective-permute-start.5 = (bf16[512,256]{1,0:T(8,128)(2,1)}, bf16[512,256]{1,0:T(8,128)(2,1)}, u32[]{:S(2)}, u32[]{:S(2)}) collective-permute-start(bf16[512,256]{1,0:T(8,128)(2,1)} %get-tuple-element.38.mine_ref), channel_id=1, source_target_pairs={{0,8},{4,12},{8,0},{12,4},{16,24},{20,28},{24,16},{28,20},{1,9},{5... | collective-permute-start | bytes 786440 | tf_op jit(solution)/shard_map/ppermute | solution.py:612
  50.5 13.4 %collective-permute-start.2 = (bf16[512,256]{1,0:T(8,128)(2,1)}, bf16[512,256]{1,0:T(8,128)(2,1)}, u32[]{:S(2)}, u32[]{:S(2)}) collective-permute-start(bf16[512,256]{1,0:T(8,128)(2,1)} %get-tuple-element.34.mine_ref), channel_id=1, source_target_pairs={{0,8},{4,12},{8,0},{12,4},{16,24},{20,28},{24,16},{28,20},{1,9},{5... | collective-permute-start | bytes 786440 | tf_op jit(solution)/shard_map/ppermute | solution.py:612
  51.0 38.4 %collective-permute-start.8 = (bf16[512,512]{1,0:T(8,128)(2,1)}, bf16[512,512]{1,0:T(8,128)(2,1)}, u32[]{:S(2)}, u32[]{:S(2)}) collective-permute-start(bf16[512,512]{1,0:T(8,128)(2,1)} %copy-done.9), channel_id=1, source_target_pairs={{0,8},{4,12},{8,0},{12,4},{16,24},{20,28},{24,16},{28,20},{1,9},{5... | collective-permute-start | bytes 1572872 | tf_op jit(solution)/shard_map/ppermute | solution.py:612
  67.5 41.1 %collective-permute-start.6 = (bf16[512,256]{1,0:T(8,128)(2,1)}, bf16[512,256]{1,0:T(8,128)(2,1)}, u32[]{:S(2)}, u32[]{:S(2)}) collective-permute-start(bf16[512,256]{1,0:T(8,128)(2,1)} %stage.7), channel_id=1, source_target_pairs={{0,16},{4,20},{8,24},{12,28},{1,17},{5,21},{9,25},{13,29},{2,18},{... | collective-permute-start | bytes 786440 | tf_op jit(solution)/shard_map/ppermute | solution.py:612
  81.8 15.1 %collective-permute-start.11 = (bf16[512,512]{1,0:T(8,128)(2,1)}, bf16[512,512]{1,0:T(8,128)(2,1)}, u32[]{:S(2)}, u32[]{:S(2)}) collective-permute-start(bf16[512,512]{1,0:T(8,128)(2,1)} %get-tuple-element.48.mine_ref), channel_id=1, source_target_pairs={{0,8},{4,12},{8,0},{12,4},{16,24},{20,28},{24,16},{28,20},{1,9},{5... | collective-permute-start | bytes 1572872 | tf_op jit(solution)/shard_map/ppermute | solution.py:612
  87.2 15.3 %collective-permute-start.13 = (bf16[512,256]{1,0:T(8,128)(2,1)}, bf16[512,256]{1,0:T(8,128)(2,1)}, u32[]{:S(2)}, u32[]{:S(2)}) collective-permute-start(bf16[512,256]{1,0:T(8,128)(2,1)} %get-tuple-element.51.mine_ref), channel_id=1, source_target_pairs={{0,8},{4,12},{8,0},{12,4},{16,24},{20,28},{24,16},{28,20},{1,9},{5... | collective-permute-start | bytes 786440 | tf_op jit(solution)/shard_map/ppermute | solution.py:612
  87.8 18.2 %collective-permute-start.15 = (bf16[512,256]{1,0:T(8,128)(2,1)}, bf16[512,256]{1,0:T(8,128)(2,1)S(1)}, u32[]{:S(2)}, u32[]{:S(2)}) collective-permute-start(bf16[512,256]{1,0:T(8,128)(2,1)} %get-tuple-element.54.mine_ref), channel_id=1, source_target_pairs={{0,8},{4,12},{8,0},{12,4},{16,24},{20,28},{24,16},{28,20},{1,9},{5... | collective-permute-start | bytes 786440 | tf_op jit(solution)/shard_map/ppermute | solution.py:612
  92.1 32.5 %collective-permute-start.9 = (bf16[512,512]{1,0:T(8,128)(2,1)S(1)}, bf16[512,512]{1,0:T(8,128)(2,1)S(1)}, u32[]{:S(2)}, u32[]{:S(2)}) collective-permute-start(bf16[512,512]{1,0:T(8,128)(2,1)S(1)} %stage.8), channel_id=1, source_target_pairs={{0,16},{4,20},{8,24},{12,28},{1,17},{5,21},{9,25},{13,29},{2,18},{... | collective-permute-start | bytes 1572872 | tf_op jit(solution)/shard_map/ppermute | solution.py:612
  96.9 1.7 %collective-permute-start.17 = (f32[4,4,128]{2,1,0:T(4,128)S(1)}, f32[4,4,128]{2,1,0:T(4,128)S(1)}, u32[]{:S(2)}, u32[]{:S(2)}) collective-permute-start(f32[4,4,128]{2,1,0:T(4,128)S(1)} %broadcast_multiply_fusion), channel_id=1, source_target_pairs={{0,4},{4,0},{8,12},{12,8},{16,20},{20,16},{24,28},{28,24},{1,5},{5... | collective-permute-start | bytes 24584 | tf_op jit(solution)/shard_map/ppermute | solution.py:647
  98.6 29.1 %collective-permute-start.12 = (bf16[512,512]{1,0:T(8,128)(2,1)S(1)}, bf16[512,512]{1,0:T(8,128)(2,1)S(1)}, u32[]{:S(2)}, u32[]{:S(2)}) collective-permute-start(bf16[512,512]{1,0:T(8,128)(2,1)S(1)} %stage.9), channel_id=1, source_target_pairs={{0,16},{4,20},{8,24},{12,28},{1,17},{5,21},{9,25},{13,29},{2,18},{... | collective-permute-start | bytes 1572872 | tf_op jit(solution)/shard_map/ppermute | solution.py:612
  102.5 19.9 %collective-permute-start.7 = (bf16[512,256]{1,0:T(8,128)(2,1)S(1)}, bf16[512,256]{1,0:T(8,128)(2,1)S(1)}, u32[]{:S(2)}, u32[]{:S(2)}) collective-permute-start(bf16[512,256]{1,0:T(8,128)(2,1)S(1)} %copy-done.14), channel_id=1, source_target_pairs={{0,16},{4,20},{8,24},{12,28},{1,17},{5,21},{9,25},{13,29},{2,18},{... | collective-permute-start | bytes 786440 | tf_op jit(solution)/shard_map/ppermute | solution.py:612
  106.0 24.4 %collective-permute-start.14 = (bf16[512,256]{1,0:T(8,128)(2,1)S(1)}, bf16[512,256]{1,0:T(8,128)(2,1)S(1)}, u32[]{:S(2)}, u32[]{:S(2)}) collective-permute-start(bf16[512,256]{1,0:T(8,128)(2,1)S(1)} %stage.10), channel_id=1, source_target_pairs={{0,16},{4,20},{8,24},{12,28},{1,17},{5,21},{9,25},{13,29},{2,18},{... | collective-permute-start | bytes 786440 | tf_op jit(solution)/shard_map/ppermute | solution.py:612
  108.6 23.9 %collective-permute-start.16 = (bf16[512,256]{1,0:T(8,128)(2,1)S(1)}, bf16[512,256]{1,0:T(8,128)(2,1)S(1)}, u32[]{:S(2)}, u32[]{:S(2)}) collective-permute-start(bf16[512,256]{1,0:T(8,128)(2,1)S(1)} %stage.11), channel_id=1, source_target_pairs={{0,16},{4,20},{8,24},{12,28},{1,17},{5,21},{9,25},{13,29},{2,18},{... | collective-permute-start | bytes 786440 | tf_op jit(solution)/shard_map/ppermute | solution.py:612
  134.3 6.1 %collective-permute-start.18 = (bf16[256,128]{1,0:T(8,128)(2,1)S(1)}, bf16[256,128]{1,0:T(8,128)(2,1)S(1)}, u32[]{:S(2)}, u32[]{:S(2)}) collective-permute-start(bf16[256,128]{1,0:T(8,128)(2,1)S(1)} %pack.1.refs_0_), channel_id=1, source_target_pairs={{0,1},{1,2},{2,3},{3,0},{4,5},{5,6},{6,7},{7,4},{8,9},{9,10},{10,1... | collective-permute-start | bytes 196616 | tf_op jit(solution)/shard_map/ppermute | solution.py:675
  136.0 5.2 %collective-permute-start.19 = (bf16[256,128]{1,0:T(8,128)(2,1)S(1)}, bf16[256,128]{1,0:T(8,128)(2,1)S(1)}, u32[]{:S(2)}, u32[]{:S(2)}) collective-permute-start(bf16[256,128]{1,0:T(8,128)(2,1)S(1)} %pack.1.refs_0_), channel_id=1, source_target_pairs={{0,2},{1,3},{2,0},{3,1},{4,6},{5,7},{6,4},{7,5},{8,10},{9,11},{10,... | collective-permute-start | bytes 196616 | tf_op jit(solution)/shard_map/ppermute | solution.py:675
  138.5 4.3 %collective-permute-start.20 = (bf16[256,128]{1,0:T(8,128)(2,1)S(1)}, bf16[256,128]{1,0:T(8,128)(2,1)S(1)}, u32[]{:S(2)}, u32[]{:S(2)}) collective-permute-start(bf16[256,128]{1,0:T(8,128)(2,1)S(1)} %pack.1.refs_0_), channel_id=1, source_target_pairs={{0,3},{1,0},{2,1},{3,2},{4,7},{5,4},{6,5},{7,6},{8,11},{9,8},{10,9... | collective-permute-start | bytes 196616 | tf_op jit(solution)/shard_map/ppermute | solution.py:675
  143.7 1.2 collective-permute-start.21
  144.9 3.6 %collective-permute-start.22 = (f32[8,128]{1,0:T(8,128)S(1)}, f32[8,128]{1,0:T(8,128)S(1)}, u32[]{:S(2)}, u32[]{:S(2)}) collective-permute-start(f32[8,128]{1,0:T(8,128)S(1)} %fusion.4), channel_id=1, source_target_pairs={{0,8},{4,12},{8,0},{12,4},{16,24},{20,28},{24,16},{28,20},{1,9},{5... | collective-permute-start | bytes 12296 | tf_op jit(solution)/shard_map/ppermute | solution.py:703
  148.5 4.1 %collective-permute-start.23 = (f32[8,128]{1,0:T(8,128)S(1)}, f32[8,128]{1,0:T(8,128)S(1)}, u32[]{:S(2)}, u32[]{:S(2)}) collective-permute-start(f32[8,128]{1,0:T(8,128)S(1)} %add.24), channel_id=1, source_target_pairs={{0,16},{4,20},{8,24},{12,28},{16,0},{20,4},{24,8},{28,12},{1,17},{... | collective-permute-start | bytes 12296 | tf_op jit(solution)/shard_map/ppermute | solution.py:703
  (21 other events, 255.4 us)
